TPU v7x, 32 devices: a whole 2x2x4 slice. The times are simulated.
32 devices in a mesh: ctx: 16 (over z, y, x), fsdp: 2 (over core).
Axes of the slice: x: 2, y: 2, z: 4, core: 2. Of those that a mesh axis runs over, the one named last changes fastest.
Arguments:
- post_stream: float32 [2, 8192, 512], P('fsdp', 'ctx'), may hold values from -6 to 6
- sum_stream: float32 [2, 8192, 512], P('fsdp', 'ctx'), may hold values from -6 to 6
- cotangent: float32 [2, 8192, 512], P('fsdp', 'ctx'), may hold values from -6 to 6
- block_order: int32 [2, 32], P('fsdp'), may hold values from 0 to 31, as said below
- block_sequence: int32 [2, 32], P('fsdp'), may hold values from 0 to 5, never falling along the last dimension, each value on 1 to 8 neighbouring positions
- query_weight: bfloat16 [512, 512], P(None, 'fsdp'), may hold values from -0.5 to 0.5
- key_weight: bfloat16 [512, 512], P(None, 'fsdp'), may hold values from -0.25 to 0.25
- value_weight: bfloat16 [512, 512], P(None, 'fsdp'), may hold values from -0.25 to 0.25
- output_weight: bfloat16 [512, 512], P('fsdp'), may hold values from -1.5 to 1.5
- query_bias: bfloat16 [512], P('fsdp'), may hold values from -3 to 3
- value_bias: bfloat16 [512], P('fsdp'), may hold values from -1.796875 to 1.796875
- output_bias: bfloat16 [512], P('fsdp'), may hold values from -1.796875 to 1.796875
- attend_gain: bfloat16 [512], P('fsdp'), may hold values from 0.5 to 1.5
- attend_shift: bfloat16 [512], P('fsdp'), may hold values from -1.796875 to 1.796875
- expand_weight: bfloat16 [512, 2048], P(None, 'fsdp'), may hold values from -0.25 to 0.25
- expand_bias: bfloat16 [2048], P('fsdp'), may hold values from -1.796875 to 1.796875
- shrink_weight: bfloat16 [2048, 512], P('fsdp'), may hold values from -0.1875 to 0.1875
- shrink_bias: bfloat16 [512], P('fsdp'), may hold values from -1.796875 to 1.796875
- middle_gain: bfloat16 [512], P('fsdp'), may hold values from 0.5 to 1.5
- middle_shift: bfloat16 [512], P('fsdp'), may hold values from -1.796875 to 1.796875
- final_gain: bfloat16 [512], P('fsdp'), may hold values from 0.5 to 1.5
- final_shift: bfloat16 [512], P('fsdp'), may hold values from -1.796875 to 1.796875
Outputs:
- layer_output: float32 [2, 8192, 512], P('fsdp', 'ctx')
- post_tangent: float32 [2, 8192, 512], P('fsdp', 'ctx')
- sum_tangent: float32 [2, 8192, 512], P('fsdp', 'ctx')
- query_slope: float32 [512, 512], P(None, 'fsdp')
- key_slope: float32 [512, 512], P(None, 'fsdp')
- value_slope: float32 [512, 512], P(None, 'fsdp')
- output_slope: float32 [512, 512], P('fsdp')
- query_drift: float32 [512], P('fsdp')
- value_drift: float32 [512], P('fsdp')
- output_drift: float32 [512], P('fsdp')
- attend_stretch: float32 [512], P('fsdp')
- attend_nudge: float32 [512], P('fsdp')
- expand_slope: float32 [512, 2048], P(None, 'fsdp')
- expand_drift: float32 [2048], P('fsdp')
- shrink_slope: float32 [2048, 512], P('fsdp')
- shrink_drift: float32 [512], P('fsdp')
- middle_stretch: float32 [512], P('fsdp')
- middle_nudge: float32 [512], P('fsdp')
- final_stretch: float32 [512], P('fsdp')
- final_nudge: float32 [512], P('fsdp')
Inputs may be any that keep to these rules, and one draw needn't show every extreme that they name: `block_order`: in each group, ctx device c holds layout blocks 2 c and 2 c + 1, and these hold blocks b and 31 - b of the group for some b, in either order; every block is held once. `block_sequence`: never falls along a group's blocks; every sequence has 1 to 8 blocks and one has exactly 8.
All inputs are finite; a program needn't handle non-finite values.
Results may differ from a plain program's by a relative error of at most 0.02.
The roundings to bfloat16 on the way count: a program that leaves them out, or rounds other values in their place, can miss the bound.
Values may be sent and summed in bfloat16 or wider, within the bound.
A program may use at most 448 MiB of HBM per device.

v0:
```python
import jax
import jax.numpy as jnp
from jax import lax
from jax.sharding import PartitionSpec as P

D = 512
H = 8
HD = 64
BLK = 256


norm_eps = 1e-05
masked_value = -1e30
gelu_coeff = 0.7978845608
gelu_cubic = 0.044715


def smooth_gate(values):
    return (
        0.5
        * values
        * (1.0 + jnp.tanh(gelu_coeff * (values + gelu_cubic * values * values * values)))
    )


def layer_norm(inputs, gain_row, shift_row):
    centre = inputs - jnp.mean(inputs, axis=-1, keepdims=True)
    spread = jnp.mean(centre * centre, axis=-1, keepdims=True)
    return centre * lax.rsqrt(spread + norm_eps) * gain_row + shift_row


def product(left_side, right_side):
    return jnp.dot(left_side, right_side, preferred_element_type=jnp.float32)


def cross_rows(left_side, right_side):
    return lax.dot_general(
        left_side, right_side, (((0,), (0,)), ((), ())), preferred_element_type=jnp.float32
    )


def cross_cols(left_side, right_side):
    return lax.dot_general(
        left_side, right_side, (((1,), (1,)), ((), ())), preferred_element_type=jnp.float32
    )


def column_total(values):
    return jnp.sum(values, axis=0, dtype=jnp.float32)


def lookup(table_row, indices):
    places = jnp.arange(table_row.shape[0], dtype=jnp.int32)
    return jnp.sum(jnp.where(indices[:, None] == places[None, :], table_row[None, :], 0), axis=1)


def block_mask(query_blocks, query_seqs, key_blocks, key_seqs):
    same_seq = query_seqs[:, None] == key_seqs[None, :]
    return same_seq & (key_blocks[None, :] <= query_blocks[:, None])


def token_mask(visible):
    return jnp.repeat(jnp.repeat(visible, BLK, axis=0), BLK, axis=1)


def fold_units(carried, members, unit_step):
    unit_count = members[0].shape[0] // BLK
    inner_count = max((divisor for divisor in range(1, 17) if unit_count % divisor == 0))
    outer_count = unit_count // inner_count

    def outer_turn(outer_index, current):

        def inner_turn(inner_index, inner_state):
            offset = (outer_index * inner_count + inner_index) * BLK
            pieces = tuple((lax.dynamic_slice_in_dim(member, offset, BLK, 0) for member in members))
            return unit_step(inner_state, pieces, offset)

        return lax.fori_loop(0, inner_count, inner_turn, current)

    return lax.fori_loop(0, outer_count, outer_turn, carried)


def shards(
    post_stream,
    sum_stream,
    cotangent,
    block_order,
    block_sequence,
    query_weight,
    key_weight,
    value_weight,
    output_weight,
    query_bias,
    value_bias,
    output_bias,
    attend_gain,
    attend_shift,
    expand_weight,
    expand_bias,
    shrink_weight,
    shrink_bias,
    middle_gain,
    middle_shift,
    final_gain,
    final_shift,
):
    (
        query_whole,
        key_whole,
        value_whole,
        output_whole,
        query_add,
        value_add,
        output_add,
        gain_one,
        shift_one,
        expand_whole,
        expand_add,
        shrink_whole,
        shrink_add,
        gain_two,
        shift_two,
        gain_last,
        shift_last,
    ) = (
        lax.all_gather(query_weight, "fsdp", axis=1, tiled=True),
        lax.all_gather(key_weight, "fsdp", axis=1, tiled=True),
        lax.all_gather(value_weight, "fsdp", axis=1, tiled=True),
        lax.all_gather(output_weight, "fsdp", axis=0, tiled=True),
        lax.all_gather(query_bias, "fsdp", axis=0, tiled=True),
        lax.all_gather(value_bias, "fsdp", axis=0, tiled=True),
        lax.all_gather(output_bias, "fsdp", axis=0, tiled=True),
        lax.all_gather(attend_gain, "fsdp", axis=0, tiled=True),
        lax.all_gather(attend_shift, "fsdp", axis=0, tiled=True),
        lax.all_gather(expand_weight, "fsdp", axis=1, tiled=True),
        lax.all_gather(expand_bias, "fsdp", axis=0, tiled=True),
        lax.all_gather(shrink_weight, "fsdp", axis=0, tiled=True),
        lax.all_gather(shrink_bias, "fsdp", axis=0, tiled=True),
        lax.all_gather(middle_gain, "fsdp", axis=0, tiled=True),
        lax.all_gather(middle_shift, "fsdp", axis=0, tiled=True),
        lax.all_gather(final_gain, "fsdp", axis=0, tiled=True),
        lax.all_gather(final_shift, "fsdp", axis=0, tiled=True),
    )
    post_rows = post_stream[0]
    summed = sum_stream[0]
    tangent = cotangent[0]
    order_row = block_order[0]
    seq_row = block_sequence[0]
    token_count = post_rows.shape[0]
    score_scale = HD ** (-0.5)
    own_blocks = lax.dynamic_slice_in_dim(
        order_row, lax.axis_index("ctx") * (token_count // BLK), token_count // BLK
    )
    own_seqs = lookup(seq_row, own_blocks)
    post_low = post_rows.astype(jnp.bfloat16)
    queries = (product(post_low, query_whole) + query_add).astype(jnp.bfloat16)
    key_rows = product(post_low, key_whole).astype(jnp.bfloat16)
    value_rows = (product(post_low, value_whole) + value_add).astype(jnp.bfloat16)
    query_heads = queries.reshape(token_count, H, HD)

    def keys_visible(first_row):
        key_block = lax.dynamic_slice_in_dim(order_row, first_row // BLK, 1)
        return block_mask(own_blocks, own_seqs, key_block, lookup(seq_row, key_block))

    def masked_fold(block_step):

        def unit_step(current, pieces, first_row):
            visible = keys_visible(first_row)
            return lax.cond(
                jnp.any(visible),
                lambda inner_state: block_step(inner_state, pieces, visible),
                lambda inner_state: inner_state,
                current,
            )

        def folded(current, pieces, first_row):
            return fold_units(current, pieces, unit_step)

        return folded

    def stats_block(current, pieces, visible):
        row_peaks, masses = current
        key_heads = pieces[0].reshape(BLK, H, HD)
        row_mask = token_mask(visible)[None]
        scores = (
            jnp.einsum("qhd,khd->hqk", query_heads, key_heads, preferred_element_type=jnp.float32)
            * score_scale
        )
        new_peaks = jnp.maximum(
            row_peaks, jnp.max(jnp.where(row_mask, scores, masked_value), axis=2)
        )
        weights = jnp.where(row_mask, jnp.exp(scores - new_peaks[:, :, None]), 0.0)
        return (new_peaks, masses * jnp.exp(row_peaks - new_peaks) + jnp.sum(weights, axis=2))

    stats_fold = masked_fold(stats_block)
    stats_start = (
        jnp.full((H, token_count), masked_value, jnp.float32),
        jnp.zeros((H, token_count), jnp.float32),
    )
    row_peaks, masses = stats_fold(
        stats_start, (lax.all_gather(key_rows, "ctx", axis=0, tiled=True),), jnp.int32(0)
    )
    log_mass = row_peaks + jnp.log(masses)

    def forward_block(current, pieces, visible):
        key_heads = pieces[0].reshape(BLK, H, HD)
        value_heads = pieces[1].reshape(BLK, H, HD)
        row_mask = token_mask(visible)[None]
        scores = (
            jnp.einsum("qhd,khd->hqk", query_heads, key_heads, preferred_element_type=jnp.float32)
            * score_scale
        )
        weights = jnp.where(row_mask, jnp.exp(scores - log_mass[:, :, None]), 0.0).astype(
            jnp.bfloat16
        )
        addition = jnp.einsum(
            "hqk,khd->qhd", weights, value_heads, preferred_element_type=jnp.float32
        )
        return current + addition.reshape(token_count, D)

    forward_fold = masked_fold(forward_block)
    zero_rows = jnp.zeros((token_count, D), jnp.float32)
    attended = forward_fold(
        zero_rows,
        (
            lax.all_gather(key_rows, "ctx", axis=0, tiled=True),
            lax.all_gather(value_rows, "ctx", axis=0, tiled=True),
        ),
        jnp.int32(0),
    )
    mixed_low = attended.astype(jnp.bfloat16)
    branch = product(mixed_low, output_whole) + output_add
    normed_one, first_pull = jax.vjp(
        layer_norm, post_rows + branch, gain_one.astype(jnp.float32), shift_one.astype(jnp.float32)
    )
    stream_one = summed + branch
    normed_low = normed_one.astype(jnp.bfloat16)
    before = product(normed_low, expand_whole) + expand_add
    gated, gate_pull = jax.vjp(smooth_gate, before)
    hidden = gated.astype(jnp.bfloat16)
    feed_out = product(hidden, shrink_whole) + shrink_add
    normed_two, middle_pull = jax.vjp(
        layer_norm,
        normed_one + feed_out,
        gain_two.astype(jnp.float32),
        shift_two.astype(jnp.float32),
    )
    stream_two = stream_one + feed_out
    last_norm, last_pull = jax.vjp(
        layer_norm, stream_two, gain_last.astype(jnp.float32), shift_last.astype(jnp.float32)
    )
    layer_output = normed_two + last_norm
    stream_tan, stretch_last, nudge_last = last_pull(tangent)
    inflow_tan, stretch_two, nudge_two = middle_pull(tangent)
    feed_tan = (stream_tan + inflow_tan).astype(jnp.bfloat16)
    slope_shrink = cross_rows(hidden, feed_tan)
    drift_shrink = column_total(feed_tan)
    before_tan = gate_pull(cross_cols(feed_tan, shrink_whole))[0].astype(jnp.bfloat16)
    slope_expand = cross_rows(normed_low, before_tan)
    drift_expand = column_total(before_tan)
    normed_tan = inflow_tan + cross_cols(before_tan, expand_whole)
    feed_parts = lax.psum(
        (
            slope_expand,
            drift_expand,
            slope_shrink,
            drift_shrink,
            stretch_two,
            nudge_two,
            stretch_last,
            nudge_last,
        ),
        "ctx",
    )
    feed_sums = (
        lax.psum_scatter(feed_parts[0], "fsdp", scatter_dimension=1, tiled=True),
        lax.psum_scatter(feed_parts[1], "fsdp", scatter_dimension=0, tiled=True),
        lax.psum_scatter(feed_parts[2], "fsdp", scatter_dimension=0, tiled=True),
        lax.psum_scatter(feed_parts[3], "fsdp", scatter_dimension=0, tiled=True),
        lax.psum_scatter(feed_parts[4], "fsdp", scatter_dimension=0, tiled=True),
        lax.psum_scatter(feed_parts[5], "fsdp", scatter_dimension=0, tiled=True),
        lax.psum_scatter(feed_parts[6], "fsdp", scatter_dimension=0, tiled=True),
        lax.psum_scatter(feed_parts[7], "fsdp", scatter_dimension=0, tiled=True),
    )
    entry_tan, stretch_one, nudge_one = first_pull(normed_tan)
    branch_tan = (stream_tan + entry_tan).astype(jnp.bfloat16)
    slope_output = cross_rows(mixed_low, branch_tan)
    drift_output = column_total(branch_tan)
    mixed_tan = cross_cols(branch_tan, output_whole).astype(jnp.bfloat16)
    tangent_heads = mixed_tan.reshape(token_count, H, HD)
    deltas = jnp.sum((mixed_tan * attended).reshape(token_count, H, HD), axis=2).T

    def query_block(current, pieces, visible):
        key_heads = pieces[0].reshape(BLK, H, HD)
        value_heads = pieces[1].reshape(BLK, H, HD)
        row_mask = token_mask(visible)[None]
        scores = (
            jnp.einsum("qhd,khd->hqk", query_heads, key_heads, preferred_element_type=jnp.float32)
            * score_scale
        )
        probability = jnp.where(row_mask, jnp.exp(scores - log_mass[:, :, None]), 0.0)
        prob_tan = jnp.einsum(
            "qhd,khd->hqk", tangent_heads, value_heads, preferred_element_type=jnp.float32
        )
        score_tan = (probability * (prob_tan - deltas[:, :, None])).astype(jnp.bfloat16)
        addition = jnp.einsum(
            "hqk,khd->qhd", score_tan, key_heads, preferred_element_type=jnp.float32
        )
        return current + addition.reshape(token_count, D) * score_scale

    query_fold = masked_fold(query_block)
    query_sum = query_fold(
        zero_rows,
        (
            lax.all_gather(key_rows, "ctx", axis=0, tiled=True),
            lax.all_gather(value_rows, "ctx", axis=0, tiled=True),
        ),
        jnp.int32(0),
    )
    gathered_mass, gathered_delta = (
        lax.all_gather(log_mass.T, "ctx", axis=0, tiled=True),
        lax.all_gather(deltas.T, "ctx", axis=0, tiled=True),
    )
    own_keys = key_rows.reshape(token_count, H, HD)
    own_values = value_rows.reshape(token_count, H, HD)

    def owner_block(current, pieces, first_row, visible):
        key_acc, value_acc = current
        part_queries = pieces[0].reshape(BLK, H, HD)
        part_tangent = pieces[1].reshape(BLK, H, HD)
        part_mass = lax.dynamic_slice_in_dim(gathered_mass, first_row, BLK, 0).T
        part_delta = lax.dynamic_slice_in_dim(gathered_delta, first_row, BLK, 0).T
        row_mask = token_mask(visible)[None]
        scores = (
            jnp.einsum("qhd,khd->hqk", part_queries, own_keys, preferred_element_type=jnp.float32)
            * score_scale
        )
        probability = jnp.where(row_mask, jnp.exp(scores - part_mass[:, :, None]), 0.0)
        value_add_rows = jnp.einsum(
            "hqk,qhd->khd",
            probability.astype(jnp.bfloat16),
            part_tangent,
            preferred_element_type=jnp.float32,
        )
        prob_tan = jnp.einsum(
            "qhd,khd->hqk", part_tangent, own_values, preferred_element_type=jnp.float32
        )
        score_tan = (probability * (prob_tan - part_delta[:, :, None])).astype(jnp.bfloat16)
        key_add_rows = jnp.einsum(
            "hqk,qhd->khd", score_tan, part_queries, preferred_element_type=jnp.float32
        )
        return (
            key_acc + key_add_rows.reshape(token_count, D) * score_scale,
            value_acc + value_add_rows.reshape(token_count, D),
        )

    def owner_unit(current, pieces, first_row):
        query_blocks = lax.dynamic_slice_in_dim(order_row, first_row // BLK, 1)
        visible = block_mask(query_blocks, lookup(seq_row, query_blocks), own_blocks, own_seqs)
        return lax.cond(
            jnp.any(visible),
            lambda inner_state: owner_block(inner_state, pieces, first_row, visible),
            lambda inner_state: inner_state,
            current,
        )

    key_sum, value_sum = fold_units(
        (zero_rows, zero_rows),
        (
            lax.all_gather(queries, "ctx", axis=0, tiled=True),
            lax.all_gather(mixed_tan, "ctx", axis=0, tiled=True),
        ),
        owner_unit,
    )
    query_tan = query_sum.astype(jnp.bfloat16)
    key_tan = key_sum.astype(jnp.bfloat16)
    value_tan = value_sum.astype(jnp.bfloat16)
    slope_query = cross_rows(post_low, query_tan)
    slope_key = cross_rows(post_low, key_tan)
    slope_value = cross_rows(post_low, value_tan)
    drift_query = column_total(query_tan)
    drift_value = column_total(value_tan)
    post_tangent = (
        entry_tan
        + cross_cols(query_tan, query_whole)
        + cross_cols(key_tan, key_whole)
        + cross_cols(value_tan, value_whole)
    )
    heads_parts = lax.psum(
        (
            slope_query,
            slope_key,
            slope_value,
            slope_output,
            drift_query,
            drift_value,
            drift_output,
            stretch_one,
            nudge_one,
        ),
        "ctx",
    )
    heads_sums = (
        lax.psum_scatter(heads_parts[0], "fsdp", scatter_dimension=1, tiled=True),
        lax.psum_scatter(heads_parts[1], "fsdp", scatter_dimension=1, tiled=True),
        lax.psum_scatter(heads_parts[2], "fsdp", scatter_dimension=1, tiled=True),
        lax.psum_scatter(heads_parts[3], "fsdp", scatter_dimension=0, tiled=True),
        lax.psum_scatter(heads_parts[4], "fsdp", scatter_dimension=0, tiled=True),
        lax.psum_scatter(heads_parts[5], "fsdp", scatter_dimension=0, tiled=True),
        lax.psum_scatter(heads_parts[6], "fsdp", scatter_dimension=0, tiled=True),
        lax.psum_scatter(heads_parts[7], "fsdp", scatter_dimension=0, tiled=True),
        lax.psum_scatter(heads_parts[8], "fsdp", scatter_dimension=0, tiled=True),
    )
    return (
        layer_output[None],
        post_tangent[None],
        stream_tan[None],
        heads_sums[0],
        heads_sums[1],
        heads_sums[2],
        heads_sums[3],
        heads_sums[4],
        heads_sums[5],
        heads_sums[6],
        heads_sums[7],
        heads_sums[8],
        feed_sums[0],
        feed_sums[1],
        feed_sums[2],
        feed_sums[3],
        feed_sums[4],
        feed_sums[5],
        feed_sums[6],
        feed_sums[7],
    )


def solution(mesh):
    return jax.shard_map(
        shards,
        mesh=mesh,
        in_specs=(
            P("fsdp", "ctx", None),
            P("fsdp", "ctx", None),
            P("fsdp", "ctx", None),
            P("fsdp", None),
            P("fsdp", None),
            P(None, "fsdp"),
            P(None, "fsdp"),
            P(None, "fsdp"),
            P("fsdp", None),
            P("fsdp"),
            P("fsdp"),
            P("fsdp"),
            P("fsdp"),
            P("fsdp"),
            P(None, "fsdp"),
            P("fsdp"),
            P("fsdp", None),
            P("fsdp"),
            P("fsdp"),
            P("fsdp"),
            P("fsdp"),
            P("fsdp"),
        ),
        out_specs=(
            P("fsdp", "ctx", None),
            P("fsdp", "ctx", None),
            P("fsdp", "ctx", None),
            P(None, "fsdp"),
            P(None, "fsdp"),
            P(None, "fsdp"),
            P("fsdp", None),
            P("fsdp"),
            P("fsdp"),
            P("fsdp"),
            P("fsdp"),
            P("fsdp"),
            P(None, "fsdp"),
            P("fsdp"),
            P("fsdp", None),
            P("fsdp"),
            P("fsdp"),
            P("fsdp"),
            P("fsdp"),
            P("fsdp"),
        ),
        check_vma=False,
    )
```

profile of v0, /device:TPU:0, one launch (start us, length us, event | category | flops | bytes accessed | tf_op | source)
XLA Modules:
  0.0 1610.4 jit_solution(8198847559941156815)
XLA Ops:
  52.0 85.8 %all-gather.17.cloned.1.call-done = bf16[8192,512]{0,1:T(8,128)(2,1)} async-done(((bf16[512,512]{0,1:T(8,128)(2,1)}), bf16[8192,512]{0,1:T(8,128)(2,1)}) %all-gather.17.cloned.1.call-update) | async-done | bytes 8388624 | tf_op jit(solution)/shard_map/all_gather | solution.py:226
  137.9 165.5 %while.191 = (s32[]{:T(128)}, f32[8,512]{1,0:T(8,128)S(1)}, f32[8,512]{1,0:T(8,128)S(1)}, s32[32]{0:T(128)S(1)}, s32[1,32]{1,0:T(1,128)S(1)}, /*index=5*/s32[2]{...) while((s32[]{:T(128)}, f32[8,512]{1,0:T(8,128)S(1)}, ...), condition=%wide.region_10.11_spmd, body=%wide.region_1.10_spmd.sunk | while | flops 141566080 | bytes 9915969 | solution.py:80
  137.9 93.3 %while.198 = (s32[]{:T(128)}, f32[8,512]{1,0:T(8,128)S(1)}, f32[8,512]{1,0:T(8,128)S(1)}, s32[]{:T(128)}, s32[32]{0:T(128)S(1)}, /*index=5*/s32[1,32]{1,0:T(1,12...) while((s32[]{:T(128)}, f32[8,512]{1,0:T(8,128)S(1)}, ...), condition=%wide.region_9.9_spmd, body=%wide.region_2.8_spmd.sunk | while | flops 141566080 | bytes 9915608 | solution.py:78
  231.2 72.2 %while.198 = (s32[]{:T(128)}, f32[8,512]{1,0:T(8,128)S(1)}, f32[8,512]{1,0:T(8,128)S(1)}, s32[]{:T(128)}, s32[32]{0:T(128)S(1)}, /*index=5*/s32[1,32]{1,0:T(1,12...) while((s32[]{:T(128)}, f32[8,512]{1,0:T(8,128)S(1)}, ...), condition=%wide.region_9.9_spmd, body=%wide.region_2.8_spmd.sunk | while | flops 141566080 | bytes 9915608 | solution.py:78
  303.5 165.6 %while.193 = (s32[]{:T(128)}, f32[512,512]{0,1:T(8,128)S(1)}, s32[32]{0:T(128)S(1)}, s32[1,32]{1,0:T(1,128)S(1)}, s32[2]{0:T(128)S(1)}, /*index=5*/s32[2]{0:T(12...) while((s32[]{:T(128)}, f32[512,512]{0,1:T(8,128)S(1)}, ...), condition=%wide.region_18.19_spmd, body=%wide.region_11.18_spmd.sunk | while | flops 272892032 | bytes 6310953 | solution.py:80
  303.6 93.4 %while.199 = (s32[]{:T(128)}, f32[512,512]{0,1:T(8,128)S(1)}, s32[]{:T(128)}, s32[32]{0:T(128)S(1)}, s32[1,32]{1,0:T(1,128)S(1)}, /*index=5*/s32[2]{0:T(128)S(1)...) while((s32[]{:T(128)}, f32[512,512]{0,1:T(8,128)S(1)}, ...), condition=%wide.region_17.17_spmd, body=%wide.region_12.16_spmd.sunk | while | flops 272892032 | bytes 6310600 | solution.py:78
  397.0 72.2 %while.199 = (s32[]{:T(128)}, f32[512,512]{0,1:T(8,128)S(1)}, s32[]{:T(128)}, s32[32]{0:T(128)S(1)}, s32[1,32]{1,0:T(1,128)S(1)}, /*index=5*/s32[2]{0:T(128)S(1)...) while((s32[]{:T(128)}, f32[512,512]{0,1:T(8,128)S(1)}, ...), condition=%wide.region_17.17_spmd, body=%wide.region_12.16_spmd.sunk | while | flops 272892032 | bytes 6310600 | solution.py:78
  472.3 5.2 fusion.53
  477.5 5.7 fusion.60
  489.5 5.1 convert_reduce_fusion
  500.4 204.2 %while.195 = (s32[]{:T(128)}, f32[512,512]{0,1:T(8,128)S(1)}, s32[32]{0:T(128)S(1)}, s32[1,32]{1,0:T(1,128)S(1)}, s32[2]{0:T(128)S(1)}, /*index=5*/s32[2]{0:T(12...) while((s32[]{:T(128)}, f32[512,512]{0,1:T(8,128)S(1)}, ...), condition=%wide.region_39.40_spmd, body=%wide.region_32.39_spmd.sunk | while | flops 409469056 | bytes 15502441 | solution.py:80
  500.4 132.0 %while.200 = (s32[]{:T(128)}, f32[512,512]{0,1:T(8,128)S(1)}, s32[]{:T(128)}, s32[32]{0:T(128)S(1)}, s32[1,32]{1,0:T(1,128)S(1)}, /*index=5*/s32[2]{0:T(128)S(1)...) while((s32[]{:T(128)}, f32[512,512]{0,1:T(8,128)S(1)}, ...), condition=%wide.region_38.38_spmd, body=%wide.region_33.37_spmd.sunk | while | flops 409469056 | bytes 15502056 | solution.py:78
  504.9 12.0 conditional.9
  521.3 12.0 conditional.9
  551.3 12.0 conditional.9
  556.8 5.0 fusion.6
  594.8 12.0 conditional.9
  620.4 12.0 conditional.9
  632.4 72.1 %while.200 = (s32[]{:T(128)}, f32[512,512]{0,1:T(8,128)S(1)}, s32[]{:T(128)}, s32[32]{0:T(128)S(1)}, s32[1,32]{1,0:T(1,128)S(1)}, /*index=5*/s32[2]{0:T(128)S(1)...) while((s32[]{:T(128)}, f32[512,512]{0,1:T(8,128)S(1)}, ...), condition=%wide.region_38.38_spmd, body=%wide.region_33.37_spmd.sunk | while | flops 409469056 | bytes 15502056 | solution.py:78
  710.1 5.2 fusion.51
  715.4 6.2 fusion.55
  721.7 178.8 %all_gather.94 = f32[8192,8]{0,1:T(8,128)S(1)} all-gather(f32[512,8]{0,1:T(8,128)S(1)} %bitcast.165), channel_id=1, replica_groups=mesh['ctx'=16,'fsdp'=2] {'ctx'}, dimensions={0}, use_global_device_ids=true | all-gather | bytes 278528 | tf_op jit(solution)/shard_map/all_gather | solution.py:322
  900.5 39.2 %all_gather.92 = f32[8192,8]{0,1:T(8,128)} all-gather(f32[512,8]{0,1:T(8,128)S(1)} %bitcast.166), channel_id=1, replica_groups=mesh['ctx'=16,'fsdp'=2] {'ctx'}, dimensions={0}, use_global_device_ids=true | all-gather | bytes 278528 | tf_op jit(solution)/shard_map/all_gather | solution.py:321
  939.9 310.9 %while.197 = (s32[]{:T(128)}, f32[512,512]{0,1:T(8,128)S(1)}, f32[512,512]{0,1:T(8,128)S(1)}, s32[32]{0:T(128)S(1)}, s32[1,32]{1,0:T(1,128)S(1)}, /*index=5*/s32...) while((s32[]{:T(128)}, f32[512,512]{0,1:T(8,128)S(1)}, ...), condition=%wide.region_47.48_spmd, body=%wide.region_40.47_spmd.sunk | while | flops 548143232 | bytes 24178388 | solution.py:80
  940.2 201.4 %while.201 = (s32[]{:T(128)}, f32[512,512]{0,1:T(8,128)S(1)}, f32[512,512]{0,1:T(8,128)S(1)}, s32[]{:T(128)}, s32[32]{0:T(128)S(1)}, /*index=5*/s32[1,32]{1,0:T(...) while((s32[]{:T(128)}, f32[512,512]{0,1:T(8,128)S(1)}, ...), condition=%wide.region_46.46_spmd, body=%wide.region_41.45_spmd.sunk | while | flops 548143232 | bytes 24177980 | solution.py:78
  944.7 18.5 %conditional.8 = ((f32[512,512]{0,1:T(8,128)S(1)}, f32[512,512]{0,1:T(8,128)S(1)})) conditional(s32[]{:T(128)} %convert_element_type.256, (f32[512,512]{0,1:T(8,128)S(1)}, f32[512,512]{0,1:T(8,128)S(1)}) %tuple.395, (s32[]{:T(128)}, s32[2]{0:T(128)S(1)}, s32[]{:T(128)}, s32[2]{0:T(128)S(1)}, s32[]{:T(128)}, /*index=5*/pred[]{:T(512)}, ...), branch_computations={%region_44.43_spmd, %region_45.44_spmd} | conditional | flops 548143104 | bytes 24177268 | solution.py:360
  956.0 5.1 fusion.18
  967.7 18.5 %conditional.8 = ((f32[512,512]{0,1:T(8,128)S(1)}, f32[512,512]{0,1:T(8,128)S(1)})) conditional(s32[]{:T(128)} %convert_element_type.256, (f32[512,512]{0,1:T(8,128)S(1)}, f32[512,512]{0,1:T(8,128)S(1)}) %tuple.395, (s32[]{:T(128)}, s32[2]{0:T(128)S(1)}, s32[]{:T(128)}, s32[2]{0:T(128)S(1)}, s32[]{:T(128)}, /*index=5*/pred[]{:T(512)}, ...), branch_computations={%region_44.43_spmd, %region_45.44_spmd} | conditional | flops 548143104 | bytes 24177268 | solution.py:360
  979.0 5.1 fusion.18
  999.7 18.5 %conditional.8 = ((f32[512,512]{0,1:T(8,128)S(1)}, f32[512,512]{0,1:T(8,128)S(1)})) conditional(s32[]{:T(128)} %convert_element_type.256, (f32[512,512]{0,1:T(8,128)S(1)}, f32[512,512]{0,1:T(8,128)S(1)}) %tuple.395, (s32[]{:T(128)}, s32[2]{0:T(128)S(1)}, s32[]{:T(128)}, s32[2]{0:T(128)S(1)}, s32[]{:T(128)}, /*index=5*/pred[]{:T(512)}, ...), branch_computations={%region_44.43_spmd, %region_45.44_spmd} | conditional | flops 548143104 | bytes 24177268 | solution.py:360
  1011.0 5.1 fusion.18
  1027.1 18.5 %conditional.8 = ((f32[512,512]{0,1:T(8,128)S(1)}, f32[512,512]{0,1:T(8,128)S(1)})) conditional(s32[]{:T(128)} %convert_element_type.256, (f32[512,512]{0,1:T(8,128)S(1)}, f32[512,512]{0,1:T(8,128)S(1)}) %tuple.395, (s32[]{:T(128)}, s32[2]{0:T(128)S(1)}, s32[]{:T(128)}, s32[2]{0:T(128)S(1)}, s32[]{:T(128)}, /*index=5*/pred[]{:T(512)}, ...), branch_computations={%region_44.43_spmd, %region_45.44_spmd} | conditional | flops 548143104 | bytes 24177268 | solution.py:360
  1038.5 5.1 fusion.18
  1054.6 18.5 %conditional.8 = ((f32[512,512]{0,1:T(8,128)S(1)}, f32[512,512]{0,1:T(8,128)S(1)})) conditional(s32[]{:T(128)} %convert_element_type.256, (f32[512,512]{0,1:T(8,128)S(1)}, f32[512,512]{0,1:T(8,128)S(1)}) %tuple.395, (s32[]{:T(128)}, s32[2]{0:T(128)S(1)}, s32[]{:T(128)}, s32[2]{0:T(128)S(1)}, s32[]{:T(128)}, /*index=5*/pred[]{:T(512)}, ...), branch_computations={%region_44.43_spmd, %region_45.44_spmd} | conditional | flops 548143104 | bytes 24177268 | solution.py:360
  1066.0 5.1 fusion.18
  1095.7 18.5 %conditional.8 = ((f32[512,512]{0,1:T(8,128)S(1)}, f32[512,512]{0,1:T(8,128)S(1)})) conditional(s32[]{:T(128)} %convert_element_type.256, (f32[512,512]{0,1:T(8,128)S(1)}, f32[512,512]{0,1:T(8,128)S(1)}) %tuple.395, (s32[]{:T(128)}, s32[2]{0:T(128)S(1)}, s32[]{:T(128)}, s32[2]{0:T(128)S(1)}, s32[]{:T(128)}, /*index=5*/pred[]{:T(512)}, ...), branch_computations={%region_44.43_spmd, %region_45.44_spmd} | conditional | flops 548143104 | bytes 24177268 | solution.py:360
  1107.0 5.1 fusion.18
  1118.6 18.5 %conditional.8 = ((f32[512,512]{0,1:T(8,128)S(1)}, f32[512,512]{0,1:T(8,128)S(1)})) conditional(s32[]{:T(128)} %convert_element_type.256, (f32[512,512]{0,1:T(8,128)S(1)}, f32[512,512]{0,1:T(8,128)S(1)}) %tuple.395, (s32[]{:T(128)}, s32[2]{0:T(128)S(1)}, s32[]{:T(128)}, s32[2]{0:T(128)S(1)}, s32[]{:T(128)}, /*index=5*/pred[]{:T(512)}, ...), branch_computations={%region_44.43_spmd, %region_45.44_spmd} | conditional | flops 548143104 | bytes 24177268 | solution.py:360
  1130.0 5.1 fusion.18
  1141.6 109.1 %while.201 = (s32[]{:T(128)}, f32[512,512]{0,1:T(8,128)S(1)}, f32[512,512]{0,1:T(8,128)S(1)}, s32[]{:T(128)}, s32[32]{0:T(128)S(1)}, /*index=5*/s32[1,32]{1,0:T(...) while((s32[]{:T(128)}, f32[512,512]{0,1:T(8,128)S(1)}, ...), condition=%wide.region_46.46_spmd, body=%wide.region_41.45_spmd.sunk | while | flops 548143232 | bytes 24177980 | solution.py:78
  1164.2 18.5 %conditional.8 = ((f32[512,512]{0,1:T(8,128)S(1)}, f32[512,512]{0,1:T(8,128)S(1)})) conditional(s32[]{:T(128)} %convert_element_type.256, (f32[512,512]{0,1:T(8,128)S(1)}, f32[512,512]{0,1:T(8,128)S(1)}) %tuple.395, (s32[]{:T(128)}, s32[2]{0:T(128)S(1)}, s32[]{:T(128)}, s32[2]{0:T(128)S(1)}, s32[]{:T(128)}, /*index=5*/pred[]{:T(512)}, ...), branch_computations={%region_44.43_spmd, %region_45.44_spmd} | conditional | flops 548143104 | bytes 24177268 | solution.py:360
  1175.5 5.1 fusion.18
  1196.2 18.5 %conditional.8 = ((f32[512,512]{0,1:T(8,128)S(1)}, f32[512,512]{0,1:T(8,128)S(1)})) conditional(s32[]{:T(128)} %convert_element_type.256, (f32[512,512]{0,1:T(8,128)S(1)}, f32[512,512]{0,1:T(8,128)S(1)}) %tuple.395, (s32[]{:T(128)}, s32[2]{0:T(128)S(1)}, s32[]{:T(128)}, s32[2]{0:T(128)S(1)}, s32[]{:T(128)}, /*index=5*/pred[]{:T(512)}, ...), branch_computations={%region_44.43_spmd, %region_45.44_spmd} | conditional | flops 548143104 | bytes 24177268 | solution.py:360
  1207.5 5.1 fusion.18
  1256.0 99.2 %reduce-scatter.9.cloned.1.call-done = f32[512,256]{0,1:T(8,128)} async-done(((f32[512,512]{0,1:T(8,128)}), f32[512,256]{0,1:T(8,128)}) %reduce-scatter.9.cloned.1.call-update) | async-done | bytes 524304 | tf_op jit(solution)/shard_map/reduce_scatter | solution.py:405
  1355.2 11.9 reduce-scatter.11.cloned.1.call-done
  1384.3 80.5 %all-reduce.10 = (f32[256]{0:T(256)}, f32[256]{0:T(256)}, f32[256]{0:T(256)}, f32[256]{0:T(256)}, f32[256]{0:T(256)}, /*index=5*/f32[1024]{0:T(1024)}, f32[256]{...) all-reduce(f32[256]{0:T(256)S(1)} %dynamic-slice.2, ...), channel_id=1, replica_groups=mesh['ctx'=16,'fsdp'=2] {'ctx'}, use_global_device_ids=true, to_apply=%region_57.58 | all-reduce | flops 3328 | bytes 26624 | tf_op jit(solution)/shard_map/psum | solution.py:389
  1464.8 125.9 %all-reduce.15.cloned.1.call-done = (f32[512,256]{0,1:T(8,128)}, f32[512,256]{0,1:T(8,128)}, f32[512,256]{0,1:T(8,128)}, f32[256,512]{1,0:T(8,128)}, f32[512,1024]{1,0:T(8,128)}, /*index=5*/f32[1024,512]{1,0:T(8,128)}) async-done(((f32[512,256]{0,1:T(8,128)}, f32[512,256]{0,1:T(8,128)}, f32[512,256]{0,1:T(8,128)}, f32[256,512]{1,0:T(8,128)}, f32[512,1024]{1,0:T(8,128)}, /*index=5*/f32[1024,512]{1,0:T(8,128)}), ...) | async-done | bytes 6291472 | tf_op jit(solution)/shard_map/psum | solution.py:389
  (948 shorter events, 845.1 us)
Async XLA Ops:
  7.2 6.5 copy-start.42
  7.2 8.4 copy-start.23
  7.2 130.7 %all-gather.17.cloned.1.call-start = ((), (), s32[]{:S(2)}) async-start(), calls=%async_computation.6 | async-start | bytes 8912896 | tf_op jit(solution)/shard_map/all_gather | solution.py:226
  8.9 11.9 copy-start.7
  8.9 16.7 %copy-start.5 = (bf16[512,512]{0,1:T(8,128)(2,1)}, bf16[512,512]{0,1:T(8,128)(2,1)S(1)}, u32[]{:S(2)}) copy-start(bf16[512,512]{0,1:T(8,128)(2,1)S(1)} %bitcast_convert_fusion) | copy-start | bytes 1572868
  9.0 12.5 copy-start.43
  9.0 14.3 copy-start.24
  13.7 289.7 %all-gather.19.cloned.1.call-start = ((), (), s32[]{:S(2)}) async-start(), calls=%async_computation.7 | async-start | bytes 8912896 | tf_op jit(solution)/shard_map/all_gather | solution.py:227
  15.6 11.4 copy-start.14
  20.0 8.3 copy-start.44
  20.0 10.1 copy-start.45
  20.0 11.9 copy-start.46
  20.0 13.7 copy-start.25
  20.0 452.2 %all-gather.21.cloned.1.call-start = ((), (), s32[]{:S(2)}) async-start(), calls=%async_computation.8 | async-start | bytes 3145728 | tf_op jit(solution)/shard_map/all_gather | solution.py:135
  20.8 456.7 %all-gather.23.cloned.1.call-start = ((), (), s32[]{:S(2)}) async-start(), calls=%async_computation.9 | async-start | bytes 3145728 | tf_op jit(solution)/shard_map/all_gather | solution.py:137
  21.4 17.2 %copy-start.47 = (bf16[256]{0:T(256)(128)(2,1)S(1)}, bf16[256]{0:T(256)(128)(2,1)}, u32[]{:S(2)}) copy-start(bf16[256]{0:T(256)(128)(2,1)} %param.63) | copy-start | bytes 1540
  21.4 19.0 %copy-start.37 = (bf16[1024]{0:T(1024)(128)(2,1)S(1)}, bf16[1024]{0:T(1024)(128)(2,1)}, u32[]{:S(2)}) copy-start(bf16[1024]{0:T(1024)(128)(2,1)} %param.61) | copy-start | bytes 6148
  21.4 20.7 %copy-start.48 = (bf16[256]{0:T(256)(128)(2,1)S(1)}, bf16[256]{0:T(256)(128)(2,1)}, u32[]{:S(2)}) copy-start(bf16[256]{0:T(256)(128)(2,1)} %param.66) | copy-start | bytes 1540
  21.4 23.1 %copy-start.49 = (bf16[256]{0:T(256)(128)(2,1)S(1)}, bf16[256]{0:T(256)(128)(2,1)}, u32[]{:S(2)}) copy-start(bf16[256]{0:T(256)(128)(2,1)} %param.64) | copy-start | bytes 1540
  21.4 25.4 %copy-start.50 = (bf16[256]{0:T(256)(128)(2,1)S(1)}, bf16[256]{0:T(256)(128)(2,1)}, u32[]{:S(2)}) copy-start(bf16[256]{0:T(256)(128)(2,1)} %param.67) | copy-start | bytes 1540
  21.4 918.2 %all-gather.25.cloned.1.call-start = ((), (), s32[]{:S(2)}) async-start(), calls=%async_computation.10 | async-start | bytes 8912896 | tf_op jit(solution)/shard_map/all_gather | solution.py:370
  23.3 25.9 %copy-start.51 = (bf16[256]{0:T(256)(128)(2,1)S(1)}, bf16[256]{0:T(256)(128)(2,1)}, u32[]{:S(2)}) copy-start(bf16[256]{0:T(256)(128)(2,1)} %param.65) | copy-start | bytes 1540
  23.3 28.5 %copy-start.52 = (s32[1,32]{1,0:T(1,128)S(1)}, s32[1,32]{1,0:T(1,128)}, u32[]{:S(2)}) copy-start(s32[1,32]{1,0:T(1,128)} %param.49) | copy-start | bytes 388
  23.3 28.5 %copy-start.53 = (s32[1,32]{1,0:T(1,128)S(1)}, s32[1,32]{1,0:T(1,128)}, u32[]{:S(2)}) copy-start(s32[1,32]{1,0:T(1,128)} %param.50) | copy-start | bytes 388
  25.6 112.2 %copy-start.17 = (bf16[512,512]{1,0:T(8,128)(2,1)}, bf16[512,512]{1,0:T(8,128)(2,1)S(1)}, u32[]{:S(2)}) copy-start(bf16[512,512]{1,0:T(8,128)(2,1)S(1)} %all_gather.74) | copy-start | bytes 1572868
  26.9 111.0 %copy-start = (bf16[512,512]{0,1:T(8,128)(2,1)S(1)}, bf16[512,512]{0,1:T(8,128)(2,1)}, u32[]{:S(2)}) copy-start(bf16[512,512]{0,1:T(8,128)(2,1)} %fusion.31) | copy-start | bytes 1572868
  26.9 912.7 %all-gather.27.cloned.1.call-start = ((), (), s32[]{:S(2)}) async-start(), calls=%async_computation.11 | async-start | bytes 8912896 | tf_op jit(solution)/shard_map/all_gather | solution.py:371
  472.0 24.8 %copy-start.4 = (f32[512,512]{0,1:T(8,128)}, f32[512,512]{0,1:T(8,128)S(1)}, u32[]{:S(2)}) copy-start(f32[512,512]{0,1:T(8,128)S(1)} %get-tuple-element.3341) | copy-start | bytes 3145732
  477.5 6.1 copy-start.8
  477.5 6.1 copy-start.26
  477.5 6.1 copy-start.27
  477.5 6.1 copy-start.30
  477.5 6.1 copy-start.31
  488.6 6.0 copy-start.21
  500.2 755.7 %reduce-scatter.7.cloned.1.call-start = ((), (), s32[]{:S(2)}) async-start(), calls=%async_computation.12 | async-start | bytes 1572864 | tf_op jit(solution)/shard_map/reduce_scatter | solution.py:404
  704.6 10.8 copy-start.1
  707.5 548.5 %reduce-scatter.13.cloned.1.call-start = ((), (), s32[]{:S(2)}) async-start(), calls=%async_computation.15 | async-start | bytes 1572864 | tf_op jit(solution)/shard_map/reduce_scatter | solution.py:407
  710.0 545.9 %reduce-scatter.15.cloned.1.call-start = ((), (), s32[]{:S(2)}) async-start(), calls=%async_computation.16 | async-start | bytes 6291456 | tf_op jit(solution)/shard_map/reduce_scatter | solution.py:276
  715.4 540.7 %reduce-scatter.17.cloned.1.call-start = ((), (), s32[]{:S(2)}) async-start(), calls=%async_computation.17 | async-start | bytes 6291456 | tf_op jit(solution)/shard_map/reduce_scatter | solution.py:278
  721.6 218.3 %copy-start.3 = (bf16[512,512]{0,1:T(8,128)(2,1)S(1)}, bf16[512,512]{0,1:T(8,128)(2,1)}, u32[]{:S(2)}) copy-start(bf16[512,512]{0,1:T(8,128)(2,1)} %convolution_convert_fusion.1) | copy-start | bytes 1572868
  721.6 633.6 %reduce-scatter.9.cloned.1.call-start = ((), (), s32[]{:S(2)}) async-start(), calls=%async_computation.13 | async-start | bytes 1572864 | tf_op jit(solution)/shard_map/reduce_scatter | solution.py:405
  1253.3 113.8 %reduce-scatter.11.cloned.1.call-start = ((), (), s32[]{:S(2)}) async-start(), calls=%async_computation.14 | async-start | bytes 1572864 | tf_op jit(solution)/shard_map/reduce_scatter | solution.py:406
  1255.8 112.8 %copy-start.54 = (u32[32]{0:T(128)S(1)}, u32[32]{0:T(128)}, u32[]{:S(2)}) copy-start(u32[32]{0:T(128)} %constant.605) | copy-start | bytes 388
  1255.9 334.8 %all-reduce.15.cloned.1.call-start = ((), (), s32[]{:S(2)}) async-start(), calls=%async_computation.18 | async-start | bytes 12582912 | tf_op jit(solution)/shard_map/psum | solution.py:389
  1367.2 8.4 copy-start.2
  1367.2 8.6 copy-start.29
  1464.8 137.7 %copy-start.40 = (f32[256]{0:T(256)}, f32[256]{0:T(256)S(1)}, u32[]{:S(2)}) copy-start(f32[256]{0:T(256)S(1)} %get-tuple-element.4587) | copy-start | bytes 3076
  1590.7 11.9 copy-start.18
  (20 other events, 46.2 us)
Sparse Core Ops, SparseCore 0:
  13.8 124.0 all-gather.16
  141.2 119.7 all-gather.18
  262.5 8.7 all-gather.20
  272.7 11.7 all-gather.22
  287.7 122.6 all-gather.24
  500.3 185.8 all-gather.26
  707.6 168.3 reduce-scatter.6
  878.3 9.6 reduce-scatter.12
  890.4 13.1 reduce-scatter.14
  905.8 13.3 reduce-scatter.16
  1253.4 101.7 reduce-scatter.8
  1357.4 9.6 reduce-scatter.10
  1373.6 217.0 all-reduce.14
where the time goes:
time: 1600 us; the launch traced here: 1610 us
  other arithmetic  484 us (30%)
  blocking collectives  331 us (21%)
  waiting for transfers between devices  324 us (20%)
  matrix products  205 us (13%)
  local copies, waits for them, and re-layouts  155 us (10%)
  loops' own time  93.7 us (6%)
  between operations  16 us (1%)
    reduce_or x96, other arithmetic, unit_step(): jnp.any(visible)  185 us
    all_gather x1, blocking collectives, shards(): lax.all_gather(deltas.T, 'ctx', axis=0, tiled=True)  179 us
    reduce_sum x129, other arithmetic, lookup(): jnp.sum(jnp.where(indices[:, None] == places[None, :], table_row[None, :]...  164 us
    psum x1, waiting for transfers between devices, shards(): lax.psum((slope_query, slope_key, slope_value, slope_output, drift_query,...  126 us
    reduce_scatter x1, waiting for transfers between devices, shards(): lax.psum_scatter(heads_parts[1], 'fsdp', scatter_dimension=1, tiled=True)  99.2 us
    another operation x8, loops' own time, outer_turn(): return lax.fori_loop(0, inner_count, inner_turn, current)  90.7 us
    all_gather x1, waiting for transfers between devices, shards(): lax.all_gather(key_rows, 'ctx', axis=0, tiled=True)  85.8 us
    psum x1, blocking collectives, shards(): lax.psum((slope_query, slope_key, slope_value, slope_output, drift_query,...  80.5 us
  transfers between devices with their start and end apart: 13, of which 4 were waited for; matrix products, arithmetic and copies ran while one was open for 51% of the time, Pallas kernels for 0%

commit v1 on v0

--- a/solution.py
+++ b/solution.py
@@ -1,12 +1,24 @@
+import functools
+
 import jax
 import jax.numpy as jnp
 from jax import lax
+from jax.experimental import pallas as pl
+from jax.experimental.pallas import tpu as pltpu
 from jax.sharding import PartitionSpec as P
 
 D = 512
 H = 8
 HD = 64
 BLK = 256
+HALF = BLK // 2
+LONG = 8
+F32 = jnp.float32
+BF16 = jnp.bfloat16
+MESH = pl.DeviceIdType.MESH
+VMEM = pl.BlockSpec(memory_space=pltpu.VMEM)
+SMEM = pl.BlockSpec(memory_space=pltpu.SMEM)
+ANY = pl.BlockSpec(memory_space=pl.ANY)
 
 
 norm_eps = 1e-05
@@ -80,7 +92,7 @@
     return lax.fori_loop(0, outer_count, outer_turn, carried)
 
 
-def shards(
+def general_shards(
     post_stream,
     sum_stream,
     cotangent,
@@ -435,9 +447,1157 @@
     )
 
 
+def low_lanes(values):
+    return lax.broadcasted_iota(jnp.int32, values.shape, 1) < HD
+
+
+def swap_lanes(values):
+    return pltpu.roll(values, HD, 1)
+
+
+def low_pair(first, second):
+    return jnp.where(low_lanes(first), first, swap_lanes(second))
+
+
+def high_pair(first, second):
+    return jnp.where(low_lanes(first), swap_lanes(first), second)
+
+
+def side_pair(side, first, second):
+    return low_pair(first, second) if side == 0 else high_pair(first, second)
+
+
+def dot_nn(left, right):
+    return jnp.dot(left, right, preferred_element_type=F32)
+
+
+def dot_nt(left, right):
+    return lax.dot_general(left, right, (((1,), (1,)), ((), ())), preferred_element_type=F32)
+
+
+def dot_tn(left, right):
+    return lax.dot_general(left, right, (((0,), (0,)), ((), ())), preferred_element_type=F32)
+
+
+class Place:
+    def __init__(self):
+        self.c = lax.axis_index("ctx")
+        self.f = lax.axis_index("fsdp")
+        self.group = self.c // H
+        self.head = self.c % H
+        self.inside = jnp.where(self.group == self.f, 1, 0)
+
+    def is_me(self, tc, tf):
+        return jnp.logical_and(self.c == tc, self.f == tf)
+
+    def signal(self, barrier, tc, tf):
+        @pl.when(jnp.logical_not(self.is_me(tc, tf)))
+        def _():
+            pl.semaphore_signal(barrier, 1, device_id=(tc, tf), device_id_type=MESH)
+
+    def greet_sources(self, n_ctx, partner):
+        barrier = pltpu.get_barrier_semaphore()
+        for tc in range(n_ctx):
+            self.signal(barrier, tc, self.group)
+        if partner:
+            pl.semaphore_signal(
+                barrier, 1, device_id=(self.c, 1 - self.f), device_id_type=MESH
+            )
+        pl.semaphore_wait(barrier, 2 * H + (1 if partner else 0) - self.inside)
+
+    def greet_owners(self, n_ctx, partner):
+        barrier = pltpu.get_barrier_semaphore()
+        for head in range(H):
+            for core in range(2):
+                self.signal(barrier, self.f * H + head, core)
+        if partner:
+            pl.semaphore_signal(
+                barrier, 1, device_id=(self.c, 1 - self.f), device_id_type=MESH
+            )
+        pl.semaphore_wait(barrier, n_ctx + (1 if partner else 0) - self.inside)
+
+    def send(self, src, dst, send_sem, recv_sem, tc, tf):
+        me = self.is_me(tc, tf)
+
+        @pl.when(me)
+        def _():
+            pltpu.make_async_copy(src, dst, recv_sem).start()
+
+        @pl.when(jnp.logical_not(me))
+        def _():
+            self.remote(src, dst, send_sem, recv_sem, tc, tf).start()
+
+    def remote(self, src, dst, send_sem, recv_sem, tc, tf):
+        return pltpu.make_async_remote_copy(
+            src_ref=src,
+            dst_ref=dst,
+            send_sem=send_sem,
+            recv_sem=recv_sem,
+            device_id=(tc, tf),
+            device_id_type=MESH,
+        )
+
+    def wait_sent(self, src, dst, send_sem, recv_sem, tc, tf):
+        @pl.when(jnp.logical_not(self.is_me(tc, tf)))
+        def _():
+            self.remote(src, dst, send_sem, recv_sem, tc, tf).wait_send()
+
+
+def project_kernel(
+    n_ctx,
+    x_ref,
+    wq_ref,
+    wk_ref,
+    wv_ref,
+    bias_ref,
+    q_out,
+    kv_out,
+    w_other,
+    x_low,
+    w_in,
+    bias_in,
+    q_send,
+    kv_send,
+    w_ss,
+    w_rs,
+    q_ss,
+    q_rs,
+    kv_ss,
+    kv_rs,
+    relay_ss,
+    relay_rs,
+):
+    at = Place()
+    other = 1 - at.f
+    at.greet_sources(n_ctx, True)
+    swaps = [
+        at.remote(src, dst, w_ss.at[i], w_rs.at[i], at.c, other)
+        for i, (src, dst) in enumerate(
+            (
+                (bias_ref, bias_in),
+                (wq_ref, w_in.at[0]),
+                (wk_ref, w_in.at[1]),
+                (wv_ref, w_in.at[2]),
+            )
+        )
+    ]
+    for swap in swaps:
+        swap.start()
+    x_low[...] = x_ref[...].astype(BF16)
+
+    def targets(half):
+        for pair in range(2):
+            for side in range(2):
+                head = half * (H // 2) + 2 * pair + side
+                for core in range(2):
+                    slot = head * 2 + core
+                    yield pair, side, head, core, (
+                        kv_send.at[head, pl.ds(core * BLK, BLK)],
+                        kv_out.at[2 * at.c + core],
+                        kv_ss.at[slot],
+                        kv_rs.at[at.c],
+                        at.f * H + head,
+                        core,
+                    ), (
+                        q_send.at[head, core],
+                        q_out.at[at.c],
+                        q_ss.at[slot],
+                        q_rs.at[at.c],
+                        at.f * H + head,
+                        core,
+                    )
+
+    def one_half(half, wq, wk, wv, bias):
+        low = x_low[...]
+        q = dot_nn(low, wq[...]) + bias[0:1, :]
+        k = dot_nn(low, wk[...])
+        v = dot_nn(low, wv[...]) + bias[1:2, :]
+        for pair, side, head, core, kv_move, q_move in targets(half):
+            columns = slice(pair * 128, pair * 128 + 128)
+            if core == 0:
+                kv_send[head] = side_pair(side, k[:, columns], v[:, columns]).astype(BF16)
+            rows = slice(core * HALF, core * HALF + HALF)
+            late = slice(BLK + core * HALF, BLK + core * HALF + HALF)
+            q_send[head, core] = side_pair(side, q[rows, columns], q[late, columns]).astype(BF16)
+            at.send(*kv_move)
+            at.send(*q_move)
+
+    one_half(at.f, wq_ref, wk_ref, wv_ref, bias_ref)
+    for swap in swaps:
+        swap.wait()
+    one_half(other, w_in.at[0], w_in.at[1], w_in.at[2], bias_in)
+    w_other[...] = w_in[...]
+
+    def relay(source):
+        mine = kv_out.at[2 * source + at.f]
+        return at.remote(mine, mine, relay_ss.at[source], relay_rs.at[source], at.c, other)
+
+    def relay_in(source):
+        theirs = kv_out.at[2 * source + other]
+        return at.remote(theirs, theirs, relay_ss.at[source], relay_rs.at[source], at.c, other)
+
+    for source in range(n_ctx):
+        arrived = kv_out.at[2 * source + at.f]
+        at.remote(arrived, arrived, kv_ss.at[0], kv_rs.at[source], at.c, other).wait_recv()
+        relay(source).start()
+    for source in range(n_ctx):
+        arrived = q_out.at[source]
+        at.remote(arrived, arrived, q_ss.at[0], q_rs.at[source], at.c, other).wait_recv()
+        relay_in(source).wait_recv()
+    for source in range(n_ctx):
+        relay(source).wait_send()
+    for half in (at.f, other):
+        for _, _, _, _, kv_move, q_move in targets(half):
+            at.wait_sent(*kv_move)
+            at.wait_sent(*q_move)
+
+
+def project_and_scatter(n_ctx, x, wq, wk, wv, bias):
+    wide = wq.shape[1]
+    return pl.pallas_call(
+        functools.partial(project_kernel, n_ctx),
+        out_shape=(
+            jax.ShapeDtypeStruct((n_ctx, HALF, 128), BF16),
+            jax.ShapeDtypeStruct((2 * n_ctx, BLK, 128), BF16),
+            jax.ShapeDtypeStruct((3, D, wide), BF16),
+        ),
+        in_specs=[VMEM] * 5,
+        out_specs=(ANY, ANY, VMEM),
+        scratch_shapes=[
+            pltpu.VMEM((2 * BLK, D), BF16),
+            pltpu.VMEM((3, D, wide), BF16),
+            pltpu.VMEM((8, wide), F32),
+            pltpu.VMEM((H, 2, HALF, 128), BF16),
+            pltpu.VMEM((H, 2 * BLK, 128), BF16),
+            pltpu.SemaphoreType.DMA((4,)),
+            pltpu.SemaphoreType.DMA((4,)),
+            pltpu.SemaphoreType.DMA((2 * H,)),
+            pltpu.SemaphoreType.DMA((n_ctx,)),
+            pltpu.SemaphoreType.DMA((2 * H,)),
+            pltpu.SemaphoreType.DMA((n_ctx,)),
+            pltpu.SemaphoreType.DMA((n_ctx,)),
+            pltpu.SemaphoreType.DMA((n_ctx,)),
+        ],
+        compiler_params=pltpu.CompilerParams(
+            collective_id=0, has_side_effects=True, vmem_limit_bytes=48 << 20
+        ),
+        name="project_scatter",
+    )(x, wq, wk, wv, bias)
+
+
+def forward_kernel(
+    blocks,
+    order_ref,
+    seq_ref,
+    q_ref,
+    kv_ref,
+    o_ref,
+    keep_ref,
+    lse_ref,
+    pairs_ref,
+    place,
+    q_low,
+    peaks,
+    masses,
+    total,
+):
+    def place_block(slot, _):
+        place[order_ref[slot]] = slot
+        return 0
+
+    lax.fori_loop(0, blocks, place_block, 0)
+
+    def unpack(source, _):
+        packed = q_ref[source].astype(F32) * (HD**-0.5)
+        q_low[2 * source] = jnp.where(low_lanes(packed), packed, 0.0).astype(BF16)
+        q_low[2 * source + 1] = jnp.where(low_lanes(packed), swap_lanes(packed), 0.0).astype(BF16)
+        return 0
+
+    lax.fori_loop(0, blocks // 2, unpack, 0)
+    q_low[blocks] = jnp.zeros((HALF, 128), BF16)
+    peaks[blocks] = jnp.zeros((HALF, 128), F32)
+    masses[blocks] = jnp.zeros((HALF, 128), F32)
+    total[blocks] = jnp.zeros((HALF, 128), F32)
+
+    count = jnp.int32(0)
+    for gap in range(1, LONG):
+
+        def look(late, found):
+            pairs_ref[0, found] = place[late]
+            pairs_ref[1, found] = place[late - gap]
+            return found + jnp.where(seq_ref[late] == seq_ref[late - gap], 1, 0)
+
+        count = lax.fori_loop(gap, blocks, look, count)
+    for spare in range(4):
+        pairs_ref[0, count + spare] = blocks
+        pairs_ref[1, count + spare] = 0
+    turns = (count + 3) // 4
+    pairs_ref[2, 0] = turns
+
+    def own_blocks(step, _):
+        for part in range(4):
+            slot = step * 4 + part
+            scores = dot_nt(q_low[slot], kv_ref[slot])
+            peak = jnp.broadcast_to(jnp.max(scores, axis=1, keepdims=True), (HALF, 128))
+            left = jnp.exp(scores[:, :128] - peak)
+            right = jnp.exp(scores[:, 128:] - peak)
+            peaks[slot] = peak
+            masses[slot] = left + right
+            weights = jnp.concatenate([left, right], axis=1).astype(BF16)
+            total[slot] = dot_nn(weights, kv_ref[slot])
+        return 0
+
+    lax.fori_loop(0, blocks // 4, own_blocks, 0)
+
+    def other_blocks(step, _):
+        for part in range(4):
+            q_slot = pairs_ref[0, step * 4 + part]
+            k_slot = pairs_ref[1, step * 4 + part]
+            scores = dot_nt(q_low[q_slot], kv_ref[k_slot])
+            before = peaks[q_slot]
+            peak = jnp.maximum(
+                before, jnp.broadcast_to(jnp.max(scores, axis=1, keepdims=True), (HALF, 128))
+            )
+            fade = jnp.exp(before - peak)
+            left = jnp.exp(scores[:, :128] - peak)
+            right = jnp.exp(scores[:, 128:] - peak)
+            peaks[q_slot] = peak
+            masses[q_slot] = masses[q_slot] * fade + (left + right)
+            weights = jnp.concatenate([left, right], axis=1).astype(BF16)
+            total[q_slot] = total[q_slot] * fade + dot_nn(weights, kv_ref[k_slot])
+        return 0
+
+    lax.fori_loop(0, turns, other_blocks, 0)
+
+    def finish(source, _):
+        results = []
+        for side in range(2):
+            slot = 2 * source + side
+            mass = jnp.broadcast_to(
+                jnp.sum(masses[slot], axis=1, keepdims=True), (HALF, 128)
+            )
+            results.append(total[slot] / mass)
+            lse_ref[slot] = jnp.transpose(peaks[slot] + jnp.log(mass))[0:8]
+        packed = high_pair(results[0], results[1])
+        keep_ref[source] = packed
+        o_ref[source] = packed.astype(BF16)
+        return 0
+
+    lax.fori_loop(0, blocks // 2, finish, 0)
+
+
+def attend(order, seqs, q, kv):
+    blocks = kv.shape[0]
+    pair_room = blocks * LONG
+    return pl.pallas_call(
+        functools.partial(forward_kernel, blocks),
+        out_shape=(
+            jax.ShapeDtypeStruct((blocks // 2, HALF, 128), BF16),
+            jax.ShapeDtypeStruct((blocks // 2, HALF, 128), F32),
+            jax.ShapeDtypeStruct((blocks, 8, HALF), F32),
+            jax.ShapeDtypeStruct((3, pair_room), jnp.int32),
+        ),
+        in_specs=[SMEM, SMEM, VMEM, VMEM],
+        out_specs=(VMEM, VMEM, VMEM, SMEM),
+        scratch_shapes=[
+            pltpu.SMEM((blocks,), jnp.int32),
+            pltpu.VMEM((blocks + 1, HALF, 128), BF16),
+            pltpu.VMEM((blocks + 1, HALF, 128), F32),
+            pltpu.VMEM((blocks + 1, HALF, 128), F32),
+            pltpu.VMEM((blocks + 1, HALF, 128), F32),
+        ],
+        compiler_params=pltpu.CompilerParams(vmem_limit_bytes=48 << 20),
+        name="attend",
+    )(order, seqs, q, kv)
+
+
+def backward_kernel(
+    blocks,
+    pairs_ref,
+    q_ref,
+    tan_ref,
+    keep_ref,
+    lse_ref,
+    kv_ref,
+    dq_ref,
+    dkv_ref,
+    both,
+    mass_rows,
+    delta_rows,
+    dq_sum,
+):
+    def unpack(source, _):
+        packed = q_ref[source].astype(F32) * (HD**-0.5)
+        tangent = tan_ref[source].astype(F32)
+        low = low_lanes(packed)
+        both[2 * source, 0:HALF] = jnp.where(low, packed, 0.0).astype(BF16)
+        both[2 * source + 1, 0:HALF] = jnp.where(low, swap_lanes(packed), 0.0).astype(BF16)
+        both[2 * source, HALF:BLK] = jnp.where(low, 0.0, swap_lanes(tangent)).astype(BF16)
+        both[2 * source + 1, HALF:BLK] = jnp.where(low, 0.0, tangent).astype(BF16)
+        across = jnp.transpose(tangent * keep_ref[source])
+        for side in range(2):
+            delta = jnp.sum(across[side * HD : side * HD + HD], axis=0, keepdims=True)
+            delta_rows[2 * source + side] = jnp.broadcast_to(delta, (8, HALF))
+            mass_rows[2 * source + side] = lse_ref[2 * source + side]
+        return 0
+
+    lax.fori_loop(0, blocks // 2, unpack, 0)
+    both[blocks] = jnp.zeros((BLK, 128), BF16)
+    mass_rows[blocks] = jnp.zeros((8, HALF), F32)
+    delta_rows[blocks] = jnp.zeros((8, HALF), F32)
+    dq_sum[blocks] = jnp.zeros((HALF, 128), F32)
+
+    def one_pair(q_slot, k_slot):
+        stacked = both[q_slot]
+        kv = kv_ref[k_slot]
+        products = dot_nt(kv, stacked)
+        weights = jnp.exp(products[:, :HALF] - mass_rows[q_slot, 0:1, :])
+        score_tan = (weights * (products[:, HALF:] - delta_rows[q_slot, 0:1, :])).astype(BF16)
+        sides = jnp.concatenate([score_tan, weights.astype(BF16)], axis=1)
+        return dot_nn(sides, stacked), dot_tn(score_tan, kv)
+
+    def own_blocks(step, _):
+        for part in range(4):
+            slot = step * 4 + part
+            dkv, dq = one_pair(slot, slot)
+            dkv_ref[slot] = dkv
+            dq_sum[slot] = dq
+        return 0
+
+    lax.fori_loop(0, blocks // 4, own_blocks, 0)
+
+    def other_blocks(step, _):
+        slots = [(pairs_ref[0, step * 4 + part], pairs_ref[1, step * 4 + part]) for part in range(4)]
+        results = [one_pair(*slot) for slot in slots]
+        for (q_slot, k_slot), (dkv, dq) in zip(slots, results):
+            dkv_ref[k_slot] = dkv_ref[k_slot] + dkv
+            dq_sum[q_slot] = dq_sum[q_slot] + dq
+        return 0
+
+    lax.fori_loop(0, pairs_ref[2, 0], other_blocks, 0)
+
+    def finish(source, _):
+        packed = low_pair(dq_sum[2 * source], dq_sum[2 * source + 1]) * (HD**-0.5)
+        dq_ref[source] = packed.astype(BF16)
+        return 0
+
+    lax.fori_loop(0, blocks // 2, finish, 0)
+
+
+def attend_back(pairs, q, tangent, keep, lse, kv):
+    blocks = kv.shape[0]
+    return pl.pallas_call(
+        functools.partial(backward_kernel, blocks),
+        out_shape=(
+            jax.ShapeDtypeStruct((blocks // 2, HALF, 128), BF16),
+            jax.ShapeDtypeStruct((blocks, BLK, 128), F32),
+        ),
+        in_specs=[SMEM, VMEM, VMEM, VMEM, VMEM, VMEM],
+        out_specs=(VMEM, VMEM),
+        scratch_shapes=[
+            pltpu.VMEM((blocks + 1, BLK, 128), BF16),
+            pltpu.VMEM((blocks + 1, 8, HALF), F32),
+            pltpu.VMEM((blocks + 1, 8, HALF), F32),
+            pltpu.VMEM((blocks + 1, HALF, 128), F32),
+        ],
+        compiler_params=pltpu.CompilerParams(vmem_limit_bytes=48 << 20),
+        name="attend_back",
+    )(pairs, q, tangent, keep, lse, kv)
+
+
+def return_kernel(n_ctx, rows_ref, out_ref, ss, rs):
+    at = Place()
+    at.greet_owners(n_ctx, False)
+
+    def move(target):
+        return (
+            rows_ref.at[target],
+            out_ref.at[at.head, at.f],
+            ss.at[target],
+            rs.at[at.head * 2 + at.f],
+            target,
+            at.group,
+        )
+
+    for target in range(n_ctx):
+        at.send(*move(target))
+    for head in range(H):
+        for core in range(2):
+            arrived = out_ref.at[head, core]
+            at.remote(
+                arrived, arrived, ss.at[0], rs.at[head * 2 + core], at.c, 1 - at.f
+            ).wait_recv()
+    for target in range(n_ctx):
+        at.wait_sent(*move(target))
+
+
+def return_rows(n_ctx, rows):
+    return pl.pallas_call(
+        functools.partial(return_kernel, n_ctx),
+        out_shape=jax.ShapeDtypeStruct((H, 2, HALF, 128), BF16),
+        in_specs=[ANY],
+        out_specs=ANY,
+        scratch_shapes=[
+            pltpu.SemaphoreType.DMA((n_ctx,)),
+            pltpu.SemaphoreType.DMA((2 * H,)),
+        ],
+        compiler_params=pltpu.CompilerParams(collective_id=1, has_side_effects=True),
+        name="return_rows",
+    )(rows)
+
+
+def scatter_kernel(n_ctx, rows_ref, out_ref, ss, rs):
+    at = Place()
+    at.greet_sources(n_ctx, False)
+
+    def moves():
+        for head in range(H):
+            for core in range(2):
+                yield (
+                    rows_ref.at[head, core],
+                    out_ref.at[at.c],
+                    ss.at[head * 2 + core],
+                    rs.at[at.c],
+                    at.f * H + head,
+                    core,
+                )
+
+    for move in moves():
+        at.send(*move)
+    for source in range(n_ctx):
+        arrived = out_ref.at[source]
+        at.remote(arrived, arrived, ss.at[0], rs.at[source], at.c, 1 - at.f).wait_recv()
+    for move in moves():
+        at.wait_sent(*move)
+
+
+def scatter_rows(n_ctx, rows):
+    return pl.pallas_call(
+        functools.partial(scatter_kernel, n_ctx),
+        out_shape=jax.ShapeDtypeStruct((n_ctx, HALF, 128), BF16),
+        in_specs=[ANY],
+        out_specs=ANY,
+        scratch_shapes=[
+            pltpu.SemaphoreType.DMA((2 * H,)),
+            pltpu.SemaphoreType.DMA((n_ctx,)),
+        ],
+        compiler_params=pltpu.CompilerParams(collective_id=2, has_side_effects=True),
+        name="scatter_rows",
+    )(rows)
+
+
+def return_grads_kernel(
+    n_ctx, dq_ref, dkv_ref, dq_out, dkv_out, own, part, ready,
+    q_ss, q_rs, kv_ss, kv_rs, part_ss, part_rs, own_sem,
+):
+    at = Place()
+    other = 1 - at.f
+    at.greet_owners(n_ctx, True)
+
+    def partial_move(source):
+        return at.remote(
+            dkv_ref.at[2 * source + other],
+            part.at[source],
+            part_ss.at[source],
+            part_rs.at[source],
+            at.c,
+            other,
+        )
+
+    def own_move(source):
+        return pltpu.make_async_copy(
+            dkv_ref.at[2 * source + at.f], own.at[source], own_sem.at[source]
+        )
+
+    def q_move(target):
+        return (
+            dq_ref.at[target],
+            dq_out.at[at.head, at.f],
+            q_ss.at[target],
+            q_rs.at[at.head * 2 + at.f],
+            target,
+            at.group,
+        )
+
+    def kv_move(target):
+        return (
+            ready.at[target],
+            dkv_out.at[at.head, pl.ds(pl.multiple_of(at.f * BLK, BLK), BLK)],
+            kv_ss.at[target],
+            kv_rs.at[at.head * 2 + at.f],
+            target,
+            at.group,
+        )
+
+    for source in range(n_ctx):
+        partial_move(source).start()
+        own_move(source).start()
+    for target in range(n_ctx):
+        at.send(*q_move(target))
+    for source in range(n_ctx):
+        own_move(source).wait()
+        partial_move(source).wait_recv()
+        ready[source] = (own[source] + part[source]).astype(BF16)
+        at.send(*kv_move(source))
+    for head in range(H):
+        for core in range(2):
+            slot = head * 2 + core
+            arrived = dq_out.at[head, core]
+            at.remote(arrived, arrived, q_ss.at[0], q_rs.at[slot], at.c, other).wait_recv()
+            arrived = dkv_out.at[head, pl.ds(core * BLK, BLK)]
+            at.remote(arrived, arrived, kv_ss.at[0], kv_rs.at[slot], at.c, other).wait_recv()
+    for target in range(n_ctx):
+        partial_move(target).wait_send()
+        at.wait_sent(*q_move(target))
+        at.wait_sent(*kv_move(target))
+
+
+def return_grads(n_ctx, dq, dkv):
+    return pl.pallas_call(
+        functools.partial(return_grads_kernel, n_ctx),
+        out_shape=(
+            jax.ShapeDtypeStruct((H, 2, HALF, 128), BF16),
+            jax.ShapeDtypeStruct((H, 2 * BLK, 128), BF16),
+        ),
+        in_specs=[ANY, ANY],
+        out_specs=(ANY, ANY),
+        scratch_shapes=[
+            pltpu.VMEM((n_ctx, BLK, 128), F32),
+            pltpu.VMEM((n_ctx, BLK, 128), F32),
+            pltpu.VMEM((n_ctx, BLK, 128), BF16),
+            pltpu.SemaphoreType.DMA((n_ctx,)),
+            pltpu.SemaphoreType.DMA((2 * H,)),
+            pltpu.SemaphoreType.DMA((n_ctx,)),
+            pltpu.SemaphoreType.DMA((2 * H,)),
+            pltpu.SemaphoreType.DMA((n_ctx,)),
+            pltpu.SemaphoreType.DMA((n_ctx,)),
+            pltpu.SemaphoreType.DMA((n_ctx,)),
+        ],
+        compiler_params=pltpu.CompilerParams(
+            collective_id=3, has_side_effects=True, vmem_limit_bytes=32 << 20
+        ),
+        name="return_grads",
+    )(dq, dkv)
+
+
+COLS = 512
+
+
+def whole_rows(own, other, first):
+    return jnp.where(
+        first,
+        jnp.concatenate([own, other], axis=1),
+        jnp.concatenate([other, own], axis=1),
+    )
+
+
+def row_mean(values):
+    return jnp.mean(values, axis=1, keepdims=True)
+
+
+def normalize(values):
+    centre = values - row_mean(values)
+    scale = lax.rsqrt(row_mean(centre * centre) + norm_eps)
+    return centre * scale, scale
+
+
+def norm_back(tangent, normed, scale, gain):
+    pushed = tangent * gain
+    return scale * (pushed - row_mean(pushed) - normed * row_mean(pushed * normed))
+
+
+def column_sum(values):
+    return jnp.sum(values, axis=0, keepdims=True)
+
+
+def dense_kernel(
+    x_ref, sum_ref, cot_ref, o_ref,
+    wo_a, wo_b, we_a, we_b, ws_a, ws_b, be_a, be_b, vec_a, vec_b,
+    out_ref, sum_tan_ref, entry_ref, tan_ref, own_ref, send_ref, vec_ref,
+    mixed, low, hidden, slope, before_tan, feed_tan, branch_tan, mixed_tan,
+):
+    f = lax.axis_index("fsdp")
+    first = f == 0
+    wo, we, ws, be = (wo_a, wo_b), (we_a, we_b), (ws_a, ws_b), (be_a, be_b)
+    halves = (f, 1 - f)
+    vectors = whole_rows(vec_a[...], vec_b[...], first)
+    (out_bias, gain_one, shift_one, shrink_bias, gain_two, shift_two, gain_last, shift_last) = (
+        vectors[i : i + 1] for i in range(8)
+    )
+    for kind in range(2):
+        for pair in range(2):
+            head = halves[kind] * (H // 2) + 2 * pair
+            for core in range(2):
+                early = o_ref[head, core].astype(F32)
+                late = o_ref[head + 1, core].astype(F32)
+                columns = slice(pair * 128, pair * 128 + 128)
+                for side in range(2):
+                    start = side * BLK + core * HALF
+                    mixed[kind, start : start + HALF, columns] = side_pair(
+                        side, early, late
+                    ).astype(BF16)
+    vec_ref[...] = jnp.zeros_like(vec_ref)
+
+    def tile(step, _):
+        rows = pl.ds(pl.multiple_of(step * BLK, BLK), BLK)
+        branch = (
+            dot_nn(mixed[0, rows, :], wo[0][...]) + dot_nn(mixed[1, rows, :], wo[1][...]) + out_bias
+        )
+        n_one, scale_one = normalize(x_ref[rows, :] + branch)
+        normed_one = n_one * gain_one + shift_one
+        stream_one = sum_ref[rows, :] + branch
+        normed_low = normed_one.astype(BF16)
+        low[rows, :] = normed_low
+        feed = jnp.zeros((BLK, D), F32)
+        for kind in range(2):
+
+            def expand(chunk, carried):
+                columns = pl.ds(pl.multiple_of(chunk * COLS, COLS), COLS)
+                v = dot_nn(normed_low, we[kind][:, columns]) + be[kind][:, columns]
+                square = v * v
+                t = jnp.tanh(gelu_coeff * (v + gelu_cubic * square * v))
+                half_up = 0.5 + 0.5 * t
+                hidden_part = (v * half_up).astype(BF16)
+                hidden[kind, rows, columns] = hidden_part
+                slope[kind, :, columns] = half_up + v * half_up * (1.0 - t) * (
+                    gelu_coeff + (3.0 * gelu_coeff * gelu_cubic) * square
+                )
+                return carried + dot_nn(hidden_part, ws[kind][columns, :])
+
+            feed = lax.fori_loop(0, ws[kind].shape[0] // COLS, expand, feed)
+        feed_out = feed + shrink_bias
+        n_two, scale_two = normalize(normed_one + feed_out)
+        n_last, scale_last = normalize(stream_one + feed_out)
+        out_ref[rows, :] = (n_two * gain_two + shift_two) + (n_last * gain_last + shift_last)
+        u = cot_ref[rows, :]
+        nudge = column_sum(u)
+        sum_tan = norm_back(u, n_last, scale_last, gain_last)
+        inflow = norm_back(u, n_two, scale_two, gain_two)
+        sum_tan_ref[rows, :] = sum_tan
+        feed_low = (sum_tan + inflow).astype(BF16)
+        feed_tan[rows, :] = feed_low
+        vec_ref[0:1, :] += column_sum(feed_low.astype(F32))
+        vec_ref[1:2, :] += column_sum(u * n_two)
+        vec_ref[2:3, :] += nudge
+        vec_ref[3:4, :] += column_sum(u * n_last)
+        vec_ref[4:5, :] += nudge
+        normed_tan = inflow
+        for kind in range(2):
+
+            def expand_back(chunk, carried):
+                columns = pl.ds(pl.multiple_of(chunk * COLS, COLS), COLS)
+                pushed = dot_nt(feed_low, ws[kind][columns, :])
+                tan_part = (pushed * slope[kind, :, columns]).astype(BF16)
+                before_tan[kind, rows, columns] = tan_part
+                vec_row = pl.ds(8 + 2 * halves[kind] + chunk, 1)
+                vec_ref[vec_row, :] += column_sum(tan_part.astype(F32))
+                return carried + dot_nt(tan_part, we[kind][:, columns])
+
+            normed_tan = lax.fori_loop(0, ws[kind].shape[0] // COLS, expand_back, normed_tan)
+        vec_ref[5:6, :] += column_sum(normed_tan * n_one)
+        vec_ref[6:7, :] += column_sum(normed_tan)
+        entry = norm_back(normed_tan, n_one, scale_one, gain_one)
+        entry_ref[rows, :] = entry
+        branch_low = (sum_tan + entry).astype(BF16)
+        branch_tan[rows, :] = branch_low
+        vec_ref[7:8, :] += column_sum(branch_low.astype(F32))
+        for kind in range(2):
+            mixed_tan[kind, rows, :] = dot_nt(branch_low, wo[kind][...])
+        return 0
+
+    lax.fori_loop(0, 2, tile, 0)
+
+    for kind in range(2):
+        for pair in range(2):
+            columns = slice(pair * 128, pair * 128 + 128)
+            for side in range(2):
+                head = halves[kind] * (H // 2) + 2 * pair + side
+                for core in range(2):
+                    early = mixed_tan[kind, core * HALF : core * HALF + HALF, columns]
+                    late = mixed_tan[kind, BLK + core * HALF : BLK + core * HALF + HALF, columns]
+                    tan_ref[head, core] = side_pair(side, early, late).astype(BF16)
+
+    for kind, grad_ref in enumerate((own_ref, send_ref)):
+        unit_count = ws[kind].shape[0] // COLS
+
+        def slopes(chunk, _):
+            columns = pl.ds(pl.multiple_of(chunk * COLS, COLS), COLS)
+            grad_ref[columns, :] = dot_tn(hidden[kind, :, columns], feed_tan[...]).astype(BF16)
+            below = pl.ds(pl.multiple_of((unit_count + chunk) * COLS, COLS), COLS)
+            grad_ref[below, :] = dot_tn(low[...], before_tan[kind, :, columns]).astype(BF16)
+            return 0
+
+        lax.fori_loop(0, unit_count, slopes, 0)
+        grad_ref[2 * unit_count * COLS : 2 * unit_count * COLS + D // 2, :] = dot_tn(
+            mixed[kind], branch_tan[...]
+        ).astype(BF16)
+
+
+def dense(x, summed, cotangent, o, wo, we, ws, be, vec):
+    tokens = x.shape[0]
+    units = ws[0].shape[0]
+    grad_rows = units + units + D // 2
+    return pl.pallas_call(
+        dense_kernel,
+        out_shape=(
+            jax.ShapeDtypeStruct((tokens, D), F32),
+            jax.ShapeDtypeStruct((tokens, D), F32),
+            jax.ShapeDtypeStruct((tokens, D), F32),
+            jax.ShapeDtypeStruct((H, 2, HALF, 128), BF16),
+            jax.ShapeDtypeStruct((grad_rows, D), BF16),
+            jax.ShapeDtypeStruct((grad_rows, D), BF16),
+            jax.ShapeDtypeStruct((16, D), F32),
+        ),
+        in_specs=[VMEM] * 14,
+        out_specs=(VMEM,) * 7,
+        scratch_shapes=[
+            pltpu.VMEM((2, tokens, D // 2), BF16),
+            pltpu.VMEM((tokens, D), BF16),
+            pltpu.VMEM((2, tokens, units), BF16),
+            pltpu.VMEM((2, BLK, units), F32),
+            pltpu.VMEM((2, tokens, units), BF16),
+            pltpu.VMEM((tokens, D), BF16),
+            pltpu.VMEM((tokens, D), BF16),
+            pltpu.VMEM((2, tokens, D // 2), F32),
+        ],
+        compiler_params=pltpu.CompilerParams(vmem_limit_bytes=56 << 20),
+        name="dense",
+    )(x, summed, cotangent, o, *wo, *we, *ws, *be, *vec)
+
+
+def last_kernel(
+    x_ref, entry_ref, dq_ref, dkv_ref, wq, wk, wv, w_other,
+    out_ref, own_ref, send_ref, vec_ref, tangents,
+):
+    f = lax.axis_index("fsdp")
+    halves = (f, 1 - f)
+    wide = D // 2
+    vec_ref[...] = jnp.zeros_like(vec_ref)
+    for kind in range(2):
+        for pair in range(2):
+            head = halves[kind] * (H // 2) + 2 * pair
+            columns = slice(pair * 128, pair * 128 + 128)
+            for core in range(2):
+                early = dq_ref[head, core].astype(F32)
+                late = dq_ref[head + 1, core].astype(F32)
+                for side in range(2):
+                    start = side * BLK + core * HALF
+                    tangents[kind, 0, start : start + HALF, columns] = side_pair(
+                        side, early, late
+                    ).astype(BF16)
+            early = dkv_ref[head].astype(F32)
+            late = dkv_ref[head + 1].astype(F32)
+            tangents[kind, 1, :, columns] = low_pair(early, late).astype(BF16)
+            tangents[kind, 2, :, columns] = high_pair(early, late).astype(BF16)
+    weights = ((wq, wk, wv), (w_other.at[0], w_other.at[1], w_other.at[2]))
+    total = entry_ref[...]
+    for kind in range(2):
+        for which in range(3):
+            total = total + dot_nt(tangents[kind, which], weights[kind][which][...])
+    out_ref[...] = total
+    low = x_ref[...].astype(BF16)
+    for kind, grad_ref in enumerate((own_ref, send_ref)):
+        grad_ref[0:D, 0:wide] = dot_tn(low, tangents[kind, 0]).astype(BF16)
+        grad_ref[0:D, wide:D] = dot_tn(low, tangents[kind, 1]).astype(BF16)
+        value_grad = dot_tn(low, tangents[kind, 2]).astype(BF16)
+        grad_ref[D : D + wide, 0:wide] = value_grad[0:wide]
+        grad_ref[D : D + wide, wide:D] = value_grad[wide:D]
+        columns = pl.ds(pl.multiple_of(halves[kind] * wide, wide), wide)
+        vec_ref[0:1, columns] = column_sum(tangents[kind, 0].astype(F32))
+        vec_ref[1:2, columns] = column_sum(tangents[kind, 2].astype(F32))
+
+
+def last_dense(x, entry, dq, dkv, wq, wk, wv, w_other):
+    tokens = x.shape[0]
+    grad_rows = D + D // 2
+    return pl.pallas_call(
+        last_kernel,
+        out_shape=(
+            jax.ShapeDtypeStruct((tokens, D), F32),
+            jax.ShapeDtypeStruct((grad_rows, D), BF16),
+            jax.ShapeDtypeStruct((grad_rows, D), BF16),
+            jax.ShapeDtypeStruct((8, D), F32),
+        ),
+        in_specs=[VMEM] * 8,
+        out_specs=(VMEM,) * 4,
+        scratch_shapes=[pltpu.VMEM((2, 3, tokens, D // 2), BF16)],
+        compiler_params=pltpu.CompilerParams(vmem_limit_bytes=48 << 20),
+        name="last_dense",
+    )(x, entry, dq, dkv, wq, wk, wv, w_other)
+
+
+def reduce_kernel(rows, own_ref, send_ref, out_ref, *scratch):
+    first_in, acc, stage = scratch[:3]
+    landing = scratch[3:7]
+    core_ss, core_rs, down_ss, down_rs, up_ss, up_rs = scratch[7:]
+    at = Place()
+    c, f = at.c, at.f
+
+    def step_of(stride):
+        bit = (c // stride) % 2
+        return bit, c + stride * (1 - 2 * bit)
+
+    x_step, y_step, near_z, far_z = step_of(1), step_of(2), step_of(4), step_of(8)
+    plans = ((x_step, y_step, far_z, near_z), (y_step, x_step, far_z, near_z))
+
+    barrier = pltpu.get_barrier_semaphore()
+    pl.semaphore_signal(barrier, 1, device_id=(c, 1 - f), device_id_type=MESH)
+    for _, peer in (x_step, y_step, near_z, far_z):
+        pl.semaphore_signal(barrier, 1, device_id=(peer, f), device_id_type=MESH)
+    pl.semaphore_wait(barrier, 5)
+
+    def span(start, size):
+        return pl.ds(pl.multiple_of(start, 32), size)
+
+    def each(start, size, body):
+        piece = 96 if size % 96 == 0 else 80
+        lax.fori_loop(0, size // piece, lambda i, _: (body(span(start + i * piece, piece)), 0)[1], 0)
+
+    ranges = []
+    for region, plan in enumerate(plans):
+        start, size, listed = region * (rows // 2), rows // 2, []
+        for bit, peer in plan:
+            size = size // 2
+            listed.append((start + bit * size, start + (1 - bit) * size, size, peer))
+            start = start + bit * size
+        ranges.append(listed)
+
+    pieces = [(0, 1), (1, 1), (0, 0), (1, 0)]
+
+    def core_move(index):
+        region, give = pieces[index]
+        kept, given, size, _ = ranges[region][0]
+        where = span(given if give else kept, size)
+        return at.remote(
+            send_ref.at[where], first_in.at[where], core_ss.at[index], core_rs.at[index], c, 1 - f
+        )
+
+    def down_move(region, step):
+        _, given, size, peer = ranges[region][step]
+        where = span(given, size)
+        slot = region * 4 + step
+        return at.remote(
+            stage.at[where], landing[step].at[where], down_ss.at[slot], down_rs.at[slot], peer, f
+        )
+
+    def down_wait(region, step):
+        kept, _, size, peer = ranges[region][step]
+        where = span(kept, size)
+        slot = region * 4 + step
+        at.remote(
+            stage.at[where], landing[step].at[where], down_ss.at[slot], down_rs.at[slot], peer, f
+        ).wait_recv()
+
+    def up_move(region, step):
+        kept, _, size, peer = ranges[region][step]
+        where = span(kept, size)
+        slot = region * 4 + step
+        return at.remote(
+            out_ref.at[where], out_ref.at[where], up_ss.at[slot], up_rs.at[slot], peer, f
+        )
+
+    def up_wait(region, step):
+        _, given, size, peer = ranges[region][step]
+        where = span(given, size)
+        slot = region * 4 + step
+        at.remote(
+            out_ref.at[where], out_ref.at[where], up_ss.at[slot], up_rs.at[slot], peer, f
+        ).wait_recv()
+
+    for index in range(4):
+        core_move(index).start()
+    for index, (region, give) in enumerate(pieces):
+        core_move(index).wait_recv()
+        kept, given, size, _ = ranges[region][0]
+
+        def join(where, target):
+            total = own_ref[where, :].astype(F32) + first_in[where, :].astype(F32)
+            target[where, :] = total.astype(target.dtype)
+
+        if give:
+            each(given, size, lambda where: join(where, stage))
+            down_move(region, 0).start()
+        else:
+            each(kept, size, lambda where: join(where, acc))
+    for step in range(1, 5):
+        for region in range(2):
+            down_wait(region, step - 1)
+            arrived = landing[step - 1]
+
+            def join(where, target):
+                total = acc[where, :] + arrived[where, :].astype(F32)
+                target[where, :] = total.astype(target.dtype)
+
+            if step < 4:
+                kept, given, size, _ = ranges[region][step]
+                each(given, size, lambda where: join(where, stage))
+                down_move(region, step).start()
+                each(kept, size, lambda where: join(where, acc))
+            else:
+                kept, _, size, _ = ranges[region][3]
+                each(kept, size, lambda where: join(where, out_ref))
+                up_move(region, 3).start()
+    for step in (3, 2, 1, 0):
+        for region in range(2):
+            up_wait(region, step)
+            if step > 0:
+                up_move(region, step - 1).start()
+    for index in range(4):
+        core_move(index).wait_send()
+    for region in range(2):
+        for step in range(4):
+            down_move(region, step).wait_send()
+            up_move(region, step).wait_send()
+
+
+def reduce_grads(own, send, ident):
+    rows = own.shape[0]
+    wide = (rows, D)
+    return pl.pallas_call(
+        functools.partial(reduce_kernel, rows),
+        out_shape=jax.ShapeDtypeStruct(wide, BF16),
+        in_specs=[VMEM, VMEM],
+        out_specs=VMEM,
+        scratch_shapes=[pltpu.VMEM(wide, BF16), pltpu.VMEM(wide, F32), pltpu.VMEM(wide, BF16)]
+        + [pltpu.VMEM(wide, BF16)] * 4
+        + [pltpu.SemaphoreType.DMA((4,))] * 2
+        + [pltpu.SemaphoreType.DMA((8,))] * 4,
+        compiler_params=pltpu.CompilerParams(
+            collective_id=ident, has_side_effects=True, vmem_limit_bytes=56 << 20
+        ),
+        name="reduce_grads",
+    )(own, send)
+
+
+def head_shards(
+    n_ctx,
+    post_stream,
+    sum_stream,
+    cotangent,
+    block_order,
+    block_sequence,
+    query_weight,
+    key_weight,
+    value_weight,
+    output_weight,
+    query_bias,
+    value_bias,
+    output_bias,
+    attend_gain,
+    attend_shift,
+    expand_weight,
+    expand_bias,
+    shrink_weight,
+    shrink_bias,
+    middle_gain,
+    middle_shift,
+    final_gain,
+    final_shift,
+):
+    x, summed, tangent = post_stream[0], sum_stream[0], cotangent[0]
+    f = lax.axis_index("fsdp")
+    swap = [(0, 1), (1, 0)]
+
+    def from_other(values):
+        return lax.ppermute(values, "fsdp", swap)
+
+    order_both = lax.all_gather(block_order, "fsdp", axis=0, tiled=True)
+    seqs_both = lax.all_gather(block_sequence, "fsdp", axis=0, tiled=True)
+    group = lax.axis_index("ctx") // H
+    order = lax.dynamic_slice_in_dim(order_both, group, 1, 0)[0]
+    seqs = lax.dynamic_slice_in_dim(seqs_both, group, 1, 0)[0]
+
+    bias = jnp.concatenate(
+        [query_bias[None], value_bias[None], jnp.zeros((6, D // 2), BF16)], axis=0
+    ).astype(F32)
+    q, kv, w_other = project_and_scatter(n_ctx, x, query_weight, key_weight, value_weight, bias)
+    o, keep, lse, pairs = attend(order, seqs, q, kv)
+    o_rows = return_rows(n_ctx, o)
+    vec = jnp.stack(
+        [
+            output_bias,
+            attend_gain,
+            attend_shift,
+            shrink_bias,
+            middle_gain,
+            middle_shift,
+            final_gain,
+            final_shift,
+        ]
+    ).astype(F32)
+    own_bias = expand_bias[None].astype(F32)
+    layer_output, sum_tan, entry, tan_rows, own_feed, send_feed, vec_feed = dense(
+        x,
+        summed,
+        tangent,
+        o_rows,
+        (output_weight, from_other(output_weight)),
+        (expand_weight, from_other(expand_weight)),
+        (shrink_weight, from_other(shrink_weight)),
+        (own_bias, from_other(own_bias)),
+        (vec, from_other(vec)),
+    )
+    tan = scatter_rows(n_ctx, tan_rows)
+    dq, dkv = attend_back(pairs, q, tan, keep, lse, kv)
+    dq_rows, dkv_rows = return_grads(n_ctx, dq, dkv)
+    post_tangent, own_last, send_last, vec_last = last_dense(
+        x, entry, dq_rows, dkv_rows, query_weight, key_weight, value_weight, w_other
+    )
+    grads = reduce_grads(
+        jnp.concatenate([own_feed, own_last]), jnp.concatenate([send_feed, send_last]), 4
+    )
+    vecs = lax.psum(jnp.concatenate([vec_feed, vec_last]), ("ctx", "fsdp"))
+    wide = D // 2
+    units = shrink_weight.shape[0]
+
+    def mine(row):
+        return lax.dynamic_slice_in_dim(vecs[row], f * wide, wide)
+
+    shrink_slope = grads[0:units].astype(F32)
+    expand_slope = jnp.concatenate(
+        [grads[units + i * D : units + i * D + D] for i in range(units // D)], axis=1
+    ).astype(F32)
+    after = 2 * units
+    output_slope = grads[after : after + wide].astype(F32)
+    after = after + wide
+    query_slope = grads[after : after + D, 0:wide].astype(F32)
+    key_slope = grads[after : after + D, wide:D].astype(F32)
+    value_slope = jnp.concatenate(
+        [grads[after + D : after + D + wide, 0:wide], grads[after + D : after + D + wide, wide:D]]
+    ).astype(F32)
+    expand_drift = lax.dynamic_slice_in_dim(vecs[8:12].reshape(4 * D), f * units, units)
+    return (
+        layer_output[None],
+        post_tangent[None],
+        sum_tan[None],
+        query_slope,
+        key_slope,
+        value_slope,
+        output_slope,
+        mine(16),
+        mine(17),
+        mine(7),
+        mine(5),
+        mine(6),
+        expand_slope,
+        expand_drift,
+        shrink_slope,
+        mine(0),
+        mine(1),
+        mine(2),
+        mine(3),
+        mine(4),
+    )
+
+
 def solution(mesh):
+    n_ctx, n_fsdp = mesh.shape["ctx"], mesh.shape["fsdp"]
+    if n_fsdp == 2 and n_ctx == n_fsdp * H:
+        body = functools.partial(head_shards, n_ctx)
+    else:
+        body = general_shards
     return jax.shard_map(
-        shards,
+        body,
         mesh=mesh,
         in_specs=(
             P("fsdp", "ctx", None),

time: 1600 us -> 410 us (0.26)
  other arithmetic: 484 us -> 15.6 us
  waiting for transfers between devices: 324 us -> 0.01 us
  Pallas kernels: 0 us -> 313 us
  blocking collectives: 331 us -> 52.8 us
  matrix products: 205 us -> 0 us
  local copies, waits for them, and re-layouts: 155 us -> 23.8 us
  loops' own time: 93.7 us -> 0 us
    pallas_call x0 -> x9, Pallas kernels: none -> 313 us  [the longest x1 106 us: reduce_grads(): pl.pallas_call(functools.partial(reduce_kernel, rows), out_shape=jax.Shap...]
    reduce_or x128 -> x0, other arithmetic: 246 us -> none  [the longest x96 185 us: unit_step(): jnp.any(visible)]
    all_gather x17 -> x2, blocking collectives: 247 us -> 3.78 us  [the longest x1 1.89 us: head_shards(): order_both = lax.all_gather(block_order, 'fsdp', axis=0, tiled=True)]
    dot_general x65 -> x0, matrix products: 205 us -> none  [the longest x9 45.5 us: owner_block(): jnp.einsum('hqk,qhd->khd', score_tan, part_queries, preferred_element_typ...]
    reduce_sum x144 -> x0, other arithmetic: 176 us -> none  [the longest x129 164 us: lookup(): jnp.sum(jnp.where(indices[:, None] == places[None, :], table_row[None, :]...]
    psum x1 -> x0, waiting for transfers between devices: 126 us -> none  [shards(): lax.psum((slope_query, slope_key, slope_value, slope_output, drift_query,...]
    dynamic_slice x161 -> x6, local copies, waits for them, and re-layouts: 115 us -> 3.43 us  [the longest x5 2.84 us: mine(): return lax.dynamic_slice_in_dim(vecs[row], f * wide, wide)]
    reduce_scatter x6 -> x0, waiting for transfers between devices: 111 us -> none  [the longest x1 99.2 us: shards(): lax.psum_scatter(heads_parts[1], 'fsdp', scatter_dimension=1, tiled=True)]
  transfers between devices with their start and end apart: 13 -> 5, of which waited for: 4 -> 0; matrix products, arithmetic and copies ran while one was open for 51% -> 2% of each run, Pallas kernels for 0% -> 22%
where the time goes in v1:
time: 410 us; the launch traced here: 407 us
  Pallas kernels  313 us (76%)
  blocking collectives  52.8 us (13%)
  local copies, waits for them, and re-layouts  23.8 us (6%)
  other arithmetic  15.6 us (4%)
    pallas_call x1, Pallas kernels, reduce_grads(): pl.pallas_call(functools.partial(reduce_kernel, rows), out_shape=jax.Shap...  106 us
    psum x1, blocking collectives, head_shards(): vecs = lax.psum(jnp.concatenate([vec_feed, vec_last]), ('ctx', 'fsdp'))  49 us
    pallas_call x1, Pallas kernels, return_grads(): pl.pallas_call(functools.partial(return_grads_kernel, n_ctx), out_shape=(...  41.6 us
    pallas_call x1, Pallas kernels, attend_back(): pl.pallas_call(functools.partial(backward_kernel, blocks), out_shape=(jax...  33.7 us
    pallas_call x1, Pallas kernels, return_rows(): pl.pallas_call(functools.partial(return_kernel, n_ctx), out_shape=jax.Sha...  31.6 us
    pallas_call x1, Pallas kernels, project_and_scatter(): pl.pallas_call(functools.partial(project_kernel, n_ctx), out_shape=(jax.S...  29.7 us
    pallas_call x1, Pallas kernels, attend(): pl.pallas_call(functools.partial(forward_kernel, blocks), out_shape=(jax....  28.8 us
    pallas_call x1, Pallas kernels, dense(): pl.pallas_call(dense_kernel, out_shape=(jax.ShapeDtypeStruct((tokens, D),...  24.3 us
  transfers between devices with their start and end apart: 5, of which 0 were waited for; matrix products, arithmetic and copies ran while one was open for 2% of the time, Pallas kernels for 22%

profile of v1, /device:TPU:0, one launch (start us, length us, event | category | flops | bytes accessed | tf_op | source)
XLA Modules:
  0.0 407.5 jit_solution(17999938454681249752)
XLA Ops:
  1.3 0.7 stack.27
  1.9 0.7 stack.28
  2.6 0.7 stack.29
  3.2 0.7 stack.30
  3.9 0.7 stack.31
  4.5 0.7 stack.32
  5.2 0.7 stack.33
  5.9 0.7 stack.34
  6.6 0.6 convert_element_type.32.vec_a
  7.6 1.3 convert_element_type.39
  9.4 0.7 broadcast_in_dim.19
  10.0 0.7 broadcast_in_dim.20
  10.8 1.9 all-gather.1
  12.7 1.9 all-gather
  14.6 1.2 copy-done
  15.9 0.9 copy-done.8
  16.8 0.9 copy-done.10
  17.8 0.9 copy-done.12
  18.7 29.7 %project_scatter.1 = (bf16[16,128,128]{2,1,0:T(8,128)(2,1)S(1)}, bf16[32,256,128]{2,1,0:T(8,128)(2,1)S(1)}, bf16[3,512,256]{2,1,0:T(8,128)(2,1)S(1)}) custom-call(f32[512,512]{1,0:T(8,128)S(1)} %bitcast.27, bf16[512,256]{1,0:T(8,128)(2,1)S(1)} %copy-done.8, bf16[512,256]{1,0:T(8,128)(2,1)S(1)} %copy-done.10, bf16[512,256]{1,0:T(8,128)(2,1)S(1)} %copy-done.12, ...), custom_call_target="tpu_custom_call" | custom-call | tf_op jit(solution)/shard_map/project_scatter/pallas_call | solution.py:657
  48.4 28.8 %attend.1 = (bf16[16,128,128]{2,1,0:T(8,128)(2,1)S(1)}, f32[16,128,128]{2,1,0:T(8,128)S(1)}, f32[32,8,128]{2,1,0:T(8,128)S(1)}, s32[3,256]{1,0:T(4,128)S(1)}) custom-call(s32[32]{0:T(128)S(1)} %fusion.order_ref, s32[32]{0:T(128)S(1)} %fusion.1.seq_ref, bf16[16,128,128]{2,1,0:T(8,128)(2,1)S(1)} %get-tuple-element.42.q_ref, ...), custom_call_target="tpu_custom_call" | custom-call | tf_op jit(solution)/shard_map/attend/pallas_call | solution.py:792
  77.2 1.0 copy-done.4
  78.2 0.8 copy-done.14
  78.9 31.6 %return_rows.1.o_ref = bf16[8,2,128,128]{3,2,1,0:T(8,128)(2,1)} custom-call(bf16[16,128,128]{2,1,0:T(8,128)(2,1)} %copy-done.14), custom_call_target="tpu_custom_call" | custom-call | tf_op jit(solution)/shard_map/return_rows/pallas_call | solution.py:935
  110.6 24.3 %dense.1 = (f32[512,512]{1,0:T(8,128)}, f32[512,512]{1,0:T(8,128)}, f32[512,512]{1,0:T(8,128)}, bf16[8,2,128,128]{3,2,1,0:T(8,128)(2,1)}, bf16[2304,512]{1,0:T(8...) custom-call(f32[512,512]{1,0:T(8,128)} %bitcast.26, f32[512,512]{1,0:T(8,128)} %bitcast.29, ...), custom_call_target="tpu_custom_call" | custom-call | tf_op jit(solution)/shard_map/dense/pallas_call | solution.py:1240
  135.0 13.2 %scatter_rows.1.tan_ref = bf16[16,128,128]{2,1,0:T(8,128)(2,1)} custom-call(bf16[8,2,128,128]{3,2,1,0:T(8,128)(2,1)} %get-tuple-element.48.rows_ref), custom_call_target="tpu_custom_call" | custom-call | tf_op jit(solution)/shard_map/scatter_rows/pallas_call | solution.py:975
  148.2 1.0 copy-done.3
  149.3 1.2 copy-done.5
  150.5 33.7 %attend_back.1 = (bf16[16,128,128]{2,1,0:T(8,128)(2,1)S(1)}, f32[32,256,128]{2,1,0:T(8,128)}) custom-call(s32[3,256]{1,0:T(4,128)S(1)} %get-tuple-element.47.pairs_ref, bf16[16,128,128]{2,1,0:T(8,128)(2,1)S(1)} %get-tuple-element.42.q_ref, bf16[16,128,128]{2,1,0:T(8,128)(2,1)S(1)} %copy-done.3, f32[16,128,128]{2,1,0:T(8,128)S(1)} %copy-done.5, ...), custom_call_target="tpu_custom_call" | custom-call | tf_op jit(solution)/shard_map/attend_back/pallas_call | solution.py:889
  184.2 2.3 copy-done.2
  186.5 41.6 %return_grads.1 = (bf16[8,2,128,128]{3,2,1,0:T(8,128)(2,1)S(1)}, bf16[8,512,128]{2,1,0:T(8,128)(2,1)S(1)}) custom-call(bf16[16,128,128]{2,1,0:T(8,128)(2,1)S(1)} %get-tuple-element.51.dq_ref, f32[32,256,128]{2,1,0:T(8,128)S(1)} %copy-done.2), custom_call_target="tpu_custom_call" | custom-call | tf_op jit(solution)/shard_map/return_grads/pallas_call | solution.py:1056
  228.1 1.0 copy-done.7
  229.1 3.5 last_dense.1
  232.6 49.0 %psum.7 = f32[24,512]{1,0:T(8,128)S(1)} all-reduce(f32[24,512]{1,0:T(8,128)S(1)} %pad_maximum_fusion.2), channel_id=1, replica_groups=mesh['ctx'=16,'fsdp'=2] {'ctx','fsdp'}, use_global_device_ids=true, to_apply=%region_0.1 | all-reduce | flops 12288 | bytes 98304 | tf_op jit(solution)/shard_map/psum | solution.py:1549
  281.7 4.5 %pad_maximum_fusion = (bf16[3072,512]{1,0:T(8,128)(2,1)}, bf16[3072,512]{1,0:T(8,128)(2,1)}) fusion(bf16[768,512]{1,0:T(8,128)(2,1)S(1)} %get-tuple-element.59, bf16[2304,512]{1,0:T(8,128)(2,1)} %get-tuple-element.58, bf16[768,512]{1,0:T(8,128)(2,1)S(1)} %get-tuple-element.61, bf16[2304,512]{1,0:T(8,128)(2,1)} %get-tuple-element.60), kind=kLoop, calls=%fused_computation | loop fusion | flops 12582912 | bytes 12582912 | tf_op jit(solution)/shard_map/concatenate | solution.py:1547
  286.2 106.5 %reduce_grads.1 = bf16[3072,512]{1,0:T(8,128)(2,1)} custom-call(bf16[3072,512]{1,0:T(8,128)(2,1)} %get-tuple-element.80.own_ref, bf16[3072,512]{1,0:T(8,128)(2,1)} %get-tuple-element.81.send_ref), custom_call_target="tpu_custom_call" | custom-call | tf_op jit(solution)/shard_map/reduce_grads/pallas_call | solution.py:1456
  392.7 1.3 fusion.2
  393.9 2.8 slice_convert_fusion
  396.8 1.0 fusion.3
  397.8 2.1 slice_convert_fusion.2
  399.8 1.8 slice_convert_fusion.1
  401.6 0.6 constant_dynamic-slice_fusion
  402.2 0.6 constant_dynamic-slice_fusion.2
  402.8 1.6 maximum_convert_fusion
  404.4 0.6 constant_dynamic-slice_fusion.4
  404.9 0.6 dynamic_slice.71
  405.5 0.6 constant_dynamic-slice_fusion.6
  406.1 0.6 constant_dynamic-slice_fusion.8
  406.7 0.8 maximum_convert_fusion.1
  (42 shorter events, 1.8 us)
Async XLA Ops:
  0.7 110.0 %collective-permute-start.1 = (bf16[512,1024]{1,0:T(8,128)(2,1)}, bf16[512,1024]{1,0:T(8,128)(2,1)}, u32[]{:S(2)}, u32[]{:S(2)}) collective-permute-start(bf16[512,1024]{1,0:T(8,128)(2,1)} %we_a.1), channel_id=1, source_target_pairs={{0,1},{1,0},{2,3},{3,2},{4,5},{5,4},{6,7},{7,6},{8,9},{9,8},{10,11... | collective-permute-start | bytes 3145736 | tf_op jit(solution)/shard_map/ppermute | solution.py:1502
  1.2 109.5 %collective-permute-start.2 = (bf16[1024,512]{1,0:T(8,128)(2,1)}, bf16[1024,512]{1,0:T(8,128)(2,1)}, u32[]{:S(2)}, u32[]{:S(2)}) collective-permute-start(bf16[1024,512]{1,0:T(8,128)(2,1)} %ws_a.1), channel_id=1, source_target_pairs={{0,1},{1,0},{2,3},{3,2},{4,5},{5,4},{6,7},{7,6},{8,9},{9,8},{10,11... | collective-permute-start | bytes 3145736 | tf_op jit(solution)/shard_map/ppermute | solution.py:1502
  7.2 103.4 %collective-permute-start.4 = (f32[8,256]{1,0:T(8,128)}, f32[8,256]{1,0:T(8,128)}, u32[]{:S(2)}, u32[]{:S(2)}) collective-permute-start(f32[8,256]{1,0:T(8,128)} %convert_element_type.32.vec_a), channel_id=1, source_target_pairs={{0,1},{1,0},{2,3},{3,2},{4,5},{5,4},{6,7},{7,6},{8,9},{9,8},{10,11... | collective-permute-start | bytes 24584 | tf_op jit(solution)/shard_map/ppermute | solution.py:1502
  8.9 101.7 %collective-permute-start.3 = (f32[1,1024]{1,0:T(1,128)}, f32[1,1024]{1,0:T(1,128)}, u32[]{:S(2)}, u32[]{:S(2)}) collective-permute-start(f32[1,1024]{1,0:T(1,128)} %bitcast.7.be_a), channel_id=1, source_target_pairs={{0,1},{1,0},{2,3},{3,2},{4,5},{5,4},{6,7},{7,6},{8,9},{9,8},{10,11... | collective-permute-start | bytes 12296 | tf_op jit(solution)/shard_map/ppermute | solution.py:1502
  8.9 101.7 %collective-permute-start = (bf16[256,512]{1,0:T(8,128)(2,1)}, bf16[256,512]{1,0:T(8,128)(2,1)}, u32[]{:S(2)}, u32[]{:S(2)}) collective-permute-start(bf16[256,512]{1,0:T(8,128)(2,1)} %wo_a.1), channel_id=1, source_target_pairs={{0,1},{1,0},{2,3},{3,2},{4,5},{5,4},{6,7},{7,6},{8,9},{9,8},{10,11... | collective-permute-start | bytes 786440 | tf_op jit(solution)/shard_map/ppermute | solution.py:1502
  14.6 1.2 copy-start
  15.9 0.9 copy-start.8
  16.8 0.9 copy-start.10
  17.8 0.9 copy-start.12
  77.2 1.0 copy-start.4
  78.2 0.8 copy-start.14
  148.2 1.0 copy-start.3
  149.3 1.2 copy-start.5
  150.5 78.6 %copy-start.6 = (f32[512,512]{1,0:T(8,128)S(1)}, f32[512,512]{1,0:T(8,128)}, u32[]{:S(2)}) copy-start(f32[512,512]{1,0:T(8,128)} %get-tuple-element.46.entry_ref) | copy-start | bytes 3145732
  150.5 78.6 %copy-start.9 = (bf16[512,256]{1,0:T(8,128)(2,1)S(1)}, bf16[512,256]{1,0:T(8,128)(2,1)}, u32[]{:S(2)}) copy-start(bf16[512,256]{1,0:T(8,128)(2,1)} %wq.1) | copy-start | bytes 786436
  150.5 78.6 %copy-start.11 = (bf16[512,256]{1,0:T(8,128)(2,1)S(1)}, bf16[512,256]{1,0:T(8,128)(2,1)}, u32[]{:S(2)}) copy-start(bf16[512,256]{1,0:T(8,128)(2,1)} %wk.1) | copy-start | bytes 786436
  150.5 78.6 %copy-start.13 = (bf16[512,256]{1,0:T(8,128)(2,1)S(1)}, bf16[512,256]{1,0:T(8,128)(2,1)}, u32[]{:S(2)}) copy-start(bf16[512,256]{1,0:T(8,128)(2,1)} %wv.1) | copy-start | bytes 786436
  184.2 44.9 %copy-start.1 = (f32[1,512,512]{2,1,0:T(8,128)S(1)}, f32[1,512,512]{2,1,0:T(8,128)}, u32[]{:S(2)}) copy-start(f32[1,512,512]{2,1,0:T(8,128)} %param.22) | copy-start | bytes 3145732
  184.2 2.3 copy-start.2
  228.1 1.0 copy-start.7
  229.1 3.5 copy-start.15

commit v2 on v1

--- a/solution.py
+++ b/solution.py
@@ -13,6 +13,9 @@
 BLK = 256
 HALF = BLK // 2
 LONG = 8
+TOGETHER = 16
+BACK_TOGETHER = 8
+MOST = LONG + 1
 F32 = jnp.float32
 BF16 = jnp.bfloat16
 MESH = pl.DeviceIdType.MESH
@@ -505,7 +508,7 @@
             )
         pl.semaphore_wait(barrier, 2 * H + (1 if partner else 0) - self.inside)
 
-    def greet_owners(self, n_ctx, partner):
+    def greet_owners(self, n_ctx, partner, more=0):
         barrier = pltpu.get_barrier_semaphore()
         for head in range(H):
             for core in range(2):
@@ -514,7 +517,7 @@
             pl.semaphore_signal(
                 barrier, 1, device_id=(self.c, 1 - self.f), device_id_type=MESH
             )
-        pl.semaphore_wait(barrier, n_ctx + (1 if partner else 0) - self.inside)
+        pl.semaphore_wait(barrier, n_ctx + (1 if partner else 0) + more - self.inside)
 
     def send(self, src, dst, send_sem, recv_sem, tc, tf):
         me = self.is_me(tc, tf)
@@ -543,41 +546,65 @@
             self.remote(src, dst, send_sem, recv_sem, tc, tf).wait_send()
 
 
+BIAS_ROWS = 16
+
+
 def project_kernel(
     n_ctx,
     x_ref,
     wq_ref,
     wk_ref,
     wv_ref,
-    bias_ref,
-    q_out,
-    kv_out,
-    w_other,
-    x_low,
-    w_in,
-    bias_in,
-    q_send,
-    kv_send,
-    w_ss,
-    w_rs,
-    q_ss,
-    q_rs,
-    kv_ss,
-    kv_rs,
-    relay_ss,
-    relay_rs,
+    order_ref,
+    seq_ref,
+    expand_ref,
+    *rest,
 ):
+    vector_refs, rest = rest[:10], rest[10:]
+    (
+        q_out,
+        kv_out,
+        w_other,
+        order_out,
+        seq_out,
+        vec_out,
+        expand_out,
+        x_low,
+        w_in,
+        bias_own,
+        bias_in,
+        order_in,
+        seq_in,
+        q_send,
+        kv_send,
+        w_ss,
+        w_rs,
+        q_ss,
+        q_rs,
+        kv_ss,
+        kv_rs,
+        relay_ss,
+        relay_rs,
+    ) = rest
     at = Place()
     other = 1 - at.f
+    wide = wq_ref.shape[1]
+    for row, ref in enumerate(vector_refs):
+        bias_own[row : row + 1, :] = ref[...].astype(F32)
+    for part in range(expand_ref.shape[1] // wide):
+        row = len(vector_refs) + part
+        bias_own[row : row + 1, :] = expand_ref[:, part * wide : part * wide + wide].astype(F32)
     at.greet_sources(n_ctx, True)
     swaps = [
         at.remote(src, dst, w_ss.at[i], w_rs.at[i], at.c, other)
         for i, (src, dst) in enumerate(
             (
-                (bias_ref, bias_in),
+                (bias_own, bias_in),
                 (wq_ref, w_in.at[0]),
                 (wk_ref, w_in.at[1]),
                 (wv_ref, w_in.at[2]),
+                (order_ref, order_in),
+                (seq_ref, seq_in),
             )
         )
     ]
@@ -622,11 +649,21 @@
             at.send(*kv_move)
             at.send(*q_move)
 
-    one_half(at.f, wq_ref, wk_ref, wv_ref, bias_ref)
+    one_half(at.f, wq_ref, wk_ref, wv_ref, bias_own)
     for swap in swaps:
         swap.wait()
     one_half(other, w_in.at[0], w_in.at[1], w_in.at[2], bias_in)
     w_other[...] = w_in[...]
+    inside = at.inside == 1
+    order_out[...] = jnp.where(inside, order_ref[...], order_in[...])
+    seq_out[...] = jnp.where(inside, seq_ref[...], seq_in[...])
+    vec_out[...] = whole_rows(bias_own[...], bias_in[...], at.f == 0)
+    for row, source in enumerate((bias_own, bias_in)):
+        for part in range(expand_ref.shape[1] // wide):
+            at_row = len(vector_refs) + part
+            expand_out[row : row + 1, part * wide : part * wide + wide] = source[
+                at_row : at_row + 1, :
+            ]
 
     def relay(source):
         mine = kv_out.at[2 * source + at.f]
@@ -652,25 +689,33 @@
             at.wait_sent(*q_move)
 
 
-def project_and_scatter(n_ctx, x, wq, wk, wv, bias):
+def project_and_scatter(n_ctx, x, wq, wk, wv, order, seqs, expand, vectors):
     wide = wq.shape[1]
+    blocks = order.shape[1]
     return pl.pallas_call(
         functools.partial(project_kernel, n_ctx),
         out_shape=(
             jax.ShapeDtypeStruct((n_ctx, HALF, 128), BF16),
             jax.ShapeDtypeStruct((2 * n_ctx, BLK, 128), BF16),
             jax.ShapeDtypeStruct((3, D, wide), BF16),
+            jax.ShapeDtypeStruct((1, blocks), jnp.int32),
+            jax.ShapeDtypeStruct((1, blocks), jnp.int32),
+            jax.ShapeDtypeStruct((BIAS_ROWS, D), F32),
+            jax.ShapeDtypeStruct((2, expand.shape[1]), F32),
         ),
-        in_specs=[VMEM] * 5,
-        out_specs=(ANY, ANY, VMEM),
+        in_specs=[VMEM] * 17,
+        out_specs=(ANY, ANY) + (VMEM,) * 5,
         scratch_shapes=[
             pltpu.VMEM((2 * BLK, D), BF16),
             pltpu.VMEM((3, D, wide), BF16),
-            pltpu.VMEM((8, wide), F32),
+            pltpu.VMEM((BIAS_ROWS, wide), F32),
+            pltpu.VMEM((BIAS_ROWS, wide), F32),
+            pltpu.VMEM((1, blocks), jnp.int32),
+            pltpu.VMEM((1, blocks), jnp.int32),
             pltpu.VMEM((H, 2, HALF, 128), BF16),
             pltpu.VMEM((H, 2 * BLK, 128), BF16),
-            pltpu.SemaphoreType.DMA((4,)),
-            pltpu.SemaphoreType.DMA((4,)),
+            pltpu.SemaphoreType.DMA((6,)),
+            pltpu.SemaphoreType.DMA((6,)),
             pltpu.SemaphoreType.DMA((2 * H,)),
             pltpu.SemaphoreType.DMA((n_ctx,)),
             pltpu.SemaphoreType.DMA((2 * H,)),
@@ -682,7 +727,7 @@
             collective_id=0, has_side_effects=True, vmem_limit_bytes=48 << 20
         ),
         name="project_scatter",
-    )(x, wq, wk, wv, bias)
+    )(x, wq, wk, wv, order, seqs, expand, *vectors)
 
 
 def forward_kernel(
@@ -700,102 +745,125 @@
     peaks,
     masses,
     total,
+    scores,
 ):
     def place_block(slot, _):
-        place[order_ref[slot]] = slot
+        place[order_ref[0, slot]] = slot
         return 0
 
     lax.fori_loop(0, blocks, place_block, 0)
 
-    def unpack(source, _):
-        packed = q_ref[source].astype(F32) * (HD**-0.5)
-        q_low[2 * source] = jnp.where(low_lanes(packed), packed, 0.0).astype(BF16)
-        q_low[2 * source + 1] = jnp.where(low_lanes(packed), swap_lanes(packed), 0.0).astype(BF16)
-        return 0
-
-    lax.fori_loop(0, blocks // 2, unpack, 0)
-    q_low[blocks] = jnp.zeros((HALF, 128), BF16)
-    peaks[blocks] = jnp.zeros((HALF, 128), F32)
-    masses[blocks] = jnp.zeros((HALF, 128), F32)
-    total[blocks] = jnp.zeros((HALF, 128), F32)
-
     count = jnp.int32(0)
-    for gap in range(1, LONG):
+    for gap in range(LONG):
 
         def look(late, found):
             pairs_ref[0, found] = place[late]
             pairs_ref[1, found] = place[late - gap]
-            return found + jnp.where(seq_ref[late] == seq_ref[late - gap], 1, 0)
+            return found + jnp.where(seq_ref[0, late] == seq_ref[0, late - gap], 1, 0)
 
         count = lax.fori_loop(gap, blocks, look, count)
-    for spare in range(4):
+    for spare in range(TOGETHER):
         pairs_ref[0, count + spare] = blocks
         pairs_ref[1, count + spare] = 0
-    turns = (count + 3) // 4
-    pairs_ref[2, 0] = turns
-
-    def own_blocks(step, _):
+    turns = (count + TOGETHER - 1) // TOGETHER
+    pairs_ref[2, 1] = (count + BACK_TOGETHER - 1) // BACK_TOGETHER
+
+    def unpack(step, _):
+        for part in range(4):
+            source = step * 4 + part
+            packed = q_ref[source].astype(F32) * (HD**-0.5)
+            low = low_lanes(packed)
+            q_low[2 * source] = jnp.where(low, packed, 0.0).astype(BF16)
+            q_low[2 * source + 1] = jnp.where(low, swap_lanes(packed), 0.0).astype(BF16)
+        return 0
+
+    lax.fori_loop(0, blocks // 8, unpack, 0)
+    q_low[blocks] = jnp.zeros((HALF, 128), BF16)
+
+    def clear(slot, _):
+        peaks[slot] = jnp.full((HALF, 128), masked_value, F32)
+        masses[slot] = jnp.zeros((HALF, 128), F32)
+        total[slot] = jnp.zeros((HALF, 128), F32)
+        return 0
+
+    lax.fori_loop(0, blocks + 1, clear, 0)
+
+    def score(step, _):
+        slots, results = [], []
+        for part in range(TOGETHER):
+            index = step * TOGETHER + part
+            q_slot = pairs_ref[0, index]
+            result = dot_nt(q_low[q_slot], kv_ref[pairs_ref[1, index]])
+            scores[index] = result
+            slots.append(q_slot)
+            results.append(jnp.maximum(result[:, :128], result[:, 128:]))
+        for q_slot, result in zip(slots, results):
+            peaks[q_slot] = jnp.maximum(peaks[q_slot], result)
+        return 0
+
+    lax.fori_loop(0, turns, score, 0)
+
+    def level(step, _):
         for part in range(4):
             slot = step * 4 + part
-            scores = dot_nt(q_low[slot], kv_ref[slot])
-            peak = jnp.broadcast_to(jnp.max(scores, axis=1, keepdims=True), (HALF, 128))
-            left = jnp.exp(scores[:, :128] - peak)
-            right = jnp.exp(scores[:, 128:] - peak)
-            peaks[slot] = peak
-            masses[slot] = left + right
+            peaks[slot] = jnp.broadcast_to(
+                jnp.max(peaks[slot], axis=1, keepdims=True), (HALF, 128)
+            )
+        return 0
+
+    lax.fori_loop(0, blocks // 4, level, 0)
+
+    def weigh(step, _):
+        slots, results = [], []
+        for part in range(TOGETHER):
+            index = step * TOGETHER + part
+            q_slot = pairs_ref[0, index]
+            peak = peaks[q_slot]
+            left = jnp.exp(scores[index, :, :128] - peak)
+            right = jnp.exp(scores[index, :, 128:] - peak)
             weights = jnp.concatenate([left, right], axis=1).astype(BF16)
-            total[slot] = dot_nn(weights, kv_ref[slot])
+            slots.append(q_slot)
+            results.append((left + right, dot_nn(weights, kv_ref[pairs_ref[1, index]])))
+        for q_slot, (mass, part_total) in zip(slots, results):
+            masses[q_slot] = masses[q_slot] + mass
+            total[q_slot] = total[q_slot] + part_total
         return 0
 
-    lax.fori_loop(0, blocks // 4, own_blocks, 0)
-
-    def other_blocks(step, _):
+    lax.fori_loop(0, turns, weigh, 0)
+
+    def finish(step, _):
         for part in range(4):
-            q_slot = pairs_ref[0, step * 4 + part]
-            k_slot = pairs_ref[1, step * 4 + part]
-            scores = dot_nt(q_low[q_slot], kv_ref[k_slot])
-            before = peaks[q_slot]
-            peak = jnp.maximum(
-                before, jnp.broadcast_to(jnp.max(scores, axis=1, keepdims=True), (HALF, 128))
-            )
-            fade = jnp.exp(before - peak)
-            left = jnp.exp(scores[:, :128] - peak)
-            right = jnp.exp(scores[:, 128:] - peak)
-            peaks[q_slot] = peak
-            masses[q_slot] = masses[q_slot] * fade + (left + right)
-            weights = jnp.concatenate([left, right], axis=1).astype(BF16)
-            total[q_slot] = total[q_slot] * fade + dot_nn(weights, kv_ref[k_slot])
+            source = step * 4 + part
+            results = []
+            for side in range(2):
+                slot = 2 * source + side
+                mass = jnp.broadcast_to(
+                    jnp.sum(masses[slot], axis=1, keepdims=True), (HALF, 128)
+                )
+                results.append(total[slot] / mass)
+                lse_ref[slot] = jnp.transpose(peaks[slot] + jnp.log(mass))[0:8]
+            packed = high_pair(results[0], results[1])
+            keep_ref[source] = packed
+            o_ref[source] = packed.astype(BF16)
         return 0
 
-    lax.fori_loop(0, turns, other_blocks, 0)
-
-    def finish(source, _):
-        results = []
-        for side in range(2):
-            slot = 2 * source + side
-            mass = jnp.broadcast_to(
-                jnp.sum(masses[slot], axis=1, keepdims=True), (HALF, 128)
-            )
-            results.append(total[slot] / mass)
-            lse_ref[slot] = jnp.transpose(peaks[slot] + jnp.log(mass))[0:8]
-        packed = high_pair(results[0], results[1])
-        keep_ref[source] = packed
-        o_ref[source] = packed.astype(BF16)
-        return 0
-
-    lax.fori_loop(0, blocks // 2, finish, 0)
+    lax.fori_loop(0, blocks // 8, finish, 0)
+
+
+def pair_room(blocks):
+    return blocks * MOST // 2 + TOGETHER
 
 
 def attend(order, seqs, q, kv):
     blocks = kv.shape[0]
-    pair_room = blocks * LONG
+    room = pair_room(blocks)
     return pl.pallas_call(
         functools.partial(forward_kernel, blocks),
         out_shape=(
             jax.ShapeDtypeStruct((blocks // 2, HALF, 128), BF16),
             jax.ShapeDtypeStruct((blocks // 2, HALF, 128), F32),
             jax.ShapeDtypeStruct((blocks, 8, HALF), F32),
-            jax.ShapeDtypeStruct((3, pair_room), jnp.int32),
+            jax.ShapeDtypeStruct((3, room), jnp.int32),
         ),
         in_specs=[SMEM, SMEM, VMEM, VMEM],
         out_specs=(VMEM, VMEM, VMEM, SMEM),
@@ -805,6 +873,7 @@
             pltpu.VMEM((blocks + 1, HALF, 128), F32),
             pltpu.VMEM((blocks + 1, HALF, 128), F32),
             pltpu.VMEM((blocks + 1, HALF, 128), F32),
+            pltpu.VMEM((room, HALF, BLK), F32),
         ],
         compiler_params=pltpu.CompilerParams(vmem_limit_bytes=48 << 20),
         name="attend",
@@ -826,25 +895,34 @@
     delta_rows,
     dq_sum,
 ):
-    def unpack(source, _):
-        packed = q_ref[source].astype(F32) * (HD**-0.5)
-        tangent = tan_ref[source].astype(F32)
-        low = low_lanes(packed)
-        both[2 * source, 0:HALF] = jnp.where(low, packed, 0.0).astype(BF16)
-        both[2 * source + 1, 0:HALF] = jnp.where(low, swap_lanes(packed), 0.0).astype(BF16)
-        both[2 * source, HALF:BLK] = jnp.where(low, 0.0, swap_lanes(tangent)).astype(BF16)
-        both[2 * source + 1, HALF:BLK] = jnp.where(low, 0.0, tangent).astype(BF16)
-        across = jnp.transpose(tangent * keep_ref[source])
-        for side in range(2):
-            delta = jnp.sum(across[side * HD : side * HD + HD], axis=0, keepdims=True)
-            delta_rows[2 * source + side] = jnp.broadcast_to(delta, (8, HALF))
-            mass_rows[2 * source + side] = lse_ref[2 * source + side]
+    def unpack(step, _):
+        for part in range(4):
+            source = step * 4 + part
+            packed = q_ref[source].astype(F32) * (HD**-0.5)
+            tangent = tan_ref[source].astype(F32)
+            low = low_lanes(packed)
+            both[2 * source, 0:HALF] = jnp.where(low, packed, 0.0).astype(BF16)
+            both[2 * source + 1, 0:HALF] = jnp.where(low, swap_lanes(packed), 0.0).astype(BF16)
+            both[2 * source, HALF:BLK] = jnp.where(low, 0.0, swap_lanes(tangent)).astype(BF16)
+            both[2 * source + 1, HALF:BLK] = jnp.where(low, 0.0, tangent).astype(BF16)
+            across = jnp.transpose(tangent * keep_ref[source])
+            for side in range(2):
+                delta = jnp.sum(across[side * HD : side * HD + HD], axis=0, keepdims=True)
+                delta_rows[2 * source + side] = jnp.broadcast_to(delta, (8, HALF))
+                mass_rows[2 * source + side] = lse_ref[2 * source + side]
         return 0
 
-    lax.fori_loop(0, blocks // 2, unpack, 0)
+    lax.fori_loop(0, blocks // 8, unpack, 0)
     both[blocks] = jnp.zeros((BLK, 128), BF16)
     mass_rows[blocks] = jnp.zeros((8, HALF), F32)
     delta_rows[blocks] = jnp.zeros((8, HALF), F32)
+
+    def clear(slot, _):
+        dq_sum[slot] = jnp.zeros((HALF, 128), F32)
+        dkv_ref[slot] = jnp.zeros((BLK, 128), F32)
+        return 0
+
+    lax.fori_loop(0, blocks, clear, 0)
     dq_sum[blocks] = jnp.zeros((HALF, 128), F32)
 
     def one_pair(q_slot, k_slot):
@@ -856,32 +934,27 @@
         sides = jnp.concatenate([score_tan, weights.astype(BF16)], axis=1)
         return dot_nn(sides, stacked), dot_tn(score_tan, kv)
 
-    def own_blocks(step, _):
-        for part in range(4):
-            slot = step * 4 + part
-            dkv, dq = one_pair(slot, slot)
-            dkv_ref[slot] = dkv
-            dq_sum[slot] = dq
-        return 0
-
-    lax.fori_loop(0, blocks // 4, own_blocks, 0)
-
-    def other_blocks(step, _):
-        slots = [(pairs_ref[0, step * 4 + part], pairs_ref[1, step * 4 + part]) for part in range(4)]
+    def pair_turn(step, _):
+        slots = [
+            (pairs_ref[0, step * BACK_TOGETHER + part], pairs_ref[1, step * BACK_TOGETHER + part])
+            for part in range(BACK_TOGETHER)
+        ]
         results = [one_pair(*slot) for slot in slots]
         for (q_slot, k_slot), (dkv, dq) in zip(slots, results):
             dkv_ref[k_slot] = dkv_ref[k_slot] + dkv
             dq_sum[q_slot] = dq_sum[q_slot] + dq
         return 0
 
-    lax.fori_loop(0, pairs_ref[2, 0], other_blocks, 0)
-
-    def finish(source, _):
-        packed = low_pair(dq_sum[2 * source], dq_sum[2 * source + 1]) * (HD**-0.5)
-        dq_ref[source] = packed.astype(BF16)
+    lax.fori_loop(0, pairs_ref[2, 1], pair_turn, 0)
+
+    def finish(step, _):
+        for part in range(4):
+            source = step * 4 + part
+            packed = low_pair(dq_sum[2 * source], dq_sum[2 * source + 1]) * (HD**-0.5)
+            dq_ref[source] = packed.astype(BF16)
         return 0
 
-    lax.fori_loop(0, blocks // 2, finish, 0)
+    lax.fori_loop(0, blocks // 8, finish, 0)
 
 
 def attend_back(pairs, q, tangent, keep, lse, kv):
@@ -946,9 +1019,34 @@
     )(rows)
 
 
-def scatter_kernel(n_ctx, rows_ref, out_ref, ss, rs):
+def pieces_of(start, size, body):
+    piece = max(n for n in range(16, 97, 16) if size % n == 0)
+    lax.fori_loop(
+        0,
+        size // piece,
+        lambda i, _: (body(i * piece, span(start + i * piece, piece), piece), 0)[1],
+        0,
+    )
+
+
+def span(start, size):
+    return pl.ds(pl.multiple_of(start, 16), size)
+
+
+def step_of(c, stride):
+    bit = (c // stride) % 2
+    return bit, c + stride * (1 - 2 * bit)
+
+
+def scatter_kernel(
+    n_ctx, rows_ref, own_ref, send_ref, out_ref, stage_a, stage_b, keep_ref, first_in,
+    ss, rs, core_ss, core_rs,
+):
     at = Place()
-    at.greet_sources(n_ctx, False)
+    at.greet_sources(n_ctx, True)
+    quarter = own_ref.shape[0] // 4
+    bits = (step_of(at.c, 1)[0], step_of(at.c, 2)[0])
+    stages = (stage_a, stage_b)
 
     def moves():
         for head in range(H):
@@ -962,37 +1060,158 @@
                     core,
                 )
 
+    def core_move(region, give):
+        bit = bits[region]
+        start = region * 2 * quarter + (1 - bit if give else bit) * quarter
+        where = span(start, quarter)
+        slot = region + 2 * (0 if give else 1)
+        return start, at.remote(
+            send_ref.at[where], first_in.at[where], core_ss.at[slot], core_rs.at[slot],
+            at.c, 1 - at.f,
+        )
+
+    order = [(0, True), (1, True), (0, False), (1, False)]
+    for step in order:
+        core_move(*step)[1].start()
     for move in moves():
         at.send(*move)
+    for region, give in order:
+        start, move = core_move(region, give)
+        move.wait_recv()
+
+        def join(offset, where, size):
+            total = own_ref[where, :].astype(F32) + first_in[where, :].astype(F32)
+            if give:
+                stages[region][span(offset, size), :] = total.astype(BF16)
+            else:
+                keep_ref[region, span(offset, size), :] = total
+
+        pieces_of(start, quarter, join)
     for source in range(n_ctx):
         arrived = out_ref.at[source]
         at.remote(arrived, arrived, ss.at[0], rs.at[source], at.c, 1 - at.f).wait_recv()
     for move in moves():
         at.wait_sent(*move)
-
-
-def scatter_rows(n_ctx, rows):
+    for step in order:
+        core_move(*step)[1].wait_send()
+
+
+def scatter_rows(n_ctx, rows, own, send):
+    grad_rows = own.shape[0]
     return pl.pallas_call(
         functools.partial(scatter_kernel, n_ctx),
-        out_shape=jax.ShapeDtypeStruct((n_ctx, HALF, 128), BF16),
-        in_specs=[ANY],
-        out_specs=ANY,
+        out_shape=(
+            jax.ShapeDtypeStruct((n_ctx, HALF, 128), BF16),
+            jax.ShapeDtypeStruct((grad_rows // 4, D), BF16),
+            jax.ShapeDtypeStruct((grad_rows // 4, D), BF16),
+            jax.ShapeDtypeStruct((2, grad_rows // 4, D), F32),
+        ),
+        in_specs=[ANY, VMEM, ANY],
+        out_specs=(ANY, VMEM, VMEM, VMEM),
         scratch_shapes=[
+            pltpu.VMEM((grad_rows, D), BF16),
             pltpu.SemaphoreType.DMA((2 * H,)),
             pltpu.SemaphoreType.DMA((n_ctx,)),
+            pltpu.SemaphoreType.DMA((4,)),
+            pltpu.SemaphoreType.DMA((4,)),
         ],
-        compiler_params=pltpu.CompilerParams(collective_id=2, has_side_effects=True),
+        compiler_params=pltpu.CompilerParams(
+            collective_id=2, has_side_effects=True, vmem_limit_bytes=32 << 20
+        ),
         name="scatter_rows",
-    )(rows)
+    )(rows, own, send)
+
+
+class Ladder:
+    def __init__(self, at, plans, starts, size, acc, stage, landing, out, sems):
+        self.at, self.acc, self.stage, self.landing, self.out = at, acc, stage, landing, out
+        self.down_ss, self.down_rs, self.up_ss, self.up_rs = sems
+        self.ranges = []
+        for plan, start in zip(plans, starts):
+            listed, rows = [], size
+            for bit, peer in plan[:-1]:
+                rows = rows // 2
+                listed.append((start + bit * rows, start + (1 - bit) * rows, rows, peer))
+                start = start + bit * rows
+            listed.append((start, start, rows, plan[-1][1]))
+            self.ranges.append(listed)
+        self.last = len(plans[0]) - 1
+
+    def slot(self, region, step):
+        return region * (self.last + 1) + step
+
+    def down(self, region, step, sent):
+        kept, given, size, peer = self.ranges[region][step]
+        where, slot = span(given if sent else kept, size), self.slot(region, step)
+        return self.at.remote(
+            self.stage[region].at[where],
+            self.landing[region][step].at[where],
+            self.down_ss.at[slot],
+            self.down_rs.at[slot],
+            peer,
+            self.at.f,
+        )
+
+    def up(self, region, step, sent):
+        kept, given, size, peer = self.ranges[region][step]
+        where, slot = span(kept if sent else given, size), self.slot(region, step)
+        return self.at.remote(
+            self.out[region].at[where],
+            self.out[region].at[where],
+            self.up_ss.at[slot],
+            self.up_rs.at[slot],
+            peer,
+            self.at.f,
+        )
+
+    def join(self, region, start, size, arrived, target):
+        def body(offset, where, _):
+            total = self.acc[region][where, :]
+            if arrived is not None:
+                total = total + arrived[where, :].astype(F32)
+            target[where, :] = total.astype(target.dtype)
+
+        pieces_of(start, size, body)
+
+    def give(self, region, step, arrived):
+        kept, given, size, _ = self.ranges[region][step]
+        self.join(region, given, size, arrived, self.stage[region])
+        self.down(region, step, True).start()
+        if step < self.last:
+            self.join(region, kept, size, arrived, self.acc[region])
+
+    def settle(self, region):
+        kept, _, size, _ = self.ranges[region][self.last]
+        arrived = self.landing[region][self.last]
+
+        def body(offset, where, _):
+            total = self.stage[region][where, :].astype(F32) + arrived[where, :].astype(F32)
+            self.out[region][where, :] = total.astype(BF16)
+
+        self.down(region, self.last, False).wait_recv()
+        pieces_of(kept, size, body)
+        self.up(region, self.last - 1, True).start()
+
+    def wait_sent(self):
+        for region in range(2):
+            for step in range(self.last + 1):
+                self.down(region, step, True).wait_send()
+            for step in range(self.last):
+                self.up(region, step, True).wait_send()
 
 
 def return_grads_kernel(
-    n_ctx, dq_ref, dkv_ref, dq_out, dkv_out, own, part, ready,
-    q_ss, q_rs, kv_ss, kv_rs, part_ss, part_rs, own_sem,
+    n_ctx, dq_ref, dkv_ref, keep_ref, land_a, land_b, dq_out, dkv_out, done_ref,
+    own, part, ready, acc, stage, landing,
+    q_ss, q_rs, kv_ss, kv_rs, part_ss, part_rs, own_sem, down_ss, down_rs, up_ss, up_rs,
 ):
     at = Place()
     other = 1 - at.f
-    at.greet_owners(n_ctx, True)
+    x_step, y_step, near, far = (step_of(at.c, stride) for stride in (1, 2, 4, 8))
+    barrier = pltpu.get_barrier_semaphore()
+    for _, peer in (x_step, y_step, near, far):
+        pl.semaphore_signal(barrier, 1, device_id=(peer, at.f), device_id_type=MESH)
+    at.greet_owners(n_ctx, True, 4)
 
     def partial_move(source):
         return at.remote(
@@ -1029,9 +1248,28 @@
             at.group,
         )
 
+    size = keep_ref.shape[1]
+    ladder = Ladder(
+        at,
+        ((y_step, near, far), (x_step, near, far)),
+        (0, 0),
+        size,
+        [acc.at[region] for region in range(2)],
+        [stage.at[region] for region in range(2)],
+        [[landing.at[region, step] for step in range(3)] for region in range(2)],
+        [done_ref.at[region] for region in range(2)],
+        (down_ss, down_rs, up_ss, up_rs),
+    )
     for source in range(n_ctx):
         partial_move(source).start()
         own_move(source).start()
+    for region, first_in in enumerate((land_a, land_b)):
+        ladder.acc[region] = keep_ref.at[region]
+        kept, given, half, _ = ladder.ranges[region][0]
+        ladder.join(region, given, half, first_in, stage.at[region])
+        ladder.down(region, 0, True).start()
+        ladder.join(region, kept, half, first_in, acc.at[region])
+        ladder.acc[region] = acc.at[region]
     for target in range(n_ctx):
         at.send(*q_move(target))
     for source in range(n_ctx):
@@ -1039,6 +1277,17 @@
         partial_move(source).wait_recv()
         ready[source] = (own[source] + part[source]).astype(BF16)
         at.send(*kv_move(source))
+    for step in (1, 2):
+        for region in range(2):
+            ladder.down(region, step - 1, False).wait_recv()
+            ladder.give(region, step, ladder.landing[region][step - 1])
+    for region in range(2):
+        ladder.settle(region)
+    for region in range(2):
+        ladder.up(region, 1, False).wait_recv()
+        ladder.up(region, 0, True).start()
+    for region in range(2):
+        ladder.up(region, 0, False).wait_recv()
     for head in range(H):
         for core in range(2):
             slot = head * 2 + core
@@ -1050,21 +1299,27 @@
         partial_move(target).wait_send()
         at.wait_sent(*q_move(target))
         at.wait_sent(*kv_move(target))
-
-
-def return_grads(n_ctx, dq, dkv):
+    ladder.wait_sent()
+
+
+def return_grads(n_ctx, dq, dkv, keep, land_a, land_b):
+    size = keep.shape[1]
     return pl.pallas_call(
         functools.partial(return_grads_kernel, n_ctx),
         out_shape=(
             jax.ShapeDtypeStruct((H, 2, HALF, 128), BF16),
             jax.ShapeDtypeStruct((H, 2 * BLK, 128), BF16),
+            jax.ShapeDtypeStruct((2, size, D), BF16),
         ),
-        in_specs=[ANY, ANY],
-        out_specs=(ANY, ANY),
+        in_specs=[ANY, ANY, VMEM, VMEM, VMEM],
+        out_specs=(ANY, ANY, VMEM),
         scratch_shapes=[
             pltpu.VMEM((n_ctx, BLK, 128), F32),
             pltpu.VMEM((n_ctx, BLK, 128), F32),
             pltpu.VMEM((n_ctx, BLK, 128), BF16),
+            pltpu.VMEM((2, size, D), F32),
+            pltpu.VMEM((2, size, D), BF16),
+            pltpu.VMEM((2, 3, size, D), BF16),
             pltpu.SemaphoreType.DMA((n_ctx,)),
             pltpu.SemaphoreType.DMA((2 * H,)),
             pltpu.SemaphoreType.DMA((n_ctx,)),
@@ -1072,12 +1327,16 @@
             pltpu.SemaphoreType.DMA((n_ctx,)),
             pltpu.SemaphoreType.DMA((n_ctx,)),
             pltpu.SemaphoreType.DMA((n_ctx,)),
+            pltpu.SemaphoreType.DMA((6,)),
+            pltpu.SemaphoreType.DMA((6,)),
+            pltpu.SemaphoreType.DMA((6,)),
+            pltpu.SemaphoreType.DMA((6,)),
         ],
         compiler_params=pltpu.CompilerParams(
-            collective_id=3, has_side_effects=True, vmem_limit_bytes=32 << 20
+            collective_id=3, has_side_effects=True, vmem_limit_bytes=40 << 20
         ),
         name="return_grads",
-    )(dq, dkv)
+    )(dq, dkv, keep, land_a, land_b)
 
 
 COLS = 512
@@ -1112,17 +1371,17 @@
 
 def dense_kernel(
     x_ref, sum_ref, cot_ref, o_ref,
-    wo_a, wo_b, we_a, we_b, ws_a, ws_b, be_a, be_b, vec_a, vec_b,
+    wo_a, wo_b, we_a, we_b, ws_a, ws_b, be_ref, vec_in,
     out_ref, sum_tan_ref, entry_ref, tan_ref, own_ref, send_ref, vec_ref,
     mixed, low, hidden, slope, before_tan, feed_tan, branch_tan, mixed_tan,
 ):
     f = lax.axis_index("fsdp")
-    first = f == 0
-    wo, we, ws, be = (wo_a, wo_b), (we_a, we_b), (ws_a, ws_b), (be_a, be_b)
+    wo, we, ws = (wo_a, wo_b), (we_a, we_b), (ws_a, ws_b)
+    be = (be_ref.at[0:1], be_ref.at[1:2])
     halves = (f, 1 - f)
-    vectors = whole_rows(vec_a[...], vec_b[...], first)
+    vectors = vec_in[...]
     (out_bias, gain_one, shift_one, shrink_bias, gain_two, shift_two, gain_last, shift_last) = (
-        vectors[i : i + 1] for i in range(8)
+        vectors[i : i + 1] for i in range(2, 10)
     )
     for kind in range(2):
         for pair in range(2):
@@ -1248,7 +1507,7 @@
             jax.ShapeDtypeStruct((grad_rows, D), BF16),
             jax.ShapeDtypeStruct((16, D), F32),
         ),
-        in_specs=[VMEM] * 14,
+        in_specs=[VMEM] * 12,
         out_specs=(VMEM,) * 7,
         scratch_shapes=[
             pltpu.VMEM((2, tokens, D // 2), BF16),
@@ -1262,7 +1521,7 @@
         ],
         compiler_params=pltpu.CompilerParams(vmem_limit_bytes=56 << 20),
         name="dense",
-    )(x, summed, cotangent, o, *wo, *we, *ws, *be, *vec)
+    )(x, summed, cotangent, o, *wo, *we, *ws, be, vec)
 
 
 def last_kernel(
@@ -1326,147 +1585,168 @@
     )(x, entry, dq, dkv, wq, wk, wv, w_other)
 
 
-def reduce_kernel(rows, own_ref, send_ref, out_ref, *scratch):
-    first_in, acc, stage = scratch[:3]
-    landing = scratch[3:7]
-    core_ss, core_rs, down_ss, down_rs, up_ss, up_rs = scratch[7:]
+def reduce_kernel(
+    own_ref, send_ref, vec_feed, vec_last, out_ref, vec_out,
+    first_in, acc, stage, landing, vec_sum, vec_in,
+    core_ss, core_rs, down_ss, down_rs, up_ss, up_rs, vec_ss, vec_rs,
+):
     at = Place()
     c, f = at.c, at.f
-
-    def step_of(stride):
-        bit = (c // stride) % 2
-        return bit, c + stride * (1 - 2 * bit)
-
-    x_step, y_step, near_z, far_z = step_of(1), step_of(2), step_of(4), step_of(8)
-    plans = ((x_step, y_step, far_z, near_z), (y_step, x_step, far_z, near_z))
-
+    rows = own_ref.shape[0]
+    quarter = rows // 4
+    x_step, y_step, near, far = (step_of(c, stride) for stride in (1, 2, 4, 8))
     barrier = pltpu.get_barrier_semaphore()
     pl.semaphore_signal(barrier, 1, device_id=(c, 1 - f), device_id_type=MESH)
-    for _, peer in (x_step, y_step, near_z, far_z):
+    for _, peer in (x_step, y_step, near, far):
         pl.semaphore_signal(barrier, 1, device_id=(peer, f), device_id_type=MESH)
     pl.semaphore_wait(barrier, 5)
 
-    def span(start, size):
-        return pl.ds(pl.multiple_of(start, 32), size)
-
-    def each(start, size, body):
-        piece = 96 if size % 96 == 0 else 80
-        lax.fori_loop(0, size // piece, lambda i, _: (body(span(start + i * piece, piece)), 0)[1], 0)
-
-    ranges = []
-    for region, plan in enumerate(plans):
-        start, size, listed = region * (rows // 2), rows // 2, []
-        for bit, peer in plan:
-            size = size // 2
-            listed.append((start + bit * size, start + (1 - bit) * size, size, peer))
-            start = start + bit * size
-        ranges.append(listed)
-
-    pieces = [(0, 1), (1, 1), (0, 0), (1, 0)]
-
-    def core_move(index):
-        region, give = pieces[index]
-        kept, given, size, _ = ranges[region][0]
+    vec_peers = [(c, 1 - f)] + [(peer, f) for _, peer in (x_step, y_step, near, far)]
+
+    def vec_move(step):
+        return at.remote(
+            vec_sum.at[step], vec_in.at[step], vec_ss.at[step], vec_rs.at[step], *vec_peers[step]
+        )
+
+    def vec_next(step):
+        vec_move(step).wait_recv()
+        target = vec_sum.at[step + 1] if step < 4 else vec_out
+        target[...] = vec_sum[step] + vec_in[step]
+        if step < 4:
+            vec_move(step + 1).start()
+
+    shared = [acc, acc], [stage, stage], [[landing.at[step] for step in range(4)]] * 2
+    ladder = Ladder(
+        at,
+        ((x_step, y_step, near, far), (y_step, x_step, near, far)),
+        (0, 2 * quarter),
+        2 * quarter,
+        shared[0],
+        shared[1],
+        shared[2],
+        [out_ref, out_ref],
+        (down_ss, down_rs, up_ss, up_rs),
+    )
+
+    def core_move(region, give):
+        kept, given, size, _ = ladder.ranges[region][0]
         where = span(given if give else kept, size)
+        slot = region + 2 * (0 if give else 1)
         return at.remote(
-            send_ref.at[where], first_in.at[where], core_ss.at[index], core_rs.at[index], c, 1 - f
-        )
-
-    def down_move(region, step):
-        _, given, size, peer = ranges[region][step]
-        where = span(given, size)
-        slot = region * 4 + step
-        return at.remote(
-            stage.at[where], landing[step].at[where], down_ss.at[slot], down_rs.at[slot], peer, f
-        )
-
-    def down_wait(region, step):
-        kept, _, size, peer = ranges[region][step]
-        where = span(kept, size)
-        slot = region * 4 + step
-        at.remote(
-            stage.at[where], landing[step].at[where], down_ss.at[slot], down_rs.at[slot], peer, f
-        ).wait_recv()
-
-    def up_move(region, step):
-        kept, _, size, peer = ranges[region][step]
-        where = span(kept, size)
-        slot = region * 4 + step
-        return at.remote(
-            out_ref.at[where], out_ref.at[where], up_ss.at[slot], up_rs.at[slot], peer, f
-        )
-
-    def up_wait(region, step):
-        _, given, size, peer = ranges[region][step]
-        where = span(given, size)
-        slot = region * 4 + step
-        at.remote(
-            out_ref.at[where], out_ref.at[where], up_ss.at[slot], up_rs.at[slot], peer, f
-        ).wait_recv()
-
-    for index in range(4):
-        core_move(index).start()
-    for index, (region, give) in enumerate(pieces):
-        core_move(index).wait_recv()
-        kept, given, size, _ = ranges[region][0]
-
-        def join(where, target):
+            send_ref.at[where], first_in.at[where], core_ss.at[slot], core_rs.at[slot], c, 1 - f
+        )
+
+    order = [(0, True), (1, True), (0, False), (1, False)]
+    for step in order:
+        core_move(*step).start()
+    feed_rows = vec_feed.shape[0]
+    vec_sum[0, 0:feed_rows] = vec_feed[...]
+    vec_sum[0, feed_rows : feed_rows + vec_last.shape[0]] = vec_last[...]
+    vec_move(0).start()
+    for region, give in order:
+        core_move(region, give).wait_recv()
+        kept, given, size, _ = ladder.ranges[region][0]
+
+        def join(offset, where, _):
             total = own_ref[where, :].astype(F32) + first_in[where, :].astype(F32)
-            target[where, :] = total.astype(target.dtype)
-
+            if give:
+                stage[where, :] = total.astype(BF16)
+            else:
+                acc[where, :] = total
+
+        pieces_of(given if give else kept, size, join)
         if give:
-            each(given, size, lambda where: join(where, stage))
-            down_move(region, 0).start()
-        else:
-            each(kept, size, lambda where: join(where, acc))
-    for step in range(1, 5):
+            ladder.down(region, 0, True).start()
+    vec_next(0)
+    for step in (1, 2, 3):
         for region in range(2):
-            down_wait(region, step - 1)
-            arrived = landing[step - 1]
-
-            def join(where, target):
-                total = acc[where, :] + arrived[where, :].astype(F32)
-                target[where, :] = total.astype(target.dtype)
-
-            if step < 4:
-                kept, given, size, _ = ranges[region][step]
-                each(given, size, lambda where: join(where, stage))
-                down_move(region, step).start()
-                each(kept, size, lambda where: join(where, acc))
-            else:
-                kept, _, size, _ = ranges[region][3]
-                each(kept, size, lambda where: join(where, out_ref))
-                up_move(region, 3).start()
-    for step in (3, 2, 1, 0):
+            ladder.down(region, step - 1, False).wait_recv()
+            ladder.give(region, step, ladder.landing[region][step - 1])
+        vec_next(step)
+    for region in range(2):
+        ladder.settle(region)
+    vec_next(4)
+    for step in (2, 1, 0):
         for region in range(2):
-            up_wait(region, step)
+            ladder.up(region, step, False).wait_recv()
             if step > 0:
-                up_move(region, step - 1).start()
-    for index in range(4):
-        core_move(index).wait_send()
-    for region in range(2):
-        for step in range(4):
-            down_move(region, step).wait_send()
-            up_move(region, step).wait_send()
-
-
-def reduce_grads(own, send, ident):
-    rows = own.shape[0]
-    wide = (rows, D)
+                ladder.up(region, step - 1, True).start()
+    for step in order:
+        core_move(*step).wait_send()
+    for step in range(5):
+        vec_move(step).wait_send()
+    ladder.wait_sent()
+
+
+def reduce_grads(own, send, vec_feed, vec_last):
+    wide = own.shape
+    vec_shape = (vec_feed.shape[0] + vec_last.shape[0], D)
     return pl.pallas_call(
-        functools.partial(reduce_kernel, rows),
-        out_shape=jax.ShapeDtypeStruct(wide, BF16),
-        in_specs=[VMEM, VMEM],
-        out_specs=VMEM,
-        scratch_shapes=[pltpu.VMEM(wide, BF16), pltpu.VMEM(wide, F32), pltpu.VMEM(wide, BF16)]
-        + [pltpu.VMEM(wide, BF16)] * 4
+        reduce_kernel,
+        out_shape=(jax.ShapeDtypeStruct(wide, BF16), jax.ShapeDtypeStruct(vec_shape, F32)),
+        in_specs=[VMEM] * 4,
+        out_specs=(VMEM, VMEM),
+        scratch_shapes=[
+            pltpu.VMEM(wide, BF16),
+            pltpu.VMEM(wide, F32),
+            pltpu.VMEM(wide, BF16),
+            pltpu.VMEM((4,) + wide, BF16),
+            pltpu.VMEM((5,) + vec_shape, F32),
+            pltpu.VMEM((5,) + vec_shape, F32),
+        ]
         + [pltpu.SemaphoreType.DMA((4,))] * 2
-        + [pltpu.SemaphoreType.DMA((8,))] * 4,
+        + [pltpu.SemaphoreType.DMA((8,))] * 4
+        + [pltpu.SemaphoreType.DMA((5,))] * 2,
         compiler_params=pltpu.CompilerParams(
-            collective_id=ident, has_side_effects=True, vmem_limit_bytes=56 << 20
+            collective_id=4, has_side_effects=True, vmem_limit_bytes=32 << 20
         ),
         name="reduce_grads",
-    )(own, send)
+    )(own, send, vec_feed, vec_last)
+
+
+def unpack_kernel(
+    done_ref, rest_a, rest_b, grads_ref, vec_ref,
+    query_ref, key_ref, value_ref, output_ref, expand_ref, shrink_ref, *rest,
+):
+    vector_outs, full = rest[:-1], rest[-1]
+    c, f = lax.axis_index("ctx"), lax.axis_index("fsdp")
+    size = done_ref.shape[1]
+    for region, far_part in enumerate((rest_a, rest_b)):
+        bit = step_of(c, 1 + region)[0]
+        start = 2 * region * size
+        full[span(start + bit * size, size), :] = done_ref[region]
+        full[span(start + (1 - bit) * size, size), :] = far_part[...]
+    units, wide = shrink_ref.shape[0], D // 2
+    shrink_ref[...] = full[0:units].astype(F32)
+    for part in range(units // D):
+        start = units + part * D
+        expand_ref[:, part * D : part * D + D] = full[start : start + D].astype(F32)
+    output_ref[...] = full[2 * units : 2 * units + wide].astype(F32)
+    query_ref[...] = grads_ref[0:D, 0:wide].astype(F32)
+    key_ref[...] = grads_ref[0:D, wide:D].astype(F32)
+    value_ref[0:wide] = grads_ref[D : D + wide, 0:wide].astype(F32)
+    value_ref[wide:D] = grads_ref[D : D + wide, wide:D].astype(F32)
+    vectors = vec_ref[...]
+    mine = jnp.where(f == 0, vectors[:, 0:wide], vectors[:, wide:D])
+    for row, ref in zip((16, 17, 7, 5, 6, 0, 1, 2, 3, 4), vector_outs):
+        ref[...] = mine[row : row + 1]
+    drift = jnp.where(f == 0, vectors[8:10], vectors[10:12])
+    for part in range(units // D):
+        vector_outs[10][:, part * D : part * D + D] = drift[part : part + 1]
+
+
+def unpack_grads(units, done, rest_a, rest_b, grads, vecs):
+    wide = D // 2
+    shapes = [(D, wide)] * 3 + [(wide, D), (D, units), (units, D)] + [(1, wide)] * 10 + [(1, units)]
+    return pl.pallas_call(
+        unpack_kernel,
+        out_shape=tuple(jax.ShapeDtypeStruct(shape, F32) for shape in shapes),
+        in_specs=[VMEM] * 5,
+        out_specs=(VMEM,) * len(shapes),
+        scratch_shapes=[pltpu.VMEM((4 * done.shape[1], D), BF16)],
+        compiler_params=pltpu.CompilerParams(vmem_limit_bytes=32 << 20),
+        name="unpack_grads",
+    )(done, rest_a, rest_b, grads, vecs)
 
 
 def head_shards(
@@ -1495,26 +1775,19 @@
     final_shift,
 ):
     x, summed, tangent = post_stream[0], sum_stream[0], cotangent[0]
-    f = lax.axis_index("fsdp")
     swap = [(0, 1), (1, 0)]
 
     def from_other(values):
         return lax.ppermute(values, "fsdp", swap)
 
-    order_both = lax.all_gather(block_order, "fsdp", axis=0, tiled=True)
-    seqs_both = lax.all_gather(block_sequence, "fsdp", axis=0, tiled=True)
-    group = lax.axis_index("ctx") // H
-    order = lax.dynamic_slice_in_dim(order_both, group, 1, 0)[0]
-    seqs = lax.dynamic_slice_in_dim(seqs_both, group, 1, 0)[0]
-
-    bias = jnp.concatenate(
-        [query_bias[None], value_bias[None], jnp.zeros((6, D // 2), BF16)], axis=0
-    ).astype(F32)
-    q, kv, w_other = project_and_scatter(n_ctx, x, query_weight, key_weight, value_weight, bias)
-    o, keep, lse, pairs = attend(order, seqs, q, kv)
-    o_rows = return_rows(n_ctx, o)
-    vec = jnp.stack(
-        [
+    def across(values, stride):
+        return lax.ppermute(values, "ctx", [(c, c ^ stride) for c in range(n_ctx)])
+
+    vectors = [
+        vector[None]
+        for vector in (
+            query_bias,
+            value_bias,
             output_bias,
             attend_gain,
             attend_shift,
@@ -1523,9 +1796,21 @@
             middle_shift,
             final_gain,
             final_shift,
-        ]
-    ).astype(F32)
-    own_bias = expand_bias[None].astype(F32)
+        )
+    ]
+    q, kv, w_other, order, seqs, vec, expand_add = project_and_scatter(
+        n_ctx,
+        x,
+        query_weight,
+        key_weight,
+        value_weight,
+        block_order,
+        block_sequence,
+        expand_bias[None],
+        vectors,
+    )
+    o, keep, lse, pairs = attend(order, seqs, q, kv)
+    o_rows = return_rows(n_ctx, o)
     layer_output, sum_tan, entry, tan_rows, own_feed, send_feed, vec_feed = dense(
         x,
         summed,
@@ -1534,38 +1819,37 @@
         (output_weight, from_other(output_weight)),
         (expand_weight, from_other(expand_weight)),
         (shrink_weight, from_other(shrink_weight)),
-        (own_bias, from_other(own_bias)),
-        (vec, from_other(vec)),
-    )
-    tan = scatter_rows(n_ctx, tan_rows)
+        expand_add,
+        vec,
+    )
+    tan, stage_a, stage_b, kept = scatter_rows(n_ctx, tan_rows, own_feed, send_feed)
+    land_a, land_b = across(stage_a, 1), across(stage_b, 2)
     dq, dkv = attend_back(pairs, q, tan, keep, lse, kv)
-    dq_rows, dkv_rows = return_grads(n_ctx, dq, dkv)
+    dq_rows, dkv_rows, done = return_grads(n_ctx, dq, dkv, kept, land_a, land_b)
+    rest_a, rest_b = across(done[0], 1), across(done[1], 2)
     post_tangent, own_last, send_last, vec_last = last_dense(
         x, entry, dq_rows, dkv_rows, query_weight, key_weight, value_weight, w_other
     )
-    grads = reduce_grads(
-        jnp.concatenate([own_feed, own_last]), jnp.concatenate([send_feed, send_last]), 4
-    )
-    vecs = lax.psum(jnp.concatenate([vec_feed, vec_last]), ("ctx", "fsdp"))
-    wide = D // 2
-    units = shrink_weight.shape[0]
-
-    def mine(row):
-        return lax.dynamic_slice_in_dim(vecs[row], f * wide, wide)
-
-    shrink_slope = grads[0:units].astype(F32)
-    expand_slope = jnp.concatenate(
-        [grads[units + i * D : units + i * D + D] for i in range(units // D)], axis=1
-    ).astype(F32)
-    after = 2 * units
-    output_slope = grads[after : after + wide].astype(F32)
-    after = after + wide
-    query_slope = grads[after : after + D, 0:wide].astype(F32)
-    key_slope = grads[after : after + D, wide:D].astype(F32)
-    value_slope = jnp.concatenate(
-        [grads[after + D : after + D + wide, 0:wide], grads[after + D : after + D + wide, wide:D]]
-    ).astype(F32)
-    expand_drift = lax.dynamic_slice_in_dim(vecs[8:12].reshape(4 * D), f * units, units)
+    grads, vecs = reduce_grads(own_last, send_last, vec_feed, vec_last)
+    (
+        query_slope,
+        key_slope,
+        value_slope,
+        output_slope,
+        expand_slope,
+        shrink_slope,
+        query_drift,
+        value_drift,
+        output_drift,
+        attend_stretch,
+        attend_nudge,
+        shrink_drift,
+        middle_stretch,
+        middle_nudge,
+        final_stretch,
+        final_nudge,
+        expand_drift,
+    ) = unpack_grads(shrink_weight.shape[0], done, rest_a, rest_b, grads, vecs)
     return (
         layer_output[None],
         post_tangent[None],
@@ -1574,19 +1858,19 @@
         key_slope,
         value_slope,
         output_slope,
-        mine(16),
-        mine(17),
-        mine(7),
-        mine(5),
-        mine(6),
+        query_drift[0],
+        value_drift[0],
+        output_drift[0],
+        attend_stretch[0],
+        attend_nudge[0],
         expand_slope,
-        expand_drift,
+        expand_drift[0],
         shrink_slope,
-        mine(0),
-        mine(1),
-        mine(2),
-        mine(3),
-        mine(4),
+        shrink_drift[0],
+        middle_stretch[0],
+        middle_nudge[0],
+        final_stretch[0],
+        final_nudge[0],
     )
 
 

time: 410 us -> 297 us (0.72)
  blocking collectives: 52.8 us -> 0 us
  Pallas kernels: 313 us -> 264 us
  other arithmetic: 15.6 us -> 0 us
  starting transfers between devices: 1.54 us -> 9.07 us
    pallas_call x2 -> x3, Pallas kernels: 120 us -> 59 us  [the longest x1 43.2 us: reduce_grads(): pl.pallas_call(reduce_kernel, out_shape=(jax.ShapeDtypeStruct(wide, BF16)...]
    psum x1 -> x0, blocking collectives: 49 us -> none  [head_shards(): vecs = lax.psum(jnp.concatenate([vec_feed, vec_last]), ('ctx', 'fsdp'))]
    pallas_call x1, Pallas kernels: 41.6 us -> 69 us  [return_grads(): pl.pallas_call(functools.partial(return_grads_kernel, n_ctx), out_shape=(...]
    pallas_call x1, Pallas kernels: 28.8 us -> 16.2 us  [attend(): pl.pallas_call(functools.partial(forward_kernel, blocks), out_shape=(jax....]
    convert_element_type x8 -> x0, other arithmetic: 11.1 us -> none  [the longest x1 2.84 us: head_shards(): shrink_slope = grads[0:units].astype(F32)]
    ppermute x0 -> x4, starting transfers between devices: none -> 8.04 us  [across(): return lax.ppermute(values, 'ctx', [(c, c ^ stride) for c in range(n_ctx)])]
    broadcast_in_dim x3 -> x11, local copies, waits for them, and re-layouts: 1.32 us -> 7.26 us  [the longest x10 6.58 us: head_shards(): vector[None]]
    another operation x9 -> x0, local copies, waits for them, and re-layouts: 5.29 us -> none  [head_shards(): jnp.stack([output_bias, attend_gain, attend_shift, shrink_bias, middle_ga...]
  transfers between devices with their start and end apart: 5 -> 7, of which waited for: 0 -> 0; matrix products, arithmetic and copies ran while one was open for 2% -> 2% of each run, Pallas kernels for 22% -> 52%
where the time goes in v2:
time: 297 us; the launch traced here: 296 us
  Pallas kernels  264 us (89%)
  local copies, waits for them, and re-layouts  22 us (7%)
  starting transfers between devices  9.07 us (3%)
    pallas_call x1, Pallas kernels, return_grads(): pl.pallas_call(functools.partial(return_grads_kernel, n_ctx), out_shape=(...  69 us
    pallas_call x1, Pallas kernels, reduce_grads(): pl.pallas_call(reduce_kernel, out_shape=(jax.ShapeDtypeStruct(wide, BF16)...  43.2 us
    pallas_call x1, Pallas kernels, return_rows(): pl.pallas_call(functools.partial(return_kernel, n_ctx), out_shape=jax.Sha...  31.5 us
    pallas_call x1, Pallas kernels, attend_back(): pl.pallas_call(functools.partial(backward_kernel, blocks), out_shape=(jax...  30.7 us
    pallas_call x1, Pallas kernels, project_and_scatter(): pl.pallas_call(functools.partial(project_kernel, n_ctx), out_shape=(jax.S...  29.8 us
    pallas_call x1, Pallas kernels, dense(): pl.pallas_call(dense_kernel, out_shape=(jax.ShapeDtypeStruct((tokens, D),...  24.4 us
    pallas_call x1, Pallas kernels, attend(): pl.pallas_call(functools.partial(forward_kernel, blocks), out_shape=(jax....  16.2 us
    unnamed x44, local copies, waits for them, and re-layouts  14.7 us
  transfers between devices with their start and end apart: 7, of which 0 were waited for; matrix products, arithmetic and copies ran while one was open for 2% of the time, Pallas kernels for 52%

profile of v2, /device:TPU:0, one launch (start us, length us, event | category | flops | bytes accessed | tf_op | source)
XLA Modules:
  0.0 296.2 jit_solution(3278653862473950000)
XLA Ops:
  0.7 0.5 collective-permute-start.1
  1.2 0.1 collective-permute-start.2
  1.3 0.4 collective-permute-start
  1.7 0.7 broadcast_in_dim.43.rest_0_
  2.3 0.7 broadcast_in_dim.44.rest_1_
  3.0 0.7 broadcast_in_dim.45.rest_2_
  3.7 0.7 broadcast_in_dim.46.rest_3_
  4.3 0.7 broadcast_in_dim.47.rest_4_
  5.0 0.7 broadcast_in_dim.48.rest_5_
  5.6 0.7 broadcast_in_dim.49.rest_6_
  6.3 0.7 broadcast_in_dim.50.rest_7_
  7.0 0.7 broadcast_in_dim.51.rest_8_
  7.6 0.7 broadcast_in_dim.52.rest_9_
  8.3 0.7 broadcast_in_dim.42.expand_ref
  9.0 1.2 copy-done
  10.2 0.9 copy-done.9
  11.1 0.9 copy-done.11
  12.1 0.9 copy-done.13
  13.0 0.7 copy-done.20
  13.7 0.7 copy-done.21
  14.3 29.8 %project_scatter.1 = (bf16[16,128,128]{2,1,0:T(8,128)(2,1)S(1)}, bf16[32,256,128]{2,1,0:T(8,128)(2,1)S(1)}, bf16[3,512,256]{2,1,0:T(8,128)(2,1)S(1)}, s32[1,32]{...) custom-call(f32[512,512]{1,0:T(8,128)S(1)} %bitcast.22, ...), custom_call_target="tpu_custom_call" | custom-call | tf_op jit(solution)/shard_map/project_scatter/pallas_call | solution.py:695
  44.1 0.0 copy-start.17
  44.1 0.0 copy-start.19
  44.1 16.2 %attend.1 = (bf16[16,128,128]{2,1,0:T(8,128)(2,1)S(1)}, f32[16,128,128]{2,1,0:T(8,128)S(1)}, f32[32,8,128]{2,1,0:T(8,128)S(1)}, s32[3,160]{1,0:T(4,128)S(1)}) custom-call(s32[1,32]{1,0:T(1,128)S(1)} %get-tuple-element.70.order_ref, s32[1,32]{1,0:T(1,128)S(1)} %get-tuple-element.71.seq_ref, bf16[16,128,128]{2,1,0:T(8,128)(2,1)S(1)} %get-tuple-element.72.q_ref, ...), custom_call_target="tpu_custom_call" | custom-call | tf_op jit(solution)/shard_map/attend/pallas_call | solution.py:860
  60.3 0.0 copy-start.6
  60.4 1.0 copy-done.6
  61.3 0.8 copy-done.16
  62.1 31.5 %return_rows.1.o_ref = bf16[8,2,128,128]{3,2,1,0:T(8,128)(2,1)} custom-call(bf16[16,128,128]{2,1,0:T(8,128)(2,1)} %copy-done.16), custom_call_target="tpu_custom_call" | custom-call | tf_op jit(solution)/shard_map/return_rows/pallas_call | solution.py:1008
  93.6 0.0 collective-permute-done.wo_b
  93.7 24.4 %dense.1 = (f32[512,512]{1,0:T(8,128)}, f32[512,512]{1,0:T(8,128)}, f32[512,512]{1,0:T(8,128)}, bf16[8,2,128,128]{3,2,1,0:T(8,128)(2,1)}, bf16[2304,512]{1,0:T(8...) custom-call(f32[512,512]{1,0:T(8,128)} %bitcast.21, f32[512,512]{1,0:T(8,128)} %bitcast.24, ...), custom_call_target="tpu_custom_call" | custom-call | tf_op jit(solution)/shard_map/dense/pallas_call | solution.py:1499
  118.1 1.7 copy-done.3
  119.7 1.7 copy-done.4
  121.4 1.0 copy-done.15
  122.4 13.0 %scatter_rows.1 = (bf16[16,128,128]{2,1,0:T(8,128)(2,1)S(1)}, bf16[576,512]{1,0:T(8,128)(2,1)S(1)}, bf16[576,512]{1,0:T(8,128)(2,1)S(1)}, f32[2,576,512]{2,1,0:T(8,128)S(1)}) custom-call(bf16[8,2,128,128]{3,2,1,0:T(8,128)(2,1)S(1)} %copy-done.15, bf16[2304,512]{1,0:T(8,128)(2,1)S(1)} %copy-done.3, bf16[2304,512]{1,0:T(8,128)(2,1)S(1)} %copy-done.4), custom_call_target="tpu_custom_call" | custom-call | tf_op jit(solution)/shard_map/scatter_rows/pallas_call | solution.py:1101
  135.4 2.6 collective-permute-start.3
  138.0 3.4 %collective-permute-start.4 = (bf16[576,512]{1,0:T(8,128)(2,1)S(1)}, bf16[576,512]{1,0:T(8,128)(2,1)S(1)}, u32[]{:S(2)}, u32[]{:S(2)}) collective-permute-start(bf16[576,512]{1,0:T(8,128)(2,1)S(1)} %get-tuple-element.90), channel_id=1, source_target_pairs={{0,4},{2,6},{4,0},{6,2},{8,12},{10,14},{12,8},{14,10},{16,20},{18,... | collective-permute-start | bytes 1769480 | tf_op jit(solution)/shard_map/ppermute | solution.py:1784
  141.4 30.7 %attend_back.1 = (bf16[16,128,128]{2,1,0:T(8,128)(2,1)S(1)}, f32[32,256,128]{2,1,0:T(8,128)}) custom-call(s32[3,160]{1,0:T(4,128)S(1)} %get-tuple-element.79.pairs_ref, bf16[16,128,128]{2,1,0:T(8,128)(2,1)S(1)} %get-tuple-element.72.q_ref, bf16[16,128,128]{2,1,0:T(8,128)(2,1)S(1)} %get-tuple-element.83.tan_ref, f32[16,128,128]{2,1,0:T(8,128)S(1)} %copy-done.7, ...), custom_call_target="tpu_custom_call" | custom-call | tf_op jit(solution)/shard_map/attend_back/pallas_call | solution.py:962
  172.1 2.2 copy-done.2
  174.3 69.0 %return_grads.1 = (bf16[8,2,128,128]{3,2,1,0:T(8,128)(2,1)S(1)}, bf16[8,512,128]{2,1,0:T(8,128)(2,1)S(1)}, bf16[2,576,512]{2,1,0:T(8,128)(2,1)S(1)}) custom-call(bf16[16,128,128]{2,1,0:T(8,128)(2,1)S(1)} %get-tuple-element.86.dq_ref, f32[32,256,128]{2,1,0:T(8,128)S(1)} %copy-done.2, f32[2,576,512]{2,1,0:T(8,128)S(1)} %get-tuple-element.88.keep_ref, ...), custom_call_target="tpu_custom_call" | custom-call | tf_op jit(solution)/shard_map/return_grads/pallas_call | solution.py:1307
  243.3 0.0 copy-start.8
  243.3 1.0 copy-done.8
  244.2 0.1 slice_bitcast_fusion
  244.3 1.3 collective-permute-start.6
  245.6 0.9 collective-permute-start.5
  246.4 0.0 copy-start.18
  246.5 3.5 %last_dense.1 = (f32[512,512]{1,0:T(8,128)}, bf16[768,512]{1,0:T(8,128)(2,1)S(1)}, bf16[768,512]{1,0:T(8,128)(2,1)S(1)}, f32[8,512]{1,0:T(8,128)S(1)}) custom-call(f32[512,512]{1,0:T(8,128)S(1)} %bitcast.23, f32[512,512]{1,0:T(8,128)S(1)} %copy-done.5, bf16[8,2,128,128]{3,2,1,0:T(8,128)(2,1)S(1)} %get-tuple-element.91.dq_ref, ...), custom_call_target="tpu_custom_call" | custom-call | tf_op jit(solution)/shard_map/last_dense/pallas_call | solution.py:1572
  250.0 43.2 %reduce_grads.1 = (bf16[768,512]{1,0:T(8,128)(2,1)S(1)}, f32[24,512]{1,0:T(8,128)S(1)}) custom-call(bf16[768,512]{1,0:T(8,128)(2,1)S(1)} %get-tuple-element.97.own_ref, bf16[768,512]{1,0:T(8,128)(2,1)S(1)} %get-tuple-element.98.send_ref, f32[16,512]{1,0:T(8,128)S(1)} %copy-done.18, f32[8,512]{1,0:T(8,128)S(1)} %get-tuple-element.100.vec_last), custom_call_target="tpu_custom_call" | custom-call | tf_op jit(solution)/shard_map/reduce_grads/pallas_call | solution.py:1684
  293.2 2.8 unpack_grads.1
  (32 shorter events, 0.1 us)
Async XLA Ops:
  0.7 93.0 %collective-permute-start.1 = (bf16[512,1024]{1,0:T(8,128)(2,1)}, bf16[512,1024]{1,0:T(8,128)(2,1)}, u32[]{:S(2)}, u32[]{:S(2)}) collective-permute-start(bf16[512,1024]{1,0:T(8,128)(2,1)} %we_a.1), channel_id=1, source_target_pairs={{0,1},{1,0},{2,3},{3,2},{4,5},{5,4},{6,7},{7,6},{8,9},{9,8},{10,11... | collective-permute-start | bytes 3145736 | tf_op jit(solution)/shard_map/ppermute | solution.py:1781
  1.2 92.5 %collective-permute-start.2 = (bf16[1024,512]{1,0:T(8,128)(2,1)}, bf16[1024,512]{1,0:T(8,128)(2,1)}, u32[]{:S(2)}, u32[]{:S(2)}) collective-permute-start(bf16[1024,512]{1,0:T(8,128)(2,1)} %ws_a.1), channel_id=1, source_target_pairs={{0,1},{1,0},{2,3},{3,2},{4,5},{5,4},{6,7},{7,6},{8,9},{9,8},{10,11... | collective-permute-start | bytes 3145736 | tf_op jit(solution)/shard_map/ppermute | solution.py:1781
  1.3 92.4 %collective-permute-start = (bf16[256,512]{1,0:T(8,128)(2,1)}, bf16[256,512]{1,0:T(8,128)(2,1)}, u32[]{:S(2)}, u32[]{:S(2)}) collective-permute-start(bf16[256,512]{1,0:T(8,128)(2,1)} %wo_a.1), channel_id=1, source_target_pairs={{0,1},{1,0},{2,3},{3,2},{4,5},{5,4},{6,7},{7,6},{8,9},{9,8},{10,11... | collective-permute-start | bytes 786440 | tf_op jit(solution)/shard_map/ppermute | solution.py:1781
  9.0 1.2 copy-start
  10.2 0.9 copy-start.9
  11.1 0.9 copy-start.11
  12.1 0.9 copy-start.13
  13.0 0.7 copy-start.20
  13.7 0.7 copy-start.21
  44.1 16.2 %copy-start.17 = (f32[16,512]{1,0:T(8,128)}, f32[16,512]{1,0:T(8,128)S(1)}, u32[]{:S(2)}) copy-start(f32[16,512]{1,0:T(8,128)S(1)} %get-tuple-element.76.vec_in) | copy-start | bytes 98308
  44.1 16.2 %copy-start.19 = (f32[2,1024]{1,0:T(2,128)}, f32[2,1024]{1,0:T(2,128)S(1)}, u32[]{:S(2)}) copy-start(f32[2,1024]{1,0:T(2,128)S(1)} %get-tuple-element.75.be_ref) | copy-start | bytes 24580
  60.3 1.0 copy-start.6
  61.3 0.8 copy-start.16
  118.0 1.7 copy-start.3
  119.7 1.7 copy-start.4
  121.4 1.0 copy-start.15
  122.4 19.0 %copy-start.7 = (f32[16,128,128]{2,1,0:T(8,128)S(1)}, f32[16,128,128]{2,1,0:T(8,128)}, u32[]{:S(2)}) copy-start(f32[16,128,128]{2,1,0:T(8,128)} %copy-done.6) | copy-start | bytes 3145732
  135.4 36.6 %collective-permute-start.3 = (bf16[576,512]{1,0:T(8,128)(2,1)S(1)}, bf16[576,512]{1,0:T(8,128)(2,1)S(1)}, u32[]{:S(2)}, u32[]{:S(2)}) collective-permute-start(bf16[576,512]{1,0:T(8,128)(2,1)S(1)} %get-tuple-element.89), channel_id=1, source_target_pairs={{0,2},{2,0},{4,6},{6,4},{8,10},{10,8},{12,14},{14,12},{16,18},{18,... | collective-permute-start | bytes 1769480 | tf_op jit(solution)/shard_map/ppermute | solution.py:1784
  138.0 34.1 %collective-permute-start.4 = (bf16[576,512]{1,0:T(8,128)(2,1)S(1)}, bf16[576,512]{1,0:T(8,128)(2,1)S(1)}, u32[]{:S(2)}, u32[]{:S(2)}) collective-permute-start(bf16[576,512]{1,0:T(8,128)(2,1)S(1)} %get-tuple-element.90), channel_id=1, source_target_pairs={{0,4},{2,6},{4,0},{6,2},{8,12},{10,14},{12,8},{14,10},{16,20},{18,... | collective-permute-start | bytes 1769480 | tf_op jit(solution)/shard_map/ppermute | solution.py:1784
  172.1 2.2 copy-start.2
  174.3 72.2 %copy-start.12 = (bf16[512,256]{1,0:T(8,128)(2,1)S(1)}, bf16[512,256]{1,0:T(8,128)(2,1)}, u32[]{:S(2)}) copy-start(bf16[512,256]{1,0:T(8,128)(2,1)} %wk.1) | copy-start | bytes 786436
  174.3 72.2 %copy-start.14 = (bf16[512,256]{1,0:T(8,128)(2,1)S(1)}, bf16[512,256]{1,0:T(8,128)(2,1)}, u32[]{:S(2)}) copy-start(bf16[512,256]{1,0:T(8,128)(2,1)} %wv.1) | copy-start | bytes 786436
  243.3 1.0 copy-start.8
  244.2 2.2 copy-start.1
  244.2 2.2 copy-start.5
  244.2 2.2 copy-start.10
  244.3 48.9 %collective-permute-start.6 = (bf16[576,512]{1,0:T(8,128)(2,1)S(1)}, bf16[576,512]{1,0:T(8,128)(2,1)S(1)}, u32[]{:S(2)}, u32[]{:S(2)}) collective-permute-start(bf16[576,512]{1,0:T(8,128)(2,1)S(1)} %get-tuple-element.120), channel_id=1, source_target_pairs={{0,4},{2,6},{4,0},{6,2},{8,12},{10,14},{12,8},{14,10},{16,20},{18,... | collective-permute-start | bytes 1769480 | tf_op jit(solution)/shard_map/ppermute | solution.py:1784
  245.6 47.7 %collective-permute-start.5 = (bf16[576,512]{1,0:T(8,128)(2,1)S(1)}, bf16[576,512]{1,0:T(8,128)(2,1)S(1)}, u32[]{:S(2)}, u32[]{:S(2)}) collective-permute-start(bf16[576,512]{1,0:T(8,128)(2,1)S(1)} %get-tuple-element.121), channel_id=1, source_target_pairs={{0,2},{2,0},{4,6},{6,4},{8,10},{10,8},{12,14},{14,12},{16,18},{18,... | collective-permute-start | bytes 1769480 | tf_op jit(solution)/shard_map/ppermute | solution.py:1784
  246.4 3.5 %copy-start.18 = (f32[16,512]{1,0:T(8,128)S(1)}, f32[16,512]{1,0:T(8,128)}, u32[]{:S(2)}) copy-start(f32[16,512]{1,0:T(8,128)} %get-tuple-element.99.vec_feed) | copy-start | bytes 98308

commit v3 on v2

--- a/solution.py
+++ b/solution.py
@@ -14,14 +14,15 @@
 HALF = BLK // 2
 LONG = 8
 TOGETHER = 16
-BACK_TOGETHER = 8
+BACK_TOGETHER = 16
 MOST = LONG + 1
 F32 = jnp.float32
 BF16 = jnp.bfloat16
 MESH = pl.DeviceIdType.MESH
+ROOM = 60 << 20
 VMEM = pl.BlockSpec(memory_space=pltpu.VMEM)
 SMEM = pl.BlockSpec(memory_space=pltpu.SMEM)
-ANY = pl.BlockSpec(memory_space=pl.ANY)
+ANY = pl.BlockSpec(memory_space=pltpu.HBM)
 
 
 norm_eps = 1e-05
@@ -546,21 +547,21 @@
             self.remote(src, dst, send_sem, recv_sem, tc, tf).wait_send()
 
 
-BIAS_ROWS = 16
+VECTORS = 10
 
 
 def project_kernel(
     n_ctx,
-    x_ref,
-    wq_ref,
-    wk_ref,
-    wv_ref,
-    order_ref,
-    seq_ref,
-    expand_ref,
+    x_hbm,
+    wq_hbm,
+    wk_hbm,
+    wv_hbm,
+    order_hbm,
+    seq_hbm,
     *rest,
 ):
-    vector_refs, rest = rest[:10], rest[10:]
+    vector_hbm, rest = rest[: VECTORS + 1], rest[VECTORS + 1 :]
+    vector_in, rest = rest[-VECTORS - 1 :], rest[: -VECTORS - 1]
     (
         q_out,
         kv_out,
@@ -569,14 +570,18 @@
         seq_out,
         vec_out,
         expand_out,
-        x_low,
+        x_in,
+        w_own,
         w_in,
         bias_own,
         bias_in,
+        order_own,
+        seq_own,
         order_in,
         seq_in,
         q_send,
         kv_send,
+        load_sem,
         w_ss,
         w_rs,
         q_ss,
@@ -588,29 +593,48 @@
     ) = rest
     at = Place()
     other = 1 - at.f
-    wide = wq_ref.shape[1]
-    for row, ref in enumerate(vector_refs):
-        bias_own[row : row + 1, :] = ref[...].astype(F32)
-    for part in range(expand_ref.shape[1] // wide):
-        row = len(vector_refs) + part
-        bias_own[row : row + 1, :] = expand_ref[:, part * wide : part * wide + wide].astype(F32)
+    loads = [
+        pltpu.make_async_copy(src, dst, load_sem.at[i])
+        for i, (src, dst) in enumerate(
+            (
+                (x_hbm, x_in),
+                (wq_hbm, w_own.at[0]),
+                (wk_hbm, w_own.at[1]),
+                (wv_hbm, w_own.at[2]),
+                (order_hbm, order_own),
+                (seq_hbm, seq_own),
+                *zip(vector_hbm, vector_in),
+            )
+        )
+    ]
+    for load in loads:
+        load.start()
     at.greet_sources(n_ctx, True)
+    for load in loads[6:]:
+        load.wait()
+    wide = bias_own.shape[1]
+    for row, ref in enumerate(vector_in[:VECTORS]):
+        bias_own[row : row + 1, :] = ref[...].astype(F32).reshape(1, wide)
+    for part in range(vector_in[VECTORS].shape[0] // wide):
+        piece = vector_in[VECTORS][part * wide : part * wide + wide]
+        bias_own[VECTORS + part : VECTORS + part + 1, :] = piece.astype(F32).reshape(1, wide)
     swaps = [
         at.remote(src, dst, w_ss.at[i], w_rs.at[i], at.c, other)
         for i, (src, dst) in enumerate(
             (
                 (bias_own, bias_in),
-                (wq_ref, w_in.at[0]),
-                (wk_ref, w_in.at[1]),
-                (wv_ref, w_in.at[2]),
-                (order_ref, order_in),
-                (seq_ref, seq_in),
+                (wq_hbm, w_in.at[0]),
+                (wk_hbm, w_in.at[1]),
+                (wv_hbm, w_in.at[2]),
+                (order_hbm, order_in),
+                (seq_hbm, seq_in),
             )
         )
     ]
     for swap in swaps:
         swap.start()
-    x_low[...] = x_ref[...].astype(BF16)
+    for load in loads[:6]:
+        load.wait()
 
     def targets(half):
         for pair in range(2):
@@ -635,7 +659,7 @@
                     )
 
     def one_half(half, wq, wk, wv, bias):
-        low = x_low[...]
+        low = x_in[...].astype(BF16)
         q = dot_nn(low, wq[...]) + bias[0:1, :]
         k = dot_nn(low, wk[...])
         v = dot_nn(low, wv[...]) + bias[1:2, :]
@@ -649,18 +673,18 @@
             at.send(*kv_move)
             at.send(*q_move)
 
-    one_half(at.f, wq_ref, wk_ref, wv_ref, bias_own)
+    one_half(at.f, w_own.at[0], w_own.at[1], w_own.at[2], bias_own)
     for swap in swaps:
         swap.wait()
     one_half(other, w_in.at[0], w_in.at[1], w_in.at[2], bias_in)
     w_other[...] = w_in[...]
     inside = at.inside == 1
-    order_out[...] = jnp.where(inside, order_ref[...], order_in[...])
-    seq_out[...] = jnp.where(inside, seq_ref[...], seq_in[...])
+    order_out[...] = jnp.where(inside, order_own[...], order_in[...])
+    seq_out[...] = jnp.where(inside, seq_own[...], seq_in[...])
     vec_out[...] = whole_rows(bias_own[...], bias_in[...], at.f == 0)
     for row, source in enumerate((bias_own, bias_in)):
-        for part in range(expand_ref.shape[1] // wide):
-            at_row = len(vector_refs) + part
+        for part in range(expand_out.shape[1] // wide):
+            at_row = VECTORS + part
             expand_out[row : row + 1, part * wide : part * wide + wide] = source[
                 at_row : at_row + 1, :
             ]
@@ -689,9 +713,11 @@
             at.wait_sent(*q_move)
 
 
-def project_and_scatter(n_ctx, x, wq, wk, wv, order, seqs, expand, vectors):
+def project_and_scatter(n_ctx, x, wq, wk, wv, order, seqs, vectors):
     wide = wq.shape[1]
     blocks = order.shape[1]
+    units = vectors[VECTORS].shape[0]
+    bias_rows = VECTORS + units // wide
     return pl.pallas_call(
         functools.partial(project_kernel, n_ctx),
         out_shape=(
@@ -700,20 +726,24 @@
             jax.ShapeDtypeStruct((3, D, wide), BF16),
             jax.ShapeDtypeStruct((1, blocks), jnp.int32),
             jax.ShapeDtypeStruct((1, blocks), jnp.int32),
-            jax.ShapeDtypeStruct((BIAS_ROWS, D), F32),
-            jax.ShapeDtypeStruct((2, expand.shape[1]), F32),
+            jax.ShapeDtypeStruct((bias_rows, D), F32),
+            jax.ShapeDtypeStruct((2, units), F32),
         ),
-        in_specs=[VMEM] * 17,
+        in_specs=[ANY] * (7 + VECTORS),
         out_specs=(ANY, ANY) + (VMEM,) * 5,
         scratch_shapes=[
-            pltpu.VMEM((2 * BLK, D), BF16),
+            pltpu.VMEM((2 * BLK, D), F32),
             pltpu.VMEM((3, D, wide), BF16),
-            pltpu.VMEM((BIAS_ROWS, wide), F32),
-            pltpu.VMEM((BIAS_ROWS, wide), F32),
+            pltpu.VMEM((3, D, wide), BF16),
+            pltpu.VMEM((bias_rows, wide), F32),
+            pltpu.VMEM((bias_rows, wide), F32),
+            pltpu.VMEM((1, blocks), jnp.int32),
+            pltpu.VMEM((1, blocks), jnp.int32),
             pltpu.VMEM((1, blocks), jnp.int32),
             pltpu.VMEM((1, blocks), jnp.int32),
             pltpu.VMEM((H, 2, HALF, 128), BF16),
             pltpu.VMEM((H, 2 * BLK, 128), BF16),
+            pltpu.SemaphoreType.DMA((7 + VECTORS,)),
             pltpu.SemaphoreType.DMA((6,)),
             pltpu.SemaphoreType.DMA((6,)),
             pltpu.SemaphoreType.DMA((2 * H,)),
@@ -722,12 +752,13 @@
             pltpu.SemaphoreType.DMA((n_ctx,)),
             pltpu.SemaphoreType.DMA((n_ctx,)),
             pltpu.SemaphoreType.DMA((n_ctx,)),
-        ],
+        ]
+        + [pltpu.VMEM(vector.shape, BF16) for vector in vectors],
         compiler_params=pltpu.CompilerParams(
-            collective_id=0, has_side_effects=True, vmem_limit_bytes=48 << 20
+            collective_id=0, has_side_effects=True, vmem_limit_bytes=ROOM
         ),
         name="project_scatter",
-    )(x, wq, wk, wv, order, seqs, expand, *vectors)
+    )(x, wq, wk, wv, order, seqs, *vectors)
 
 
 def forward_kernel(
@@ -841,7 +872,7 @@
                     jnp.sum(masses[slot], axis=1, keepdims=True), (HALF, 128)
                 )
                 results.append(total[slot] / mass)
-                lse_ref[slot] = jnp.transpose(peaks[slot] + jnp.log(mass))[0:8]
+                lse_ref[slot] = peaks[slot] + jnp.log(mass)
             packed = high_pair(results[0], results[1])
             keep_ref[source] = packed
             o_ref[source] = packed.astype(BF16)
@@ -862,7 +893,7 @@
         out_shape=(
             jax.ShapeDtypeStruct((blocks // 2, HALF, 128), BF16),
             jax.ShapeDtypeStruct((blocks // 2, HALF, 128), F32),
-            jax.ShapeDtypeStruct((blocks, 8, HALF), F32),
+            jax.ShapeDtypeStruct((blocks, HALF, 128), F32),
             jax.ShapeDtypeStruct((3, room), jnp.int32),
         ),
         in_specs=[SMEM, SMEM, VMEM, VMEM],
@@ -875,7 +906,7 @@
             pltpu.VMEM((blocks + 1, HALF, 128), F32),
             pltpu.VMEM((room, HALF, BLK), F32),
         ],
-        compiler_params=pltpu.CompilerParams(vmem_limit_bytes=48 << 20),
+        compiler_params=pltpu.CompilerParams(vmem_limit_bytes=ROOM),
         name="attend",
     )(order, seqs, q, kv)
 
@@ -891,9 +922,11 @@
     dq_ref,
     dkv_ref,
     both,
-    mass_rows,
-    delta_rows,
+    turned,
+    masses,
+    deltas,
     dq_sum,
+    dkv_sum,
 ):
     def unpack(step, _):
         for part in range(4):
@@ -901,38 +934,44 @@
             packed = q_ref[source].astype(F32) * (HD**-0.5)
             tangent = tan_ref[source].astype(F32)
             low = low_lanes(packed)
-            both[2 * source, 0:HALF] = jnp.where(low, packed, 0.0).astype(BF16)
-            both[2 * source + 1, 0:HALF] = jnp.where(low, swap_lanes(packed), 0.0).astype(BF16)
-            both[2 * source, HALF:BLK] = jnp.where(low, 0.0, swap_lanes(tangent)).astype(BF16)
-            both[2 * source + 1, HALF:BLK] = jnp.where(low, 0.0, tangent).astype(BF16)
-            across = jnp.transpose(tangent * keep_ref[source])
+            product = tangent * keep_ref[source]
             for side in range(2):
-                delta = jnp.sum(across[side * HD : side * HD + HD], axis=0, keepdims=True)
-                delta_rows[2 * source + side] = jnp.broadcast_to(delta, (8, HALF))
-                mass_rows[2 * source + side] = lse_ref[2 * source + side]
+                slot = 2 * source + side
+                q = packed if side == 0 else swap_lanes(packed)
+                tan = tangent if side == 1 else swap_lanes(tangent)
+                both[slot, 0:HALF] = jnp.where(low, q, 0.0).astype(BF16)
+                both[slot, HALF:BLK] = jnp.where(low, 0.0, tan).astype(BF16)
+                turned[slot] = jnp.transpose(both[slot])
+                mine = jnp.where(low == (side == 0), product, 0.0)
+                deltas[slot] = jnp.broadcast_to(
+                    jnp.sum(mine, axis=1, keepdims=True), (HALF, 128)
+                )
+                masses[slot] = lse_ref[slot]
         return 0
 
     lax.fori_loop(0, blocks // 8, unpack, 0)
     both[blocks] = jnp.zeros((BLK, 128), BF16)
-    mass_rows[blocks] = jnp.zeros((8, HALF), F32)
-    delta_rows[blocks] = jnp.zeros((8, HALF), F32)
+    turned[blocks] = jnp.zeros((128, BLK), BF16)
+    masses[blocks] = jnp.zeros((HALF, 128), F32)
+    deltas[blocks] = jnp.zeros((HALF, 128), F32)
 
     def clear(slot, _):
         dq_sum[slot] = jnp.zeros((HALF, 128), F32)
-        dkv_ref[slot] = jnp.zeros((BLK, 128), F32)
+        dkv_sum[slot] = jnp.zeros((128, BLK), F32)
         return 0
 
     lax.fori_loop(0, blocks, clear, 0)
     dq_sum[blocks] = jnp.zeros((HALF, 128), F32)
 
     def one_pair(q_slot, k_slot):
-        stacked = both[q_slot]
         kv = kv_ref[k_slot]
-        products = dot_nt(kv, stacked)
-        weights = jnp.exp(products[:, :HALF] - mass_rows[q_slot, 0:1, :])
-        score_tan = (weights * (products[:, HALF:] - delta_rows[q_slot, 0:1, :])).astype(BF16)
-        sides = jnp.concatenate([score_tan, weights.astype(BF16)], axis=1)
-        return dot_nn(sides, stacked), dot_tn(score_tan, kv)
+        products = dot_nt(both[q_slot], kv)
+        mass, delta = masses[q_slot], deltas[q_slot]
+        weights = jnp.exp(products[:HALF] - jnp.concatenate([mass, mass], axis=1))
+        score_tan = weights * (products[HALF:] - jnp.concatenate([delta, delta], axis=1))
+        score_tan = score_tan.astype(BF16)
+        sides = jnp.concatenate([score_tan, weights.astype(BF16)], axis=0)
+        return dot_nn(turned[q_slot], sides), dot_nn(score_tan, kv)
 
     def pair_turn(step, _):
         slots = [
@@ -941,20 +980,22 @@
         ]
         results = [one_pair(*slot) for slot in slots]
         for (q_slot, k_slot), (dkv, dq) in zip(slots, results):
-            dkv_ref[k_slot] = dkv_ref[k_slot] + dkv
+            dkv_sum[k_slot] = dkv_sum[k_slot] + dkv
             dq_sum[q_slot] = dq_sum[q_slot] + dq
         return 0
 
     lax.fori_loop(0, pairs_ref[2, 1], pair_turn, 0)
 
-    def finish(step, _):
+    def finish_rows(step, _):
         for part in range(4):
             source = step * 4 + part
             packed = low_pair(dq_sum[2 * source], dq_sum[2 * source + 1]) * (HD**-0.5)
             dq_ref[source] = packed.astype(BF16)
+            for slot in (2 * source, 2 * source + 1):
+                dkv_ref[slot] = jnp.transpose(dkv_sum[slot])
         return 0
 
-    lax.fori_loop(0, blocks // 8, finish, 0)
+    lax.fori_loop(0, blocks // 8, finish_rows, 0)
 
 
 def attend_back(pairs, q, tangent, keep, lse, kv):
@@ -969,11 +1010,13 @@
         out_specs=(VMEM, VMEM),
         scratch_shapes=[
             pltpu.VMEM((blocks + 1, BLK, 128), BF16),
-            pltpu.VMEM((blocks + 1, 8, HALF), F32),
-            pltpu.VMEM((blocks + 1, 8, HALF), F32),
+            pltpu.VMEM((blocks + 1, 128, BLK), BF16),
             pltpu.VMEM((blocks + 1, HALF, 128), F32),
+            pltpu.VMEM((blocks + 1, HALF, 128), F32),
+            pltpu.VMEM((blocks + 1, HALF, 128), F32),
+            pltpu.VMEM((blocks, 128, BLK), F32),
         ],
-        compiler_params=pltpu.CompilerParams(vmem_limit_bytes=48 << 20),
+        compiler_params=pltpu.CompilerParams(vmem_limit_bytes=ROOM),
         name="attend_back",
     )(pairs, q, tangent, keep, lse, kv)
 
@@ -1014,7 +1057,9 @@
             pltpu.SemaphoreType.DMA((n_ctx,)),
             pltpu.SemaphoreType.DMA((2 * H,)),
         ],
-        compiler_params=pltpu.CompilerParams(collective_id=1, has_side_effects=True),
+        compiler_params=pltpu.CompilerParams(
+            collective_id=1, has_side_effects=True, vmem_limit_bytes=ROOM
+        ),
         name="return_rows",
     )(rows)
 
@@ -1038,13 +1083,31 @@
     return bit, c + stride * (1 - 2 * bit)
 
 
+def feed_slopes(kind, target, mixed, low_turned, hidden, before_tan, feed_tan, branch_tan):
+    unit_count = hidden.shape[2] // COLS
+
+    def chunk_slopes(chunk, _):
+        columns = pl.ds(pl.multiple_of(chunk * COLS, COLS), COLS)
+        target[columns, :] = dot_tn(hidden[kind, :, columns], feed_tan[...]).astype(target.dtype)
+        below = pl.ds(pl.multiple_of((unit_count + chunk) * COLS, COLS), COLS)
+        target[below, :] = dot_nn(low_turned[...], before_tan[kind, :, columns]).astype(
+            target.dtype
+        )
+        return 0
+
+    lax.fori_loop(0, unit_count, chunk_slopes, 0)
+    start = 2 * unit_count * COLS
+    target[start : start + D // 2, :] = dot_tn(mixed[kind], branch_tan[...]).astype(target.dtype)
+
+
 def scatter_kernel(
-    n_ctx, rows_ref, own_ref, send_ref, out_ref, stage_a, stage_b, keep_ref, first_in,
+    n_ctx, rows_ref, mixed, low, hidden, before_tan, feed_tan, branch_tan,
+    out_ref, stage_a, stage_b, keep_ref, own_grads, send_grads, first_in, low_turned,
     ss, rs, core_ss, core_rs,
 ):
     at = Place()
     at.greet_sources(n_ctx, True)
-    quarter = own_ref.shape[0] // 4
+    quarter = first_in.shape[0] // 4
     bits = (step_of(at.c, 1)[0], step_of(at.c, 2)[0])
     stages = (stage_a, stage_b)
 
@@ -1066,21 +1129,25 @@
         where = span(start, quarter)
         slot = region + 2 * (0 if give else 1)
         return start, at.remote(
-            send_ref.at[where], first_in.at[where], core_ss.at[slot], core_rs.at[slot],
+            send_grads.at[where], first_in.at[where], core_ss.at[slot], core_rs.at[slot],
             at.c, 1 - at.f,
         )
 
     order = [(0, True), (1, True), (0, False), (1, False)]
+    for move in moves():
+        at.send(*move)
+    low_turned[...] = jnp.transpose(low[...])
+    operands = (mixed, low_turned, hidden, before_tan, feed_tan, branch_tan)
+    feed_slopes(1, send_grads, *operands)
     for step in order:
         core_move(*step)[1].start()
-    for move in moves():
-        at.send(*move)
+    feed_slopes(0, own_grads, *operands)
     for region, give in order:
         start, move = core_move(region, give)
         move.wait_recv()
 
         def join(offset, where, size):
-            total = own_ref[where, :].astype(F32) + first_in[where, :].astype(F32)
+            total = own_grads[where, :] + first_in[where, :].astype(F32)
             if give:
                 stages[region][span(offset, size), :] = total.astype(BF16)
             else:
@@ -1096,8 +1163,9 @@
         core_move(*step)[1].wait_send()
 
 
-def scatter_rows(n_ctx, rows, own, send):
-    grad_rows = own.shape[0]
+def scatter_rows(n_ctx, rows, operands):
+    mixed, low, hidden = operands[:3]
+    grad_rows = 2 * hidden.shape[2] + D // 2
     return pl.pallas_call(
         functools.partial(scatter_kernel, n_ctx),
         out_shape=(
@@ -1106,24 +1174,28 @@
             jax.ShapeDtypeStruct((grad_rows // 4, D), BF16),
             jax.ShapeDtypeStruct((2, grad_rows // 4, D), F32),
         ),
-        in_specs=[ANY, VMEM, ANY],
+        in_specs=[ANY] + [VMEM] * 6,
         out_specs=(ANY, VMEM, VMEM, VMEM),
         scratch_shapes=[
+            pltpu.VMEM((grad_rows, D), F32),
             pltpu.VMEM((grad_rows, D), BF16),
+            pltpu.VMEM((grad_rows, D), BF16),
+            pltpu.VMEM((D, low.shape[0]), BF16),
             pltpu.SemaphoreType.DMA((2 * H,)),
             pltpu.SemaphoreType.DMA((n_ctx,)),
             pltpu.SemaphoreType.DMA((4,)),
             pltpu.SemaphoreType.DMA((4,)),
         ],
         compiler_params=pltpu.CompilerParams(
-            collective_id=2, has_side_effects=True, vmem_limit_bytes=32 << 20
+            collective_id=2, has_side_effects=True, vmem_limit_bytes=ROOM
         ),
         name="scatter_rows",
-    )(rows, own, send)
+    )(rows, *operands)
 
 
 class Ladder:
-    def __init__(self, at, plans, starts, size, acc, stage, landing, out, sems):
+    def __init__(self, at, plans, starts, size, acc, stage, landing, out, sems, bases=(0, 0)):
+        self.bases = bases
         self.at, self.acc, self.stage, self.landing, self.out = at, acc, stage, landing, out
         self.down_ss, self.down_rs, self.up_ss, self.up_rs = sems
         self.ranges = []
@@ -1154,7 +1226,8 @@
 
     def up(self, region, step, sent):
         kept, given, size, peer = self.ranges[region][step]
-        where, slot = span(kept if sent else given, size), self.slot(region, step)
+        start = self.bases[region] + (kept if sent else given)
+        where, slot = span(start, size), self.slot(region, step)
         return self.at.remote(
             self.out[region].at[where],
             self.out[region].at[where],
@@ -1184,9 +1257,9 @@
         kept, _, size, _ = self.ranges[region][self.last]
         arrived = self.landing[region][self.last]
 
-        def body(offset, where, _):
+        def body(offset, where, rows):
             total = self.stage[region][where, :].astype(F32) + arrived[where, :].astype(F32)
-            self.out[region][where, :] = total.astype(BF16)
+            self.out[region][span(self.bases[region] + kept + offset, rows), :] = total.astype(BF16)
 
         self.down(region, self.last, False).wait_recv()
         pieces_of(kept, size, body)
@@ -1200,145 +1273,6 @@
                 self.up(region, step, True).wait_send()
 
 
-def return_grads_kernel(
-    n_ctx, dq_ref, dkv_ref, keep_ref, land_a, land_b, dq_out, dkv_out, done_ref,
-    own, part, ready, acc, stage, landing,
-    q_ss, q_rs, kv_ss, kv_rs, part_ss, part_rs, own_sem, down_ss, down_rs, up_ss, up_rs,
-):
-    at = Place()
-    other = 1 - at.f
-    x_step, y_step, near, far = (step_of(at.c, stride) for stride in (1, 2, 4, 8))
-    barrier = pltpu.get_barrier_semaphore()
-    for _, peer in (x_step, y_step, near, far):
-        pl.semaphore_signal(barrier, 1, device_id=(peer, at.f), device_id_type=MESH)
-    at.greet_owners(n_ctx, True, 4)
-
-    def partial_move(source):
-        return at.remote(
-            dkv_ref.at[2 * source + other],
-            part.at[source],
-            part_ss.at[source],
-            part_rs.at[source],
-            at.c,
-            other,
-        )
-
-    def own_move(source):
-        return pltpu.make_async_copy(
-            dkv_ref.at[2 * source + at.f], own.at[source], own_sem.at[source]
-        )
-
-    def q_move(target):
-        return (
-            dq_ref.at[target],
-            dq_out.at[at.head, at.f],
-            q_ss.at[target],
-            q_rs.at[at.head * 2 + at.f],
-            target,
-            at.group,
-        )
-
-    def kv_move(target):
-        return (
-            ready.at[target],
-            dkv_out.at[at.head, pl.ds(pl.multiple_of(at.f * BLK, BLK), BLK)],
-            kv_ss.at[target],
-            kv_rs.at[at.head * 2 + at.f],
-            target,
-            at.group,
-        )
-
-    size = keep_ref.shape[1]
-    ladder = Ladder(
-        at,
-        ((y_step, near, far), (x_step, near, far)),
-        (0, 0),
-        size,
-        [acc.at[region] for region in range(2)],
-        [stage.at[region] for region in range(2)],
-        [[landing.at[region, step] for step in range(3)] for region in range(2)],
-        [done_ref.at[region] for region in range(2)],
-        (down_ss, down_rs, up_ss, up_rs),
-    )
-    for source in range(n_ctx):
-        partial_move(source).start()
-        own_move(source).start()
-    for region, first_in in enumerate((land_a, land_b)):
-        ladder.acc[region] = keep_ref.at[region]
-        kept, given, half, _ = ladder.ranges[region][0]
-        ladder.join(region, given, half, first_in, stage.at[region])
-        ladder.down(region, 0, True).start()
-        ladder.join(region, kept, half, first_in, acc.at[region])
-        ladder.acc[region] = acc.at[region]
-    for target in range(n_ctx):
-        at.send(*q_move(target))
-    for source in range(n_ctx):
-        own_move(source).wait()
-        partial_move(source).wait_recv()
-        ready[source] = (own[source] + part[source]).astype(BF16)
-        at.send(*kv_move(source))
-    for step in (1, 2):
-        for region in range(2):
-            ladder.down(region, step - 1, False).wait_recv()
-            ladder.give(region, step, ladder.landing[region][step - 1])
-    for region in range(2):
-        ladder.settle(region)
-    for region in range(2):
-        ladder.up(region, 1, False).wait_recv()
-        ladder.up(region, 0, True).start()
-    for region in range(2):
-        ladder.up(region, 0, False).wait_recv()
-    for head in range(H):
-        for core in range(2):
-            slot = head * 2 + core
-            arrived = dq_out.at[head, core]
-            at.remote(arrived, arrived, q_ss.at[0], q_rs.at[slot], at.c, other).wait_recv()
-            arrived = dkv_out.at[head, pl.ds(core * BLK, BLK)]
-            at.remote(arrived, arrived, kv_ss.at[0], kv_rs.at[slot], at.c, other).wait_recv()
-    for target in range(n_ctx):
-        partial_move(target).wait_send()
-        at.wait_sent(*q_move(target))
-        at.wait_sent(*kv_move(target))
-    ladder.wait_sent()
-
-
-def return_grads(n_ctx, dq, dkv, keep, land_a, land_b):
-    size = keep.shape[1]
-    return pl.pallas_call(
-        functools.partial(return_grads_kernel, n_ctx),
-        out_shape=(
-            jax.ShapeDtypeStruct((H, 2, HALF, 128), BF16),
-            jax.ShapeDtypeStruct((H, 2 * BLK, 128), BF16),
-            jax.ShapeDtypeStruct((2, size, D), BF16),
-        ),
-        in_specs=[ANY, ANY, VMEM, VMEM, VMEM],
-        out_specs=(ANY, ANY, VMEM),
-        scratch_shapes=[
-            pltpu.VMEM((n_ctx, BLK, 128), F32),
-            pltpu.VMEM((n_ctx, BLK, 128), F32),
-            pltpu.VMEM((n_ctx, BLK, 128), BF16),
-            pltpu.VMEM((2, size, D), F32),
-            pltpu.VMEM((2, size, D), BF16),
-            pltpu.VMEM((2, 3, size, D), BF16),
-            pltpu.SemaphoreType.DMA((n_ctx,)),
-            pltpu.SemaphoreType.DMA((2 * H,)),
-            pltpu.SemaphoreType.DMA((n_ctx,)),
-            pltpu.SemaphoreType.DMA((2 * H,)),
-            pltpu.SemaphoreType.DMA((n_ctx,)),
-            pltpu.SemaphoreType.DMA((n_ctx,)),
-            pltpu.SemaphoreType.DMA((n_ctx,)),
-            pltpu.SemaphoreType.DMA((6,)),
-            pltpu.SemaphoreType.DMA((6,)),
-            pltpu.SemaphoreType.DMA((6,)),
-            pltpu.SemaphoreType.DMA((6,)),
-        ],
-        compiler_params=pltpu.CompilerParams(
-            collective_id=3, has_side_effects=True, vmem_limit_bytes=40 << 20
-        ),
-        name="return_grads",
-    )(dq, dkv, keep, land_a, land_b)
-
-
 COLS = 512
 
 
@@ -1372,8 +1306,8 @@
 def dense_kernel(
     x_ref, sum_ref, cot_ref, o_ref,
     wo_a, wo_b, we_a, we_b, ws_a, ws_b, be_ref, vec_in,
-    out_ref, sum_tan_ref, entry_ref, tan_ref, own_ref, send_ref, vec_ref,
-    mixed, low, hidden, slope, before_tan, feed_tan, branch_tan, mixed_tan,
+    out_ref, sum_tan_ref, entry_ref, tan_ref, vec_ref,
+    mixed, low, hidden, before_tan, feed_tan, branch_tan, slope, mixed_tan,
 ):
     f = lax.axis_index("fsdp")
     wo, we, ws = (wo_a, wo_b), (we_a, we_b), (ws_a, ws_b)
@@ -1476,26 +1410,10 @@
                     late = mixed_tan[kind, BLK + core * HALF : BLK + core * HALF + HALF, columns]
                     tan_ref[head, core] = side_pair(side, early, late).astype(BF16)
 
-    for kind, grad_ref in enumerate((own_ref, send_ref)):
-        unit_count = ws[kind].shape[0] // COLS
-
-        def slopes(chunk, _):
-            columns = pl.ds(pl.multiple_of(chunk * COLS, COLS), COLS)
-            grad_ref[columns, :] = dot_tn(hidden[kind, :, columns], feed_tan[...]).astype(BF16)
-            below = pl.ds(pl.multiple_of((unit_count + chunk) * COLS, COLS), COLS)
-            grad_ref[below, :] = dot_tn(low[...], before_tan[kind, :, columns]).astype(BF16)
-            return 0
-
-        lax.fori_loop(0, unit_count, slopes, 0)
-        grad_ref[2 * unit_count * COLS : 2 * unit_count * COLS + D // 2, :] = dot_tn(
-            mixed[kind], branch_tan[...]
-        ).astype(BF16)
-
 
 def dense(x, summed, cotangent, o, wo, we, ws, be, vec):
     tokens = x.shape[0]
     units = ws[0].shape[0]
-    grad_rows = units + units + D // 2
     return pl.pallas_call(
         dense_kernel,
         out_shape=(
@@ -1503,105 +1421,189 @@
             jax.ShapeDtypeStruct((tokens, D), F32),
             jax.ShapeDtypeStruct((tokens, D), F32),
             jax.ShapeDtypeStruct((H, 2, HALF, 128), BF16),
-            jax.ShapeDtypeStruct((grad_rows, D), BF16),
-            jax.ShapeDtypeStruct((grad_rows, D), BF16),
             jax.ShapeDtypeStruct((16, D), F32),
+            jax.ShapeDtypeStruct((2, tokens, D // 2), BF16),
+            jax.ShapeDtypeStruct((tokens, D), BF16),
+            jax.ShapeDtypeStruct((2, tokens, units), BF16),
+            jax.ShapeDtypeStruct((2, tokens, units), BF16),
+            jax.ShapeDtypeStruct((tokens, D), BF16),
+            jax.ShapeDtypeStruct((tokens, D), BF16),
         ),
         in_specs=[VMEM] * 12,
-        out_specs=(VMEM,) * 7,
+        out_specs=(VMEM,) * 11,
         scratch_shapes=[
-            pltpu.VMEM((2, tokens, D // 2), BF16),
-            pltpu.VMEM((tokens, D), BF16),
-            pltpu.VMEM((2, tokens, units), BF16),
             pltpu.VMEM((2, BLK, units), F32),
-            pltpu.VMEM((2, tokens, units), BF16),
-            pltpu.VMEM((tokens, D), BF16),
-            pltpu.VMEM((tokens, D), BF16),
             pltpu.VMEM((2, tokens, D // 2), F32),
         ],
-        compiler_params=pltpu.CompilerParams(vmem_limit_bytes=56 << 20),
+        compiler_params=pltpu.CompilerParams(vmem_limit_bytes=ROOM),
         name="dense",
     )(x, summed, cotangent, o, *wo, *we, *ws, be, vec)
 
 
-def last_kernel(
-    x_ref, entry_ref, dq_ref, dkv_ref, wq, wk, wv, w_other,
-    out_ref, own_ref, send_ref, vec_ref, tangents,
-):
-    f = lax.axis_index("fsdp")
-    halves = (f, 1 - f)
-    wide = D // 2
-    vec_ref[...] = jnp.zeros_like(vec_ref)
-    for kind in range(2):
-        for pair in range(2):
-            head = halves[kind] * (H // 2) + 2 * pair
-            columns = slice(pair * 128, pair * 128 + 128)
-            for core in range(2):
-                early = dq_ref[head, core].astype(F32)
-                late = dq_ref[head + 1, core].astype(F32)
-                for side in range(2):
-                    start = side * BLK + core * HALF
-                    tangents[kind, 0, start : start + HALF, columns] = side_pair(
-                        side, early, late
-                    ).astype(BF16)
-            early = dkv_ref[head].astype(F32)
-            late = dkv_ref[head + 1].astype(F32)
-            tangents[kind, 1, :, columns] = low_pair(early, late).astype(BF16)
-            tangents[kind, 2, :, columns] = high_pair(early, late).astype(BF16)
-    weights = ((wq, wk, wv), (w_other.at[0], w_other.at[1], w_other.at[2]))
-    total = entry_ref[...]
-    for kind in range(2):
-        for which in range(3):
-            total = total + dot_nt(tangents[kind, which], weights[kind][which][...])
-    out_ref[...] = total
-    low = x_ref[...].astype(BF16)
-    for kind, grad_ref in enumerate((own_ref, send_ref)):
-        grad_ref[0:D, 0:wide] = dot_tn(low, tangents[kind, 0]).astype(BF16)
-        grad_ref[0:D, wide:D] = dot_tn(low, tangents[kind, 1]).astype(BF16)
-        value_grad = dot_tn(low, tangents[kind, 2]).astype(BF16)
-        grad_ref[D : D + wide, 0:wide] = value_grad[0:wide]
-        grad_ref[D : D + wide, wide:D] = value_grad[wide:D]
-        columns = pl.ds(pl.multiple_of(halves[kind] * wide, wide), wide)
-        vec_ref[0:1, columns] = column_sum(tangents[kind, 0].astype(F32))
-        vec_ref[1:2, columns] = column_sum(tangents[kind, 2].astype(F32))
-
-
-def last_dense(x, entry, dq, dkv, wq, wk, wv, w_other):
-    tokens = x.shape[0]
-    grad_rows = D + D // 2
-    return pl.pallas_call(
-        last_kernel,
-        out_shape=(
-            jax.ShapeDtypeStruct((tokens, D), F32),
-            jax.ShapeDtypeStruct((grad_rows, D), BF16),
-            jax.ShapeDtypeStruct((grad_rows, D), BF16),
-            jax.ShapeDtypeStruct((8, D), F32),
-        ),
-        in_specs=[VMEM] * 8,
-        out_specs=(VMEM,) * 4,
-        scratch_shapes=[pltpu.VMEM((2, 3, tokens, D // 2), BF16)],
-        compiler_params=pltpu.CompilerParams(vmem_limit_bytes=48 << 20),
-        name="last_dense",
-    )(x, entry, dq, dkv, wq, wk, wv, w_other)
-
-
-def reduce_kernel(
-    own_ref, send_ref, vec_feed, vec_last, out_ref, vec_out,
-    first_in, acc, stage, landing, vec_sum, vec_in,
-    core_ss, core_rs, down_ss, down_rs, up_ss, up_rs, vec_ss, vec_rs,
+def finish_kernel(
+    n_ctx,
+    dq_ref, dkv_ref, keep_hbm, land_a, land_b, x_hbm, entry_hbm, wq_hbm, wk_hbm, wv_hbm,
+    w_other_hbm, vec_feed,
+    post_ref, feed_ref, grads_ref, vec_out,
+    own, part, ready, dq_in, dkv_in, keep, acc, stage, landing,
+    x_in, entry_in, w_in, w_far, low_turned, tangents,
+    own_grads, send_grads, first_in, acc_last, stage_last, landing_last, vec_sum, vec_in,
+    load_sem, q_ss, q_rs, kv_ss, kv_rs, part_ss, part_rs, own_sem,
+    down_ss, down_rs, up_ss, up_rs, top_ss, top_rs,
+    core_ss, core_rs, down_ss2, down_rs2, up_ss2, up_rs2, vec_ss, vec_rs,
 ):
     at = Place()
     c, f = at.c, at.f
-    rows = own_ref.shape[0]
-    quarter = rows // 4
+    other = 1 - f
+    halves = (f, other)
+    wide = D // 2
+    loads = [
+        pltpu.make_async_copy(src, dst, load_sem.at[i])
+        for i, (src, dst) in enumerate(
+            (
+                (keep_hbm, keep),
+                (x_hbm, x_in),
+                (entry_hbm, entry_in),
+                (wq_hbm, w_in.at[0]),
+                (wk_hbm, w_in.at[1]),
+                (wv_hbm, w_in.at[2]),
+                (w_other_hbm, w_far),
+            )
+        )
+    ]
+    for load in loads:
+        load.start()
     x_step, y_step, near, far = (step_of(c, stride) for stride in (1, 2, 4, 8))
     barrier = pltpu.get_barrier_semaphore()
-    pl.semaphore_signal(barrier, 1, device_id=(c, 1 - f), device_id_type=MESH)
     for _, peer in (x_step, y_step, near, far):
         pl.semaphore_signal(barrier, 1, device_id=(peer, f), device_id_type=MESH)
-    pl.semaphore_wait(barrier, 5)
-
-    vec_peers = [(c, 1 - f)] + [(peer, f) for _, peer in (x_step, y_step, near, far)]
+    at.greet_owners(n_ctx, True, 4)
+
+    def partial_move(source):
+        return at.remote(
+            dkv_ref.at[2 * source + other],
+            part.at[source],
+            part_ss.at[source],
+            part_rs.at[source],
+            c,
+            other,
+        )
+
+    def own_move(source):
+        return pltpu.make_async_copy(
+            dkv_ref.at[2 * source + f], own.at[source], own_sem.at[source]
+        )
+
+    def q_move(target):
+        return (
+            dq_ref.at[target],
+            dq_in.at[at.head, f],
+            q_ss.at[target],
+            q_rs.at[at.head * 2 + f],
+            target,
+            at.group,
+        )
+
+    def kv_move(target):
+        return (
+            ready.at[target],
+            dkv_in.at[at.head, pl.ds(pl.multiple_of(f * BLK, BLK), BLK)],
+            kv_ss.at[target],
+            kv_rs.at[at.head * 2 + f],
+            target,
+            at.group,
+        )
+
+    for source in range(n_ctx):
+        partial_move(source).start()
+        own_move(source).start()
+    for target in range(n_ctx):
+        at.send(*q_move(target))
+
+    size = keep.shape[1]
+    firsts = (x_step, y_step)
+    bases = [2 * size * region + firsts[region][0] * size for region in range(2)]
+    feed = Ladder(
+        at,
+        ((y_step, near, far), (x_step, near, far)),
+        (0, 0),
+        size,
+        [keep.at[region] for region in range(2)],
+        [stage.at[region] for region in range(2)],
+        [[landing.at[region, step] for step in range(3)] for region in range(2)],
+        [feed_ref, feed_ref],
+        (down_ss, down_rs, up_ss, up_rs),
+        bases,
+    )
+
+    def top_move(region, sent):
+        kept = bases[region]
+        given = 2 * size * region + (1 - firsts[region][0]) * size
+        where = span(kept if sent else given, size)
+        return at.remote(
+            feed_ref.at[where],
+            feed_ref.at[where],
+            top_ss.at[region],
+            top_rs.at[region],
+            firsts[region][1],
+            f,
+        )
+
+    loads[0].wait()
+    for region, first in enumerate((land_a, land_b)):
+        kept, given, half, _ = feed.ranges[region][0]
+        feed.join(region, given, half, first, stage.at[region])
+        feed.down(region, 0, True).start()
+        feed.join(region, kept, half, first, acc.at[region])
+        feed.acc[region] = acc.at[region]
+    for source in range(n_ctx):
+        own_move(source).wait()
+        partial_move(source).wait_recv()
+        ready[source] = (own[source] + part[source]).astype(BF16)
+        at.send(*kv_move(source))
+    for load in loads[1:]:
+        load.wait()
+    low_turned[...] = jnp.transpose(x_in[...]).astype(BF16)
+    for step in (1, 2):
+        for region in range(2):
+            feed.down(region, step - 1, False).wait_recv()
+            feed.give(region, step, feed.landing[region][step - 1])
+
+    for head in range(H):
+        for core in range(2):
+            slot = head * 2 + core
+            arrived = dq_in.at[head, core]
+            at.remote(arrived, arrived, q_ss.at[0], q_rs.at[slot], c, other).wait_recv()
+            arrived = dkv_in.at[head, pl.ds(core * BLK, BLK)]
+            at.remote(arrived, arrived, kv_ss.at[0], kv_rs.at[slot], c, other).wait_recv()
+    feed_rows = vec_feed.shape[0]
+    vec_sum[0, 0:feed_rows] = vec_feed[...]
+    vec_sum[0, feed_rows:] = jnp.zeros_like(vec_sum[0, feed_rows:])
+
+    plans = ((x_step, y_step, near, far), (y_step, x_step, near, far))
+    quarter = first_in.shape[0] // 4
+    last = Ladder(
+        at,
+        plans,
+        (0, 2 * quarter),
+        2 * quarter,
+        [acc_last, acc_last],
+        [stage_last, stage_last],
+        [[landing_last.at[step] for step in range(4)]] * 2,
+        [grads_ref, grads_ref],
+        (down_ss2, down_rs2, up_ss2, up_rs2),
+    )
+
+    def core_move(region, give):
+        kept, given, rows, _ = last.ranges[region][0]
+        where = span(given if give else kept, rows)
+        slot = region + 2 * (0 if give else 1)
+        return at.remote(
+            send_grads.at[where], first_in.at[where], core_ss.at[slot], core_rs.at[slot], c, other
+        )
+
+    order = [(0, True), (1, True), (0, False), (1, False)]
+    vec_peers = [(c, other)] + [(peer, f) for _, peer in (x_step, y_step, near, far)]
 
     def vec_move(step):
         return at.remote(
@@ -1615,107 +1617,156 @@
         if step < 4:
             vec_move(step + 1).start()
 
-    shared = [acc, acc], [stage, stage], [[landing.at[step] for step in range(4)]] * 2
-    ladder = Ladder(
-        at,
-        ((x_step, y_step, near, far), (y_step, x_step, near, far)),
-        (0, 2 * quarter),
-        2 * quarter,
-        shared[0],
-        shared[1],
-        shared[2],
-        [out_ref, out_ref],
-        (down_ss, down_rs, up_ss, up_rs),
-    )
-
-    def core_move(region, give):
-        kept, given, size, _ = ladder.ranges[region][0]
-        where = span(given if give else kept, size)
-        slot = region + 2 * (0 if give else 1)
-        return at.remote(
-            send_ref.at[where], first_in.at[where], core_ss.at[slot], core_rs.at[slot], c, 1 - f
-        )
-
-    order = [(0, True), (1, True), (0, False), (1, False)]
-    for step in order:
-        core_move(*step).start()
-    feed_rows = vec_feed.shape[0]
-    vec_sum[0, 0:feed_rows] = vec_feed[...]
-    vec_sum[0, feed_rows : feed_rows + vec_last.shape[0]] = vec_last[...]
+    for kind, grad_ref in ((1, send_grads), (0, own_grads)):
+        for pair in range(2):
+            head = halves[kind] * (H // 2) + 2 * pair
+            columns = slice(pair * 128, pair * 128 + 128)
+            for core in range(2):
+                early = dq_in[head, core].astype(F32)
+                late = dq_in[head + 1, core].astype(F32)
+                for side in range(2):
+                    start = side * BLK + core * HALF
+                    tangents[kind, 0, start : start + HALF, columns] = side_pair(
+                        side, early, late
+                    ).astype(BF16)
+            early = dkv_in[head].astype(F32)
+            late = dkv_in[head + 1].astype(F32)
+            tangents[kind, 1, :, columns] = low_pair(early, late).astype(BF16)
+            tangents[kind, 2, :, columns] = high_pair(early, late).astype(BF16)
+        turned = low_turned[...]
+        grad_ref[0:D, 0:wide] = dot_nn(turned, tangents[kind, 0]).astype(grad_ref.dtype)
+        grad_ref[0:D, wide:D] = dot_nn(turned, tangents[kind, 1]).astype(grad_ref.dtype)
+        value_grad = dot_nn(turned, tangents[kind, 2]).astype(grad_ref.dtype)
+        grad_ref[D : D + wide, 0:wide] = value_grad[0:wide]
+        grad_ref[D : D + wide, wide:D] = value_grad[wide:D]
+        columns = pl.ds(pl.multiple_of(halves[kind] * wide, wide), wide)
+        vec_sum[0, feed_rows : feed_rows + 1, columns] = column_sum(tangents[kind, 0].astype(F32))
+        vec_sum[0, feed_rows + 1 : feed_rows + 2, columns] = column_sum(
+            tangents[kind, 2].astype(F32)
+        )
+        if kind == 1:
+            for step in order:
+                core_move(*step).start()
     vec_move(0).start()
+    for region in range(2):
+        feed.settle(region)
     for region, give in order:
         core_move(region, give).wait_recv()
-        kept, given, size, _ = ladder.ranges[region][0]
+        kept, given, rows, _ = last.ranges[region][0]
 
         def join(offset, where, _):
-            total = own_ref[where, :].astype(F32) + first_in[where, :].astype(F32)
+            total = own_grads[where, :] + first_in[where, :].astype(F32)
             if give:
-                stage[where, :] = total.astype(BF16)
+                stage_last[where, :] = total.astype(BF16)
             else:
-                acc[where, :] = total
-
-        pieces_of(given if give else kept, size, join)
+                acc_last[where, :] = total
+
+        pieces_of(given if give else kept, rows, join)
         if give:
-            ladder.down(region, 0, True).start()
+            last.down(region, 0, True).start()
     vec_next(0)
-    for step in (1, 2, 3):
+    total = entry_in[...]
+    for which in range(3):
+        total = total + dot_nt(tangents[0, which], w_in[which])
+        total = total + dot_nt(tangents[1, which], w_far[which])
+    post_ref[...] = total
+    for region in range(2):
+        feed.up(region, 1, False).wait_recv()
+        feed.up(region, 0, True).start()
+    for step in (1, 2):
         for region in range(2):
-            ladder.down(region, step - 1, False).wait_recv()
-            ladder.give(region, step, ladder.landing[region][step - 1])
+            last.down(region, step - 1, False).wait_recv()
+            last.give(region, step, last.landing[region][step - 1])
         vec_next(step)
     for region in range(2):
-        ladder.settle(region)
+        feed.up(region, 0, False).wait_recv()
+        top_move(region, True).start()
+    for region in range(2):
+        last.down(region, 2, False).wait_recv()
+        last.give(region, 3, last.landing[region][2])
+    vec_next(3)
+    for region in range(2):
+        last.settle(region)
     vec_next(4)
     for step in (2, 1, 0):
         for region in range(2):
-            ladder.up(region, step, False).wait_recv()
+            last.up(region, step, False).wait_recv()
             if step > 0:
-                ladder.up(region, step - 1, True).start()
+                last.up(region, step - 1, True).start()
+    for region in range(2):
+        top_move(region, False).wait_recv()
+
+    for target in range(n_ctx):
+        partial_move(target).wait_send()
+        at.wait_sent(*q_move(target))
+        at.wait_sent(*kv_move(target))
     for step in order:
         core_move(*step).wait_send()
     for step in range(5):
         vec_move(step).wait_send()
-    ladder.wait_sent()
-
-
-def reduce_grads(own, send, vec_feed, vec_last):
-    wide = own.shape
-    vec_shape = (vec_feed.shape[0] + vec_last.shape[0], D)
+    for region in range(2):
+        top_move(region, True).wait_send()
+    feed.wait_sent()
+    last.wait_sent()
+
+
+def finish(n_ctx, dq, dkv, keep, land_a, land_b, x, entry, wq, wk, wv, w_other, vec_feed):
+    size, tokens, wide = keep.shape[1], x.shape[0], D // 2
+    last_shape = (D + wide, D)
+    vec_shape = (vec_feed.shape[0] + 8, D)
+
+    def sems(*counts):
+        return [pltpu.SemaphoreType.DMA((count,)) for count in counts]
+
     return pl.pallas_call(
-        reduce_kernel,
-        out_shape=(jax.ShapeDtypeStruct(wide, BF16), jax.ShapeDtypeStruct(vec_shape, F32)),
-        in_specs=[VMEM] * 4,
-        out_specs=(VMEM, VMEM),
+        functools.partial(finish_kernel, n_ctx),
+        out_shape=(
+            jax.ShapeDtypeStruct((tokens, D), F32),
+            jax.ShapeDtypeStruct((4 * size, D), BF16),
+            jax.ShapeDtypeStruct(last_shape, BF16),
+            jax.ShapeDtypeStruct(vec_shape, F32),
+        ),
+        in_specs=[ANY, ANY, ANY, VMEM, VMEM] + [ANY] * 6 + [VMEM],
+        out_specs=(VMEM,) * 4,
         scratch_shapes=[
-            pltpu.VMEM(wide, BF16),
-            pltpu.VMEM(wide, F32),
-            pltpu.VMEM(wide, BF16),
-            pltpu.VMEM((4,) + wide, BF16),
+            pltpu.VMEM((n_ctx, BLK, 128), F32),
+            pltpu.VMEM((n_ctx, BLK, 128), F32),
+            pltpu.VMEM((n_ctx, BLK, 128), BF16),
+            pltpu.VMEM((H, 2, HALF, 128), BF16),
+            pltpu.VMEM((H, 2 * BLK, 128), BF16),
+            pltpu.VMEM((2, size, D), F32),
+            pltpu.VMEM((2, size, D), F32),
+            pltpu.VMEM((2, size, D), BF16),
+            pltpu.VMEM((2, 3, size, D), BF16),
+            pltpu.VMEM((tokens, D), F32),
+            pltpu.VMEM((tokens, D), F32),
+            pltpu.VMEM((3, D, wide), BF16),
+            pltpu.VMEM((3, D, wide), BF16),
+            pltpu.VMEM((D, tokens), BF16),
+            pltpu.VMEM((2, 3, tokens, wide), BF16),
+            pltpu.VMEM(last_shape, F32),
+            pltpu.VMEM(last_shape, BF16),
+            pltpu.VMEM(last_shape, BF16),
+            pltpu.VMEM(last_shape, F32),
+            pltpu.VMEM(last_shape, BF16),
+            pltpu.VMEM((4,) + last_shape, BF16),
             pltpu.VMEM((5,) + vec_shape, F32),
             pltpu.VMEM((5,) + vec_shape, F32),
         ]
-        + [pltpu.SemaphoreType.DMA((4,))] * 2
-        + [pltpu.SemaphoreType.DMA((8,))] * 4
-        + [pltpu.SemaphoreType.DMA((5,))] * 2,
+        + sems(7, n_ctx, 2 * H, n_ctx, 2 * H, n_ctx, n_ctx, n_ctx)
+        + sems(6, 6, 6, 6, 2, 2, 4, 4, 8, 8, 8, 8, 5, 5),
         compiler_params=pltpu.CompilerParams(
-            collective_id=4, has_side_effects=True, vmem_limit_bytes=32 << 20
+            collective_id=3, has_side_effects=True, vmem_limit_bytes=ROOM
         ),
-        name="reduce_grads",
-    )(own, send, vec_feed, vec_last)
+        name="finish",
+    )(dq, dkv, keep, land_a, land_b, x, entry, wq, wk, wv, w_other, vec_feed)
 
 
 def unpack_kernel(
-    done_ref, rest_a, rest_b, grads_ref, vec_ref,
-    query_ref, key_ref, value_ref, output_ref, expand_ref, shrink_ref, *rest,
+    full, grads_ref, vec_ref,
+    query_ref, key_ref, value_ref, output_ref, expand_ref, shrink_ref, *vector_outs,
 ):
-    vector_outs, full = rest[:-1], rest[-1]
-    c, f = lax.axis_index("ctx"), lax.axis_index("fsdp")
-    size = done_ref.shape[1]
-    for region, far_part in enumerate((rest_a, rest_b)):
-        bit = step_of(c, 1 + region)[0]
-        start = 2 * region * size
-        full[span(start + bit * size, size), :] = done_ref[region]
-        full[span(start + (1 - bit) * size, size), :] = far_part[...]
+    f = lax.axis_index("fsdp")
     units, wide = shrink_ref.shape[0], D // 2
     shrink_ref[...] = full[0:units].astype(F32)
     for part in range(units // D):
@@ -1735,18 +1786,17 @@
         vector_outs[10][:, part * D : part * D + D] = drift[part : part + 1]
 
 
-def unpack_grads(units, done, rest_a, rest_b, grads, vecs):
+def unpack_grads(units, full, grads, vecs):
     wide = D // 2
     shapes = [(D, wide)] * 3 + [(wide, D), (D, units), (units, D)] + [(1, wide)] * 10 + [(1, units)]
     return pl.pallas_call(
         unpack_kernel,
         out_shape=tuple(jax.ShapeDtypeStruct(shape, F32) for shape in shapes),
-        in_specs=[VMEM] * 5,
+        in_specs=[VMEM] * 3,
         out_specs=(VMEM,) * len(shapes),
-        scratch_shapes=[pltpu.VMEM((4 * done.shape[1], D), BF16)],
-        compiler_params=pltpu.CompilerParams(vmem_limit_bytes=32 << 20),
+        compiler_params=pltpu.CompilerParams(vmem_limit_bytes=ROOM),
         name="unpack_grads",
-    )(done, rest_a, rest_b, grads, vecs)
+    )(full, grads, vecs)
 
 
 def head_shards(
@@ -1784,34 +1834,24 @@
         return lax.ppermute(values, "ctx", [(c, c ^ stride) for c in range(n_ctx)])
 
     vectors = [
-        vector[None]
-        for vector in (
-            query_bias,
-            value_bias,
-            output_bias,
-            attend_gain,
-            attend_shift,
-            shrink_bias,
-            middle_gain,
-            middle_shift,
-            final_gain,
-            final_shift,
-        )
+        query_bias,
+        value_bias,
+        output_bias,
+        attend_gain,
+        attend_shift,
+        shrink_bias,
+        middle_gain,
+        middle_shift,
+        final_gain,
+        final_shift,
+        expand_bias,
     ]
     q, kv, w_other, order, seqs, vec, expand_add = project_and_scatter(
-        n_ctx,
-        x,
-        query_weight,
-        key_weight,
-        value_weight,
-        block_order,
-        block_sequence,
-        expand_bias[None],
-        vectors,
+        n_ctx, x, query_weight, key_weight, value_weight, block_order, block_sequence, vectors
     )
     o, keep, lse, pairs = attend(order, seqs, q, kv)
     o_rows = return_rows(n_ctx, o)
-    layer_output, sum_tan, entry, tan_rows, own_feed, send_feed, vec_feed = dense(
+    layer_output, sum_tan, entry, tan_rows, vec_feed, *operands = dense(
         x,
         summed,
         tangent,
@@ -1822,15 +1862,24 @@
         expand_add,
         vec,
     )
-    tan, stage_a, stage_b, kept = scatter_rows(n_ctx, tan_rows, own_feed, send_feed)
+    tan, stage_a, stage_b, kept = scatter_rows(n_ctx, tan_rows, operands)
     land_a, land_b = across(stage_a, 1), across(stage_b, 2)
     dq, dkv = attend_back(pairs, q, tan, keep, lse, kv)
-    dq_rows, dkv_rows, done = return_grads(n_ctx, dq, dkv, kept, land_a, land_b)
-    rest_a, rest_b = across(done[0], 1), across(done[1], 2)
-    post_tangent, own_last, send_last, vec_last = last_dense(
-        x, entry, dq_rows, dkv_rows, query_weight, key_weight, value_weight, w_other
-    )
-    grads, vecs = reduce_grads(own_last, send_last, vec_feed, vec_last)
+    post_tangent, feed_sums, last_sums, vecs = finish(
+        n_ctx,
+        dq,
+        dkv,
+        kept,
+        land_a,
+        land_b,
+        x,
+        entry,
+        query_weight,
+        key_weight,
+        value_weight,
+        w_other,
+        vec_feed,
+    )
     (
         query_slope,
         key_slope,
@@ -1849,7 +1898,7 @@
         final_stretch,
         final_nudge,
         expand_drift,
-    ) = unpack_grads(shrink_weight.shape[0], done, rest_a, rest_b, grads, vecs)
+    ) = unpack_grads(shrink_weight.shape[0], feed_sums, last_sums, vecs)
     return (
         layer_output[None],
         post_tangent[None],

time: 297 us -> 255 us (0.86)
  Pallas kernels: 264 us -> 245 us
  local copies, waits for them, and re-layouts: 22 us -> 3.38 us
  starting transfers between devices: 9.07 us -> 5.59 us
    pallas_call x3 -> x1, Pallas kernels: 116 us -> 97.2 us  [finish(): pl.pallas_call(functools.partial(finish_kernel, n_ctx), out_shape=(jax.Sh...]
    unnamed x44 -> x13, local copies, waits for them, and re-layouts: 14.7 us -> 3.38 us
    pallas_call x1, Pallas kernels: 30.7 us -> 21.3 us  [attend_back(): pl.pallas_call(functools.partial(backward_kernel, blocks), out_shape=(jax...]
    broadcast_in_dim x11 -> x0, local copies, waits for them, and re-layouts: 7.26 us -> none  [the longest x10 6.58 us: head_shards(): vector[None]]
    pallas_call x1, Pallas kernels: 13 us -> 19.3 us  [scatter_rows(): pl.pallas_call(functools.partial(scatter_kernel, n_ctx), out_shape=(jax.S...]
    ppermute x4 -> x2, starting transfers between devices: 8.04 us -> 4.56 us  [across(): return lax.ppermute(values, 'ctx', [(c, c ^ stride) for c in range(n_ctx)])]
  transfers between devices with their start and end apart: 7 -> 5, of which waited for: 0 -> 0; matrix products, arithmetic and copies ran while one was open for 2% -> 0% of each run, Pallas kernels for 52% -> 40%
where the time goes in v3:
time: 255 us
  Pallas kernels  245 us (96%)
  starting transfers between devices  5.59 us (2%)
  local copies, waits for them, and re-layouts  3.38 us (1%)
    pallas_call x1, Pallas kernels, finish(): pl.pallas_call(functools.partial(finish_kernel, n_ctx), out_shape=(jax.Sh...  97.2 us
    pallas_call x1, Pallas kernels, return_rows(): pl.pallas_call(functools.partial(return_kernel, n_ctx), out_shape=jax.Sha...  31.6 us
    pallas_call x1, Pallas kernels, project_and_scatter(): pl.pallas_call(functools.partial(project_kernel, n_ctx), out_shape=(jax.S...  31.3 us
    pallas_call x1, Pallas kernels, dense(): pl.pallas_call(dense_kernel, out_shape=(jax.ShapeDtypeStruct((tokens, D),...  21.4 us
    pallas_call x1, Pallas kernels, attend_back(): pl.pallas_call(functools.partial(backward_kernel, blocks), out_shape=(jax...  21.3 us
    pallas_call x1, Pallas kernels, scatter_rows(): pl.pallas_call(functools.partial(scatter_kernel, n_ctx), out_shape=(jax.S...  19.3 us
    pallas_call x1, Pallas kernels, attend(): pl.pallas_call(functools.partial(forward_kernel, blocks), out_shape=(jax....  18.5 us
  transfers between devices with their start and end apart: 5, of which 0 were waited for; matrix products, arithmetic and copies ran while one was open for 0% of the time, Pallas kernels for 40%

profile of v3, /device:TPU:0, one launch (start us, length us, event | category | flops | bytes accessed | tf_op | source)
XLA Modules:
  0.0 255.1 jit_solution(15764016274934216615)
XLA Ops:
  0.7 0.5 collective-permute-start.1
  1.2 0.1 collective-permute-start.2
  1.3 0.4 collective-permute-start
  1.7 31.3 %project_scatter.1 = (bf16[16,128,128]{2,1,0:T(8,128)(2,1)}, bf16[32,256,128]{2,1,0:T(8,128)(2,1)}, bf16[3,512,256]{2,1,0:T(8,128)(2,1)}, s32[1,32]{1,0:T(1,128)...) custom-call(f32[512,512]{1,0:T(8,128)} %bitcast.17, bf16[512,256]{1,0:T(8,128)(2,1)} %wq_hbm.3, ...), custom_call_target="tpu_custom_call" | custom-call | tf_op jit(solution)/shard_map/project_scatter/pallas_call | solution.py:721
  33.0 18.5 %attend.1 = (bf16[16,128,128]{2,1,0:T(8,128)(2,1)}, f32[16,128,128]{2,1,0:T(8,128)}, f32[32,128,128]{2,1,0:T(8,128)}, s32[3,160]{1,0:T(4,128)}) custom-call(s32[1,32]{1,0:T(1,128)} %get-tuple-element.69.order_ref, s32[1,32]{1,0:T(1,128)} %get-tuple-element.70.seq_ref, bf16[16,128,128]{2,1,0:T(8,128)(2,1)} %get-tuple-element.71.q_ref, ...), custom_call_target="tpu_custom_call" | custom-call | tf_op jit(solution)/shard_map/attend/pallas_call | solution.py:891
  51.5 31.6 %return_rows.1.o_ref = bf16[8,2,128,128]{3,2,1,0:T(8,128)(2,1)} custom-call(bf16[16,128,128]{2,1,0:T(8,128)(2,1)} %get-tuple-element.73.rows_ref), custom_call_target="tpu_custom_call" | custom-call | tf_op jit(solution)/shard_map/return_rows/pallas_call | solution.py:1051
  83.0 0.0 collective-permute-done.wo_b
  83.0 0.0 copy-start.5
  83.0 0.0 collective-permute-done.1.we_b
  83.1 0.0 copy-start
  83.1 0.0 collective-permute-done.2.ws_b
  83.1 0.0 copy-start.1
  83.1 0.7 copy-done.5
  83.7 0.4 copy-done
  84.1 0.4 copy-done.1
  84.5 21.4 %dense.1 = (f32[512,512]{1,0:T(8,128)}, f32[512,512]{1,0:T(8,128)}, f32[512,512]{1,0:T(8,128)}, bf16[8,2,128,128]{3,2,1,0:T(8,128)(2,1)}, f32[16,512]{1,0:T(8,12...) custom-call(f32[512,512]{1,0:T(8,128)} %bitcast.18, ...), custom_call_target="tpu_custom_call" | custom-call | tf_op jit(solution)/shard_map/dense/pallas_call | solution.py:1417
  105.9 19.3 %scatter_rows.1 = (bf16[16,128,128]{2,1,0:T(8,128)(2,1)}, bf16[576,512]{1,0:T(8,128)(2,1)}, bf16[576,512]{1,0:T(8,128)(2,1)}, f32[2,576,512]{2,1,0:T(8,128)}) custom-call(bf16[8,2,128,128]{3,2,1,0:T(8,128)(2,1)} %get-tuple-element.78.rows_ref, bf16[2,512,256]{2,1,0:T(8,128)(2,1)} %get-tuple-element.79.mixed, bf16[512,512]{1,0:T(8,128)(2,1)} %get-tuple-element.80.low, ...), custom_call_target="tpu_custom_call" | custom-call | tf_op jit(solution)/shard_map/scatter_rows/pallas_call | solution.py:1169
  125.2 1.2 collective-permute-start.3
  126.4 3.3 %collective-permute-start.4 = (bf16[576,512]{1,0:T(8,128)(2,1)}, bf16[576,512]{1,0:T(8,128)(2,1)S(1)}, u32[]{:S(2)}, u32[]{:S(2)}) collective-permute-start(bf16[576,512]{1,0:T(8,128)(2,1)} %get-tuple-element.92), channel_id=1, source_target_pairs={{0,4},{2,6},{4,0},{6,2},{8,12},{10,14},{12,8},{14,10},{16,20},{18,... | collective-permute-start | bytes 1769480 | tf_op jit(solution)/shard_map/ppermute | solution.py:1834
  129.8 21.3 %attend_back.1 = (bf16[16,128,128]{2,1,0:T(8,128)(2,1)}, f32[32,256,128]{2,1,0:T(8,128)}) custom-call(s32[3,160]{1,0:T(4,128)} %get-tuple-element.77.pairs_ref, bf16[16,128,128]{2,1,0:T(8,128)(2,1)} %get-tuple-element.71.q_ref, bf16[16,128,128]{2,1,0:T(8,128)(2,1)} %get-tuple-element.85.tan_ref, f32[16,128,128]{2,1,0:T(8,128)} %get-tuple-element.86.keep_ref, ...), custom_call_target="tpu_custom_call" | custom-call | tf_op jit(solution)/shard_map/attend_back/pallas_call | solution.py:1003
  151.0 0.0 collective-permute-done.3.land_a
  151.0 0.0 copy-start.3
  151.0 0.0 collective-permute-done.4.land_b
  151.0 0.0 copy-start.4
  151.0 0.8 copy-done.3
  151.8 0.2 copy-done.4
  152.0 97.2 %finish.1 = (f32[512,512]{1,0:T(8,128)}, bf16[2304,512]{1,0:T(8,128)(2,1)}, bf16[768,512]{1,0:T(8,128)(2,1)}, f32[24,512]{1,0:T(8,128)}) custom-call(bf16[16,128,128]{2,1,0:T(8,128)(2,1)} %get-tuple-element.88.dq_ref, f32[32,256,128]{2,1,0:T(8,128)} %get-tuple-element.89.dkv_ref, f32[2,576,512]{2,1,0:T(8,128)} %get-tuple-element.90.keep_hbm, ...), custom_call_target="tpu_custom_call" | custom-call | tf_op jit(solution)/shard_map/finish/pallas_call | solution.py:1721
  249.2 0.0 copy-start.2
  249.2 4.9 %unpack_grads.1 = (f32[512,256]{1,0:T(8,128)}, f32[512,256]{1,0:T(8,128)}, f32[512,256]{1,0:T(8,128)}, f32[256,512]{1,0:T(8,128)}, f32[512,1024]{1,0:T(8,128)}, ...) custom-call(bf16[2304,512]{1,0:T(8,128)(2,1)} %get-tuple-element.98., ...), custom_call_target="tpu_custom_call" | custom-call | tf_op jit(solution)/shard_map/unpack_grads/pallas_call | solution.py:1792
  254.1 0.0 copy-done.2
  254.1 1.0 copy.43
Async XLA Ops:
  0.7 82.4 %collective-permute-start.1 = (bf16[512,1024]{1,0:T(8,128)(2,1)}, bf16[512,1024]{1,0:T(8,128)(2,1)S(1)}, u32[]{:S(2)}, u32[]{:S(2)}) collective-permute-start(bf16[512,1024]{1,0:T(8,128)(2,1)} %we_a.1), channel_id=1, source_target_pairs={{0,1},{1,0},{2,3},{3,2},{4,5},{5,4},{6,7},{7,6},{8,9},{9,8},{10,11... | collective-permute-start | bytes 3145736 | tf_op jit(solution)/shard_map/ppermute | solution.py:1831
  1.2 81.9 %collective-permute-start.2 = (bf16[1024,512]{1,0:T(8,128)(2,1)}, bf16[1024,512]{1,0:T(8,128)(2,1)S(1)}, u32[]{:S(2)}, u32[]{:S(2)}) collective-permute-start(bf16[1024,512]{1,0:T(8,128)(2,1)} %ws_a.1), channel_id=1, source_target_pairs={{0,1},{1,0},{2,3},{3,2},{4,5},{5,4},{6,7},{7,6},{8,9},{9,8},{10,11... | collective-permute-start | bytes 3145736 | tf_op jit(solution)/shard_map/ppermute | solution.py:1831
  1.3 81.8 %collective-permute-start = (bf16[256,512]{1,0:T(8,128)(2,1)}, bf16[256,512]{1,0:T(8,128)(2,1)S(1)}, u32[]{:S(2)}, u32[]{:S(2)}) collective-permute-start(bf16[256,512]{1,0:T(8,128)(2,1)} %wo_a.1), channel_id=1, source_target_pairs={{0,1},{1,0},{2,3},{3,2},{4,5},{5,4},{6,7},{7,6},{8,9},{9,8},{10,11... | collective-permute-start | bytes 786440 | tf_op jit(solution)/shard_map/ppermute | solution.py:1831
  83.0 0.7 copy-start.5
  83.1 1.1 copy-start
  83.1 1.4 copy-start.1
  125.2 25.8 %collective-permute-start.3 = (bf16[576,512]{1,0:T(8,128)(2,1)}, bf16[576,512]{1,0:T(8,128)(2,1)S(1)}, u32[]{:S(2)}, u32[]{:S(2)}) collective-permute-start(bf16[576,512]{1,0:T(8,128)(2,1)} %get-tuple-element.91), channel_id=1, source_target_pairs={{0,2},{2,0},{4,6},{6,4},{8,10},{10,8},{12,14},{14,12},{16,18},{18,... | collective-permute-start | bytes 1769480 | tf_op jit(solution)/shard_map/ppermute | solution.py:1834
  126.4 24.6 %collective-permute-start.4 = (bf16[576,512]{1,0:T(8,128)(2,1)}, bf16[576,512]{1,0:T(8,128)(2,1)S(1)}, u32[]{:S(2)}, u32[]{:S(2)}) collective-permute-start(bf16[576,512]{1,0:T(8,128)(2,1)} %get-tuple-element.92), channel_id=1, source_target_pairs={{0,4},{2,6},{4,0},{6,2},{8,12},{10,14},{12,8},{14,10},{16,20},{18,... | collective-permute-start | bytes 1769480 | tf_op jit(solution)/shard_map/ppermute | solution.py:1834
  151.0 0.8 copy-start.3
  151.0 1.0 copy-start.4
  249.2 4.9 %copy-start.2 = (f32[512,512]{1,0:T(8,128)S(1)}, f32[512,512]{1,0:T(8,128)}, u32[]{:S(2)}) copy-start(f32[512,512]{1,0:T(8,128)} %get-tuple-element.96) | copy-start | bytes 3145732

commit v4 on v3

--- a/solution.py
+++ b/solution.py
@@ -865,17 +865,16 @@
     def finish(step, _):
         for part in range(4):
             source = step * 4 + part
-            results = []
             for side in range(2):
                 slot = 2 * source + side
                 mass = jnp.broadcast_to(
                     jnp.sum(masses[slot], axis=1, keepdims=True), (HALF, 128)
                 )
-                results.append(total[slot] / mass)
+                result = total[slot] / mass
                 lse_ref[slot] = peaks[slot] + jnp.log(mass)
-            packed = high_pair(results[0], results[1])
-            keep_ref[source] = packed
-            o_ref[source] = packed.astype(BF16)
+                packed = high_pair(result[: HALF // 2], result[HALF // 2 :])
+                keep_ref[source, side] = packed
+                o_ref[source, side] = packed.astype(BF16)
         return 0
 
     lax.fori_loop(0, blocks // 8, finish, 0)
@@ -891,8 +890,8 @@
     return pl.pallas_call(
         functools.partial(forward_kernel, blocks),
         out_shape=(
-            jax.ShapeDtypeStruct((blocks // 2, HALF, 128), BF16),
-            jax.ShapeDtypeStruct((blocks // 2, HALF, 128), F32),
+            jax.ShapeDtypeStruct((blocks // 2, 2, HALF // 2, 128), BF16),
+            jax.ShapeDtypeStruct((blocks // 2, 2, HALF // 2, 128), F32),
             jax.ShapeDtypeStruct((blocks, HALF, 128), F32),
             jax.ShapeDtypeStruct((3, room), jnp.int32),
         ),
@@ -932,20 +931,27 @@
         for part in range(4):
             source = step * 4 + part
             packed = q_ref[source].astype(F32) * (HD**-0.5)
-            tangent = tan_ref[source].astype(F32)
             low = low_lanes(packed)
-            product = tangent * keep_ref[source]
             for side in range(2):
                 slot = 2 * source + side
                 q = packed if side == 0 else swap_lanes(packed)
-                tan = tangent if side == 1 else swap_lanes(tangent)
                 both[slot, 0:HALF] = jnp.where(low, q, 0.0).astype(BF16)
-                both[slot, HALF:BLK] = jnp.where(low, 0.0, tan).astype(BF16)
+                tangent = tan_ref[source, side].astype(F32)
+                first = low_lanes(tangent)
+                both[slot, HALF : HALF + HALF // 2] = jnp.where(
+                    first, 0.0, swap_lanes(tangent)
+                ).astype(BF16)
+                both[slot, HALF + HALF // 2 : BLK] = jnp.where(first, 0.0, tangent).astype(BF16)
                 turned[slot] = jnp.transpose(both[slot])
-                mine = jnp.where(low == (side == 0), product, 0.0)
-                deltas[slot] = jnp.broadcast_to(
-                    jnp.sum(mine, axis=1, keepdims=True), (HALF, 128)
+                product = tangent * keep_ref[source, side]
+                delta = jnp.concatenate(
+                    [
+                        jnp.sum(jnp.where(first, product, 0.0), axis=1, keepdims=True),
+                        jnp.sum(jnp.where(first, 0.0, product), axis=1, keepdims=True),
+                    ],
+                    axis=0,
                 )
+                deltas[slot] = jnp.broadcast_to(delta, (HALF, 128))
                 masses[slot] = lse_ref[slot]
         return 0
 
@@ -1021,49 +1027,6 @@
     )(pairs, q, tangent, keep, lse, kv)
 
 
-def return_kernel(n_ctx, rows_ref, out_ref, ss, rs):
-    at = Place()
-    at.greet_owners(n_ctx, False)
-
-    def move(target):
-        return (
-            rows_ref.at[target],
-            out_ref.at[at.head, at.f],
-            ss.at[target],
-            rs.at[at.head * 2 + at.f],
-            target,
-            at.group,
-        )
-
-    for target in range(n_ctx):
-        at.send(*move(target))
-    for head in range(H):
-        for core in range(2):
-            arrived = out_ref.at[head, core]
-            at.remote(
-                arrived, arrived, ss.at[0], rs.at[head * 2 + core], at.c, 1 - at.f
-            ).wait_recv()
-    for target in range(n_ctx):
-        at.wait_sent(*move(target))
-
-
-def return_rows(n_ctx, rows):
-    return pl.pallas_call(
-        functools.partial(return_kernel, n_ctx),
-        out_shape=jax.ShapeDtypeStruct((H, 2, HALF, 128), BF16),
-        in_specs=[ANY],
-        out_specs=ANY,
-        scratch_shapes=[
-            pltpu.SemaphoreType.DMA((n_ctx,)),
-            pltpu.SemaphoreType.DMA((2 * H,)),
-        ],
-        compiler_params=pltpu.CompilerParams(
-            collective_id=1, has_side_effects=True, vmem_limit_bytes=ROOM
-        ),
-        name="return_rows",
-    )(rows)
-
-
 def pieces_of(start, size, body):
     piece = max(n for n in range(16, 97, 16) if size % n == 0)
     lax.fori_loop(
@@ -1081,116 +1044,6 @@
 def step_of(c, stride):
     bit = (c // stride) % 2
     return bit, c + stride * (1 - 2 * bit)
-
-
-def feed_slopes(kind, target, mixed, low_turned, hidden, before_tan, feed_tan, branch_tan):
-    unit_count = hidden.shape[2] // COLS
-
-    def chunk_slopes(chunk, _):
-        columns = pl.ds(pl.multiple_of(chunk * COLS, COLS), COLS)
-        target[columns, :] = dot_tn(hidden[kind, :, columns], feed_tan[...]).astype(target.dtype)
-        below = pl.ds(pl.multiple_of((unit_count + chunk) * COLS, COLS), COLS)
-        target[below, :] = dot_nn(low_turned[...], before_tan[kind, :, columns]).astype(
-            target.dtype
-        )
-        return 0
-
-    lax.fori_loop(0, unit_count, chunk_slopes, 0)
-    start = 2 * unit_count * COLS
-    target[start : start + D // 2, :] = dot_tn(mixed[kind], branch_tan[...]).astype(target.dtype)
-
-
-def scatter_kernel(
-    n_ctx, rows_ref, mixed, low, hidden, before_tan, feed_tan, branch_tan,
-    out_ref, stage_a, stage_b, keep_ref, own_grads, send_grads, first_in, low_turned,
-    ss, rs, core_ss, core_rs,
-):
-    at = Place()
-    at.greet_sources(n_ctx, True)
-    quarter = first_in.shape[0] // 4
-    bits = (step_of(at.c, 1)[0], step_of(at.c, 2)[0])
-    stages = (stage_a, stage_b)
-
-    def moves():
-        for head in range(H):
-            for core in range(2):
-                yield (
-                    rows_ref.at[head, core],
-                    out_ref.at[at.c],
-                    ss.at[head * 2 + core],
-                    rs.at[at.c],
-                    at.f * H + head,
-                    core,
-                )
-
-    def core_move(region, give):
-        bit = bits[region]
-        start = region * 2 * quarter + (1 - bit if give else bit) * quarter
-        where = span(start, quarter)
-        slot = region + 2 * (0 if give else 1)
-        return start, at.remote(
-            send_grads.at[where], first_in.at[where], core_ss.at[slot], core_rs.at[slot],
-            at.c, 1 - at.f,
-        )
-
-    order = [(0, True), (1, True), (0, False), (1, False)]
-    for move in moves():
-        at.send(*move)
-    low_turned[...] = jnp.transpose(low[...])
-    operands = (mixed, low_turned, hidden, before_tan, feed_tan, branch_tan)
-    feed_slopes(1, send_grads, *operands)
-    for step in order:
-        core_move(*step)[1].start()
-    feed_slopes(0, own_grads, *operands)
-    for region, give in order:
-        start, move = core_move(region, give)
-        move.wait_recv()
-
-        def join(offset, where, size):
-            total = own_grads[where, :] + first_in[where, :].astype(F32)
-            if give:
-                stages[region][span(offset, size), :] = total.astype(BF16)
-            else:
-                keep_ref[region, span(offset, size), :] = total
-
-        pieces_of(start, quarter, join)
-    for source in range(n_ctx):
-        arrived = out_ref.at[source]
-        at.remote(arrived, arrived, ss.at[0], rs.at[source], at.c, 1 - at.f).wait_recv()
-    for move in moves():
-        at.wait_sent(*move)
-    for step in order:
-        core_move(*step)[1].wait_send()
-
-
-def scatter_rows(n_ctx, rows, operands):
-    mixed, low, hidden = operands[:3]
-    grad_rows = 2 * hidden.shape[2] + D // 2
-    return pl.pallas_call(
-        functools.partial(scatter_kernel, n_ctx),
-        out_shape=(
-            jax.ShapeDtypeStruct((n_ctx, HALF, 128), BF16),
-            jax.ShapeDtypeStruct((grad_rows // 4, D), BF16),
-            jax.ShapeDtypeStruct((grad_rows // 4, D), BF16),
-            jax.ShapeDtypeStruct((2, grad_rows // 4, D), F32),
-        ),
-        in_specs=[ANY] + [VMEM] * 6,
-        out_specs=(ANY, VMEM, VMEM, VMEM),
-        scratch_shapes=[
-            pltpu.VMEM((grad_rows, D), F32),
-            pltpu.VMEM((grad_rows, D), BF16),
-            pltpu.VMEM((grad_rows, D), BF16),
-            pltpu.VMEM((D, low.shape[0]), BF16),
-            pltpu.SemaphoreType.DMA((2 * H,)),
-            pltpu.SemaphoreType.DMA((n_ctx,)),
-            pltpu.SemaphoreType.DMA((4,)),
-            pltpu.SemaphoreType.DMA((4,)),
-        ],
-        compiler_params=pltpu.CompilerParams(
-            collective_id=2, has_side_effects=True, vmem_limit_bytes=ROOM
-        ),
-        name="scatter_rows",
-    )(rows, *operands)
 
 
 class Ladder:
@@ -1303,39 +1156,124 @@
     return jnp.sum(values, axis=0, keepdims=True)
 
 
-def dense_kernel(
-    x_ref, sum_ref, cot_ref, o_ref,
-    wo_a, wo_b, we_a, we_b, ws_a, ws_b, be_ref, vec_in,
-    out_ref, sum_tan_ref, entry_ref, tan_ref, vec_ref,
-    mixed, low, hidden, before_tan, feed_tan, branch_tan, slope, mixed_tan,
+def feed_slopes(kind, target, mixed, low_turned, hidden, before_tan, feed_tan, branch_tan):
+    unit_count = hidden.shape[2] // COLS
+
+    def chunk_slopes(chunk, _):
+        columns = pl.ds(pl.multiple_of(chunk * COLS, COLS), COLS)
+        target[columns, :] = dot_tn(hidden[kind, :, columns], feed_tan[...]).astype(target.dtype)
+        below = pl.ds(pl.multiple_of((unit_count + chunk) * COLS, COLS), COLS)
+        target[below, :] = dot_nn(low_turned[...], before_tan[kind, :, columns]).astype(
+            target.dtype
+        )
+        return 0
+
+    lax.fori_loop(0, unit_count, chunk_slopes, 0)
+    start = 2 * unit_count * COLS
+    target[start : start + D // 2, :] = dot_tn(mixed[kind], branch_tan[...]).astype(target.dtype)
+
+
+def middle_kernel(
+    n_ctx,
+    o_hbm, x_hbm, sum_hbm, cot_hbm, wo_a, wo_b, we_a, we_b, ws_a, ws_b, be_ref, vec_in,
+    out_hbm, sum_tan_hbm, entry_hbm, tan_out, vec_ref, stage_a, stage_b, keep_ref,
+    o_in, x_ref, sum_ref, cot_ref, wo, we, ws, out_ref, sum_tan_ref, entry_ref,
+    mixed, low, hidden, before_tan, feed_tan, branch_tan, slope, mixed_tan, tan_send,
+    own_grads, send_grads, first_in, low_turned,
+    load_sem, store_sem, o_ss, o_rs, tan_ss, tan_rs, core_ss, core_rs,
 ):
-    f = lax.axis_index("fsdp")
-    wo, we, ws = (wo_a, wo_b), (we_a, we_b), (ws_a, ws_b)
-    be = (be_ref.at[0:1], be_ref.at[1:2])
-    halves = (f, 1 - f)
+    at = Place()
+    f = at.f
+    other = 1 - f
+    halves = (f, other)
+    piece = HALF // 2
+    loads = [
+        pltpu.make_async_copy(src, dst, load_sem.at[i])
+        for i, (src, dst) in enumerate(
+            (
+                (x_hbm, x_ref),
+                (wo_a, wo.at[0]),
+                (wo_b, wo.at[1]),
+                (we_a, we.at[0]),
+                (we_b, we.at[1]),
+                (ws_a, ws.at[0]),
+                (ws_b, ws.at[1]),
+                (sum_hbm, sum_ref),
+                (cot_hbm, cot_ref),
+            )
+        )
+    ]
+    for load in loads:
+        load.start()
+    barrier = pltpu.get_barrier_semaphore()
+    for target in range(n_ctx):
+        at.signal(barrier, target, at.group)
+    at.greet_owners(n_ctx, True, 2 * H - at.inside)
+
+    def o_move(target, side):
+        return (
+            o_hbm.at[target, side],
+            o_in.at[side, at.head, f],
+            o_ss.at[2 * target + side],
+            o_rs.at[side * 2 * H + at.head * 2 + f],
+            target,
+            at.group,
+        )
+
+    def tan_move(side, head, core):
+        return (
+            tan_send.at[side, head, core],
+            tan_out.at[at.c, side],
+            tan_ss.at[side * 2 * H + head * 2 + core],
+            tan_rs.at[at.c * 2 + side],
+            f * H + head,
+            core,
+        )
+
+    for side in range(2):
+        for target in range(n_ctx):
+            at.send(*o_move(target, side))
+    vec_ref[...] = jnp.zeros_like(vec_ref)
     vectors = vec_in[...]
     (out_bias, gain_one, shift_one, shrink_bias, gain_two, shift_two, gain_last, shift_last) = (
         vectors[i : i + 1] for i in range(2, 10)
     )
-    for kind in range(2):
-        for pair in range(2):
-            head = halves[kind] * (H // 2) + 2 * pair
+    be = (be_ref.at[0:1], be_ref.at[1:2])
+    for load in loads:
+        load.wait()
+
+    def stores(step):
+        rows = pl.ds(pl.multiple_of(step * BLK, BLK), BLK)
+        return [
+            pltpu.make_async_copy(src.at[rows], dst.at[rows], store_sem.at[3 * step + i])
+            for i, (src, dst) in enumerate(
+                ((out_ref, out_hbm), (sum_tan_ref, sum_tan_hbm), (entry_ref, entry_hbm))
+            )
+        ]
+
+    def tile(step, _):
+        first_row = pl.multiple_of(step * BLK, BLK)
+        rows = pl.ds(first_row, BLK)
+        for head in range(H):
             for core in range(2):
-                early = o_ref[head, core].astype(F32)
-                late = o_ref[head + 1, core].astype(F32)
+                arrived = o_in.at[step, head, core]
+                at.remote(
+                    arrived, arrived, o_ss.at[0], o_rs.at[step * 2 * H + head * 2 + core],
+                    at.c, other,
+                ).wait_recv()
+        for kind in range(2):
+            for pair in range(2):
+                head = halves[kind] * (H // 2) + 2 * pair
                 columns = slice(pair * 128, pair * 128 + 128)
-                for side in range(2):
-                    start = side * BLK + core * HALF
-                    mixed[kind, start : start + HALF, columns] = side_pair(
-                        side, early, late
-                    ).astype(BF16)
-    vec_ref[...] = jnp.zeros_like(vec_ref)
-
-    def tile(step, _):
-        rows = pl.ds(pl.multiple_of(step * BLK, BLK), BLK)
-        branch = (
-            dot_nn(mixed[0, rows, :], wo[0][...]) + dot_nn(mixed[1, rows, :], wo[1][...]) + out_bias
-        )
+                for core in range(2):
+                    early = o_in[step, head, core].astype(F32)
+                    late = o_in[step, head + 1, core].astype(F32)
+                    for part in range(2):
+                        start = pl.multiple_of(first_row + core * HALF + part * piece, piece)
+                        mixed[kind, pl.ds(start, piece), columns] = side_pair(
+                            part, early, late
+                        ).astype(BF16)
+        branch = dot_nn(mixed[0, rows, :], wo[0]) + dot_nn(mixed[1, rows, :], wo[1]) + out_bias
         n_one, scale_one = normalize(x_ref[rows, :] + branch)
         normed_one = n_one * gain_one + shift_one
         stream_one = sum_ref[rows, :] + branch
@@ -1346,7 +1284,7 @@
 
             def expand(chunk, carried):
                 columns = pl.ds(pl.multiple_of(chunk * COLS, COLS), COLS)
-                v = dot_nn(normed_low, we[kind][:, columns]) + be[kind][:, columns]
+                v = dot_nn(normed_low, we[kind, :, columns]) + be[kind][:, columns]
                 square = v * v
                 t = jnp.tanh(gelu_coeff * (v + gelu_cubic * square * v))
                 half_up = 0.5 + 0.5 * t
@@ -1355,9 +1293,9 @@
                 slope[kind, :, columns] = half_up + v * half_up * (1.0 - t) * (
                     gelu_coeff + (3.0 * gelu_coeff * gelu_cubic) * square
                 )
-                return carried + dot_nn(hidden_part, ws[kind][columns, :])
-
-            feed = lax.fori_loop(0, ws[kind].shape[0] // COLS, expand, feed)
+                return carried + dot_nn(hidden_part, ws[kind, columns, :])
+
+            feed = lax.fori_loop(0, ws.shape[1] // COLS, expand, feed)
         feed_out = feed + shrink_bias
         n_two, scale_two = normalize(normed_one + feed_out)
         n_last, scale_last = normalize(stream_one + feed_out)
@@ -1379,14 +1317,14 @@
 
             def expand_back(chunk, carried):
                 columns = pl.ds(pl.multiple_of(chunk * COLS, COLS), COLS)
-                pushed = dot_nt(feed_low, ws[kind][columns, :])
+                pushed = dot_nt(feed_low, ws[kind, columns, :])
                 tan_part = (pushed * slope[kind, :, columns]).astype(BF16)
                 before_tan[kind, rows, columns] = tan_part
                 vec_row = pl.ds(8 + 2 * halves[kind] + chunk, 1)
                 vec_ref[vec_row, :] += column_sum(tan_part.astype(F32))
-                return carried + dot_nt(tan_part, we[kind][:, columns])
-
-            normed_tan = lax.fori_loop(0, ws[kind].shape[0] // COLS, expand_back, normed_tan)
+                return carried + dot_nt(tan_part, we[kind, :, columns])
+
+            normed_tan = lax.fori_loop(0, ws.shape[1] // COLS, expand_back, normed_tan)
         vec_ref[5:6, :] += column_sum(normed_tan * n_one)
         vec_ref[6:7, :] += column_sum(normed_tan)
         entry = norm_back(normed_tan, n_one, scale_one, gain_one)
@@ -1395,49 +1333,129 @@
         branch_tan[rows, :] = branch_low
         vec_ref[7:8, :] += column_sum(branch_low.astype(F32))
         for kind in range(2):
-            mixed_tan[kind, rows, :] = dot_nt(branch_low, wo[kind][...])
+            mixed_tan[kind] = dot_nt(branch_low, wo[kind])
+        for kind in range(2):
+            for pair in range(2):
+                columns = slice(pair * 128, pair * 128 + 128)
+                for side in range(2):
+                    head = halves[kind] * (H // 2) + 2 * pair + side
+                    for core in range(2):
+                        start = core * HALF
+                        early = mixed_tan[kind, start : start + piece, columns]
+                        late = mixed_tan[kind, start + piece : start + HALF, columns]
+                        tan_send[step, head, core] = side_pair(side, early, late).astype(BF16)
+                        at.send(*tan_move(step, head, core))
+        for store in stores(step):
+            store.start()
         return 0
 
     lax.fori_loop(0, 2, tile, 0)
 
-    for kind in range(2):
-        for pair in range(2):
-            columns = slice(pair * 128, pair * 128 + 128)
-            for side in range(2):
-                head = halves[kind] * (H // 2) + 2 * pair + side
-                for core in range(2):
-                    early = mixed_tan[kind, core * HALF : core * HALF + HALF, columns]
-                    late = mixed_tan[kind, BLK + core * HALF : BLK + core * HALF + HALF, columns]
-                    tan_ref[head, core] = side_pair(side, early, late).astype(BF16)
-
-
-def dense(x, summed, cotangent, o, wo, we, ws, be, vec):
-    tokens = x.shape[0]
-    units = ws[0].shape[0]
+    quarter = first_in.shape[0] // 4
+    bits = (step_of(at.c, 1)[0], step_of(at.c, 2)[0])
+    stages = (stage_a, stage_b)
+
+    def core_move(region, give):
+        bit = bits[region]
+        start = region * 2 * quarter + (1 - bit if give else bit) * quarter
+        where = span(start, quarter)
+        slot = region + 2 * (0 if give else 1)
+        return start, at.remote(
+            send_grads.at[where], first_in.at[where], core_ss.at[slot], core_rs.at[slot],
+            at.c, other,
+        )
+
+    order = [(0, True), (1, True), (0, False), (1, False)]
+    low_turned[...] = jnp.transpose(low[...])
+    operands = (mixed, low_turned, hidden, before_tan, feed_tan, branch_tan)
+    feed_slopes(1, send_grads, *operands)
+    for step in order:
+        core_move(*step)[1].start()
+    feed_slopes(0, own_grads, *operands)
+    for region, give in order:
+        start, move = core_move(region, give)
+        move.wait_recv()
+
+        def join(offset, where, size):
+            total = own_grads[where, :] + first_in[where, :].astype(F32)
+            if give:
+                stages[region][span(offset, size), :] = total.astype(BF16)
+            else:
+                keep_ref[region, span(offset, size), :] = total
+
+        pieces_of(start, quarter, join)
+    for source in range(n_ctx):
+        for side in range(2):
+            arrived = tan_out.at[source, side]
+            at.remote(
+                arrived, arrived, tan_ss.at[0], tan_rs.at[source * 2 + side], at.c, other
+            ).wait_recv()
+    for step in range(2):
+        for store in stores(step):
+            store.wait()
+    for side in range(2):
+        for target in range(n_ctx):
+            at.wait_sent(*o_move(target, side))
+        for head in range(H):
+            for core in range(2):
+                at.wait_sent(*tan_move(side, head, core))
+    for step in order:
+        core_move(*step)[1].wait_send()
+
+
+def middle(n_ctx, o, x, summed, cotangent, wo, we, ws, be, vec):
+    tokens, wide, units = x.shape[0], D // 2, ws[0].shape[0]
+    grad_rows = 2 * units + wide
+    rows = jax.ShapeDtypeStruct((tokens, D), F32)
+
+    def sems(*counts):
+        return [pltpu.SemaphoreType.DMA((count,)) for count in counts]
+
     return pl.pallas_call(
-        dense_kernel,
+        functools.partial(middle_kernel, n_ctx),
         out_shape=(
-            jax.ShapeDtypeStruct((tokens, D), F32),
-            jax.ShapeDtypeStruct((tokens, D), F32),
-            jax.ShapeDtypeStruct((tokens, D), F32),
-            jax.ShapeDtypeStruct((H, 2, HALF, 128), BF16),
+            rows,
+            rows,
+            rows,
+            jax.ShapeDtypeStruct((n_ctx, 2, HALF // 2, 128), BF16),
             jax.ShapeDtypeStruct((16, D), F32),
-            jax.ShapeDtypeStruct((2, tokens, D // 2), BF16),
-            jax.ShapeDtypeStruct((tokens, D), BF16),
-            jax.ShapeDtypeStruct((2, tokens, units), BF16),
-            jax.ShapeDtypeStruct((2, tokens, units), BF16),
-            jax.ShapeDtypeStruct((tokens, D), BF16),
-            jax.ShapeDtypeStruct((tokens, D), BF16),
+            jax.ShapeDtypeStruct((grad_rows // 4, D), BF16),
+            jax.ShapeDtypeStruct((grad_rows // 4, D), BF16),
+            jax.ShapeDtypeStruct((2, grad_rows // 4, D), F32),
         ),
-        in_specs=[VMEM] * 12,
-        out_specs=(VMEM,) * 11,
+        in_specs=[ANY] * 10 + [VMEM] * 2,
+        out_specs=(ANY,) * 4 + (VMEM,) * 4,
         scratch_shapes=[
+            pltpu.VMEM((2, H, 2, HALF // 2, 128), BF16),
+            pltpu.VMEM((tokens, D), F32),
+            pltpu.VMEM((tokens, D), F32),
+            pltpu.VMEM((tokens, D), F32),
+            pltpu.VMEM((2, wide, D), BF16),
+            pltpu.VMEM((2, D, units), BF16),
+            pltpu.VMEM((2, units, D), BF16),
+            pltpu.VMEM((tokens, D), F32),
+            pltpu.VMEM((tokens, D), F32),
+            pltpu.VMEM((tokens, D), F32),
+            pltpu.VMEM((2, tokens, wide), BF16),
+            pltpu.VMEM((tokens, D), BF16),
+            pltpu.VMEM((2, tokens, units), BF16),
+            pltpu.VMEM((2, tokens, units), BF16),
+            pltpu.VMEM((tokens, D), BF16),
+            pltpu.VMEM((tokens, D), BF16),
             pltpu.VMEM((2, BLK, units), F32),
-            pltpu.VMEM((2, tokens, D // 2), F32),
-        ],
-        compiler_params=pltpu.CompilerParams(vmem_limit_bytes=ROOM),
-        name="dense",
-    )(x, summed, cotangent, o, *wo, *we, *ws, be, vec)
+            pltpu.VMEM((2, BLK, wide), F32),
+            pltpu.VMEM((2, H, 2, HALF // 2, 128), BF16),
+            pltpu.VMEM((grad_rows, D), F32),
+            pltpu.VMEM((grad_rows, D), BF16),
+            pltpu.VMEM((grad_rows, D), BF16),
+            pltpu.VMEM((D, tokens), BF16),
+        ]
+        + sems(9, 6, 2 * n_ctx, 4 * H, 4 * H, 2 * n_ctx, 4, 4),
+        compiler_params=pltpu.CompilerParams(
+            collective_id=1, has_side_effects=True, vmem_limit_bytes=ROOM
+        ),
+        name="middle",
+    )(o, x, summed, cotangent, *wo, *we, *ws, be, vec)
 
 
 def finish_kernel(
@@ -1850,19 +1868,18 @@
         n_ctx, x, query_weight, key_weight, value_weight, block_order, block_sequence, vectors
     )
     o, keep, lse, pairs = attend(order, seqs, q, kv)
-    o_rows = return_rows(n_ctx, o)
-    layer_output, sum_tan, entry, tan_rows, vec_feed, *operands = dense(
+    layer_output, sum_tan, entry, tan, vec_feed, stage_a, stage_b, kept = middle(
+        n_ctx,
+        o,
         x,
         summed,
         tangent,
-        o_rows,
         (output_weight, from_other(output_weight)),
         (expand_weight, from_other(expand_weight)),
         (shrink_weight, from_other(shrink_weight)),
         expand_add,
         vec,
     )
-    tan, stage_a, stage_b, kept = scatter_rows(n_ctx, tan_rows, operands)
     land_a, land_b = across(stage_a, 1), across(stage_b, 2)
     dq, dkv = attend_back(pairs, q, tan, keep, lse, kv)
     post_tangent, feed_sums, last_sums, vecs = finish(

time: 255 us -> 240 us (0.941)
  Pallas kernels: 245 us -> 230 us
    pallas_call x3 -> x1, Pallas kernels: 72.3 us -> 55.8 us  [middle(): pl.pallas_call(functools.partial(middle_kernel, n_ctx), out_shape=(rows,...]
    unnamed x13 -> x19, local copies, waits for them, and re-layouts: 3.38 us -> 5.28 us
  transfers between devices with their start and end apart: 5 -> 5, of which waited for: 0 -> 0; matrix products, arithmetic and copies ran while one was open for 0% -> 0% of each run, Pallas kernels for 40% -> 30%
where the time goes in v4:
time: 240 us; the launch traced here: 239 us
  Pallas kernels  230 us (96%)
  local copies, waits for them, and re-layouts  5.28 us (2%)
  starting transfers between devices  3.48 us (1%)
    pallas_call x1, Pallas kernels, finish(): pl.pallas_call(functools.partial(finish_kernel, n_ctx), out_shape=(jax.Sh...  96.1 us
    pallas_call x1, Pallas kernels, middle(): pl.pallas_call(functools.partial(middle_kernel, n_ctx), out_shape=(rows,...  55.8 us
    pallas_call x1, Pallas kernels, project_and_scatter(): pl.pallas_call(functools.partial(project_kernel, n_ctx), out_shape=(jax.S...  31.3 us
    pallas_call x1, Pallas kernels, attend_back(): pl.pallas_call(functools.partial(backward_kernel, blocks), out_shape=(jax...  22.1 us
    pallas_call x1, Pallas kernels, attend(): pl.pallas_call(functools.partial(forward_kernel, blocks), out_shape=(jax....  19.4 us
    unnamed x19, local copies, waits for them, and re-layouts  5.28 us
    pallas_call x1, Pallas kernels, unpack_grads(): pl.pallas_call(unpack_kernel, out_shape=tuple((jax.ShapeDtypeStruct(shape...  4.94 us
  transfers between devices with their start and end apart: 5, of which 0 were waited for; matrix products, arithmetic and copies ran while one was open for 0% of the time, Pallas kernels for 30%

profile of v4, /device:TPU:0, one launch (start us, length us, event | category | flops | bytes accessed | tf_op | source)
XLA Modules:
  0.0 239.3 jit_solution(16594203740052776931)
XLA Ops:
  0.7 0.5 collective-permute-start.1
  1.2 0.1 collective-permute-start.2
  1.3 0.4 collective-permute-start
  1.7 31.3 %project_scatter.1 = (bf16[16,128,128]{2,1,0:T(8,128)(2,1)}, bf16[32,256,128]{2,1,0:T(8,128)(2,1)}, bf16[3,512,256]{2,1,0:T(8,128)(2,1)}, s32[1,32]{1,0:T(1,128)...) custom-call(f32[512,512]{1,0:T(8,128)} %bitcast.17, bf16[512,256]{1,0:T(8,128)(2,1)} %wq_hbm.3, ...), custom_call_target="tpu_custom_call" | custom-call | tf_op jit(solution)/shard_map/project_scatter/pallas_call | solution.py:721
  33.0 19.4 %attend.1 = (bf16[16,2,64,128]{3,2,1,0:T(8,128)(2,1)}, f32[16,2,64,128]{3,2,1,0:T(8,128)}, f32[32,128,128]{2,1,0:T(8,128)}, s32[3,160]{1,0:T(4,128)}) custom-call(s32[1,32]{1,0:T(1,128)} %get-tuple-element.62.order_ref, s32[1,32]{1,0:T(1,128)} %get-tuple-element.63.seq_ref, bf16[16,128,128]{2,1,0:T(8,128)(2,1)} %get-tuple-element.64.q_ref, ...), custom_call_target="tpu_custom_call" | custom-call | tf_op jit(solution)/shard_map/attend/pallas_call | solution.py:890
  52.5 0.0 collective-permute-done.wo_b
  52.5 0.0 copy-start.7
  52.5 0.0 collective-permute-done.1.we_b
  52.5 0.0 copy-start
  52.5 0.0 collective-permute-done.2.ws_b
  52.5 0.0 copy-start.1
  52.5 0.6 copy-done.7
  53.2 0.4 copy-done
  53.5 0.3 copy-done.1
  53.9 55.8 %middle.1 = (f32[512,512]{1,0:T(8,128)}, f32[512,512]{1,0:T(8,128)}, f32[512,512]{1,0:T(8,128)}, bf16[16,2,64,128]{3,2,1,0:T(8,128)(2,1)}, f32[16,512]{1,0:T(8,1...) custom-call(bf16[16,2,64,128]{3,2,1,0:T(8,128)(2,1)} %get-tuple-element.66.o_hbm, ...), custom_call_target="tpu_custom_call" | custom-call | tf_op jit(solution)/shard_map/middle/pallas_call | solution.py:1414
  109.7 1.0 collective-permute-start.3
  110.8 1.4 collective-permute-start.4
  112.2 22.1 %attend_back.1 = (bf16[16,128,128]{2,1,0:T(8,128)(2,1)}, f32[32,256,128]{2,1,0:T(8,128)}) custom-call(s32[3,160]{1,0:T(4,128)} %get-tuple-element.70.pairs_ref, bf16[16,128,128]{2,1,0:T(8,128)(2,1)} %get-tuple-element.64.q_ref, bf16[16,2,64,128]{3,2,1,0:T(8,128)(2,1)} %get-tuple-element.71.tan_ref, f32[16,2,64,128]{3,2,1,0:T(8,128)} %get-tuple-element.72.keep_ref, ...), custom_call_target="tpu_custom_call" | custom-call | tf_op jit(solution)/shard_map/attend_back/pallas_call | solution.py:1009
  134.3 0.0 collective-permute-done.3.land_a
  134.3 0.0 copy-start.5
  134.3 0.0 collective-permute-done.4.land_b
  134.3 0.0 copy-start.6
  134.3 0.8 copy-done.5
  135.1 0.2 copy-done.6
  135.3 96.1 %finish.1 = (f32[512,512]{1,0:T(8,128)}, bf16[2304,512]{1,0:T(8,128)(2,1)}, bf16[768,512]{1,0:T(8,128)(2,1)}, f32[24,512]{1,0:T(8,128)}) custom-call(bf16[16,128,128]{2,1,0:T(8,128)(2,1)} %get-tuple-element.74.dq_ref, f32[32,256,128]{2,1,0:T(8,128)} %get-tuple-element.75.dkv_ref, f32[2,576,512]{2,1,0:T(8,128)} %get-tuple-element.76.keep_hbm, ...), custom_call_target="tpu_custom_call" | custom-call | tf_op jit(solution)/shard_map/finish/pallas_call | solution.py:1739
  231.4 0.0 copy-start.3
  231.4 0.0 copy-start.4
  231.5 4.9 %unpack_grads.1 = (f32[512,256]{1,0:T(8,128)}, f32[512,256]{1,0:T(8,128)}, f32[512,256]{1,0:T(8,128)}, f32[256,512]{1,0:T(8,128)}, f32[512,1024]{1,0:T(8,128)}, ...) custom-call(bf16[2304,512]{1,0:T(8,128)(2,1)} %get-tuple-element.84., ...), custom_call_target="tpu_custom_call" | custom-call | tf_op jit(solution)/shard_map/unpack_grads/pallas_call | solution.py:1810
  236.4 0.0 copy-done.3
  236.4 0.0 copy-start.2
  236.4 1.0 copy.45
  237.4 0.0 copy-done.4
  237.4 1.0 copy.46
  238.4 0.0 copy-done.2
  238.4 1.0 copy.47
Async XLA Ops:
  0.7 51.8 %collective-permute-start.1 = (bf16[512,1024]{1,0:T(8,128)(2,1)}, bf16[512,1024]{1,0:T(8,128)(2,1)S(1)}, u32[]{:S(2)}, u32[]{:S(2)}) collective-permute-start(bf16[512,1024]{1,0:T(8,128)(2,1)} %we_a.1), channel_id=1, source_target_pairs={{0,1},{1,0},{2,3},{3,2},{4,5},{5,4},{6,7},{7,6},{8,9},{9,8},{10,11... | collective-permute-start | bytes 3145736 | tf_op jit(solution)/shard_map/ppermute | solution.py:1849
  1.2 51.3 %collective-permute-start.2 = (bf16[1024,512]{1,0:T(8,128)(2,1)}, bf16[1024,512]{1,0:T(8,128)(2,1)S(1)}, u32[]{:S(2)}, u32[]{:S(2)}) collective-permute-start(bf16[1024,512]{1,0:T(8,128)(2,1)} %ws_a.1), channel_id=1, source_target_pairs={{0,1},{1,0},{2,3},{3,2},{4,5},{5,4},{6,7},{7,6},{8,9},{9,8},{10,11... | collective-permute-start | bytes 3145736 | tf_op jit(solution)/shard_map/ppermute | solution.py:1849
  1.3 51.2 %collective-permute-start = (bf16[256,512]{1,0:T(8,128)(2,1)}, bf16[256,512]{1,0:T(8,128)(2,1)S(1)}, u32[]{:S(2)}, u32[]{:S(2)}) collective-permute-start(bf16[256,512]{1,0:T(8,128)(2,1)} %wo_a.1), channel_id=1, source_target_pairs={{0,1},{1,0},{2,3},{3,2},{4,5},{5,4},{6,7},{7,6},{8,9},{9,8},{10,11... | collective-permute-start | bytes 786440 | tf_op jit(solution)/shard_map/ppermute | solution.py:1849
  52.5 0.7 copy-start.7
  52.5 1.0 copy-start
  52.5 1.4 copy-start.1
  109.7 24.6 %collective-permute-start.3 = (bf16[576,512]{1,0:T(8,128)(2,1)}, bf16[576,512]{1,0:T(8,128)(2,1)S(1)}, u32[]{:S(2)}, u32[]{:S(2)}) collective-permute-start(bf16[576,512]{1,0:T(8,128)(2,1)} %get-tuple-element.77), channel_id=1, source_target_pairs={{0,2},{2,0},{4,6},{6,4},{8,10},{10,8},{12,14},{14,12},{16,18},{18,... | collective-permute-start | bytes 1769480 | tf_op jit(solution)/shard_map/ppermute | solution.py:1852
  110.8 23.5 %collective-permute-start.4 = (bf16[576,512]{1,0:T(8,128)(2,1)}, bf16[576,512]{1,0:T(8,128)(2,1)S(1)}, u32[]{:S(2)}, u32[]{:S(2)}) collective-permute-start(bf16[576,512]{1,0:T(8,128)(2,1)} %get-tuple-element.78), channel_id=1, source_target_pairs={{0,4},{2,6},{4,0},{6,2},{8,12},{10,14},{12,8},{14,10},{16,20},{18,... | collective-permute-start | bytes 1769480 | tf_op jit(solution)/shard_map/ppermute | solution.py:1852
  134.3 0.8 copy-start.5
  134.3 1.0 copy-start.6
  231.4 5.0 %copy-start.3 = (f32[512,512]{1,0:T(8,128)S(1)}, f32[512,512]{1,0:T(8,128)}, u32[]{:S(2)}) copy-start(f32[512,512]{1,0:T(8,128)} %get-tuple-element.69) | copy-start | bytes 3145732
  231.4 5.9 %copy-start.4 = (f32[512,512]{1,0:T(8,128)S(1)}, f32[512,512]{1,0:T(8,128)}, u32[]{:S(2)}) copy-start(f32[512,512]{1,0:T(8,128)} %get-tuple-element.82) | copy-start | bytes 3145732
  236.4 2.0 copy-start.2

commit v5 on v4

--- a/solution.py
+++ b/solution.py
@@ -14,7 +14,6 @@
 HALF = BLK // 2
 LONG = 8
 TOGETHER = 16
-BACK_TOGETHER = 16
 MOST = LONG + 1
 F32 = jnp.float32
 BF16 = jnp.bfloat16
@@ -785,19 +784,16 @@
     lax.fori_loop(0, blocks, place_block, 0)
 
     count = jnp.int32(0)
-    for gap in range(LONG):
-
-        def look(late, found):
-            pairs_ref[0, found] = place[late]
-            pairs_ref[1, found] = place[late - gap]
-            return found + jnp.where(seq_ref[0, late] == seq_ref[0, late - gap], 1, 0)
-
-        count = lax.fori_loop(gap, blocks, look, count)
+    for gap in range(1, LONG):
+        for late in range(gap, blocks):
+            pairs_ref[0, count] = place[late]
+            pairs_ref[1, count] = place[late - gap]
+            count = count + jnp.where(seq_ref[0, late] == seq_ref[0, late - gap], 1, 0)
     for spare in range(TOGETHER):
         pairs_ref[0, count + spare] = blocks
         pairs_ref[1, count + spare] = 0
     turns = (count + TOGETHER - 1) // TOGETHER
-    pairs_ref[2, 1] = (count + BACK_TOGETHER - 1) // BACK_TOGETHER
+    pairs_ref[2, 0] = turns
 
     def unpack(step, _):
         for part in range(4):
@@ -811,28 +807,42 @@
     lax.fori_loop(0, blocks // 8, unpack, 0)
     q_low[blocks] = jnp.zeros((HALF, 128), BF16)
 
-    def clear(slot, _):
-        peaks[slot] = jnp.full((HALF, 128), masked_value, F32)
-        masses[slot] = jnp.zeros((HALF, 128), F32)
-        total[slot] = jnp.zeros((HALF, 128), F32)
+    peaks[blocks] = jnp.zeros((HALF, 128), F32)
+    masses[blocks] = jnp.zeros((HALF, 128), F32)
+    total[blocks] = jnp.zeros((HALF, 128), F32)
+    lse_ref[blocks] = jnp.zeros((HALF, 128), F32)
+
+    def own_slots(step):
+        return [(step * TOGETHER + part,) * 2 for part in range(TOGETHER)]
+
+    def pair_slots(step):
+        return [
+            (pairs_ref[0, step * TOGETHER + part], pairs_ref[1, step * TOGETHER + part])
+            for part in range(TOGETHER)
+        ]
+
+    def score(slots, base):
+        results = []
+        for part, (q_slot, k_slot) in enumerate(slots):
+            result = dot_nt(q_low[q_slot], kv_ref[k_slot])
+            scores[base + part] = result
+            results.append(jnp.maximum(result[:, :128], result[:, 128:]))
+        return results
+
+    def score_own(step, _):
+        slots = own_slots(step)
+        for (q_slot, _), result in zip(slots, score(slots, step * TOGETHER)):
+            peaks[q_slot] = result
         return 0
 
-    lax.fori_loop(0, blocks + 1, clear, 0)
-
-    def score(step, _):
-        slots, results = [], []
-        for part in range(TOGETHER):
-            index = step * TOGETHER + part
-            q_slot = pairs_ref[0, index]
-            result = dot_nt(q_low[q_slot], kv_ref[pairs_ref[1, index]])
-            scores[index] = result
-            slots.append(q_slot)
-            results.append(jnp.maximum(result[:, :128], result[:, 128:]))
-        for q_slot, result in zip(slots, results):
+    def score_pairs(step, _):
+        slots = pair_slots(step)
+        for (q_slot, _), result in zip(slots, score(slots, blocks + step * TOGETHER)):
             peaks[q_slot] = jnp.maximum(peaks[q_slot], result)
         return 0
 
-    lax.fori_loop(0, turns, score, 0)
+    lax.fori_loop(0, blocks // TOGETHER, score_own, 0)
+    lax.fori_loop(0, turns, score_pairs, 0)
 
     def level(step, _):
         for part in range(4):
@@ -844,23 +854,32 @@
 
     lax.fori_loop(0, blocks // 4, level, 0)
 
-    def weigh(step, _):
-        slots, results = [], []
-        for part in range(TOGETHER):
-            index = step * TOGETHER + part
-            q_slot = pairs_ref[0, index]
+    def weigh(slots, base):
+        results = []
+        for part, (q_slot, k_slot) in enumerate(slots):
             peak = peaks[q_slot]
-            left = jnp.exp(scores[index, :, :128] - peak)
-            right = jnp.exp(scores[index, :, 128:] - peak)
+            left = jnp.exp(scores[base + part, :, :128] - peak)
+            right = jnp.exp(scores[base + part, :, 128:] - peak)
             weights = jnp.concatenate([left, right], axis=1).astype(BF16)
-            slots.append(q_slot)
-            results.append((left + right, dot_nn(weights, kv_ref[pairs_ref[1, index]])))
-        for q_slot, (mass, part_total) in zip(slots, results):
+            results.append((left + right, dot_nn(weights, kv_ref[k_slot])))
+        return results
+
+    def weigh_own(step, _):
+        slots = own_slots(step)
+        for (q_slot, _), (mass, result) in zip(slots, weigh(slots, step * TOGETHER)):
+            masses[q_slot] = mass
+            total[q_slot] = result
+        return 0
+
+    def weigh_pairs(step, _):
+        slots = pair_slots(step)
+        for (q_slot, _), (mass, result) in zip(slots, weigh(slots, blocks + step * TOGETHER)):
             masses[q_slot] = masses[q_slot] + mass
-            total[q_slot] = total[q_slot] + part_total
+            total[q_slot] = total[q_slot] + result
         return 0
 
-    lax.fori_loop(0, turns, weigh, 0)
+    lax.fori_loop(0, blocks // TOGETHER, weigh_own, 0)
+    lax.fori_loop(0, turns, weigh_pairs, 0)
 
     def finish(step, _):
         for part in range(4):
@@ -881,7 +900,7 @@
 
 
 def pair_room(blocks):
-    return blocks * MOST // 2 + TOGETHER
+    return blocks * MOST // 2 + 2 * TOGETHER
 
 
 def attend(order, seqs, q, kv):
@@ -892,7 +911,7 @@
         out_shape=(
             jax.ShapeDtypeStruct((blocks // 2, 2, HALF // 2, 128), BF16),
             jax.ShapeDtypeStruct((blocks // 2, 2, HALF // 2, 128), F32),
-            jax.ShapeDtypeStruct((blocks, HALF, 128), F32),
+            jax.ShapeDtypeStruct((blocks + 1, HALF, 128), F32),
             jax.ShapeDtypeStruct((3, room), jnp.int32),
         ),
         in_specs=[SMEM, SMEM, VMEM, VMEM],
@@ -918,15 +937,30 @@
     keep_ref,
     lse_ref,
     kv_ref,
+    pass_a,
+    pass_b,
     dq_ref,
-    dkv_ref,
+    dkv_sum,
+    out_a,
+    out_b,
     both,
     turned,
-    masses,
     deltas,
     dq_sum,
-    dkv_sum,
+    held,
+    pass_sem,
 ):
+    fetches = [
+        pltpu.make_async_copy(src, held.at[i], pass_sem.at[i])
+        for i, src in enumerate((pass_a, pass_b))
+    ]
+    passes = [
+        pltpu.make_async_copy(held.at[i], dst, pass_sem.at[2 + i])
+        for i, dst in enumerate((out_a, out_b))
+    ]
+    for fetch in fetches:
+        fetch.start()
+
     def unpack(step, _):
         for part in range(4):
             source = step * 4 + part
@@ -952,37 +986,36 @@
                     axis=0,
                 )
                 deltas[slot] = jnp.broadcast_to(delta, (HALF, 128))
-                masses[slot] = lse_ref[slot]
         return 0
 
     lax.fori_loop(0, blocks // 8, unpack, 0)
     both[blocks] = jnp.zeros((BLK, 128), BF16)
     turned[blocks] = jnp.zeros((128, BLK), BF16)
-    masses[blocks] = jnp.zeros((HALF, 128), F32)
     deltas[blocks] = jnp.zeros((HALF, 128), F32)
-
-    def clear(slot, _):
-        dq_sum[slot] = jnp.zeros((HALF, 128), F32)
-        dkv_sum[slot] = jnp.zeros((128, BLK), F32)
-        return 0
-
-    lax.fori_loop(0, blocks, clear, 0)
     dq_sum[blocks] = jnp.zeros((HALF, 128), F32)
 
     def one_pair(q_slot, k_slot):
         kv = kv_ref[k_slot]
         products = dot_nt(both[q_slot], kv)
-        mass, delta = masses[q_slot], deltas[q_slot]
+        mass, delta = lse_ref[q_slot], deltas[q_slot]
         weights = jnp.exp(products[:HALF] - jnp.concatenate([mass, mass], axis=1))
         score_tan = weights * (products[HALF:] - jnp.concatenate([delta, delta], axis=1))
         score_tan = score_tan.astype(BF16)
         sides = jnp.concatenate([score_tan, weights.astype(BF16)], axis=0)
         return dot_nn(turned[q_slot], sides), dot_nn(score_tan, kv)
 
+    def own_turn(step, _):
+        slots = [step * TOGETHER + part for part in range(TOGETHER)]
+        results = [one_pair(slot, slot) for slot in slots]
+        for slot, (dkv, dq) in zip(slots, results):
+            dkv_sum[slot] = dkv
+            dq_sum[slot] = dq
+        return 0
+
     def pair_turn(step, _):
         slots = [
-            (pairs_ref[0, step * BACK_TOGETHER + part], pairs_ref[1, step * BACK_TOGETHER + part])
-            for part in range(BACK_TOGETHER)
+            (pairs_ref[0, step * TOGETHER + part], pairs_ref[1, step * TOGETHER + part])
+            for part in range(TOGETHER)
         ]
         results = [one_pair(*slot) for slot in slots]
         for (q_slot, k_slot), (dkv, dq) in zip(slots, results):
@@ -990,41 +1023,47 @@
             dq_sum[q_slot] = dq_sum[q_slot] + dq
         return 0
 
-    lax.fori_loop(0, pairs_ref[2, 1], pair_turn, 0)
+    lax.fori_loop(0, blocks // TOGETHER, own_turn, 0)
+    for fetch, move in zip(fetches, passes):
+        fetch.wait()
+        move.start()
+    lax.fori_loop(0, pairs_ref[2, 0], pair_turn, 0)
 
     def finish_rows(step, _):
         for part in range(4):
             source = step * 4 + part
             packed = low_pair(dq_sum[2 * source], dq_sum[2 * source + 1]) * (HD**-0.5)
             dq_ref[source] = packed.astype(BF16)
-            for slot in (2 * source, 2 * source + 1):
-                dkv_ref[slot] = jnp.transpose(dkv_sum[slot])
         return 0
 
     lax.fori_loop(0, blocks // 8, finish_rows, 0)
-
-
-def attend_back(pairs, q, tangent, keep, lse, kv):
+    for move in passes:
+        move.wait()
+
+
+def attend_back(pairs, q, tangent, keep, lse, kv, passed):
     blocks = kv.shape[0]
     return pl.pallas_call(
         functools.partial(backward_kernel, blocks),
         out_shape=(
             jax.ShapeDtypeStruct((blocks // 2, HALF, 128), BF16),
-            jax.ShapeDtypeStruct((blocks, BLK, 128), F32),
+            jax.ShapeDtypeStruct((blocks, 128, BLK), F32),
+            jax.ShapeDtypeStruct(passed[0].shape, F32),
+            jax.ShapeDtypeStruct(passed[1].shape, F32),
         ),
-        in_specs=[SMEM, VMEM, VMEM, VMEM, VMEM, VMEM],
-        out_specs=(VMEM, VMEM),
+        in_specs=[SMEM, VMEM, VMEM, VMEM, VMEM, VMEM, ANY, ANY],
+        out_specs=(VMEM, VMEM, ANY, ANY),
         scratch_shapes=[
             pltpu.VMEM((blocks + 1, BLK, 128), BF16),
             pltpu.VMEM((blocks + 1, 128, BLK), BF16),
             pltpu.VMEM((blocks + 1, HALF, 128), F32),
             pltpu.VMEM((blocks + 1, HALF, 128), F32),
-            pltpu.VMEM((blocks + 1, HALF, 128), F32),
-            pltpu.VMEM((blocks, 128, BLK), F32),
+            pltpu.VMEM((2,) + passed[0].shape, F32),
+            pltpu.SemaphoreType.DMA((4,)),
         ],
         compiler_params=pltpu.CompilerParams(vmem_limit_bytes=ROOM),
         name="attend_back",
-    )(pairs, q, tangent, keep, lse, kv)
+    )(pairs, q, tangent, keep, lse, kv, *passed)
 
 
 def pieces_of(start, size, body):
@@ -1046,13 +1085,22 @@
     return bit, c + stride * (1 - 2 * bit)
 
 
+REGIONS = 4
+
+
+def columns_of(region):
+    wide = D // (REGIONS // 2)
+    return slice(region // 2 * wide, region // 2 * wide + wide)
+
+
 class Ladder:
     def __init__(self, at, plans, starts, size, acc, stage, landing, out, sems, bases=(0, 0)):
         self.bases = bases
         self.at, self.acc, self.stage, self.landing, self.out = at, acc, stage, landing, out
         self.down_ss, self.down_rs, self.up_ss, self.up_rs = sems
         self.ranges = []
-        for plan, start in zip(plans, starts):
+        for region in range(REGIONS):
+            plan, start = plans[region % 2], starts[region % 2]
             listed, rows = [], size
             for bit, peer in plan[:-1]:
                 rows = rows // 2
@@ -1068,9 +1116,10 @@
     def down(self, region, step, sent):
         kept, given, size, peer = self.ranges[region][step]
         where, slot = span(given if sent else kept, size), self.slot(region, step)
+        columns = columns_of(region)
         return self.at.remote(
-            self.stage[region].at[where],
-            self.landing[region][step].at[where],
+            self.stage[region % 2].at[where, columns],
+            self.landing[region % 2][step].at[where, columns],
             self.down_ss.at[slot],
             self.down_rs.at[slot],
             peer,
@@ -1079,11 +1128,12 @@
 
     def up(self, region, step, sent):
         kept, given, size, peer = self.ranges[region][step]
-        start = self.bases[region] + (kept if sent else given)
+        start = self.bases[region % 2] + (kept if sent else given)
+        columns = columns_of(region)
         where, slot = span(start, size), self.slot(region, step)
         return self.at.remote(
-            self.out[region].at[where],
-            self.out[region].at[where],
+            self.out.at[where, columns],
+            self.out.at[where, columns],
             self.up_ss.at[slot],
             self.up_rs.at[slot],
             peer,
@@ -1091,35 +1141,37 @@
         )
 
     def join(self, region, start, size, arrived, target):
+        columns, acc = columns_of(region), self.acc[region % 2]
+
         def body(offset, where, _):
-            total = self.acc[region][where, :]
-            if arrived is not None:
-                total = total + arrived[where, :].astype(F32)
-            target[where, :] = total.astype(target.dtype)
+            total = acc[where, columns] + arrived[where, columns].astype(F32)
+            target[where, columns] = total.astype(target.dtype)
 
         pieces_of(start, size, body)
 
     def give(self, region, step, arrived):
         kept, given, size, _ = self.ranges[region][step]
-        self.join(region, given, size, arrived, self.stage[region])
+        self.join(region, given, size, arrived, self.stage[region % 2])
         self.down(region, step, True).start()
         if step < self.last:
-            self.join(region, kept, size, arrived, self.acc[region])
+            self.join(region, kept, size, arrived, self.acc[region % 2])
 
     def settle(self, region):
         kept, _, size, _ = self.ranges[region][self.last]
-        arrived = self.landing[region][self.last]
+        arrived = self.landing[region % 2][self.last]
+        columns, stage = columns_of(region), self.stage[region % 2]
 
         def body(offset, where, rows):
-            total = self.stage[region][where, :].astype(F32) + arrived[where, :].astype(F32)
-            self.out[region][span(self.bases[region] + kept + offset, rows), :] = total.astype(BF16)
+            total = stage[where, columns].astype(F32) + arrived[where, columns].astype(F32)
+            row = span(self.bases[region % 2] + kept + offset, rows)
+            self.out[row, columns] = total.astype(BF16)
 
         self.down(region, self.last, False).wait_recv()
         pieces_of(kept, size, body)
         self.up(region, self.last - 1, True).start()
 
     def wait_sent(self):
-        for region in range(2):
+        for region in range(REGIONS):
             for step in range(self.last + 1):
                 self.down(region, step, True).wait_send()
             for step in range(self.last):
@@ -1549,43 +1601,47 @@
         [keep.at[region] for region in range(2)],
         [stage.at[region] for region in range(2)],
         [[landing.at[region, step] for step in range(3)] for region in range(2)],
-        [feed_ref, feed_ref],
+        feed_ref,
         (down_ss, down_rs, up_ss, up_rs),
         bases,
     )
 
     def top_move(region, sent):
-        kept = bases[region]
-        given = 2 * size * region + (1 - firsts[region][0]) * size
-        where = span(kept if sent else given, size)
+        side, columns = region % 2, columns_of(region)
+        given = 2 * size * side + (1 - firsts[side][0]) * size
+        where = span(bases[side] if sent else given, size)
         return at.remote(
-            feed_ref.at[where],
-            feed_ref.at[where],
+            feed_ref.at[where, columns],
+            feed_ref.at[where, columns],
             top_ss.at[region],
             top_rs.at[region],
-            firsts[region][1],
+            firsts[side][1],
             f,
         )
 
     loads[0].wait()
-    for region, first in enumerate((land_a, land_b)):
+    kept_acc = [keep.at[region] for region in range(2)]
+    sums = [acc.at[region] for region in range(2)]
+    for region in range(REGIONS):
+        first = (land_a, land_b)[region % 2]
         kept, given, half, _ = feed.ranges[region][0]
-        feed.join(region, given, half, first, stage.at[region])
+        feed.acc = kept_acc
+        feed.join(region, given, half, first, stage.at[region % 2])
         feed.down(region, 0, True).start()
-        feed.join(region, kept, half, first, acc.at[region])
-        feed.acc[region] = acc.at[region]
+        feed.join(region, kept, half, first, sums[region % 2])
+    feed.acc = sums
     for source in range(n_ctx):
         own_move(source).wait()
         partial_move(source).wait_recv()
-        ready[source] = (own[source] + part[source]).astype(BF16)
+        ready[source] = jnp.transpose(own[source] + part[source]).astype(BF16)
         at.send(*kv_move(source))
     for load in loads[1:]:
         load.wait()
     low_turned[...] = jnp.transpose(x_in[...]).astype(BF16)
     for step in (1, 2):
-        for region in range(2):
+        for region in range(REGIONS):
             feed.down(region, step - 1, False).wait_recv()
-            feed.give(region, step, feed.landing[region][step - 1])
+            feed.give(region, step, feed.landing[region % 2][step - 1])
 
     for head in range(H):
         for core in range(2):
@@ -1608,19 +1664,24 @@
         [acc_last, acc_last],
         [stage_last, stage_last],
         [[landing_last.at[step] for step in range(4)]] * 2,
-        [grads_ref, grads_ref],
+        grads_ref,
         (down_ss2, down_rs2, up_ss2, up_rs2),
     )
 
     def core_move(region, give):
         kept, given, rows, _ = last.ranges[region][0]
         where = span(given if give else kept, rows)
-        slot = region + 2 * (0 if give else 1)
+        slot, columns = region + REGIONS * (0 if give else 1), columns_of(region)
         return at.remote(
-            send_grads.at[where], first_in.at[where], core_ss.at[slot], core_rs.at[slot], c, other
-        )
-
-    order = [(0, True), (1, True), (0, False), (1, False)]
+            send_grads.at[where, columns],
+            first_in.at[where, columns],
+            core_ss.at[slot],
+            core_rs.at[slot],
+            c,
+            other,
+        )
+
+    order = [(region, give) for give in (True, False) for region in range(REGIONS)]
     vec_peers = [(c, other)] + [(peer, f) for _, peer in (x_step, y_step, near, far)]
 
     def vec_move(step):
@@ -1666,18 +1727,19 @@
             for step in order:
                 core_move(*step).start()
     vec_move(0).start()
-    for region in range(2):
+    for region in range(REGIONS):
         feed.settle(region)
     for region, give in order:
         core_move(region, give).wait_recv()
         kept, given, rows, _ = last.ranges[region][0]
+        columns = columns_of(region)
 
         def join(offset, where, _):
-            total = own_grads[where, :] + first_in[where, :].astype(F32)
+            total = own_grads[where, columns] + first_in[where, columns].astype(F32)
             if give:
-                stage_last[where, :] = total.astype(BF16)
+                stage_last[where, columns] = total.astype(BF16)
             else:
-                acc_last[where, :] = total
+                acc_last[where, columns] = total
 
         pieces_of(given if give else kept, rows, join)
         if give:
@@ -1688,30 +1750,30 @@
         total = total + dot_nt(tangents[0, which], w_in[which])
         total = total + dot_nt(tangents[1, which], w_far[which])
     post_ref[...] = total
-    for region in range(2):
+    for region in range(REGIONS):
         feed.up(region, 1, False).wait_recv()
         feed.up(region, 0, True).start()
     for step in (1, 2):
-        for region in range(2):
+        for region in range(REGIONS):
             last.down(region, step - 1, False).wait_recv()
-            last.give(region, step, last.landing[region][step - 1])
+            last.give(region, step, last.landing[region % 2][step - 1])
         vec_next(step)
-    for region in range(2):
+    for region in range(REGIONS):
         feed.up(region, 0, False).wait_recv()
         top_move(region, True).start()
-    for region in range(2):
+    for region in range(REGIONS):
         last.down(region, 2, False).wait_recv()
-        last.give(region, 3, last.landing[region][2])
+        last.give(region, 3, last.landing[region % 2][2])
     vec_next(3)
-    for region in range(2):
+    for region in range(REGIONS):
         last.settle(region)
     vec_next(4)
     for step in (2, 1, 0):
-        for region in range(2):
+        for region in range(REGIONS):
             last.up(region, step, False).wait_recv()
             if step > 0:
                 last.up(region, step - 1, True).start()
-    for region in range(2):
+    for region in range(REGIONS):
         top_move(region, False).wait_recv()
 
     for target in range(n_ctx):
@@ -1722,7 +1784,7 @@
         core_move(*step).wait_send()
     for step in range(5):
         vec_move(step).wait_send()
-    for region in range(2):
+    for region in range(REGIONS):
         top_move(region, True).wait_send()
     feed.wait_sent()
     last.wait_sent()
@@ -1747,8 +1809,8 @@
         in_specs=[ANY, ANY, ANY, VMEM, VMEM] + [ANY] * 6 + [VMEM],
         out_specs=(VMEM,) * 4,
         scratch_shapes=[
-            pltpu.VMEM((n_ctx, BLK, 128), F32),
-            pltpu.VMEM((n_ctx, BLK, 128), F32),
+            pltpu.VMEM((n_ctx, 128, BLK), F32),
+            pltpu.VMEM((n_ctx, 128, BLK), F32),
             pltpu.VMEM((n_ctx, BLK, 128), BF16),
             pltpu.VMEM((H, 2, HALF, 128), BF16),
             pltpu.VMEM((H, 2 * BLK, 128), BF16),
@@ -1772,7 +1834,7 @@
             pltpu.VMEM((5,) + vec_shape, F32),
         ]
         + sems(7, n_ctx, 2 * H, n_ctx, 2 * H, n_ctx, n_ctx, n_ctx)
-        + sems(6, 6, 6, 6, 2, 2, 4, 4, 8, 8, 8, 8, 5, 5),
+        + sems(12, 12, 12, 12, 4, 4, 8, 8, 16, 16, 16, 16, 5, 5),
         compiler_params=pltpu.CompilerParams(
             collective_id=3, has_side_effects=True, vmem_limit_bytes=ROOM
         ),
@@ -1781,20 +1843,72 @@
 
 
 def unpack_kernel(
-    full, grads_ref, vec_ref,
-    query_ref, key_ref, value_ref, output_ref, expand_ref, shrink_ref, *vector_outs,
+    full_hbm, grads_hbm, post_hbm, vec_ref,
+    query_hbm, key_hbm, value_hbm, output_hbm, expand_hbm, shrink_hbm, post_out, *rest,
 ):
+    vector_outs, (low_full, low_last, full, last, held, load_sem, store_sem, post_sem) = (
+        rest[:11],
+        rest[11:],
+    )
     f = lax.axis_index("fsdp")
-    units, wide = shrink_ref.shape[0], D // 2
-    shrink_ref[...] = full[0:units].astype(F32)
+    units, wide = shrink_hbm.shape[0], D // 2
+    post_in = pltpu.make_async_copy(post_hbm, held, post_sem.at[0])
+    post = pltpu.make_async_copy(held, post_out, post_sem.at[1])
+    post_in.start()
+    parts = [
+        (low_last, last, 0, D, [(query_hbm, slice(0, wide)), (key_hbm, slice(wide, D))]),
+        (
+            low_last,
+            last,
+            D,
+            wide,
+            [
+                (value_hbm.at[0:wide], slice(0, wide)),
+                (value_hbm.at[wide:D], slice(wide, D)),
+            ],
+        ),
+    ]
     for part in range(units // D):
-        start = units + part * D
-        expand_ref[:, part * D : part * D + D] = full[start : start + D].astype(F32)
-    output_ref[...] = full[2 * units : 2 * units + wide].astype(F32)
-    query_ref[...] = grads_ref[0:D, 0:wide].astype(F32)
-    key_ref[...] = grads_ref[0:D, wide:D].astype(F32)
-    value_ref[0:wide] = grads_ref[D : D + wide, 0:wide].astype(F32)
-    value_ref[wide:D] = grads_ref[D : D + wide, wide:D].astype(F32)
+        parts.append(
+            (
+                low_full,
+                full,
+                part * D,
+                D,
+                [(shrink_hbm.at[part * D : part * D + D], slice(0, D))],
+            )
+        )
+    for part in range(units // D):
+        parts.append(
+            (
+                low_full,
+                full,
+                units + part * D,
+                D,
+                [(expand_hbm.at[:, part * D : part * D + D], slice(0, D))],
+            )
+        )
+    parts.append((low_full, full, 2 * units, wide, [(output_hbm, slice(0, D))]))
+    loads = []
+    for i, (low, _, start, rows, _) in enumerate(parts):
+        src = grads_hbm if low is low_last else full_hbm
+        where = pl.ds(start, rows)
+        loads.append(pltpu.make_async_copy(src.at[where], low.at[where], load_sem.at[i]))
+        loads[-1].start()
+    post_in.wait()
+    post.start()
+    stores = []
+    for load, (low, wide_rows, start, rows, targets) in zip(loads, parts):
+        load.wait()
+        where = pl.ds(start, rows)
+        wide_rows[where, :] = low[where, :].astype(F32)
+        for target, columns in targets:
+            stores.append(
+                pltpu.make_async_copy(
+                    wide_rows.at[where, columns], target, store_sem.at[len(stores)]
+                )
+            )
+            stores[-1].start()
     vectors = vec_ref[...]
     mine = jnp.where(f == 0, vectors[:, 0:wide], vectors[:, wide:D])
     for row, ref in zip((16, 17, 7, 5, 6, 0, 1, 2, 3, 4), vector_outs):
@@ -1802,19 +1916,34 @@
     drift = jnp.where(f == 0, vectors[8:10], vectors[10:12])
     for part in range(units // D):
         vector_outs[10][:, part * D : part * D + D] = drift[part : part + 1]
-
-
-def unpack_grads(units, full, grads, vecs):
+    for store in stores:
+        store.wait()
+    post.wait()
+
+
+def unpack_grads(units, full, grads, post, vecs):
     wide = D // 2
-    shapes = [(D, wide)] * 3 + [(wide, D), (D, units), (units, D)] + [(1, wide)] * 10 + [(1, units)]
+    shapes = [(D, wide)] * 3 + [(wide, D), (D, units), (units, D), post.shape]
+    vectors = [(1, wide)] * 10 + [(1, units)]
+    part_count = 3 + 2 * (units // D)
     return pl.pallas_call(
         unpack_kernel,
-        out_shape=tuple(jax.ShapeDtypeStruct(shape, F32) for shape in shapes),
-        in_specs=[VMEM] * 3,
-        out_specs=(VMEM,) * len(shapes),
+        out_shape=tuple(jax.ShapeDtypeStruct(shape, F32) for shape in shapes + vectors),
+        in_specs=[ANY] * 3 + [VMEM],
+        out_specs=(ANY,) * len(shapes) + (VMEM,) * len(vectors),
+        scratch_shapes=[
+            pltpu.VMEM(full.shape, BF16),
+            pltpu.VMEM(grads.shape, BF16),
+            pltpu.VMEM(full.shape, F32),
+            pltpu.VMEM(grads.shape, F32),
+            pltpu.VMEM(post.shape, F32),
+            pltpu.SemaphoreType.DMA((part_count,)),
+            pltpu.SemaphoreType.DMA((part_count + 2,)),
+            pltpu.SemaphoreType.DMA((2,)),
+        ],
         compiler_params=pltpu.CompilerParams(vmem_limit_bytes=ROOM),
         name="unpack_grads",
-    )(full, grads, vecs)
+    )(full, grads, post, vecs)
 
 
 def head_shards(
@@ -1881,7 +2010,9 @@
         vec,
     )
     land_a, land_b = across(stage_a, 1), across(stage_b, 2)
-    dq, dkv = attend_back(pairs, q, tan, keep, lse, kv)
+    dq, dkv, layer_output, sum_tan = attend_back(
+        pairs, q, tan, keep, lse, kv, (layer_output, sum_tan)
+    )
     post_tangent, feed_sums, last_sums, vecs = finish(
         n_ctx,
         dq,
@@ -1904,6 +2035,7 @@
         output_slope,
         expand_slope,
         shrink_slope,
+        post_tangent,
         query_drift,
         value_drift,
         output_drift,
@@ -1915,7 +2047,7 @@
         final_stretch,
         final_nudge,
         expand_drift,
-    ) = unpack_grads(shrink_weight.shape[0], feed_sums, last_sums, vecs)
+    ) = unpack_grads(shrink_weight.shape[0], feed_sums, last_sums, post_tangent, vecs)
     return (
         layer_output[None],
         post_tangent[None],

time: 240 us -> 234 us (0.975)
  Pallas kernels: 230 us -> 227 us
  local copies, waits for them, and re-layouts: 5.28 us -> 2.34 us
    unnamed x19 -> x10, local copies, waits for them, and re-layouts: 5.28 us -> 2.34 us
where the time goes in v5:
time: 234 us; the launch traced here: 233 us
  Pallas kernels  227 us (97%)
  starting transfers between devices  3.49 us (1%)
  local copies, waits for them, and re-layouts  2.34 us (1%)
    pallas_call x1, Pallas kernels, finish(): pl.pallas_call(functools.partial(finish_kernel, n_ctx), out_shape=(jax.Sh...  94.7 us
    pallas_call x1, Pallas kernels, middle(): pl.pallas_call(functools.partial(middle_kernel, n_ctx), out_shape=(rows,...  55.9 us
    pallas_call x1, Pallas kernels, project_and_scatter(): pl.pallas_call(functools.partial(project_kernel, n_ctx), out_shape=(jax.S...  31.3 us
    pallas_call x1, Pallas kernels, attend_back(): pl.pallas_call(functools.partial(backward_kernel, blocks), out_shape=(jax...  20.5 us
    pallas_call x1, Pallas kernels, attend(): pl.pallas_call(functools.partial(forward_kernel, blocks), out_shape=(jax....  17.6 us
    pallas_call x1, Pallas kernels, unpack_grads(): pl.pallas_call(unpack_kernel, out_shape=tuple((jax.ShapeDtypeStruct(shape...  6.76 us
  transfers between devices with their start and end apart: 5, of which 0 were waited for; matrix products, arithmetic and copies ran while one was open for 0% of the time, Pallas kernels for 30%

profile of v5, /device:TPU:0, one launch (start us, length us, event | category | flops | bytes accessed | tf_op | source)
XLA Modules:
  0.0 233.5 jit_solution(11619007237428240135)
XLA Ops:
  0.7 0.5 collective-permute-start.1
  1.2 0.1 collective-permute-start.2
  1.3 0.4 collective-permute-start
  1.7 31.3 %project_scatter.1 = (bf16[16,128,128]{2,1,0:T(8,128)(2,1)}, bf16[32,256,128]{2,1,0:T(8,128)(2,1)}, bf16[3,512,256]{2,1,0:T(8,128)(2,1)}, s32[1,32]{1,0:T(1,128)...) custom-call(f32[512,512]{1,0:T(8,128)} %bitcast.17, bf16[512,256]{1,0:T(8,128)(2,1)} %wq_hbm.3, ...), custom_call_target="tpu_custom_call" | custom-call | tf_op jit(solution)/shard_map/project_scatter/pallas_call | solution.py:720
  33.0 17.6 %attend.1 = (bf16[16,2,64,128]{3,2,1,0:T(8,128)(2,1)}, f32[16,2,64,128]{3,2,1,0:T(8,128)}, f32[33,128,128]{2,1,0:T(8,128)}, s32[3,176]{1,0:T(4,128)}) custom-call(s32[1,32]{1,0:T(1,128)} %get-tuple-element.65.order_ref, s32[1,32]{1,0:T(1,128)} %get-tuple-element.66.seq_ref, bf16[16,128,128]{2,1,0:T(8,128)(2,1)} %get-tuple-element.67.q_ref, ...), custom_call_target="tpu_custom_call" | custom-call | tf_op jit(solution)/shard_map/attend/pallas_call | solution.py:909
  50.6 0.0 collective-permute-done.wo_b
  50.6 0.0 copy-start.4
  50.6 0.0 collective-permute-done.1.we_b
  50.6 0.0 copy-start
  50.6 0.0 collective-permute-done.2.ws_b
  50.6 0.0 copy-start.1
  50.6 0.6 copy-done.4
  51.3 0.4 copy-done
  51.6 0.3 copy-done.1
  52.0 55.9 %middle.1 = (f32[512,512]{1,0:T(8,128)}, f32[512,512]{1,0:T(8,128)}, f32[512,512]{1,0:T(8,128)}, bf16[16,2,64,128]{3,2,1,0:T(8,128)(2,1)}, f32[16,512]{1,0:T(8,1...) custom-call(bf16[16,2,64,128]{3,2,1,0:T(8,128)(2,1)} %get-tuple-element.70.o_hbm, ...), custom_call_target="tpu_custom_call" | custom-call | tf_op jit(solution)/shard_map/middle/pallas_call | solution.py:1466
  107.9 1.0 collective-permute-start.3
  108.9 1.4 collective-permute-start.4
  110.3 20.5 %attend_back.1 = (bf16[16,128,128]{2,1,0:T(8,128)(2,1)}, f32[32,128,256]{2,1,0:T(8,128)}, f32[512,512]{1,0:T(8,128)}, f32[512,512]{1,0:T(8,128)}) custom-call(s32[3,176]{1,0:T(4,128)} %get-tuple-element.69.pairs_ref, bf16[16,128,128]{2,1,0:T(8,128)(2,1)} %get-tuple-element.67.q_ref, bf16[16,2,64,128]{3,2,1,0:T(8,128)(2,1)} %get-tuple-element.73.tan_ref, ...), custom_call_target="tpu_custom_call" | custom-call | tf_op jit(solution)/shard_map/attend_back/pallas_call | solution.py:1046
  130.8 0.0 collective-permute-done.3.land_a
  130.8 0.0 copy-start.2
  130.8 0.0 collective-permute-done.4.land_b
  130.8 0.0 copy-start.3
  130.8 0.8 copy-done.2
  131.6 0.2 copy-done.3
  131.8 94.7 %finish.1 = (f32[512,512]{1,0:T(8,128)}, bf16[2304,512]{1,0:T(8,128)(2,1)}, bf16[768,512]{1,0:T(8,128)(2,1)}, f32[24,512]{1,0:T(8,128)}) custom-call(bf16[16,128,128]{2,1,0:T(8,128)(2,1)} %get-tuple-element.79.dq_ref, f32[32,128,256]{2,1,0:T(8,128)} %get-tuple-element.80.dkv_ref, f32[2,576,512]{2,1,0:T(8,128)} %get-tuple-element.81.keep_hbm, ...), custom_call_target="tpu_custom_call" | custom-call | tf_op jit(solution)/shard_map/finish/pallas_call | solution.py:1801
  226.5 6.8 %unpack_grads.1 = (f32[512,256]{1,0:T(8,128)}, f32[512,256]{1,0:T(8,128)}, f32[512,256]{1,0:T(8,128)}, f32[256,512]{1,0:T(8,128)}, f32[512,1024]{1,0:T(8,128)}, ...) custom-call(bf16[2304,512]{1,0:T(8,128)(2,1)} %get-tuple-element.87., ...), custom_call_target="tpu_custom_call" | custom-call | tf_op jit(solution)/shard_map/unpack_grads/pallas_call | solution.py:1929
Async XLA Ops:
  0.7 49.9 %collective-permute-start.1 = (bf16[512,1024]{1,0:T(8,128)(2,1)}, bf16[512,1024]{1,0:T(8,128)(2,1)S(1)}, u32[]{:S(2)}, u32[]{:S(2)}) collective-permute-start(bf16[512,1024]{1,0:T(8,128)(2,1)} %we_a.1), channel_id=1, source_target_pairs={{0,1},{1,0},{2,3},{3,2},{4,5},{5,4},{6,7},{7,6},{8,9},{9,8},{10,11... | collective-permute-start | bytes 3145736 | tf_op jit(solution)/shard_map/ppermute | solution.py:1978
  1.2 49.4 %collective-permute-start.2 = (bf16[1024,512]{1,0:T(8,128)(2,1)}, bf16[1024,512]{1,0:T(8,128)(2,1)S(1)}, u32[]{:S(2)}, u32[]{:S(2)}) collective-permute-start(bf16[1024,512]{1,0:T(8,128)(2,1)} %ws_a.1), channel_id=1, source_target_pairs={{0,1},{1,0},{2,3},{3,2},{4,5},{5,4},{6,7},{7,6},{8,9},{9,8},{10,11... | collective-permute-start | bytes 3145736 | tf_op jit(solution)/shard_map/ppermute | solution.py:1978
  1.3 49.3 %collective-permute-start = (bf16[256,512]{1,0:T(8,128)(2,1)}, bf16[256,512]{1,0:T(8,128)(2,1)S(1)}, u32[]{:S(2)}, u32[]{:S(2)}) collective-permute-start(bf16[256,512]{1,0:T(8,128)(2,1)} %wo_a.1), channel_id=1, source_target_pairs={{0,1},{1,0},{2,3},{3,2},{4,5},{5,4},{6,7},{7,6},{8,9},{9,8},{10,11... | collective-permute-start | bytes 786440 | tf_op jit(solution)/shard_map/ppermute | solution.py:1978
  50.6 0.7 copy-start.4
  50.6 1.0 copy-start
  50.6 1.4 copy-start.1
  107.9 22.9 %collective-permute-start.3 = (bf16[576,512]{1,0:T(8,128)(2,1)}, bf16[576,512]{1,0:T(8,128)(2,1)S(1)}, u32[]{:S(2)}, u32[]{:S(2)}) collective-permute-start(bf16[576,512]{1,0:T(8,128)(2,1)} %get-tuple-element.82), channel_id=1, source_target_pairs={{0,2},{2,0},{4,6},{6,4},{8,10},{10,8},{12,14},{14,12},{16,18},{18,... | collective-permute-start | bytes 1769480 | tf_op jit(solution)/shard_map/ppermute | solution.py:1981
  108.9 21.9 %collective-permute-start.4 = (bf16[576,512]{1,0:T(8,128)(2,1)}, bf16[576,512]{1,0:T(8,128)(2,1)S(1)}, u32[]{:S(2)}, u32[]{:S(2)}) collective-permute-start(bf16[576,512]{1,0:T(8,128)(2,1)} %get-tuple-element.83), channel_id=1, source_target_pairs={{0,4},{2,6},{4,0},{6,2},{8,12},{10,14},{12,8},{14,10},{16,20},{18,... | collective-permute-start | bytes 1769480 | tf_op jit(solution)/shard_map/ppermute | solution.py:1981
  130.8 0.8 copy-start.2
  130.8 1.0 copy-start.3

commit v6 on v5

--- a/solution.py
+++ b/solution.py
@@ -498,6 +498,9 @@
         def _():
             pl.semaphore_signal(barrier, 1, device_id=(tc, tf), device_id_type=MESH)
 
+    def turn(self, i, n):
+        return (self.c + 5 * i) % n
+
     def greet_sources(self, n_ctx, partner):
         barrier = pltpu.get_barrier_semaphore()
         for tc in range(n_ctx):
@@ -609,68 +612,71 @@
     for load in loads:
         load.start()
     at.greet_sources(n_ctx, True)
-    for load in loads[6:]:
+    wide = bias_own.shape[1]
+    swaps = [
+        at.remote(src, dst, w_ss.at[i], w_rs.at[i], at.c, other)
+        for i, (src, dst) in enumerate(
+            (
+                (wq_hbm, w_in.at[0]),
+                (wk_hbm, w_in.at[1]),
+                (wv_hbm, w_in.at[2]),
+                (order_hbm, order_in),
+                (seq_hbm, seq_in),
+                (bias_own, bias_in),
+            )
+        )
+    ]
+    for swap in swaps[:-1]:
+        swap.start()
+    for load in loads:
         load.wait()
-    wide = bias_own.shape[1]
     for row, ref in enumerate(vector_in[:VECTORS]):
         bias_own[row : row + 1, :] = ref[...].astype(F32).reshape(1, wide)
     for part in range(vector_in[VECTORS].shape[0] // wide):
         piece = vector_in[VECTORS][part * wide : part * wide + wide]
         bias_own[VECTORS + part : VECTORS + part + 1, :] = piece.astype(F32).reshape(1, wide)
-    swaps = [
-        at.remote(src, dst, w_ss.at[i], w_rs.at[i], at.c, other)
-        for i, (src, dst) in enumerate(
-            (
-                (bias_own, bias_in),
-                (wq_hbm, w_in.at[0]),
-                (wk_hbm, w_in.at[1]),
-                (wv_hbm, w_in.at[2]),
-                (order_hbm, order_in),
-                (seq_hbm, seq_in),
-            )
-        )
-    ]
-    for swap in swaps:
-        swap.start()
-    for load in loads[:6]:
-        load.wait()
-
-    def targets(half):
-        for pair in range(2):
-            for side in range(2):
-                head = half * (H // 2) + 2 * pair + side
-                for core in range(2):
-                    slot = head * 2 + core
-                    yield pair, side, head, core, (
-                        kv_send.at[head, pl.ds(core * BLK, BLK)],
-                        kv_out.at[2 * at.c + core],
-                        kv_ss.at[slot],
-                        kv_rs.at[at.c],
-                        at.f * H + head,
-                        core,
-                    ), (
-                        q_send.at[head, core],
-                        q_out.at[at.c],
-                        q_ss.at[slot],
-                        q_rs.at[at.c],
-                        at.f * H + head,
-                        core,
-                    )
+    swaps[-1].start()
+
+    def moves(half):
+        for i in range(H // 2):
+            head = half * (H // 2) + at.turn(i, H // 2)
+            for core in range(2):
+                slot = head * 2 + core
+                yield (
+                    kv_send.at[head, pl.ds(core * BLK, BLK)],
+                    kv_out.at[2 * at.c + core],
+                    kv_ss.at[slot],
+                    kv_rs.at[at.c],
+                    at.f * H + head,
+                    core,
+                )
+                yield (
+                    q_send.at[head, core],
+                    q_out.at[at.c],
+                    q_ss.at[slot],
+                    q_rs.at[at.c],
+                    at.f * H + head,
+                    core,
+                )
 
     def one_half(half, wq, wk, wv, bias):
         low = x_in[...].astype(BF16)
         q = dot_nn(low, wq[...]) + bias[0:1, :]
         k = dot_nn(low, wk[...])
         v = dot_nn(low, wv[...]) + bias[1:2, :]
-        for pair, side, head, core, kv_move, q_move in targets(half):
+        for pair in range(2):
             columns = slice(pair * 128, pair * 128 + 128)
-            if core == 0:
+            for side in range(2):
+                head = half * (H // 2) + 2 * pair + side
                 kv_send[head] = side_pair(side, k[:, columns], v[:, columns]).astype(BF16)
-            rows = slice(core * HALF, core * HALF + HALF)
-            late = slice(BLK + core * HALF, BLK + core * HALF + HALF)
-            q_send[head, core] = side_pair(side, q[rows, columns], q[late, columns]).astype(BF16)
-            at.send(*kv_move)
-            at.send(*q_move)
+                for core in range(2):
+                    rows = slice(core * HALF, core * HALF + HALF)
+                    late = slice(BLK + core * HALF, BLK + core * HALF + HALF)
+                    q_send[head, core] = side_pair(side, q[rows, columns], q[late, columns]).astype(
+                        BF16
+                    )
+        for move in moves(half):
+            at.send(*move)
 
     one_half(at.f, w_own.at[0], w_own.at[1], w_own.at[2], bias_own)
     for swap in swaps:
@@ -707,9 +713,8 @@
     for source in range(n_ctx):
         relay(source).wait_send()
     for half in (at.f, other):
-        for _, _, _, _, kv_move, q_move in targets(half):
-            at.wait_sent(*kv_move)
-            at.wait_sent(*q_move)
+        for move in moves(half):
+            at.wait_sent(*move)
 
 
 def project_and_scatter(n_ctx, x, wq, wk, wv, order, seqs, vectors):
@@ -1283,8 +1288,8 @@
         )
 
     for side in range(2):
-        for target in range(n_ctx):
-            at.send(*o_move(target, side))
+        for i in range(n_ctx):
+            at.send(*o_move(at.turn(i, n_ctx), side))
     vec_ref[...] = jnp.zeros_like(vec_ref)
     vectors = vec_in[...]
     (out_bias, gain_one, shift_one, shrink_bias, gain_two, shift_two, gain_last, shift_last) = (
@@ -1335,7 +1340,7 @@
         for kind in range(2):
 
             def expand(chunk, carried):
-                columns = pl.ds(pl.multiple_of(chunk * COLS, COLS), COLS)
+                columns = slice(chunk * COLS, chunk * COLS + COLS)
                 v = dot_nn(normed_low, we[kind, :, columns]) + be[kind][:, columns]
                 square = v * v
                 t = jnp.tanh(gelu_coeff * (v + gelu_cubic * square * v))
@@ -1347,7 +1352,8 @@
                 )
                 return carried + dot_nn(hidden_part, ws[kind, columns, :])
 
-            feed = lax.fori_loop(0, ws.shape[1] // COLS, expand, feed)
+            for chunk in range(ws.shape[1] // COLS):
+                feed = expand(chunk, feed)
         feed_out = feed + shrink_bias
         n_two, scale_two = normalize(normed_one + feed_out)
         n_last, scale_last = normalize(stream_one + feed_out)
@@ -1368,7 +1374,7 @@
         for kind in range(2):
 
             def expand_back(chunk, carried):
-                columns = pl.ds(pl.multiple_of(chunk * COLS, COLS), COLS)
+                columns = slice(chunk * COLS, chunk * COLS + COLS)
                 pushed = dot_nt(feed_low, ws[kind, columns, :])
                 tan_part = (pushed * slope[kind, :, columns]).astype(BF16)
                 before_tan[kind, rows, columns] = tan_part
@@ -1376,7 +1382,8 @@
                 vec_ref[vec_row, :] += column_sum(tan_part.astype(F32))
                 return carried + dot_nt(tan_part, we[kind, :, columns])
 
-            normed_tan = lax.fori_loop(0, ws.shape[1] // COLS, expand_back, normed_tan)
+            for chunk in range(ws.shape[1] // COLS):
+                normed_tan = expand_back(chunk, normed_tan)
         vec_ref[5:6, :] += column_sum(normed_tan * n_one)
         vec_ref[6:7, :] += column_sum(normed_tan)
         entry = norm_back(normed_tan, n_one, scale_one, gain_one)
@@ -1396,7 +1403,9 @@
                         early = mixed_tan[kind, start : start + piece, columns]
                         late = mixed_tan[kind, start + piece : start + HALF, columns]
                         tan_send[step, head, core] = side_pair(side, early, late).astype(BF16)
-                        at.send(*tan_move(step, head, core))
+        for i in range(H):
+            for core in range(2):
+                at.send(*tan_move(step, at.turn(i, H), core))
         for store in stores(step):
             store.start()
         return 0
@@ -1584,11 +1593,12 @@
             at.group,
         )
 
-    for source in range(n_ctx):
+    for i in range(n_ctx):
+        source = at.turn(i, n_ctx)
         partial_move(source).start()
         own_move(source).start()
-    for target in range(n_ctx):
-        at.send(*q_move(target))
+    for i in range(n_ctx):
+        at.send(*q_move(at.turn(i, n_ctx)))
 
     size = keep.shape[1]
     firsts = (x_step, y_step)
@@ -1630,7 +1640,8 @@
         feed.down(region, 0, True).start()
         feed.join(region, kept, half, first, sums[region % 2])
     feed.acc = sums
-    for source in range(n_ctx):
+    for i in range(n_ctx):
+        source = at.turn(i, n_ctx)
         own_move(source).wait()
         partial_move(source).wait_recv()
         ready[source] = jnp.transpose(own[source] + part[source]).astype(BF16)

time: 234 us -> 226 us (0.966)
  Pallas kernels: 227 us -> 219 us
    pallas_call x1, Pallas kernels: 55.9 us -> 46 us  [middle(): pl.pallas_call(functools.partial(middle_kernel, n_ctx), out_shape=(rows,...]
    pallas_call x1, Pallas kernels: 31.3 us -> 36.5 us  [project_and_scatter(): pl.pallas_call(functools.partial(project_kernel, n_ctx), out_shape=(jax.S...]
    pallas_call x1, Pallas kernels: 94.7 us -> 91.7 us  [finish(): pl.pallas_call(functools.partial(finish_kernel, n_ctx), out_shape=(jax.Sh...]
  transfers between devices with their start and end apart: 5 -> 5, of which waited for: 0 -> 0; matrix products, arithmetic and copies ran while one was open for 0% -> 0% of each run, Pallas kernels for 30% -> 33%
where the time goes in v6:
time: 226 us
  Pallas kernels  219 us (97%)
  starting transfers between devices  3.72 us (2%)
  local copies, waits for them, and re-layouts  2.34 us (1%)
    pallas_call x1, Pallas kernels, finish(): pl.pallas_call(functools.partial(finish_kernel, n_ctx), out_shape=(jax.Sh...  91.7 us
    pallas_call x1, Pallas kernels, middle(): pl.pallas_call(functools.partial(middle_kernel, n_ctx), out_shape=(rows,...  46 us
    pallas_call x1, Pallas kernels, project_and_scatter(): pl.pallas_call(functools.partial(project_kernel, n_ctx), out_shape=(jax.S...  36.5 us
    pallas_call x1, Pallas kernels, attend_back(): pl.pallas_call(functools.partial(backward_kernel, blocks), out_shape=(jax...  20.5 us
    pallas_call x1, Pallas kernels, attend(): pl.pallas_call(functools.partial(forward_kernel, blocks), out_shape=(jax....  17.6 us
    pallas_call x1, Pallas kernels, unpack_grads(): pl.pallas_call(unpack_kernel, out_shape=tuple((jax.ShapeDtypeStruct(shape...  6.76 us
  transfers between devices with their start and end apart: 5, of which 0 were waited for; matrix products, arithmetic and copies ran while one was open for 0% of the time, Pallas kernels for 33%

profile of v6, /device:TPU:0, one launch (start us, length us, event | category | flops | bytes accessed | tf_op | source)
XLA Modules:
  0.0 226.1 jit_solution(7575498398412848072)
XLA Ops:
  0.7 0.5 collective-permute-start.1
  1.2 0.1 collective-permute-start.2
  1.3 0.4 collective-permute-start
  1.7 36.5 %project_scatter.1 = (bf16[16,128,128]{2,1,0:T(8,128)(2,1)}, bf16[32,256,128]{2,1,0:T(8,128)(2,1)}, bf16[3,512,256]{2,1,0:T(8,128)(2,1)}, s32[1,32]{1,0:T(1,128)...) custom-call(f32[512,512]{1,0:T(8,128)} %bitcast.17, bf16[512,256]{1,0:T(8,128)(2,1)} %wq_hbm.3, ...), custom_call_target="tpu_custom_call" | custom-call | tf_op jit(solution)/shard_map/project_scatter/pallas_call | solution.py:725
  38.2 17.6 %attend.1 = (bf16[16,2,64,128]{3,2,1,0:T(8,128)(2,1)}, f32[16,2,64,128]{3,2,1,0:T(8,128)}, f32[33,128,128]{2,1,0:T(8,128)}, s32[3,176]{1,0:T(4,128)}) custom-call(s32[1,32]{1,0:T(1,128)} %get-tuple-element.65.order_ref, s32[1,32]{1,0:T(1,128)} %get-tuple-element.66.seq_ref, bf16[16,128,128]{2,1,0:T(8,128)(2,1)} %get-tuple-element.67.q_ref, ...), custom_call_target="tpu_custom_call" | custom-call | tf_op jit(solution)/shard_map/attend/pallas_call | solution.py:914
  55.8 0.0 collective-permute-done.wo_b
  55.8 0.0 copy-start.4
  55.9 0.0 collective-permute-done.1.we_b
  55.9 0.0 copy-start
  55.9 0.0 collective-permute-done.2.ws_b
  55.9 0.0 copy-start.1
  55.9 0.6 copy-done.4
  56.6 0.4 copy-done
  56.9 0.3 copy-done.1
  57.3 46.0 %middle.1 = (f32[512,512]{1,0:T(8,128)}, f32[512,512]{1,0:T(8,128)}, f32[512,512]{1,0:T(8,128)}, bf16[16,2,64,128]{3,2,1,0:T(8,128)(2,1)}, f32[16,512]{1,0:T(8,1...) custom-call(bf16[16,2,64,128]{3,2,1,0:T(8,128)(2,1)} %get-tuple-element.70.o_hbm, ...), custom_call_target="tpu_custom_call" | custom-call | tf_op jit(solution)/shard_map/middle/pallas_call | solution.py:1475
  103.2 0.5 collective-permute-start.3
  103.8 2.2 collective-permute-start.4
  105.9 20.5 %attend_back.1 = (bf16[16,128,128]{2,1,0:T(8,128)(2,1)}, f32[32,128,256]{2,1,0:T(8,128)}, f32[512,512]{1,0:T(8,128)}, f32[512,512]{1,0:T(8,128)}) custom-call(s32[3,176]{1,0:T(4,128)} %get-tuple-element.69.pairs_ref, bf16[16,128,128]{2,1,0:T(8,128)(2,1)} %get-tuple-element.67.q_ref, bf16[16,2,64,128]{3,2,1,0:T(8,128)(2,1)} %get-tuple-element.73.tan_ref, ...), custom_call_target="tpu_custom_call" | custom-call | tf_op jit(solution)/shard_map/attend_back/pallas_call | solution.py:1051
  126.4 0.0 collective-permute-done.3.land_a
  126.4 0.0 copy-start.2
  126.4 0.0 collective-permute-done.4.land_b
  126.4 0.0 copy-start.3
  126.4 0.8 copy-done.2
  127.2 0.2 copy-done.3
  127.4 91.7 %finish.1 = (f32[512,512]{1,0:T(8,128)}, bf16[2304,512]{1,0:T(8,128)(2,1)}, bf16[768,512]{1,0:T(8,128)(2,1)}, f32[24,512]{1,0:T(8,128)}) custom-call(bf16[16,128,128]{2,1,0:T(8,128)(2,1)} %get-tuple-element.79.dq_ref, f32[32,128,256]{2,1,0:T(8,128)} %get-tuple-element.80.dkv_ref, f32[2,576,512]{2,1,0:T(8,128)} %get-tuple-element.81.keep_hbm, ...), custom_call_target="tpu_custom_call" | custom-call | tf_op jit(solution)/shard_map/finish/pallas_call | solution.py:1812
  219.1 6.8 %unpack_grads.1 = (f32[512,256]{1,0:T(8,128)}, f32[512,256]{1,0:T(8,128)}, f32[512,256]{1,0:T(8,128)}, f32[256,512]{1,0:T(8,128)}, f32[512,1024]{1,0:T(8,128)}, ...) custom-call(bf16[2304,512]{1,0:T(8,128)(2,1)} %get-tuple-element.87., ...), custom_call_target="tpu_custom_call" | custom-call | tf_op jit(solution)/shard_map/unpack_grads/pallas_call | solution.py:1940
Async XLA Ops:
  0.7 55.2 %collective-permute-start.1 = (bf16[512,1024]{1,0:T(8,128)(2,1)}, bf16[512,1024]{1,0:T(8,128)(2,1)S(1)}, u32[]{:S(2)}, u32[]{:S(2)}) collective-permute-start(bf16[512,1024]{1,0:T(8,128)(2,1)} %we_a.1), channel_id=1, source_target_pairs={{0,1},{1,0},{2,3},{3,2},{4,5},{5,4},{6,7},{7,6},{8,9},{9,8},{10,11... | collective-permute-start | bytes 3145736 | tf_op jit(solution)/shard_map/ppermute | solution.py:1989
  1.2 54.7 %collective-permute-start.2 = (bf16[1024,512]{1,0:T(8,128)(2,1)}, bf16[1024,512]{1,0:T(8,128)(2,1)S(1)}, u32[]{:S(2)}, u32[]{:S(2)}) collective-permute-start(bf16[1024,512]{1,0:T(8,128)(2,1)} %ws_a.1), channel_id=1, source_target_pairs={{0,1},{1,0},{2,3},{3,2},{4,5},{5,4},{6,7},{7,6},{8,9},{9,8},{10,11... | collective-permute-start | bytes 3145736 | tf_op jit(solution)/shard_map/ppermute | solution.py:1989
  1.3 54.6 %collective-permute-start = (bf16[256,512]{1,0:T(8,128)(2,1)}, bf16[256,512]{1,0:T(8,128)(2,1)S(1)}, u32[]{:S(2)}, u32[]{:S(2)}) collective-permute-start(bf16[256,512]{1,0:T(8,128)(2,1)} %wo_a.1), channel_id=1, source_target_pairs={{0,1},{1,0},{2,3},{3,2},{4,5},{5,4},{6,7},{7,6},{8,9},{9,8},{10,11... | collective-permute-start | bytes 786440 | tf_op jit(solution)/shard_map/ppermute | solution.py:1989
  55.8 0.7 copy-start.4
  55.9 1.0 copy-start
  55.9 1.4 copy-start.1
  103.2 23.2 %collective-permute-start.3 = (bf16[576,512]{1,0:T(8,128)(2,1)}, bf16[576,512]{1,0:T(8,128)(2,1)S(1)}, u32[]{:S(2)}, u32[]{:S(2)}) collective-permute-start(bf16[576,512]{1,0:T(8,128)(2,1)} %get-tuple-element.82), channel_id=1, source_target_pairs={{0,2},{2,0},{4,6},{6,4},{8,10},{10,8},{12,14},{14,12},{16,18},{18,... | collective-permute-start | bytes 1769480 | tf_op jit(solution)/shard_map/ppermute | solution.py:1992
  103.8 22.7 %collective-permute-start.4 = (bf16[576,512]{1,0:T(8,128)(2,1)}, bf16[576,512]{1,0:T(8,128)(2,1)S(1)}, u32[]{:S(2)}, u32[]{:S(2)}) collective-permute-start(bf16[576,512]{1,0:T(8,128)(2,1)} %get-tuple-element.83), channel_id=1, source_target_pairs={{0,4},{2,6},{4,0},{6,2},{8,12},{10,14},{12,8},{14,10},{16,20},{18,... | collective-permute-start | bytes 1769480 | tf_op jit(solution)/shard_map/ppermute | solution.py:1992
  126.4 0.8 copy-start.2
  126.4 1.0 copy-start.3

commit v7 on v6

--- a/solution.py
+++ b/solution.py
@@ -19,6 +19,7 @@
 BF16 = jnp.bfloat16
 MESH = pl.DeviceIdType.MESH
 ROOM = 60 << 20
+UNPACK_ROOM = 60 << 20
 VMEM = pl.BlockSpec(memory_space=pltpu.VMEM)
 SMEM = pl.BlockSpec(memory_space=pltpu.SMEM)
 ANY = pl.BlockSpec(memory_space=pltpu.HBM)
@@ -562,6 +563,7 @@
     seq_hbm,
     *rest,
 ):
+    dense_hbm, rest = rest[:3], rest[3:]
     vector_hbm, rest = rest[: VECTORS + 1], rest[VECTORS + 1 :]
     vector_in, rest = rest[-VECTORS - 1 :], rest[: -VECTORS - 1]
     (
@@ -572,6 +574,9 @@
         seq_out,
         vec_out,
         expand_out,
+        wo_other,
+        we_other,
+        ws_other,
         x_in,
         w_own,
         w_in,
@@ -682,6 +687,12 @@
     for swap in swaps:
         swap.wait()
     one_half(other, w_in.at[0], w_in.at[1], w_in.at[2], bias_in)
+    dense_swaps = [
+        at.remote(src, dst, w_ss.at[6 + i], w_rs.at[6 + i], at.c, other)
+        for i, (src, dst) in enumerate(zip(dense_hbm, (wo_other, we_other, ws_other)))
+    ]
+    for swap in dense_swaps:
+        swap.start()
     w_other[...] = w_in[...]
     inside = at.inside == 1
     order_out[...] = jnp.where(inside, order_own[...], order_in[...])
@@ -706,18 +717,20 @@
         arrived = kv_out.at[2 * source + at.f]
         at.remote(arrived, arrived, kv_ss.at[0], kv_rs.at[source], at.c, other).wait_recv()
         relay(source).start()
+    for half in (at.f, other):
+        for move in moves(half):
+            at.wait_sent(*move)
     for source in range(n_ctx):
         arrived = q_out.at[source]
         at.remote(arrived, arrived, q_ss.at[0], q_rs.at[source], at.c, other).wait_recv()
         relay_in(source).wait_recv()
     for source in range(n_ctx):
         relay(source).wait_send()
-    for half in (at.f, other):
-        for move in moves(half):
-            at.wait_sent(*move)
-
-
-def project_and_scatter(n_ctx, x, wq, wk, wv, order, seqs, vectors):
+    for swap in dense_swaps:
+        swap.wait()
+
+
+def project_and_scatter(n_ctx, x, wq, wk, wv, order, seqs, dense_weights, vectors):
     wide = wq.shape[1]
     blocks = order.shape[1]
     units = vectors[VECTORS].shape[0]
@@ -732,9 +745,10 @@
             jax.ShapeDtypeStruct((1, blocks), jnp.int32),
             jax.ShapeDtypeStruct((bias_rows, D), F32),
             jax.ShapeDtypeStruct((2, units), F32),
+            *[jax.ShapeDtypeStruct(w.shape, BF16) for w in dense_weights],
         ),
-        in_specs=[ANY] * (7 + VECTORS),
-        out_specs=(ANY, ANY) + (VMEM,) * 5,
+        in_specs=[ANY] * (10 + VECTORS),
+        out_specs=(ANY, ANY) + (VMEM,) * 5 + (ANY,) * 3,
         scratch_shapes=[
             pltpu.VMEM((2 * BLK, D), F32),
             pltpu.VMEM((3, D, wide), BF16),
@@ -748,8 +762,8 @@
             pltpu.VMEM((H, 2, HALF, 128), BF16),
             pltpu.VMEM((H, 2 * BLK, 128), BF16),
             pltpu.SemaphoreType.DMA((7 + VECTORS,)),
-            pltpu.SemaphoreType.DMA((6,)),
-            pltpu.SemaphoreType.DMA((6,)),
+            pltpu.SemaphoreType.DMA((9,)),
+            pltpu.SemaphoreType.DMA((9,)),
             pltpu.SemaphoreType.DMA((2 * H,)),
             pltpu.SemaphoreType.DMA((n_ctx,)),
             pltpu.SemaphoreType.DMA((2 * H,)),
@@ -762,7 +776,7 @@
             collective_id=0, has_side_effects=True, vmem_limit_bytes=ROOM
         ),
         name="project_scatter",
-    )(x, wq, wk, wv, order, seqs, *vectors)
+    )(x, wq, wk, wv, order, seqs, *dense_weights, *vectors)
 
 
 def forward_kernel(
@@ -1072,7 +1086,7 @@
 
 
 def pieces_of(start, size, body):
-    piece = max(n for n in range(16, 97, 16) if size % n == 0)
+    piece = max(n for n in range(16, 289, 16) if size % n == 0)
     lax.fori_loop(
         0,
         size // piece,
@@ -1433,6 +1447,9 @@
     for step in order:
         core_move(*step)[1].start()
     feed_slopes(0, own_grads, *operands)
+    for side in range(2):
+        for target in range(n_ctx):
+            at.wait_sent(*o_move(target, side))
     for region, give in order:
         start, move = core_move(region, give)
         move.wait_recv()
@@ -1455,8 +1472,6 @@
         for store in stores(step):
             store.wait()
     for side in range(2):
-        for target in range(n_ctx):
-            at.wait_sent(*o_move(target, side))
         for head in range(H):
             for core in range(2):
                 at.wait_sent(*tan_move(side, head, core))
@@ -1654,6 +1669,10 @@
             feed.down(region, step - 1, False).wait_recv()
             feed.give(region, step, feed.landing[region % 2][step - 1])
 
+    for target in range(n_ctx):
+        partial_move(target).wait_send()
+        at.wait_sent(*q_move(target))
+
     for head in range(H):
         for core in range(2):
             slot = head * 2 + core
@@ -1761,6 +1780,10 @@
         total = total + dot_nt(tangents[0, which], w_in[which])
         total = total + dot_nt(tangents[1, which], w_far[which])
     post_ref[...] = total
+    for target in range(n_ctx):
+        at.wait_sent(*kv_move(target))
+    for step in order:
+        core_move(*step).wait_send()
     for region in range(REGIONS):
         feed.up(region, 1, False).wait_recv()
         feed.up(region, 0, True).start()
@@ -1787,12 +1810,6 @@
     for region in range(REGIONS):
         top_move(region, False).wait_recv()
 
-    for target in range(n_ctx):
-        partial_move(target).wait_send()
-        at.wait_sent(*q_move(target))
-        at.wait_sent(*kv_move(target))
-    for step in order:
-        core_move(*step).wait_send()
     for step in range(5):
         vec_move(step).wait_send()
     for region in range(REGIONS):
@@ -1854,72 +1871,21 @@
 
 
 def unpack_kernel(
-    full_hbm, grads_hbm, post_hbm, vec_ref,
-    query_hbm, key_hbm, value_hbm, output_hbm, expand_hbm, shrink_hbm, post_out, *rest,
+    full, grads, post, vec_ref,
+    query_ref, key_ref, value_ref, output_ref, expand_ref, shrink_ref, post_out, *vector_outs,
 ):
-    vector_outs, (low_full, low_last, full, last, held, load_sem, store_sem, post_sem) = (
-        rest[:11],
-        rest[11:],
-    )
     f = lax.axis_index("fsdp")
-    units, wide = shrink_hbm.shape[0], D // 2
-    post_in = pltpu.make_async_copy(post_hbm, held, post_sem.at[0])
-    post = pltpu.make_async_copy(held, post_out, post_sem.at[1])
-    post_in.start()
-    parts = [
-        (low_last, last, 0, D, [(query_hbm, slice(0, wide)), (key_hbm, slice(wide, D))]),
-        (
-            low_last,
-            last,
-            D,
-            wide,
-            [
-                (value_hbm.at[0:wide], slice(0, wide)),
-                (value_hbm.at[wide:D], slice(wide, D)),
-            ],
-        ),
-    ]
+    units, wide = shrink_ref.shape[0], D // 2
+    shrink_ref[...] = full[0:units].astype(F32)
     for part in range(units // D):
-        parts.append(
-            (
-                low_full,
-                full,
-                part * D,
-                D,
-                [(shrink_hbm.at[part * D : part * D + D], slice(0, D))],
-            )
-        )
-    for part in range(units // D):
-        parts.append(
-            (
-                low_full,
-                full,
-                units + part * D,
-                D,
-                [(expand_hbm.at[:, part * D : part * D + D], slice(0, D))],
-            )
-        )
-    parts.append((low_full, full, 2 * units, wide, [(output_hbm, slice(0, D))]))
-    loads = []
-    for i, (low, _, start, rows, _) in enumerate(parts):
-        src = grads_hbm if low is low_last else full_hbm
-        where = pl.ds(start, rows)
-        loads.append(pltpu.make_async_copy(src.at[where], low.at[where], load_sem.at[i]))
-        loads[-1].start()
-    post_in.wait()
-    post.start()
-    stores = []
-    for load, (low, wide_rows, start, rows, targets) in zip(loads, parts):
-        load.wait()
-        where = pl.ds(start, rows)
-        wide_rows[where, :] = low[where, :].astype(F32)
-        for target, columns in targets:
-            stores.append(
-                pltpu.make_async_copy(
-                    wide_rows.at[where, columns], target, store_sem.at[len(stores)]
-                )
-            )
-            stores[-1].start()
+        start = units + part * D
+        expand_ref[:, part * D : part * D + D] = full[start : start + D].astype(F32)
+    output_ref[...] = full[2 * units : 2 * units + wide].astype(F32)
+    query_ref[...] = grads[0:D, 0:wide].astype(F32)
+    key_ref[...] = grads[0:D, wide:D].astype(F32)
+    value_ref[0:wide] = grads[D : D + wide, 0:wide].astype(F32)
+    value_ref[wide:D] = grads[D : D + wide, wide:D].astype(F32)
+    post_out[...] = post[...]
     vectors = vec_ref[...]
     mine = jnp.where(f == 0, vectors[:, 0:wide], vectors[:, wide:D])
     for row, ref in zip((16, 17, 7, 5, 6, 0, 1, 2, 3, 4), vector_outs):
@@ -1927,32 +1893,18 @@
     drift = jnp.where(f == 0, vectors[8:10], vectors[10:12])
     for part in range(units // D):
         vector_outs[10][:, part * D : part * D + D] = drift[part : part + 1]
-    for store in stores:
-        store.wait()
-    post.wait()
 
 
 def unpack_grads(units, full, grads, post, vecs):
     wide = D // 2
     shapes = [(D, wide)] * 3 + [(wide, D), (D, units), (units, D), post.shape]
-    vectors = [(1, wide)] * 10 + [(1, units)]
-    part_count = 3 + 2 * (units // D)
+    shapes = shapes + [(1, wide)] * 10 + [(1, units)]
     return pl.pallas_call(
         unpack_kernel,
-        out_shape=tuple(jax.ShapeDtypeStruct(shape, F32) for shape in shapes + vectors),
-        in_specs=[ANY] * 3 + [VMEM],
-        out_specs=(ANY,) * len(shapes) + (VMEM,) * len(vectors),
-        scratch_shapes=[
-            pltpu.VMEM(full.shape, BF16),
-            pltpu.VMEM(grads.shape, BF16),
-            pltpu.VMEM(full.shape, F32),
-            pltpu.VMEM(grads.shape, F32),
-            pltpu.VMEM(post.shape, F32),
-            pltpu.SemaphoreType.DMA((part_count,)),
-            pltpu.SemaphoreType.DMA((part_count + 2,)),
-            pltpu.SemaphoreType.DMA((2,)),
-        ],
-        compiler_params=pltpu.CompilerParams(vmem_limit_bytes=ROOM),
+        out_shape=tuple(jax.ShapeDtypeStruct(shape, F32) for shape in shapes),
+        in_specs=[VMEM] * 4,
+        out_specs=(VMEM,) * len(shapes),
+        compiler_params=pltpu.CompilerParams(vmem_limit_bytes=UNPACK_ROOM),
         name="unpack_grads",
     )(full, grads, post, vecs)
 
@@ -1983,11 +1935,6 @@
     final_shift,
 ):
     x, summed, tangent = post_stream[0], sum_stream[0], cotangent[0]
-    swap = [(0, 1), (1, 0)]
-
-    def from_other(values):
-        return lax.ppermute(values, "fsdp", swap)
-
     def across(values, stride):
         return lax.ppermute(values, "ctx", [(c, c ^ stride) for c in range(n_ctx)])
 
@@ -2004,8 +1951,18 @@
         final_shift,
         expand_bias,
     ]
-    q, kv, w_other, order, seqs, vec, expand_add = project_and_scatter(
-        n_ctx, x, query_weight, key_weight, value_weight, block_order, block_sequence, vectors
+    q, kv, w_other, order, seqs, vec, expand_add, wo_other, we_other, ws_other = (
+        project_and_scatter(
+            n_ctx,
+            x,
+            query_weight,
+            key_weight,
+            value_weight,
+            block_order,
+            block_sequence,
+            (output_weight, expand_weight, shrink_weight),
+            vectors,
+        )
     )
     o, keep, lse, pairs = attend(order, seqs, q, kv)
     layer_output, sum_tan, entry, tan, vec_feed, stage_a, stage_b, kept = middle(
@@ -2014,9 +1971,9 @@
         x,
         summed,
         tangent,
-        (output_weight, from_other(output_weight)),
-        (expand_weight, from_other(expand_weight)),
-        (shrink_weight, from_other(shrink_weight)),
+        (output_weight, wo_other),
+        (expand_weight, we_other),
+        (shrink_weight, ws_other),
         expand_add,
         vec,
     )

time: 226 us -> 223 us (0.987)
  transfers between devices with their start and end apart: 5 -> 2, of which waited for: 0 -> 0; matrix products, arithmetic and copies ran while one was open for 0% -> 0% of each run, Pallas kernels for 33% -> 9%
where the time goes in v7:
time: 223 us; the launch traced here: 222 us
  Pallas kernels  218 us (98%)
  starting transfers between devices  2.71 us (1%)
    pallas_call x1, Pallas kernels, finish(): pl.pallas_call(functools.partial(finish_kernel, n_ctx), out_shape=(jax.Sh...  91.6 us
    pallas_call x1, Pallas kernels, middle(): pl.pallas_call(functools.partial(middle_kernel, n_ctx), out_shape=(rows,...  45.9 us
    pallas_call x1, Pallas kernels, project_and_scatter(): pl.pallas_call(functools.partial(project_kernel, n_ctx), out_shape=(jax.S...  37 us
    pallas_call x1, Pallas kernels, attend_back(): pl.pallas_call(functools.partial(backward_kernel, blocks), out_shape=(jax...  20.5 us
    pallas_call x1, Pallas kernels, attend(): pl.pallas_call(functools.partial(forward_kernel, blocks), out_shape=(jax....  17.6 us
    pallas_call x1, Pallas kernels, unpack_grads(): pl.pallas_call(unpack_kernel, out_shape=tuple((jax.ShapeDtypeStruct(shape...  5.39 us
  transfers between devices with their start and end apart: 2, of which 0 were waited for; matrix products, arithmetic and copies ran while one was open for 0% of the time, Pallas kernels for 9%

profile of v7, /device:TPU:0, one launch (start us, length us, event | category | flops | bytes accessed | tf_op | source)
XLA Modules:
  0.0 222.4 jit_solution(13775250289126290350)
XLA Ops:
  0.7 37.0 %project_scatter.1 = (bf16[16,128,128]{2,1,0:T(8,128)(2,1)}, bf16[32,256,128]{2,1,0:T(8,128)(2,1)}, bf16[3,512,256]{2,1,0:T(8,128)(2,1)}, s32[1,32]{1,0:T(1,128)...) custom-call(f32[512,512]{1,0:T(8,128)} %bitcast.17, ...), custom_call_target="tpu_custom_call" | custom-call | tf_op jit(solution)/shard_map/project_scatter/pallas_call | solution.py:738
  37.6 17.6 %attend.1 = (bf16[16,2,64,128]{3,2,1,0:T(8,128)(2,1)}, f32[16,2,64,128]{3,2,1,0:T(8,128)}, f32[33,128,128]{2,1,0:T(8,128)}, s32[3,176]{1,0:T(4,128)}) custom-call(s32[1,32]{1,0:T(1,128)} %get-tuple-element.68.order_ref, s32[1,32]{1,0:T(1,128)} %get-tuple-element.69.seq_ref, bf16[16,128,128]{2,1,0:T(8,128)(2,1)} %get-tuple-element.70.q_ref, ...), custom_call_target="tpu_custom_call" | custom-call | tf_op jit(solution)/shard_map/attend/pallas_call | solution.py:928
  55.2 45.9 %middle.1 = (f32[512,512]{1,0:T(8,128)}, f32[512,512]{1,0:T(8,128)}, f32[512,512]{1,0:T(8,128)}, bf16[16,2,64,128]{3,2,1,0:T(8,128)(2,1)}, f32[16,512]{1,0:T(8,1...) custom-call(bf16[16,2,64,128]{3,2,1,0:T(8,128)(2,1)} %get-tuple-element.73.o_hbm, ...), custom_call_target="tpu_custom_call" | custom-call | tf_op jit(solution)/shard_map/middle/pallas_call | solution.py:1490
  101.1 0.5 collective-permute-start
  101.6 2.2 collective-permute-start.1
  103.8 20.5 %attend_back.1 = (bf16[16,128,128]{2,1,0:T(8,128)(2,1)}, f32[32,128,256]{2,1,0:T(8,128)}, f32[512,512]{1,0:T(8,128)}, f32[512,512]{1,0:T(8,128)}) custom-call(s32[3,176]{1,0:T(4,128)} %get-tuple-element.72.pairs_ref, bf16[16,128,128]{2,1,0:T(8,128)(2,1)} %get-tuple-element.70.q_ref, bf16[16,2,64,128]{3,2,1,0:T(8,128)(2,1)} %get-tuple-element.79.tan_ref, ...), custom_call_target="tpu_custom_call" | custom-call | tf_op jit(solution)/shard_map/attend_back/pallas_call | solution.py:1065
  124.3 0.0 collective-permute-done.land_a
  124.3 0.0 copy-start
  124.3 0.0 collective-permute-done.1.land_b
  124.3 0.0 copy-start.1
  124.3 0.8 copy-done
  125.1 0.2 copy-done.1
  125.3 91.6 %finish.1 = (f32[512,512]{1,0:T(8,128)}, bf16[2304,512]{1,0:T(8,128)(2,1)}, bf16[768,512]{1,0:T(8,128)(2,1)}, f32[24,512]{1,0:T(8,128)}) custom-call(bf16[16,128,128]{2,1,0:T(8,128)(2,1)} %get-tuple-element.85.dq_ref, f32[32,128,256]{2,1,0:T(8,128)} %get-tuple-element.86.dkv_ref, f32[2,576,512]{2,1,0:T(8,128)} %get-tuple-element.87.keep_hbm, ...), custom_call_target="tpu_custom_call" | custom-call | tf_op jit(solution)/shard_map/finish/pallas_call | solution.py:1829
  216.9 5.4 %unpack_grads.1 = (f32[512,256]{1,0:T(8,128)}, f32[512,256]{1,0:T(8,128)}, f32[512,256]{1,0:T(8,128)}, f32[256,512]{1,0:T(8,128)}, f32[512,1024]{1,0:T(8,128)}, ...) custom-call(bf16[2304,512]{1,0:T(8,128)(2,1)} %get-tuple-element.93., ...), custom_call_target="tpu_custom_call" | custom-call | tf_op jit(solution)/shard_map/unpack_grads/pallas_call | solution.py:1902
Async XLA Ops:
  101.1 23.2 %collective-permute-start = (bf16[576,512]{1,0:T(8,128)(2,1)}, bf16[576,512]{1,0:T(8,128)(2,1)S(1)}, u32[]{:S(2)}, u32[]{:S(2)}) collective-permute-start(bf16[576,512]{1,0:T(8,128)(2,1)} %get-tuple-element.88), channel_id=1, source_target_pairs={{0,2},{2,0},{4,6},{6,4},{8,10},{10,8},{12,14},{14,12},{16,18},{18,... | collective-permute-start | bytes 1769480 | tf_op jit(solution)/shard_map/ppermute | solution.py:1939
  101.6 22.7 %collective-permute-start.1 = (bf16[576,512]{1,0:T(8,128)(2,1)}, bf16[576,512]{1,0:T(8,128)(2,1)S(1)}, u32[]{:S(2)}, u32[]{:S(2)}) collective-permute-start(bf16[576,512]{1,0:T(8,128)(2,1)} %get-tuple-element.89), channel_id=1, source_target_pairs={{0,4},{2,6},{4,0},{6,2},{8,12},{10,14},{12,8},{14,10},{16,20},{18,... | collective-permute-start | bytes 1769480 | tf_op jit(solution)/shard_map/ppermute | solution.py:1939
  124.3 0.8 copy-start
  124.3 1.0 copy-start.1

commit v8 on v7

--- a/solution.py
+++ b/solution.py
@@ -1189,11 +1189,14 @@
         pieces_of(kept, size, body)
         self.up(region, self.last - 1, True).start()
 
-    def wait_sent(self):
+    def wait_down(self):
         for region in range(REGIONS):
             for step in range(self.last + 1):
                 self.down(region, step, True).wait_send()
-            for step in range(self.last):
+
+    def wait_up(self, steps):
+        for region in range(REGIONS):
+            for step in steps:
                 self.up(region, step, True).wait_send()
 
 
@@ -1660,7 +1663,8 @@
         own_move(source).wait()
         partial_move(source).wait_recv()
         ready[source] = jnp.transpose(own[source] + part[source]).astype(BF16)
-        at.send(*kv_move(source))
+        if i < n_ctx - 8:
+            at.send(*kv_move(source))
     for load in loads[1:]:
         load.wait()
     low_turned[...] = jnp.transpose(x_in[...]).astype(BF16)
@@ -1668,6 +1672,9 @@
         for region in range(REGIONS):
             feed.down(region, step - 1, False).wait_recv()
             feed.give(region, step, feed.landing[region % 2][step - 1])
+        if step == 1:
+            for i in range(n_ctx - 8, n_ctx):
+                at.send(*kv_move(at.turn(i, n_ctx)))
 
     for target in range(n_ctx):
         partial_move(target).wait_send()
@@ -1757,8 +1764,6 @@
             for step in order:
                 core_move(*step).start()
     vec_move(0).start()
-    for region in range(REGIONS):
-        feed.settle(region)
     for region, give in order:
         core_move(region, give).wait_recv()
         kept, given, rows, _ = last.ranges[region][0]
@@ -1785,16 +1790,21 @@
     for step in order:
         core_move(*step).wait_send()
     for region in range(REGIONS):
+        feed.settle(region)
+    for region in range(REGIONS):
         feed.up(region, 1, False).wait_recv()
         feed.up(region, 0, True).start()
-    for step in (1, 2):
-        for region in range(REGIONS):
-            last.down(region, step - 1, False).wait_recv()
-            last.give(region, step, last.landing[region % 2][step - 1])
-        vec_next(step)
+    for region in range(REGIONS):
+        last.down(region, 0, False).wait_recv()
+        last.give(region, 1, last.landing[region % 2][0])
+    vec_next(1)
     for region in range(REGIONS):
         feed.up(region, 0, False).wait_recv()
         top_move(region, True).start()
+    for region in range(REGIONS):
+        last.down(region, 1, False).wait_recv()
+        last.give(region, 2, last.landing[region % 2][1])
+    vec_next(2)
     for region in range(REGIONS):
         last.down(region, 2, False).wait_recv()
         last.give(region, 3, last.landing[region % 2][2])
@@ -1802,20 +1812,25 @@
     for region in range(REGIONS):
         last.settle(region)
     vec_next(4)
+    feed.wait_down()
     for step in (2, 1, 0):
         for region in range(REGIONS):
             last.up(region, step, False).wait_recv()
             if step > 0:
                 last.up(region, step - 1, True).start()
+        if step == 2:
+            last.wait_down()
+        if step == 1:
+            feed.wait_up((0, 1))
+            last.wait_up((1, 2))
+            for index in range(5):
+                vec_move(index).wait_send()
     for region in range(REGIONS):
         top_move(region, False).wait_recv()
 
-    for step in range(5):
-        vec_move(step).wait_send()
     for region in range(REGIONS):
         top_move(region, True).wait_send()
-    feed.wait_sent()
-    last.wait_sent()
+    last.wait_up((0,))
 
 
 def finish(n_ctx, dq, dkv, keep, land_a, land_b, x, entry, wq, wk, wv, w_other, vec_feed):

time: 223 us -> 220 us (0.987)
  Pallas kernels: 218 us -> 215 us
    pallas_call x1, Pallas kernels: 91.6 us -> 88.4 us  [finish(): pl.pallas_call(functools.partial(finish_kernel, n_ctx), out_shape=(jax.Sh...]
where the time goes in v8:
time: 220 us; the launch traced here: 219 us
  Pallas kernels  215 us (98%)
  starting transfers between devices  2.71 us (1%)
    pallas_call x1, Pallas kernels, finish(): pl.pallas_call(functools.partial(finish_kernel, n_ctx), out_shape=(jax.Sh...  88.4 us
    pallas_call x1, Pallas kernels, middle(): pl.pallas_call(functools.partial(middle_kernel, n_ctx), out_shape=(rows,...  45.9 us
    pallas_call x1, Pallas kernels, project_and_scatter(): pl.pallas_call(functools.partial(project_kernel, n_ctx), out_shape=(jax.S...  37 us
    pallas_call x1, Pallas kernels, attend_back(): pl.pallas_call(functools.partial(backward_kernel, blocks), out_shape=(jax...  20.5 us
    pallas_call x1, Pallas kernels, attend(): pl.pallas_call(functools.partial(forward_kernel, blocks), out_shape=(jax....  17.6 us
    pallas_call x1, Pallas kernels, unpack_grads(): pl.pallas_call(unpack_kernel, out_shape=tuple((jax.ShapeDtypeStruct(shape...  5.39 us
  transfers between devices with their start and end apart: 2, of which 0 were waited for; matrix products, arithmetic and copies ran while one was open for 0% of the time, Pallas kernels for 9%

profile of v8, /device:TPU:0, one launch (start us, length us, event | category | flops | bytes accessed | tf_op | source)
XLA Modules:
  0.0 219.3 jit_solution(16585755240717710886)
XLA Ops:
  0.7 37.0 %project_scatter.1 = (bf16[16,128,128]{2,1,0:T(8,128)(2,1)}, bf16[32,256,128]{2,1,0:T(8,128)(2,1)}, bf16[3,512,256]{2,1,0:T(8,128)(2,1)}, s32[1,32]{1,0:T(1,128)...) custom-call(f32[512,512]{1,0:T(8,128)} %bitcast.17, ...), custom_call_target="tpu_custom_call" | custom-call | tf_op jit(solution)/shard_map/project_scatter/pallas_call | solution.py:738
  37.6 17.6 %attend.1 = (bf16[16,2,64,128]{3,2,1,0:T(8,128)(2,1)}, f32[16,2,64,128]{3,2,1,0:T(8,128)}, f32[33,128,128]{2,1,0:T(8,128)}, s32[3,176]{1,0:T(4,128)}) custom-call(s32[1,32]{1,0:T(1,128)} %get-tuple-element.68.order_ref, s32[1,32]{1,0:T(1,128)} %get-tuple-element.69.seq_ref, bf16[16,128,128]{2,1,0:T(8,128)(2,1)} %get-tuple-element.70.q_ref, ...), custom_call_target="tpu_custom_call" | custom-call | tf_op jit(solution)/shard_map/attend/pallas_call | solution.py:928
  55.2 45.9 %middle.1 = (f32[512,512]{1,0:T(8,128)}, f32[512,512]{1,0:T(8,128)}, f32[512,512]{1,0:T(8,128)}, bf16[16,2,64,128]{3,2,1,0:T(8,128)(2,1)}, f32[16,512]{1,0:T(8,1...) custom-call(bf16[16,2,64,128]{3,2,1,0:T(8,128)(2,1)} %get-tuple-element.73.o_hbm, ...), custom_call_target="tpu_custom_call" | custom-call | tf_op jit(solution)/shard_map/middle/pallas_call | solution.py:1493
  101.1 0.5 collective-permute-start
  101.6 2.2 collective-permute-start.1
  103.8 20.5 %attend_back.1 = (bf16[16,128,128]{2,1,0:T(8,128)(2,1)}, f32[32,128,256]{2,1,0:T(8,128)}, f32[512,512]{1,0:T(8,128)}, f32[512,512]{1,0:T(8,128)}) custom-call(s32[3,176]{1,0:T(4,128)} %get-tuple-element.72.pairs_ref, bf16[16,128,128]{2,1,0:T(8,128)(2,1)} %get-tuple-element.70.q_ref, bf16[16,2,64,128]{3,2,1,0:T(8,128)(2,1)} %get-tuple-element.79.tan_ref, ...), custom_call_target="tpu_custom_call" | custom-call | tf_op jit(solution)/shard_map/attend_back/pallas_call | solution.py:1065
  124.3 0.0 collective-permute-done.land_a
  124.3 0.0 copy-start
  124.3 0.0 collective-permute-done.1.land_b
  124.3 0.0 copy-start.1
  124.3 0.8 copy-done
  125.1 0.2 copy-done.1
  125.3 88.4 %finish.1 = (f32[512,512]{1,0:T(8,128)}, bf16[2304,512]{1,0:T(8,128)(2,1)}, bf16[768,512]{1,0:T(8,128)(2,1)}, f32[24,512]{1,0:T(8,128)}) custom-call(bf16[16,128,128]{2,1,0:T(8,128)(2,1)} %get-tuple-element.85.dq_ref, f32[32,128,256]{2,1,0:T(8,128)} %get-tuple-element.86.dkv_ref, f32[2,576,512]{2,1,0:T(8,128)} %get-tuple-element.87.keep_hbm, ...), custom_call_target="tpu_custom_call" | custom-call | tf_op jit(solution)/shard_map/finish/pallas_call | solution.py:1844
  213.7 5.4 %unpack_grads.1 = (f32[512,256]{1,0:T(8,128)}, f32[512,256]{1,0:T(8,128)}, f32[512,256]{1,0:T(8,128)}, f32[256,512]{1,0:T(8,128)}, f32[512,1024]{1,0:T(8,128)}, ...) custom-call(bf16[2304,512]{1,0:T(8,128)(2,1)} %get-tuple-element.93., ...), custom_call_target="tpu_custom_call" | custom-call | tf_op jit(solution)/shard_map/unpack_grads/pallas_call | solution.py:1917
Async XLA Ops:
  101.1 23.2 %collective-permute-start = (bf16[576,512]{1,0:T(8,128)(2,1)}, bf16[576,512]{1,0:T(8,128)(2,1)S(1)}, u32[]{:S(2)}, u32[]{:S(2)}) collective-permute-start(bf16[576,512]{1,0:T(8,128)(2,1)} %get-tuple-element.88), channel_id=1, source_target_pairs={{0,2},{2,0},{4,6},{6,4},{8,10},{10,8},{12,14},{14,12},{16,18},{18,... | collective-permute-start | bytes 1769480 | tf_op jit(solution)/shard_map/ppermute | solution.py:1954
  101.6 22.7 %collective-permute-start.1 = (bf16[576,512]{1,0:T(8,128)(2,1)}, bf16[576,512]{1,0:T(8,128)(2,1)S(1)}, u32[]{:S(2)}, u32[]{:S(2)}) collective-permute-start(bf16[576,512]{1,0:T(8,128)(2,1)} %get-tuple-element.89), channel_id=1, source_target_pairs={{0,4},{2,6},{4,0},{6,2},{8,12},{10,14},{12,8},{14,10},{16,20},{18,... | collective-permute-start | bytes 1769480 | tf_op jit(solution)/shard_map/ppermute | solution.py:1954
  124.3 0.8 copy-start
  124.3 1.0 copy-start.1

commit v9 on v8

--- a/solution.py
+++ b/solution.py
@@ -13,7 +13,7 @@
 BLK = 256
 HALF = BLK // 2
 LONG = 8
-TOGETHER = 16
+TOGETHER = 32
 MOST = LONG + 1
 F32 = jnp.float32
 BF16 = jnp.bfloat16
@@ -642,45 +642,54 @@
         bias_own[VECTORS + part : VECTORS + part + 1, :] = piece.astype(F32).reshape(1, wide)
     swaps[-1].start()
 
-    def moves(half):
+    def kv_moves(half):
         for i in range(H // 2):
             head = half * (H // 2) + at.turn(i, H // 2)
             for core in range(2):
-                slot = head * 2 + core
                 yield (
                     kv_send.at[head, pl.ds(core * BLK, BLK)],
                     kv_out.at[2 * at.c + core],
-                    kv_ss.at[slot],
+                    kv_ss.at[head * 2 + core],
                     kv_rs.at[at.c],
                     at.f * H + head,
                     core,
                 )
+
+    def q_moves(half):
+        for i in range(H // 2):
+            head = half * (H // 2) + at.turn(i, H // 2)
+            for core in range(2):
                 yield (
                     q_send.at[head, core],
                     q_out.at[at.c],
-                    q_ss.at[slot],
+                    q_ss.at[head * 2 + core],
                     q_rs.at[at.c],
                     at.f * H + head,
                     core,
                 )
 
+    def heads_of(half):
+        for pair in range(2):
+            for side in range(2):
+                yield side, half * (H // 2) + 2 * pair + side, slice(pair * 128, pair * 128 + 128)
+
     def one_half(half, wq, wk, wv, bias):
         low = x_in[...].astype(BF16)
-        q = dot_nn(low, wq[...]) + bias[0:1, :]
         k = dot_nn(low, wk[...])
         v = dot_nn(low, wv[...]) + bias[1:2, :]
-        for pair in range(2):
-            columns = slice(pair * 128, pair * 128 + 128)
-            for side in range(2):
-                head = half * (H // 2) + 2 * pair + side
-                kv_send[head] = side_pair(side, k[:, columns], v[:, columns]).astype(BF16)
-                for core in range(2):
-                    rows = slice(core * HALF, core * HALF + HALF)
-                    late = slice(BLK + core * HALF, BLK + core * HALF + HALF)
-                    q_send[head, core] = side_pair(side, q[rows, columns], q[late, columns]).astype(
-                        BF16
-                    )
-        for move in moves(half):
+        for side, head, columns in heads_of(half):
+            kv_send[head] = side_pair(side, k[:, columns], v[:, columns]).astype(BF16)
+        for move in kv_moves(half):
+            at.send(*move)
+        q = dot_nn(low, wq[...]) + bias[0:1, :]
+        for side, head, columns in heads_of(half):
+            for core in range(2):
+                rows = slice(core * HALF, core * HALF + HALF)
+                late = slice(BLK + core * HALF, BLK + core * HALF + HALF)
+                q_send[head, core] = side_pair(side, q[rows, columns], q[late, columns]).astype(
+                    BF16
+                )
+        for move in q_moves(half):
             at.send(*move)
 
     one_half(at.f, w_own.at[0], w_own.at[1], w_own.at[2], bias_own)
@@ -718,7 +727,9 @@
         at.remote(arrived, arrived, kv_ss.at[0], kv_rs.at[source], at.c, other).wait_recv()
         relay(source).start()
     for half in (at.f, other):
-        for move in moves(half):
+        for move in kv_moves(half):
+            at.wait_sent(*move)
+        for move in q_moves(half):
             at.wait_sent(*move)
     for source in range(n_ctx):
         arrived = q_out.at[source]

time: 220 us -> 216 us (0.982)
  Pallas kernels: 215 us -> 211 us
where the time goes in v9:
time: 216 us; the launch traced here: 215 us
  Pallas kernels  211 us (98%)
  starting transfers between devices  2.7 us (1%)
    pallas_call x1, Pallas kernels, finish(): pl.pallas_call(functools.partial(finish_kernel, n_ctx), out_shape=(jax.Sh...  89 us
    pallas_call x1, Pallas kernels, middle(): pl.pallas_call(functools.partial(middle_kernel, n_ctx), out_shape=(rows,...  45.8 us
    pallas_call x1, Pallas kernels, project_and_scatter(): pl.pallas_call(functools.partial(project_kernel, n_ctx), out_shape=(jax.S...  34.9 us
    pallas_call x1, Pallas kernels, attend_back(): pl.pallas_call(functools.partial(backward_kernel, blocks), out_shape=(jax...  19.2 us
    pallas_call x1, Pallas kernels, attend(): pl.pallas_call(functools.partial(forward_kernel, blocks), out_shape=(jax....  16.4 us
    pallas_call x1, Pallas kernels, unpack_grads(): pl.pallas_call(unpack_kernel, out_shape=tuple((jax.ShapeDtypeStruct(shape...  5.39 us
  transfers between devices with their start and end apart: 2, of which 0 were waited for; matrix products, arithmetic and copies ran while one was open for 0% of the time, Pallas kernels for 9%

profile of v9, /device:TPU:0, one launch (start us, length us, event | category | flops | bytes accessed | tf_op | source)
XLA Modules:
  0.0 215.2 jit_solution(10554064698834612369)
XLA Ops:
  0.7 34.9 %project_scatter.1 = (bf16[16,128,128]{2,1,0:T(8,128)(2,1)}, bf16[32,256,128]{2,1,0:T(8,128)(2,1)}, bf16[3,512,256]{2,1,0:T(8,128)(2,1)}, s32[1,32]{1,0:T(1,128)...) custom-call(f32[512,512]{1,0:T(8,128)} %bitcast.17, ...), custom_call_target="tpu_custom_call" | custom-call | tf_op jit(solution)/shard_map/project_scatter/pallas_call | solution.py:749
  35.5 16.4 %attend.1 = (bf16[16,2,64,128]{3,2,1,0:T(8,128)(2,1)}, f32[16,2,64,128]{3,2,1,0:T(8,128)}, f32[33,128,128]{2,1,0:T(8,128)}, s32[3,208]{1,0:T(4,128)}) custom-call(s32[1,32]{1,0:T(1,128)} %get-tuple-element.68.order_ref, s32[1,32]{1,0:T(1,128)} %get-tuple-element.69.seq_ref, bf16[16,128,128]{2,1,0:T(8,128)(2,1)} %get-tuple-element.70.q_ref, ...), custom_call_target="tpu_custom_call" | custom-call | tf_op jit(solution)/shard_map/attend/pallas_call | solution.py:939
  52.0 45.8 %middle.1 = (f32[512,512]{1,0:T(8,128)}, f32[512,512]{1,0:T(8,128)}, f32[512,512]{1,0:T(8,128)}, bf16[16,2,64,128]{3,2,1,0:T(8,128)(2,1)}, f32[16,512]{1,0:T(8,1...) custom-call(bf16[16,2,64,128]{3,2,1,0:T(8,128)(2,1)} %get-tuple-element.73.o_hbm, ...), custom_call_target="tpu_custom_call" | custom-call | tf_op jit(solution)/shard_map/middle/pallas_call | solution.py:1504
  97.7 0.5 collective-permute-start
  98.3 2.2 %collective-permute-start.1 = (bf16[576,512]{1,0:T(8,128)(2,1)}, bf16[576,512]{1,0:T(8,128)(2,1)S(1)}, u32[]{:S(2)}, u32[]{:S(2)}) collective-permute-start(bf16[576,512]{1,0:T(8,128)(2,1)} %get-tuple-element.89), channel_id=1, source_target_pairs={{0,4},{2,6},{4,0},{6,2},{8,12},{10,14},{12,8},{14,10},{16,20},{18,... | collective-permute-start | bytes 1769480 | tf_op jit(solution)/shard_map/ppermute | solution.py:1965
  100.4 19.2 %attend_back.1 = (bf16[16,128,128]{2,1,0:T(8,128)(2,1)}, f32[32,128,256]{2,1,0:T(8,128)}, f32[512,512]{1,0:T(8,128)}, f32[512,512]{1,0:T(8,128)}) custom-call(s32[3,208]{1,0:T(4,128)} %get-tuple-element.72.pairs_ref, bf16[16,128,128]{2,1,0:T(8,128)(2,1)} %get-tuple-element.70.q_ref, bf16[16,2,64,128]{3,2,1,0:T(8,128)(2,1)} %get-tuple-element.79.tan_ref, ...), custom_call_target="tpu_custom_call" | custom-call | tf_op jit(solution)/shard_map/attend_back/pallas_call | solution.py:1076
  119.6 0.0 collective-permute-done.land_a
  119.6 0.0 copy-start
  119.6 0.0 collective-permute-done.1.land_b
  119.6 0.0 copy-start.1
  119.7 0.8 copy-done
  120.4 0.2 copy-done.1
  120.6 89.0 %finish.1 = (f32[512,512]{1,0:T(8,128)}, bf16[2304,512]{1,0:T(8,128)(2,1)}, bf16[768,512]{1,0:T(8,128)(2,1)}, f32[24,512]{1,0:T(8,128)}) custom-call(bf16[16,128,128]{2,1,0:T(8,128)(2,1)} %get-tuple-element.85.dq_ref, f32[32,128,256]{2,1,0:T(8,128)} %get-tuple-element.86.dkv_ref, f32[2,576,512]{2,1,0:T(8,128)} %get-tuple-element.87.keep_hbm, ...), custom_call_target="tpu_custom_call" | custom-call | tf_op jit(solution)/shard_map/finish/pallas_call | solution.py:1855
  209.6 5.4 %unpack_grads.1 = (f32[512,256]{1,0:T(8,128)}, f32[512,256]{1,0:T(8,128)}, f32[512,256]{1,0:T(8,128)}, f32[256,512]{1,0:T(8,128)}, f32[512,1024]{1,0:T(8,128)}, ...) custom-call(bf16[2304,512]{1,0:T(8,128)(2,1)} %get-tuple-element.93., ...), custom_call_target="tpu_custom_call" | custom-call | tf_op jit(solution)/shard_map/unpack_grads/pallas_call | solution.py:1928
Async XLA Ops:
  97.7 21.9 %collective-permute-start = (bf16[576,512]{1,0:T(8,128)(2,1)}, bf16[576,512]{1,0:T(8,128)(2,1)S(1)}, u32[]{:S(2)}, u32[]{:S(2)}) collective-permute-start(bf16[576,512]{1,0:T(8,128)(2,1)} %get-tuple-element.88), channel_id=1, source_target_pairs={{0,2},{2,0},{4,6},{6,4},{8,10},{10,8},{12,14},{14,12},{16,18},{18,... | collective-permute-start | bytes 1769480 | tf_op jit(solution)/shard_map/ppermute | solution.py:1965
  98.3 21.4 %collective-permute-start.1 = (bf16[576,512]{1,0:T(8,128)(2,1)}, bf16[576,512]{1,0:T(8,128)(2,1)S(1)}, u32[]{:S(2)}, u32[]{:S(2)}) collective-permute-start(bf16[576,512]{1,0:T(8,128)(2,1)} %get-tuple-element.89), channel_id=1, source_target_pairs={{0,4},{2,6},{4,0},{6,2},{8,12},{10,14},{12,8},{14,10},{16,20},{18,... | collective-permute-start | bytes 1769480 | tf_op jit(solution)/shard_map/ppermute | solution.py:1965
  119.6 0.8 copy-start
  119.6 1.0 copy-start.1

commit v10 on v9

--- a/solution.py
+++ b/solution.py
@@ -1461,9 +1461,6 @@
     for step in order:
         core_move(*step)[1].start()
     feed_slopes(0, own_grads, *operands)
-    for side in range(2):
-        for target in range(n_ctx):
-            at.wait_sent(*o_move(target, side))
     for region, give in order:
         start, move = core_move(region, give)
         move.wait_recv()
@@ -1485,6 +1482,9 @@
     for step in range(2):
         for store in stores(step):
             store.wait()
+    for side in range(2):
+        for target in range(n_ctx):
+            at.wait_sent(*o_move(target, side))
     for side in range(2):
         for head in range(H):
             for core in range(2):
@@ -1674,7 +1674,7 @@
         own_move(source).wait()
         partial_move(source).wait_recv()
         ready[source] = jnp.transpose(own[source] + part[source]).astype(BF16)
-        if i < n_ctx - 8:
+        if i < n_ctx - 6:
             at.send(*kv_move(source))
     for load in loads[1:]:
         load.wait()
@@ -1684,7 +1684,7 @@
             feed.down(region, step - 1, False).wait_recv()
             feed.give(region, step, feed.landing[region % 2][step - 1])
         if step == 1:
-            for i in range(n_ctx - 8, n_ctx):
+            for i in range(n_ctx - 6, n_ctx):
                 at.send(*kv_move(at.turn(i, n_ctx)))
 
     for target in range(n_ctx):

time: 216 us -> 216 us (level)
  no operation moved by 1% of the time
where the time goes in v10:
time: 216 us; the launch traced here: 215 us
  Pallas kernels  211 us (98%)
  starting transfers between devices  2.7 us (1%)
    pallas_call x1, Pallas kernels, finish(): pl.pallas_call(functools.partial(finish_kernel, n_ctx), out_shape=(jax.Sh...  89 us
    pallas_call x1, Pallas kernels, middle(): pl.pallas_call(functools.partial(middle_kernel, n_ctx), out_shape=(rows,...  45.8 us
    pallas_call x1, Pallas kernels, project_and_scatter(): pl.pallas_call(functools.partial(project_kernel, n_ctx), out_shape=(jax.S...  34.9 us
    pallas_call x1, Pallas kernels, attend_back(): pl.pallas_call(functools.partial(backward_kernel, blocks), out_shape=(jax...  19.2 us
    pallas_call x1, Pallas kernels, attend(): pl.pallas_call(functools.partial(forward_kernel, blocks), out_shape=(jax....  16.4 us
    pallas_call x1, Pallas kernels, unpack_grads(): pl.pallas_call(unpack_kernel, out_shape=tuple((jax.ShapeDtypeStruct(shape...  5.39 us
  transfers between devices with their start and end apart: 2, of which 0 were waited for; matrix products, arithmetic and copies ran while one was open for 0% of the time, Pallas kernels for 9%

profile of v10, /device:TPU:0, one launch (start us, length us, event | category | flops | bytes accessed | tf_op | source)
XLA Modules:
  0.0 215.3 jit_solution(18207789909755626134)
XLA Ops:
  0.7 34.9 %project_scatter.1 = (bf16[16,128,128]{2,1,0:T(8,128)(2,1)}, bf16[32,256,128]{2,1,0:T(8,128)(2,1)}, bf16[3,512,256]{2,1,0:T(8,128)(2,1)}, s32[1,32]{1,0:T(1,128)...) custom-call(f32[512,512]{1,0:T(8,128)} %bitcast.17, ...), custom_call_target="tpu_custom_call" | custom-call | tf_op jit(solution)/shard_map/project_scatter/pallas_call | solution.py:749
  35.5 16.4 %attend.1 = (bf16[16,2,64,128]{3,2,1,0:T(8,128)(2,1)}, f32[16,2,64,128]{3,2,1,0:T(8,128)}, f32[33,128,128]{2,1,0:T(8,128)}, s32[3,208]{1,0:T(4,128)}) custom-call(s32[1,32]{1,0:T(1,128)} %get-tuple-element.68.order_ref, s32[1,32]{1,0:T(1,128)} %get-tuple-element.69.seq_ref, bf16[16,128,128]{2,1,0:T(8,128)(2,1)} %get-tuple-element.70.q_ref, ...), custom_call_target="tpu_custom_call" | custom-call | tf_op jit(solution)/shard_map/attend/pallas_call | solution.py:939
  52.0 45.8 %middle.1 = (f32[512,512]{1,0:T(8,128)}, f32[512,512]{1,0:T(8,128)}, f32[512,512]{1,0:T(8,128)}, bf16[16,2,64,128]{3,2,1,0:T(8,128)(2,1)}, f32[16,512]{1,0:T(8,1...) custom-call(bf16[16,2,64,128]{3,2,1,0:T(8,128)(2,1)} %get-tuple-element.73.o_hbm, ...), custom_call_target="tpu_custom_call" | custom-call | tf_op jit(solution)/shard_map/middle/pallas_call | solution.py:1504
  97.8 0.5 collective-permute-start
  98.3 2.2 %collective-permute-start.1 = (bf16[576,512]{1,0:T(8,128)(2,1)}, bf16[576,512]{1,0:T(8,128)(2,1)S(1)}, u32[]{:S(2)}, u32[]{:S(2)}) collective-permute-start(bf16[576,512]{1,0:T(8,128)(2,1)} %get-tuple-element.89), channel_id=1, source_target_pairs={{0,4},{2,6},{4,0},{6,2},{8,12},{10,14},{12,8},{14,10},{16,20},{18,... | collective-permute-start | bytes 1769480 | tf_op jit(solution)/shard_map/ppermute | solution.py:1965
  100.5 19.2 %attend_back.1 = (bf16[16,128,128]{2,1,0:T(8,128)(2,1)}, f32[32,128,256]{2,1,0:T(8,128)}, f32[512,512]{1,0:T(8,128)}, f32[512,512]{1,0:T(8,128)}) custom-call(s32[3,208]{1,0:T(4,128)} %get-tuple-element.72.pairs_ref, bf16[16,128,128]{2,1,0:T(8,128)(2,1)} %get-tuple-element.70.q_ref, bf16[16,2,64,128]{3,2,1,0:T(8,128)(2,1)} %get-tuple-element.79.tan_ref, ...), custom_call_target="tpu_custom_call" | custom-call | tf_op jit(solution)/shard_map/attend_back/pallas_call | solution.py:1076
  119.7 0.0 collective-permute-done.land_a
  119.7 0.0 copy-start
  119.7 0.0 collective-permute-done.1.land_b
  119.7 0.0 copy-start.1
  119.7 0.8 copy-done
  120.5 0.2 copy-done.1
  120.7 89.0 %finish.1 = (f32[512,512]{1,0:T(8,128)}, bf16[2304,512]{1,0:T(8,128)(2,1)}, bf16[768,512]{1,0:T(8,128)(2,1)}, f32[24,512]{1,0:T(8,128)}) custom-call(bf16[16,128,128]{2,1,0:T(8,128)(2,1)} %get-tuple-element.85.dq_ref, f32[32,128,256]{2,1,0:T(8,128)} %get-tuple-element.86.dkv_ref, f32[2,576,512]{2,1,0:T(8,128)} %get-tuple-element.87.keep_hbm, ...), custom_call_target="tpu_custom_call" | custom-call | tf_op jit(solution)/shard_map/finish/pallas_call | solution.py:1855
  209.7 5.4 %unpack_grads.1 = (f32[512,256]{1,0:T(8,128)}, f32[512,256]{1,0:T(8,128)}, f32[512,256]{1,0:T(8,128)}, f32[256,512]{1,0:T(8,128)}, f32[512,1024]{1,0:T(8,128)}, ...) custom-call(bf16[2304,512]{1,0:T(8,128)(2,1)} %get-tuple-element.93., ...), custom_call_target="tpu_custom_call" | custom-call | tf_op jit(solution)/shard_map/unpack_grads/pallas_call | solution.py:1928
Async XLA Ops:
  97.8 21.9 %collective-permute-start = (bf16[576,512]{1,0:T(8,128)(2,1)}, bf16[576,512]{1,0:T(8,128)(2,1)S(1)}, u32[]{:S(2)}, u32[]{:S(2)}) collective-permute-start(bf16[576,512]{1,0:T(8,128)(2,1)} %get-tuple-element.88), channel_id=1, source_target_pairs={{0,2},{2,0},{4,6},{6,4},{8,10},{10,8},{12,14},{14,12},{16,18},{18,... | collective-permute-start | bytes 1769480 | tf_op jit(solution)/shard_map/ppermute | solution.py:1965
  98.3 21.4 %collective-permute-start.1 = (bf16[576,512]{1,0:T(8,128)(2,1)}, bf16[576,512]{1,0:T(8,128)(2,1)S(1)}, u32[]{:S(2)}, u32[]{:S(2)}) collective-permute-start(bf16[576,512]{1,0:T(8,128)(2,1)} %get-tuple-element.89), channel_id=1, source_target_pairs={{0,4},{2,6},{4,0},{6,2},{8,12},{10,14},{12,8},{14,10},{16,20},{18,... | collective-permute-start | bytes 1769480 | tf_op jit(solution)/shard_map/ppermute | solution.py:1965
  119.7 0.8 copy-start
  119.7 1.0 copy-start.1
